TPU v7x, 256 devices: a whole 4x4x8 slice. The times are simulated.
256 devices in a mesh: batch: 2 (over z_lo), seq: 128 (over z_hi, y, x, core).
Axes of the slice: x: 4, y: 4, z: 8 (z_hi: 4, z_lo: 2; z = z_hi * 2 + z_lo), core: 2. Of those that a mesh axis runs over, the one named last changes fastest.
Arguments:
- signal: bfloat16 [2, 262144, 384], P('batch', 'seq'), may hold values from -6 to 6
- conv_weight: float32 [4, 384], replicated, may hold values from -2.5 to 2.5
- first_factor: bfloat16 [512, 512, 512], P('seq'), may hold values from -0.25 to 0.25
- second_factor: bfloat16 [512, 512, 512], P('seq'), may hold values from -0.25 to 0.25
- grad_output: bfloat16 [2, 262144, 384], P('batch', 'seq'), may hold values from -3 to 3
Outputs:
- grad_signal: bfloat16 [2, 262144, 384], P('batch', 'seq')
- grad_first: bfloat16 [512, 512, 512], P('seq', 'batch')
- grad_second: bfloat16 [512, 512, 512], P('seq', 'batch')
All inputs are finite; a program needn't handle non-finite values.
Results may differ from a plain program's by a relative error of at most 0.0065.
Values may be sent and summed in bfloat16 or wider, within the bound.
A program may use at most 128 MiB of HBM per device.

v0:
```python
import jax
import jax.numpy as jnp
from jax import lax
from jax.sharding import PartitionSpec as P


def passed_along(value, axis, steps):
    count = lax.axis_size(axis)
    initial, last = (max(0, -steps), min(count, count - steps))
    return lax.ppermute(value, axis, [(source, source + steps) for source in range(initial, last)])


def body(signal, conv_weight, first_factor, second_factor, grad_output):
    seq_count, tok_rows, channels = signal.shape
    blocks = first_factor.shape[0]
    block_order = first_factor.shape[1]
    col_blocks = second_factor.shape[0]
    block_count = second_factor.shape[1]
    tap_count = conv_weight.shape[0]
    previous = passed_along(signal[:, tok_rows - (tap_count - 1) :, :], "seq", 1)
    padded_in = jnp.concatenate([previous, signal], axis=1).astype(jnp.float32)
    conv_out = sum(
        (
            conv_weight[r][None, None, :]
            * padded_in[:, tap_count - 1 - r : tap_count - 1 - r + tok_rows, :]
            for r in range(tap_count)
        )
    )
    gate_val = jax.nn.sigmoid(conv_out)
    hidden = (conv_out * gate_val).astype(jnp.bfloat16)
    hidden_blocks = hidden.reshape(seq_count, blocks, block_order, channels)
    mixed = jnp.einsum(
        "ikj,sijd->sikd", first_factor, hidden_blocks, preferred_element_type=jnp.float32
    ).astype(jnp.bfloat16)
    columns = lax.all_to_all(mixed, "seq", split_axis=2, concat_axis=1, tiled=True)
    upstream = grad_output.reshape(seq_count, col_blocks, block_count, channels)
    grad_mixed = jnp.einsum(
        "kmi,skmd->sikd", second_factor, upstream, preferred_element_type=jnp.float32
    ).astype(jnp.bfloat16)
    grad_second = jnp.einsum(
        "skmd,sikd->kmi", upstream, columns, preferred_element_type=jnp.float32
    )
    grad_rows = lax.all_to_all(grad_mixed, "seq", split_axis=1, concat_axis=2, tiled=True)
    grad_hidden = jnp.einsum(
        "ikj,sikd->sijd", first_factor, grad_rows, preferred_element_type=jnp.float32
    ).reshape(seq_count, tok_rows, channels)
    grad_conv = (grad_hidden * gate_val * (1.0 + conv_out * (1.0 - gate_val))).astype(jnp.bfloat16)
    following = passed_along(grad_conv[:, : tap_count - 1, :], "seq", -1)
    extended = jnp.concatenate([grad_conv, following], axis=1).astype(jnp.float32)
    grad_signal = sum(
        (conv_weight[r][None, None, :] * extended[:, r : r + tok_rows, :] for r in range(tap_count))
    ).astype(jnp.bfloat16)
    grad_first = jnp.einsum(
        "sikd,sijd->ikj", grad_rows, hidden_blocks, preferred_element_type=jnp.float32
    )
    total_first, total_second = (
        lax.psum(grad_first.astype(jnp.bfloat16), "batch").astype(jnp.float32),
        lax.psum(grad_second.astype(jnp.bfloat16), "batch").astype(jnp.float32),
    )
    batch_index = lax.axis_index("batch")
    half_first = total_first.shape[1] // lax.axis_size("batch")
    half_second = total_second.shape[1] // lax.axis_size("batch")
    share_first = lax.dynamic_slice_in_dim(total_first, batch_index * half_first, half_first, 1)
    share_second = lax.dynamic_slice_in_dim(total_second, batch_index * half_second, half_second, 1)
    return (grad_signal, share_first.astype(jnp.bfloat16), share_second.astype(jnp.bfloat16))


def solution(mesh):
    placed = (
        P("batch", "seq", None),
        P(),
        P("seq", None, None),
        P("seq", None, None),
        P("batch", "seq", None),
    )
    return jax.shard_map(
        body,
        mesh=mesh,
        in_specs=placed,
        out_specs=(P("batch", "seq", None), P("seq", "batch", None), P("seq", "batch", None)),
        check_vma=False,
    )
```

profile of v0, /device:TPU:1, one launch (start us, length us, event | category | flops | bytes accessed | tf_op | source)
XLA Modules:
  0.0 269.5 jit_solution(10913673899404368837)
XLA Ops:
  7.2 4.4 %fusion.9 = bf16[1,512,4,384]{1,3,2,0:T(8,128)(2,1)} fusion(bf16[4,512,384]{2,1,0:T(8,128)(2,1)} %bitcast.39, bf16[4,512,512]{2,1,0:T(8,128)(2,1)} %param.8), kind=kOutput, calls=%fused_computation.29 | convolution fusion | flops 806092800 | bytes 5242880 | tf_op jit(solution)/shard_map/kmi,skmd->sikd/dot_general | solution.py:37
  11.6 3.8 %copy.25 = bf16[1,512,4,384]{3,2,0,1:T(4,128)(2,1)} copy(bf16[1,512,4,384]{1,3,2,0:T(8,128)(2,1)} %fusion.9) | data formatting | bytes 3145728 | tf_op jit(solution)/shard_map/convert_element_type | solution.py:39
  15.3 16.9 %all-to-all-start = ((bf16[1,512,4,384]{3,2,0,1:T(4,128)(2,1)}), bf16[1,512,4,384]{3,2,0,1:T(4,128)(2,1)}, u32[]{:S(2)}, u32[]{:S(2)}) async-start(bf16[1,512,4,384]{3,2,0,1:T(4,128)(2,1)} %copy.25), calls=%async_computation | async-start | bytes 3145728 | tf_op jit(solution)/shard_map/all_to_all | solution.py:43
  33.0 3.5 %collective-permute-start = (bf16[1,3,384]{2,1,0:T(4,128)(2,1)S(1)}, bf16[1,3,384]{2,1,0:T(4,128)(2,1)S(1)}, u32[]{:S(2)}, u32[]{:S(2)}) collective-permute-start(bf16[1,3,384]{2,1,0:T(4,128)(2,1)S(1)} %slice.47), channel_id=1, source_target_pairs={{0,1},{1,2},{2,3},{3,4},{4,5},{5,6},{6,7},{7,8},{8,9},{9,10},{10,1... | collective-permute-start | bytes 6920 | tf_op jit(solution)/shard_map/ppermute | solution.py:10
  37.2 1.7 maximum_convert_fusion
  39.0 3.1 %multiply_convert_fusion = (bf16[1,2048,384]{2,1,0:T(8,128)(2,1)S(1)}, f32[1,2048,384]{2,1,0:T(8,128)}) fusion(f32[1,2051,384]{2,1,0:T(8,128)S(1)} %maximum_convert_fusion, f32[384]{0:T(512)S(1)} %get-tuple-element.14, f32[384]{0:T(512)S(1)} %get-tuple-element.15, f32[384]{0:T(512)S(1)} %get-tuple-element.13, f32[384]{0:T(512)S(1)} %get-tuple-element.12), kind=kLoop, calls=%fused_computation.18 | loop fusion | flops 9437184 | bytes 17307648 | tf_op jit(solution)/shard_map/convert_element_type | solution.py:30
  43.3 2.3 fusion.10
  45.6 3.8 %copy.31 = bf16[1,4,512,384]{3,1,0,2:T(4,128)(2,1)} copy(bf16[1,4,512,384]{2,3,1,0:T(8,128)(2,1)} %fusion.10) | data formatting | bytes 3145728 | tf_op jit(solution)/shard_map/convert_element_type | solution.py:34
  49.4 23.6 %all-to-all-done = bf16[1,512,4,384]{3,2,0,1:T(4,128)(2,1)} async-done(((bf16[1,512,4,384]{3,2,0,1:T(4,128)(2,1)}), bf16[1,512,4,384]{3,2,0,1:T(4,128)(2,1)}, u32[]{:S(2)}, u32[]{:S(2)}) %all-to-all-start) | async-done | bytes 1572896 | tf_op jit(solution)/shard_map/all_to_all | solution.py:43
  73.0 17.0 %all-to-all-start.1 = ((bf16[1,4,512,384]{3,1,0,2:T(4,128)(2,1)}), bf16[1,4,512,384]{3,1,0,2:T(4,128)(2,1)}, u32[]{:S(2)}, u32[]{:S(2)}) async-start(bf16[1,4,512,384]{3,1,0,2:T(4,128)(2,1)} %copy.31), calls=%async_computation.1 | async-start | bytes 3145728 | tf_op jit(solution)/shard_map/all_to_all | solution.py:35
  90.2 2.1 copy.26
  93.5 2.6 convolution_convert_fusion
  96.1 30.5 %all-to-all-done.1 = bf16[1,4,512,384]{3,1,0,2:T(4,128)(2,1)} async-done(((bf16[1,4,512,384]{3,1,0,2:T(4,128)(2,1)}), bf16[1,4,512,384]{3,1,0,2:T(4,128)(2,1)}, u32[]{:S(2)}, u32[]{:S(2)}) %all-to-all-start.1) | async-done | bytes 1572896 | tf_op jit(solution)/shard_map/all_to_all | solution.py:35
  126.6 3.1 %copy.32 = bf16[1,128,4,4,384]{4,2,1,3,0:T(4,128)(2,1)} copy(bf16[1,128,4,4,384]{4,2,3,1,0:T(4,128)(2,1)} %bitcast.13) | data formatting | bytes 3145728 | tf_op jit(solution)/shard_map/all_to_all | solution.py:35
  129.7 3.7 %reshape.110 = bf16[512,4,384]{2,0,1:T(8,128)(2,1)} reshape(bf16[1,128,4,4,384]{4,2,1,3,0:T(4,128)(2,1)} %copy.32) | data formatting | bytes 3145728 | tf_op jit(solution)/shard_map/reshape.23
  133.4 4.6 %convert_bitcast_fusion = bf16[4,512,512]{1,2,0:T(8,128)(2,1)} fusion(bf16[512,4,384]{2,0,1:T(8,128)(2,1)} %reshape.110, bf16[4,512,384]{2,1,0:T(8,128)(2,1)} %bitcast.40), kind=kOutput, calls=%fused_computation.21 | convolution fusion | flops 806354944 | bytes 5242880 | tf_op jit(solution)/shard_map/skmd,sikd->kmi/dot_general | solution.py:40
  138.0 4.1 %convolution_bitcast_fusion = f32[1,4,512,384]{2,3,1,0:T(8,128)} fusion(bf16[4,512,512]{2,1,0:T(8,128)(2,1)S(1)} %copy-done, bf16[4,512,384]{2,0,1:T(4,128)(2,1)} %bitcast.42), kind=kOutput, calls=%fused_computation.24 | convolution fusion | flops 805306368 | bytes 6815744 | tf_op jit(solution)/shard_map/ikj,sikd->sijd/dot_general | solution.py:44
  142.2 3.6 %copy.28 = f32[1,4,512,384]{3,2,1,0:T(8,128)} copy(f32[1,4,512,384]{2,3,1,0:T(8,128)} %convolution_bitcast_fusion) | data formatting | bytes 6291456 | tf_op jit(solution)/shard_map/ikj,sikd->sijd/transpose | solution.py:44
  145.7 4.0 %fusion.8 = bf16[1,2048,384]{2,1,0:T(8,128)(2,1)S(1)} fusion(f32[1,4,512,384]{3,2,1,0:T(8,128)} %copy.28, f32[1,2048,384]{2,1,0:T(8,128)} %get-tuple-element.19), kind=kLoop, calls=%fused_computation.17 | loop fusion | flops 7077888 | bytes 7864320 | tf_op jit(solution)/shard_map/convert_element_type | solution.py:47
  150.8 10.2 %collective-permute-start.1 = (bf16[1,3,384]{2,1,0:T(4,128)(2,1)S(1)}, bf16[1,3,384]{2,1,0:T(4,128)(2,1)S(1)}, u32[]{:S(2)}, u32[]{:S(2)}) collective-permute-start(bf16[1,3,384]{2,1,0:T(4,128)(2,1)S(1)} %slice.64), channel_id=1, source_target_pairs={{1,0},{2,1},{3,2},{4,3},{5,4},{6,5},{7,6},{8,7},{9,8},{10,9},{11,1... | collective-permute-start | bytes 6920 | tf_op jit(solution)/shard_map/ppermute | solution.py:10
  161.9 1.6 maximum_convert_fusion.1
  163.5 2.5 fusion.1
  166.1 91.7 %all-reduce.3.cloned.1.call-done = (bf16[4,512,512]{2,1,0:T(8,128)(2,1)}, bf16[4,512,512]{1,2,0:T(8,128)(2,1)}) async-done(((bf16[4,512,512]{2,1,0:T(8,128)(2,1)}, bf16[4,512,512]{1,2,0:T(8,128)(2,1)}), (bf16[4,512,512]{2,1,0:T(8,128)(2,1)}, bf16[4,512,512]{1,2,0:T(8,128)(2,1)})) %all-reduce.3.cloned.1.call-update) | async-done | bytes 4194320 | tf_op jit(solution)/shard_map/psum | solution.py:57
  260.4 2.3 convert_convert_fusion.1
  (21 shorter events, 8.6 us)
Async XLA Ops:
  7.2 36.1 %copy-start = (bf16[4,512,512]{2,1,0:T(8,128)(2,1)S(1)}, bf16[4,512,512]{2,1,0:T(8,128)(2,1)}, u32[]{:S(2)}) copy-start(bf16[4,512,512]{2,1,0:T(8,128)(2,1)} %param.7) | copy-start | bytes 6291460
  15.3 21.2 %copy-start.5 = (f32[4,384]{1,0:T(4,128)S(1)}, f32[4,384]{1,0:T(4,128)}, u32[]{:S(2)}) copy-start(f32[4,384]{1,0:T(4,128)} %param.6) | copy-start | bytes 18436
  15.3 57.7 %all-to-all-start = ((bf16[1,512,4,384]{3,2,0,1:T(4,128)(2,1)}), bf16[1,512,4,384]{3,2,0,1:T(4,128)(2,1)}, u32[]{:S(2)}, u32[]{:S(2)}) async-start(bf16[1,512,4,384]{3,2,0,1:T(4,128)(2,1)} %copy.25), calls=%async_computation | async-start | bytes 3145728 | tf_op jit(solution)/shard_map/all_to_all | solution.py:43
  33.0 4.3 %collective-permute-start = (bf16[1,3,384]{2,1,0:T(4,128)(2,1)S(1)}, bf16[1,3,384]{2,1,0:T(4,128)(2,1)S(1)}, u32[]{:S(2)}, u32[]{:S(2)}) collective-permute-start(bf16[1,3,384]{2,1,0:T(4,128)(2,1)S(1)} %slice.47), channel_id=1, source_target_pairs={{0,1},{1,2},{2,3},{3,4},{4,5},{5,6},{6,7},{7,8},{8,9},{9,10},{10,1... | collective-permute-start | bytes 6920 | tf_op jit(solution)/shard_map/ppermute | solution.py:10
  42.1 1.2 copy-start.3
  73.0 53.6 %all-to-all-start.1 = ((bf16[1,4,512,384]{3,1,0,2:T(4,128)(2,1)}), bf16[1,4,512,384]{3,1,0,2:T(4,128)(2,1)}, u32[]{:S(2)}, u32[]{:S(2)}) async-start(bf16[1,4,512,384]{3,1,0,2:T(4,128)(2,1)} %copy.31), calls=%async_computation.1 | async-start | bytes 3145728 | tf_op jit(solution)/shard_map/all_to_all | solution.py:35
  90.0 167.8 %all-reduce.3.cloned.1.call-start = ((), (), s32[]{:S(2)}) async-start(), calls=%async_computation.2 | async-start | bytes 8388608 | tf_op jit(solution)/shard_map/psum | solution.py:57
  90.2 3.3 %copy-start.4 = (bf16[1,2048,384]{2,1,0:T(8,128)(2,1)S(1)}, bf16[1,2048,384]{2,1,0:T(8,128)(2,1)}, u32[]{:S(2)}) copy-start(bf16[1,2048,384]{2,1,0:T(8,128)(2,1)} %copy-done.3) | copy-start | bytes 4718596
  92.4 1.1 copy-start.2
  149.7 1.1 copy-start.1
  150.8 11.1 %collective-permute-start.1 = (bf16[1,3,384]{2,1,0:T(4,128)(2,1)S(1)}, bf16[1,3,384]{2,1,0:T(4,128)(2,1)S(1)}, u32[]{:S(2)}, u32[]{:S(2)}) collective-permute-start(bf16[1,3,384]{2,1,0:T(4,128)(2,1)S(1)} %slice.64), channel_id=1, source_target_pairs={{1,0},{2,1},{3,2},{4,3},{5,4},{6,5},{7,6},{8,7},{9,8},{10,9},{11,1... | collective-permute-start | bytes 6920 | tf_op jit(solution)/shard_map/ppermute | solution.py:10
Sparse Core Ops, SparseCore 0:
  138.2 119.5 all-reduce.2
where the time goes:
time: 270 us
  waiting for transfers between devices  147 us (54%)
  starting transfers between devices  47.9 us (18%)
  local copies, waits for them, and re-layouts  25.7 us (10%)
  matrix products  18 us (7%)
  other arithmetic  16.5 us (6%)
  between operations  14.1 us (5%)
    psum x1, waiting for transfers between devices, body(): lax.psum(grad_first.astype(jnp.bfloat16), 'batch').astype(jnp.float32)  91.7 us
    all_to_all x1, waiting for transfers between devices, body(): lax.all_to_all(mixed, 'seq', split_axis=2, concat_axis=1, tiled=True)  30.5 us
    all_to_all x1, waiting for transfers between devices, body(): lax.all_to_all(grad_mixed, 'seq', split_axis=1, concat_axis=2, tiled=True)  23.6 us
    all_to_all x1, starting transfers between devices, body(): lax.all_to_all(mixed, 'seq', split_axis=2, concat_axis=1, tiled=True)  17 us
    all_to_all x1, starting transfers between devices, body(): lax.all_to_all(grad_mixed, 'seq', split_axis=1, concat_axis=2, tiled=True)  16.9 us
    ppermute x2, starting transfers between devices, passed_along(): lax.ppermute(value, axis, [(source, source + steps) for source in range(i...  13.8 us
  transfers between devices with their start and end apart: 5, of which 5 were waited for; matrix products, arithmetic and copies ran while one was open for 12% of the time, Pallas kernels for 0%

commit v1 on v0

v1 whole, which is shorter than its diff:
```python
import jax
import jax.numpy as jnp
from jax import lax
from jax.sharding import PartitionSpec as P


def passed_along(value, axis, steps):
    count = lax.axis_size(axis)
    initial, last = (max(0, -steps), min(count, count - steps))
    return lax.ppermute(value, axis, [(source, source + steps) for source in range(initial, last)])


def body(signal, conv_weight, first_factor, second_factor, grad_output):
    seq_count, tok_rows, channels = signal.shape
    blocks = first_factor.shape[0]
    block_order = first_factor.shape[1]
    col_blocks = second_factor.shape[0]
    block_count = second_factor.shape[1]
    tap_count = conv_weight.shape[0]
    peers = lax.axis_size("seq")
    previous = passed_along(signal[:, tok_rows - (tap_count - 1) :, :], "seq", 1)
    padded_in = jnp.concatenate([previous, signal], axis=1).astype(jnp.float32)
    conv_out = sum(
        (
            conv_weight[r][None, None, :]
            * padded_in[:, tap_count - 1 - r : tap_count - 1 - r + tok_rows, :]
            for r in range(tap_count)
        )
    )
    gate_val = jax.nn.sigmoid(conv_out)
    hidden = (conv_out * gate_val).astype(jnp.bfloat16)
    hidden_blocks = hidden.reshape(seq_count, blocks, block_order, channels)
    first_split = first_factor.reshape(blocks, peers, col_blocks, block_order)
    mixed_chunks = jnp.einsum(
        "ipqj,sijd->psiqd", first_split, hidden_blocks, preferred_element_type=jnp.float32
    ).astype(jnp.bfloat16)
    upstream = grad_output.reshape(seq_count, col_blocks, block_count, channels)
    second_split = second_factor.reshape(col_blocks, block_count, peers, blocks)
    grad_chunks = jnp.einsum(
        "kmpi,skmd->psikd", second_split, upstream, preferred_element_type=jnp.float32
    ).astype(jnp.bfloat16)
    sent = jnp.stack([mixed_chunks, grad_chunks], axis=1)
    got = lax.all_to_all(sent, "seq", split_axis=0, concat_axis=0, tiled=True)
    columns = got[:, 0]
    grad_rows = got[:, 1]
    halves = lax.axis_size("batch")
    me = lax.axis_index("batch")
    other = halves - 1 - me
    rows_half = block_count // halves
    peers_half = peers // halves

    def second_part(half):
        up = lax.dynamic_slice_in_dim(upstream, half * rows_half, rows_half, 2)
        return jnp.einsum(
            "skmd,psikd->kmpi", up, columns, preferred_element_type=jnp.float32
        ).reshape(col_blocks, rows_half, peers * blocks).astype(jnp.bfloat16)

    def first_part(half):
        gr = lax.dynamic_slice_in_dim(grad_rows, half * peers_half, peers_half, 0)
        return jnp.einsum(
            "psiqd,sijd->ipqj", gr, hidden_blocks, preferred_element_type=jnp.float32
        ).reshape(blocks, peers_half * col_blocks, block_order).astype(jnp.bfloat16)

    swap = [(0, 1), (1, 0)]
    sent_second = lax.ppermute(second_part(other), "batch", swap)
    sent_first = lax.ppermute(first_part(other), "batch", swap)
    grad_hidden = jnp.einsum(
        "ipqj,psiqd->sijd", first_split, grad_rows, preferred_element_type=jnp.float32
    ).reshape(seq_count, tok_rows, channels)
    part_second = (
        second_part(me).astype(jnp.float32) + sent_second.astype(jnp.float32)
    ).astype(jnp.bfloat16)
    part_first = (
        first_part(me).astype(jnp.float32) + sent_first.astype(jnp.float32)
    ).astype(jnp.bfloat16)
    grad_conv = (grad_hidden * gate_val * (1.0 + conv_out * (1.0 - gate_val))).astype(jnp.bfloat16)
    following = passed_along(grad_conv[:, : tap_count - 1, :], "seq", -1)
    extended = jnp.concatenate([grad_conv, following], axis=1).astype(jnp.float32)
    grad_signal = sum(
        (conv_weight[r][None, None, :] * extended[:, r : r + tok_rows, :] for r in range(tap_count))
    ).astype(jnp.bfloat16)
    return (grad_signal, part_first, part_second)


def solution(mesh):
    placed = (
        P("batch", "seq", None),
        P(),
        P("seq", None, None),
        P("seq", None, None),
        P("batch", "seq", None),
    )
    return jax.shard_map(
        body,
        mesh=mesh,
        in_specs=placed,
        out_specs=(P("batch", "seq", None), P("seq", "batch", None), P("seq", "batch", None)),
        check_vma=False,
    )
```

time: 270 us -> 190 us (0.70)
  waiting for transfers between devices: 147 us -> 90.7 us
  starting transfers between devices: 47.9 us -> 27.6 us
  between operations: 14.1 us -> 0.83 us
  local copies, waits for them, and re-layouts: 25.7 us -> 37.1 us
    psum x1 -> x0, waiting for transfers between devices: 91.7 us -> none  [body(): lax.psum(grad_first.astype(jnp.bfloat16), 'batch').astype(jnp.float32)]
    all_to_all x2 -> x1, waiting for transfers between devices: 54.1 us -> 73.9 us  [body(): got = lax.all_to_all(sent, 'seq', split_axis=0, concat_axis=0, tiled=True)]
    all_to_all x2 -> x1, starting transfers between devices: 33.9 us -> 15.1 us  [body(): got = lax.all_to_all(sent, 'seq', split_axis=0, concat_axis=0, tiled=True)]
    ppermute x0 -> x2, waiting for transfers between devices: none -> 16.7 us  [the longest x1 16.7 us: body(): sent_second = lax.ppermute(second_part(other), 'batch', swap)]
    unnamed x13 -> x22, local copies, waits for them, and re-layouts: 4.84 us -> 11 us
    all_to_all x2 -> x0, local copies, waits for them, and re-layouts: 5.24 us -> none  [the longest x1 3.09 us: body(): lax.all_to_all(mixed, 'seq', split_axis=2, concat_axis=1, tiled=True)]
    ppermute x2, starting transfers between devices: 13.8 us -> 8.88 us  [passed_along(): lax.ppermute(value, axis, [(source, source + steps) for source in range(i...]
    slice x0 -> x1, local copies, waits for them, and re-layouts: none -> 4.65 us  [body(): columns = got[:, 0]]
  transfers between devices with their start and end apart: 5 -> 5, of which waited for: 5 -> 2; matrix products, arithmetic and copies ran while one was open for 12% -> 19% of each run, Pallas kernels for 0% -> 0%
where the time goes in v1:
time: 190 us; the launch traced here: 188 us
  waiting for transfers between devices  90.7 us (48%)
  local copies, waits for them, and re-layouts  37.1 us (20%)
  starting transfers between devices  27.6 us (15%)
  matrix products  16.8 us (9%)
  other arithmetic  14.8 us (8%)
    all_to_all x1, waiting for transfers between devices, body(): got = lax.all_to_all(sent, 'seq', split_axis=0, concat_axis=0, tiled=True)  73.9 us
    ppermute x1, waiting for transfers between devices, body(): sent_second = lax.ppermute(second_part(other), 'batch', swap)  16.7 us
    all_to_all x1, starting transfers between devices, body(): got = lax.all_to_all(sent, 'seq', split_axis=0, concat_axis=0, tiled=True)  15.1 us
    unnamed x22, local copies, waits for them, and re-layouts  11 us
    ppermute x2, starting transfers between devices, passed_along(): lax.ppermute(value, axis, [(source, source + steps) for source in range(i...  8.88 us
    another operation x1, local copies, waits for them, and re-layouts, body(): sent = jnp.stack([mixed_chunks, grad_chunks], axis=1)  6.29 us
    dot_general x1, matrix products, body(): jnp.einsum('kmpi,skmd->psikd', second_split, upstream, preferred_element_...  5.63 us
    slice x1, local copies, waits for them, and re-layouts, body(): columns = got[:, 0]  4.65 us
  transfers between devices with their start and end apart: 5, of which 2 were waited for; matrix products, arithmetic and copies ran while one was open for 19% of the time, Pallas kernels for 0%

profile of v1, /device:TPU:1, one launch (start us, length us, event | category | flops | bytes accessed | tf_op | source)
XLA Modules:
  0.0 187.7 jit_solution(17297493227538673372)
XLA Ops:
  1.5 4.5 %collective-permute-start = (bf16[1,3,384]{2,1,0:T(4,128)(2,1)S(1)}, bf16[1,3,384]{2,1,0:T(4,128)(2,1)S(1)}, u32[]{:S(2)}, u32[]{:S(2)}) collective-permute-start(bf16[1,3,384]{2,1,0:T(4,128)(2,1)S(1)} %slice.53), channel_id=1, source_target_pairs={{0,1},{1,2},{2,3},{3,4},{4,5},{5,6},{6,7},{7,8},{8,9},{9,10},{10,1... | collective-permute-start | bytes 6920 | tf_op jit(solution)/shard_map/ppermute | solution.py:10
  6.0 4.5 %copy.36 = bf16[4,512,512]{1,0,2:T(4,128)(2,1)} copy(bf16[4,512,512]{2,1,0:T(8,128)(2,1)} %param.8) | data formatting | bytes 4194304 | tf_op args[3]
  10.5 5.6 %fusion.39 = bf16[128,1,1,4,4,384]{0,5,4,3,2,1:T(8,128)(2,1)} fusion(bf16[4,512,384,1]{2,1,0,3:T(8,128)(2,1)S(1)} %bitcast.85, bf16[4,512,128,4]{1,0,3,2:T(4,128)(2,1)} %bitcast.91), kind=kOutput, calls=%fused_computation.49 | convolution fusion | flops 806092800 | bytes 5242880 | tf_op jit(solution)/shard_map/kmpi,skmd->psikd/dot_general | solution.py:39
  16.2 4.1 %reshape.143 = bf16[4,128,4,512]{3,2,1,0:T(4,128)(2,1)} reshape(bf16[4,512,512]{2,1,0:T(8,128)(2,1)} %param.7) | data formatting | bytes 4194304 | tf_op jit(solution)/shard_map/reshape | solution.py:33
  20.6 3.1 %multiply_convert_fusion = (bf16[1,2048,384]{2,1,0:T(8,128)(2,1)S(1)}, f32[1,2048,384]{2,1,0:T(8,128)}) fusion(f32[1,2051,384]{2,1,0:T(8,128)S(1)} %maximum_convert_fusion, f32[384]{0:T(512)S(1)} %get-tuple-element.11, f32[384]{0:T(512)S(1)} %get-tuple-element.12, f32[384]{0:T(512)S(1)} %get-tuple-element.10, f32[384]{0:T(512)S(1)} %get-tuple-element.9), kind=kLoop, calls=%fused_computation.19 | loop fusion | flops 9437184 | bytes 17307648 | tf_op jit(solution)/shard_map/convert_element_type | solution.py:31
  25.7 2.0 %pad_maximum_fusion = bf16[128,2,1,4,4,384]{0,5,4,3,2,1:T(8,128)(2,1)} fusion(bf16[128,1,1,4,4,384]{0,5,4,3,2,1:T(8,128)(2,1)S(1)} %copy-done.7, bf16[128,1,1,4,4,384]{0,5,4,3,2,1:T(8,128)(2,1)S(1)} %fusion.42), kind=kLoop, calls=%fused_computation.15 | loop fusion | flops 1572864 | bytes 6291456 | tf_op jit(solution)/shard_map/stack | solution.py:42
  27.6 6.3 %copy.40 = bf16[128,2,1,4,4,384]{5,4,3,2,1,0:T(4,128)(2,1)} copy(bf16[128,2,1,4,4,384]{0,5,4,3,2,1:T(8,128)(2,1)} %pad_maximum_fusion) | data formatting | bytes 6291456 | tf_op jit(solution)/shard_map/stack | solution.py:42
  33.9 15.1 %all-to-all-start = ((bf16[128,2,1,4,4,384]{5,4,3,2,1,0:T(4,128)(2,1)}), bf16[128,2,1,4,4,384]{5,4,3,2,1,0:T(4,128)(2,1)}, u32[]{:S(2)}, u32[]{:S(2)}) async-start(bf16[128,2,1,4,4,384]{5,4,3,2,1,0:T(4,128)(2,1)} %copy.40), calls=%async_computation | async-start | bytes 6291456 | tf_op jit(solution)/shard_map/all_to_all | solution.py:43
  49.0 73.9 %all-to-all-done = bf16[128,2,1,4,4,384]{5,4,3,2,1,0:T(4,128)(2,1)} async-done(((bf16[128,2,1,4,4,384]{5,4,3,2,1,0:T(4,128)(2,1)}), bf16[128,2,1,4,4,384]{5,4,3,2,1,0:T(4,128)(2,1)}, u32[]{:S(2)}, u32[]{:S(2)}) %all-to-all-start) | async-done | bytes 3145760 | tf_op jit(solution)/shard_map/all_to_all | solution.py:43
  123.0 4.7 %fusion.54 = (bf16[128,1,1,4,4,384]{5,4,3,2,1,0:T(4,128)(2,1)}, bf16[128,1,1,4,4,384]{5,4,3,2,1,0:T(4,128)(2,1)}) fusion(bf16[128,2,1,4,4,384]{5,4,3,2,1,0:T(4,128)(2,1)} %all-to-all-done), kind=kLoop, calls=%fused_computation.63 | loop fusion | bytes 6291456 | tf_op jit(solution)/shard_map/slice | solution.py:44
  127.6 3.0 %copy.65 = bf16[128,1,1,4,4,384]{0,5,4,3,2,1:T(8,128)(2,1)S(1)} copy(bf16[128,1,1,4,4,384]{5,4,3,2,1,0:T(4,128)(2,1)} %get-tuple-element.16) | data formatting | bytes 3145728
  130.6 4.5 %convolution_bitcast_fusion = f32[1,4,512,384]{2,3,1,0:T(8,128)} fusion(bf16[4,128,4,512]{3,2,1,0:T(4,128)(2,1)} %reshape.143, bf16[128,1,1,4,4,384]{0,5,4,3,2,1:T(8,128)(2,1)S(1)} %copy.65), kind=kOutput, calls=%fused_computation.27 | convolution fusion | flops 805306368 | bytes 6815744 | tf_op jit(solution)/shard_map/ipqj,psiqd->sijd/dot_general | solution.py:67
  135.1 1.9 %fusion.36 = bf16[4,64,4,512]{3,1,2,0:T(8,128)(2,1)S(1)} fusion(bf16[4,512,384,1]{2,1,3,0:T(8,128)(2,1)S(1)} %bitcast.89, bf16[128,1,1,4,4,384]{0,5,4,3,2,1:T(8,128)(2,1)S(1)} %copy.65, s32[]{:T(128)S(6)} %select_n.13), kind=kOutput, calls=%fused_computation.48 | convolution fusion | flops 403177472 | bytes 4194308 | tf_op jit(solution)/shard_map/psiqd,sijd->ipqj/dot_general | solution.py:60
  137.0 1.8 copy.47
  138.8 2.7 %collective-permute-start.2 = (bf16[4,256,512]{2,0,1:T(4,128)(2,1)}, bf16[4,256,512]{2,0,1:T(4,128)(2,1)}, u32[]{:S(2)}, u32[]{:S(2)}) collective-permute-start(bf16[4,256,512]{2,0,1:T(4,128)(2,1)} %bitcast.24), channel_id=1, source_target_pairs={{0,128},{128,0},{1,129},{129,1},{2,130},{130,2},{3,131},{131,3},{4... | collective-permute-start | bytes 3145736 | tf_op jit(solution)/shard_map/ppermute | solution.py:66
  141.5 1.9 %fusion.33 = f32[4,64,4,512]{3,1,2,0:T(8,128)S(1)} fusion(bf16[4,512,384,1]{2,1,3,0:T(8,128)(2,1)S(1)} %bitcast.90, bf16[128,1,1,4,4,384]{0,5,4,3,2,1:T(8,128)(2,1)S(1)} %copy.65, s32[]{:T(128)S(6)} %select_n.12), kind=kOutput, calls=%fused_computation.47 | convolution fusion | flops 403701760 | bytes 5242884 | tf_op jit(solution)/shard_map/psiqd,sijd->ipqj/dot_general | solution.py:60
  143.4 2.7 %copy.45 = f32[4,64,4,512]{3,0,2,1:T(4,128)} copy(f32[4,64,4,512]{3,1,2,0:T(8,128)S(1)} %fusion.33) | data formatting | bytes 4194304 | tf_op jit(solution)/shard_map/convert_element_type | solution.py:74
  146.1 3.6 %copy.43 = f32[1,4,512,384]{3,2,1,0:T(8,128)} copy(f32[1,4,512,384]{2,3,1,0:T(8,128)} %convolution_bitcast_fusion) | data formatting | bytes 6291456 | tf_op jit(solution)/shard_map/ipqj,psiqd->sijd/transpose | solution.py:67
  149.7 4.1 %fusion.8 = bf16[1,2048,384]{2,1,0:T(8,128)(2,1)S(1)} fusion(f32[1,4,512,384]{3,2,1,0:T(8,128)} %copy.43, f32[1,2048,384]{2,1,0:T(8,128)} %get-tuple-element.14), kind=kLoop, calls=%fused_computation.18 | loop fusion | flops 7077888 | bytes 7864320 | tf_op jit(solution)/shard_map/convert_element_type | solution.py:76
  153.7 4.4 %collective-permute-start.1 = (bf16[1,3,384]{2,1,0:T(4,128)(2,1)S(1)}, bf16[1,3,384]{2,1,0:T(4,128)(2,1)S(1)}, u32[]{:S(2)}, u32[]{:S(2)}) collective-permute-start(bf16[1,3,384]{2,1,0:T(4,128)(2,1)S(1)} %slice.73), channel_id=1, source_target_pairs={{1,0},{2,1},{3,2},{4,3},{5,4},{6,5},{7,6},{8,7},{9,8},{10,9},{11,1... | collective-permute-start | bytes 6920 | tf_op jit(solution)/shard_map/ppermute | solution.py:10
  162.9 2.5 %fusion.1 = bf16[1,2048,384]{2,1,0:T(8,128)(2,1)} fusion(f32[1,2051,384]{2,1,0:T(8,128)S(1)} %maximum_convert_fusion.1, f32[384]{0:T(512)S(1)} %get-tuple-element.11, f32[384]{0:T(512)S(1)} %get-tuple-element.12, f32[384]{0:T(512)S(1)} %get-tuple-element.10, f32[384]{0:T(512)S(1)} %get-tuple-element.9), kind=kLoop, calls=%fused_computation.2 | loop fusion | flops 6291456 | bytes 14161920 | tf_op jit(solution)/shard_map/convert_element_type | solution.py:81
  165.5 1.9 %fusion.10 = bf16[4,256,512]{2,0,1:T(4,128)(2,1)S(1)} fusion(f32[4,64,4,512]{3,0,2,1:T(4,128)S(1)} %copy-done.4, bf16[4,256,512]{2,0,1:T(4,128)(2,1)} %collective-permute-done.2), kind=kLoop, calls=%fused_computation.24 | loop fusion | flops 1572864 | bytes 4194304 | tf_op jit(solution)/shard_map/convert_element_type | solution.py:75
  168.6 16.7 %collective-permute-done.3 = bf16[4,256,512]{1,0,2:T(4,128)(2,1)S(1)} collective-permute-done((bf16[4,256,512]{1,0,2:T(4,128)(2,1)S(1)}, bf16[4,256,512]{1,0,2:T(4,128)(2,1)S(1)}, u32[]{:S(2)}, u32[]{:S(2)}) %collective-permute-start.3) | collective-permute-done | bytes 1048608 | tf_op jit(solution)/shard_map/ppermute | solution.py:65
  186.0 1.7 copy.52
  (34 shorter events, 9.8 us)
Async XLA Ops:
  0.6 9.8 %copy-start = (bf16[1,2048,384]{2,1,0:T(8,128)(2,1)S(1)}, bf16[1,2048,384]{2,1,0:T(8,128)(2,1)}, u32[]{:S(2)}) copy-start(bf16[1,2048,384]{2,1,0:T(8,128)(2,1)} %param.9) | copy-start | bytes 4718596
  1.5 18.8 %collective-permute-start = (bf16[1,3,384]{2,1,0:T(4,128)(2,1)S(1)}, bf16[1,3,384]{2,1,0:T(4,128)(2,1)S(1)}, u32[]{:S(2)}, u32[]{:S(2)}) collective-permute-start(bf16[1,3,384]{2,1,0:T(4,128)(2,1)S(1)} %slice.53), channel_id=1, source_target_pairs={{0,1},{1,2},{2,3},{3,4},{4,5},{5,6},{6,7},{7,8},{8,9},{9,10},{10,1... | collective-permute-start | bytes 6920 | tf_op jit(solution)/shard_map/ppermute | solution.py:10
  10.5 5.6 %copy-start.8 = (f32[4,384]{1,0:T(4,128)S(1)}, f32[4,384]{1,0:T(4,128)}, u32[]{:S(2)}) copy-start(f32[4,384]{1,0:T(4,128)} %param.6) | copy-start | bytes 18436
  16.1 4.1 %copy-start.6 = (bf16[1,2048,384]{2,1,0:T(8,128)(2,1)S(1)}, bf16[1,2048,384]{2,1,0:T(8,128)(2,1)}, u32[]{:S(2)}) copy-start(bf16[1,2048,384]{2,1,0:T(8,128)(2,1)} %param.5) | copy-start | bytes 4718596
  20.6 3.1 %copy-start.3 = (bf16[4,128,4,512]{3,2,1,0:T(4,128)(2,1)S(1)}, bf16[4,128,4,512]{3,2,1,0:T(4,128)(2,1)}, u32[]{:S(2)}) copy-start(bf16[4,128,4,512]{3,2,1,0:T(4,128)(2,1)} %reshape.143) | copy-start | bytes 6291460
  23.7 1.4 copy-start.1
  23.7 2.0 %copy-start.7 = (bf16[128,1,1,4,4,384]{0,5,4,3,2,1:T(8,128)(2,1)S(1)}, bf16[128,1,1,4,4,384]{0,5,4,3,2,1:T(8,128)(2,1)}, u32[]{:S(2)}) copy-start(bf16[128,1,1,4,4,384]{0,5,4,3,2,1:T(8,128)(2,1)} %fusion.39) | copy-start | bytes 4718596
  33.9 89.1 %all-to-all-start = ((bf16[128,2,1,4,4,384]{5,4,3,2,1,0:T(4,128)(2,1)}), bf16[128,2,1,4,4,384]{5,4,3,2,1,0:T(4,128)(2,1)}, u32[]{:S(2)}, u32[]{:S(2)}) async-start(bf16[128,2,1,4,4,384]{5,4,3,2,1,0:T(4,128)(2,1)} %copy.40), calls=%async_computation | async-start | bytes 6291456 | tf_op jit(solution)/shard_map/all_to_all | solution.py:43
  130.6 4.5 %copy-start.2 = (bf16[1,2048,384]{2,1,0:T(8,128)(2,1)S(1)}, bf16[1,2048,384]{2,1,0:T(8,128)(2,1)}, u32[]{:S(2)}) copy-start(bf16[1,2048,384]{2,1,0:T(8,128)(2,1)} %copy-done.1) | copy-start | bytes 4718596
  138.8 26.7 %collective-permute-start.2 = (bf16[4,256,512]{2,0,1:T(4,128)(2,1)}, bf16[4,256,512]{2,0,1:T(4,128)(2,1)}, u32[]{:S(2)}, u32[]{:S(2)}) collective-permute-start(bf16[4,256,512]{2,0,1:T(4,128)(2,1)} %bitcast.24), channel_id=1, source_target_pairs={{0,128},{128,0},{1,129},{129,1},{2,130},{130,2},{3,131},{131,3},{4... | collective-permute-start | bytes 3145736 | tf_op jit(solution)/shard_map/ppermute | solution.py:66
  149.7 8.5 %copy-start.5 = (bf16[128,1,1,4,4,384]{5,4,3,2,1,0:T(4,128)(2,1)S(1)}, bf16[128,1,1,4,4,384]{5,4,3,2,1,0:T(4,128)(2,1)}, u32[]{:S(2)}) copy-start(bf16[128,1,1,4,4,384]{5,4,3,2,1,0:T(4,128)(2,1)} %get-tuple-element.15) | copy-start | bytes 4718596
  153.7 9.0 %collective-permute-start.1 = (bf16[1,3,384]{2,1,0:T(4,128)(2,1)S(1)}, bf16[1,3,384]{2,1,0:T(4,128)(2,1)S(1)}, u32[]{:S(2)}, u32[]{:S(2)}) collective-permute-start(bf16[1,3,384]{2,1,0:T(4,128)(2,1)S(1)} %slice.73), channel_id=1, source_target_pairs={{1,0},{2,1},{3,2},{4,3},{5,4},{6,5},{7,6},{8,7},{9,8},{10,9},{11,1... | collective-permute-start | bytes 6920 | tf_op jit(solution)/shard_map/ppermute | solution.py:10
  159.7 25.6 %collective-permute-start.3 = (bf16[4,256,512]{1,0,2:T(4,128)(2,1)S(1)}, bf16[4,256,512]{1,0,2:T(4,128)(2,1)S(1)}, u32[]{:S(2)}, u32[]{:S(2)}) collective-permute-start(bf16[4,256,512]{1,0,2:T(4,128)(2,1)S(1)} %bitcast.92), channel_id=1, source_target_pairs={{0,128},{128,0},{1,129},{129,1},{2,130},{130,2},{3,131},{131,3},{4... | collective-permute-start | bytes 3145736 | tf_op jit(solution)/shard_map/ppermute | solution.py:65
  162.9 2.6 %copy-start.4 = (f32[4,64,4,512]{3,0,2,1:T(4,128)S(1)}, f32[4,64,4,512]{3,0,2,1:T(4,128)}, u32[]{:S(2)}) copy-start(f32[4,64,4,512]{3,0,2,1:T(4,128)} %copy.45) | copy-start | bytes 6291460

commit v2 on v1

--- a/solution.py
+++ b/solution.py
@@ -39,10 +39,8 @@
     grad_chunks = jnp.einsum(
         "kmpi,skmd->psikd", second_split, upstream, preferred_element_type=jnp.float32
     ).astype(jnp.bfloat16)
-    sent = jnp.stack([mixed_chunks, grad_chunks], axis=1)
-    got = lax.all_to_all(sent, "seq", split_axis=0, concat_axis=0, tiled=True)
-    columns = got[:, 0]
-    grad_rows = got[:, 1]
+    grad_rows = lax.all_to_all(grad_chunks, "seq", split_axis=0, concat_axis=0, tiled=True)
+    columns = lax.all_to_all(mixed_chunks, "seq", split_axis=0, concat_axis=0, tiled=True)
     halves = lax.axis_size("batch")
     me = lax.axis_index("batch")
     other = halves - 1 - me

time: 190 us -> 172 us (0.905)
  waiting for transfers between devices: 90.7 us -> 52.1 us
  starting transfers between devices: 27.6 us -> 51.8 us
  local copies, waits for them, and re-layouts: 37.1 us -> 34.2 us
    all_to_all x1 -> x2, waiting for transfers between devices: 73.9 us -> 28.3 us  [the longest x1 20.2 us: body(): lax.all_to_all(grad_chunks, 'seq', split_axis=0, concat_axis=0, tiled=True)]
    all_to_all x1 -> x2, starting transfers between devices: 15.1 us -> 34 us  [the longest x1 17.4 us: body(): lax.all_to_all(mixed_chunks, 'seq', split_axis=0, concat_axis=0, tiled=True)]
    ppermute x1, starting transfers between devices: 0.86 us -> 8.31 us  [body(): sent_second = lax.ppermute(second_part(other), 'batch', swap)]
    convert_element_type x0 -> x2, local copies, waits for them, and re-layouts: none -> 6.41 us  [the longest x1 3.95 us: body(): mixed_chunks = jnp.einsum('ipqj,sijd->psiqd', first_split, hidden_blocks,...]
    another operation x1 -> x0, local copies, waits for them, and re-layouts: 6.29 us -> none  [body(): sent = jnp.stack([mixed_chunks, grad_chunks], axis=1)]
    slice x1 -> x0, local copies, waits for them, and re-layouts: 4.65 us -> none  [body(): columns = got[:, 0]]
    ppermute x1, waiting for transfers between devices: 0.01 us -> 4.52 us  [body(): sent_first = lax.ppermute(first_part(other), 'batch', swap)]
    dot_general x2, matrix products: 1.51 us -> 4.32 us  [second_part(): jnp.einsum('skmd,psikd->kmpi', up, columns, preferred_element_type=jnp.fl...]
  transfers between devices with their start and end apart: 5 -> 6, of which waited for: 2 -> 4; matrix products, arithmetic and copies ran while one was open for 19% -> 29% of each run, Pallas kernels for 0% -> 0%
where the time goes in v2:
time: 172 us; the launch traced here: 171 us
  waiting for transfers between devices  52.1 us (30%)
  starting transfers between devices  51.8 us (30%)
  local copies, waits for them, and re-layouts  34.2 us (20%)
  matrix products  17.7 us (10%)
  other arithmetic  14.1 us (8%)
    all_to_all x1, waiting for transfers between devices, body(): lax.all_to_all(grad_chunks, 'seq', split_axis=0, concat_axis=0, tiled=True)  20.2 us
    ppermute x1, waiting for transfers between devices, body(): sent_second = lax.ppermute(second_part(other), 'batch', swap)  19.3 us
    all_to_all x1, starting transfers between devices, body(): lax.all_to_all(mixed_chunks, 'seq', split_axis=0, concat_axis=0, tiled=True)  17.4 us
    all_to_all x1, starting transfers between devices, body(): lax.all_to_all(grad_chunks, 'seq', split_axis=0, concat_axis=0, tiled=True)  16.5 us
    unnamed x15, local copies, waits for them, and re-layouts  9.54 us
    ppermute x1, starting transfers between devices, body(): sent_second = lax.ppermute(second_part(other), 'batch', swap)  8.31 us
    all_to_all x1, waiting for transfers between devices, body(): lax.all_to_all(mixed_chunks, 'seq', split_axis=0, concat_axis=0, tiled=True)  8.1 us
    ppermute x2, starting transfers between devices, passed_along(): lax.ppermute(value, axis, [(source, source + steps) for source in range(i...  6.85 us
  transfers between devices with their start and end apart: 6, of which 4 were waited for; matrix products, arithmetic and copies ran while one was open for 29% of the time, Pallas kernels for 0%

profile of v2, /device:TPU:1, one launch (start us, length us, event | category | flops | bytes accessed | tf_op | source)
XLA Modules:
  0.0 170.8 jit_solution(16030517863060255524)
XLA Ops:
  0.6 4.6 %copy.34 = bf16[4,512,512]{1,0,2:T(4,128)(2,1)} copy(bf16[4,512,512]{2,1,0:T(8,128)(2,1)} %param.8) | data formatting | bytes 4194304 | tf_op args[3]
  5.3 4.5 %fusion.44 = bf16[128,1,4,4,384]{0,4,2,3,1:T(8,128)(2,1)S(1)} fusion(bf16[4,512,384,1]{2,1,3,0:T(8,128)(2,1)S(1)} %bitcast.81, bf16[4,512,128,4]{1,0,3,2:T(4,128)(2,1)} %bitcast.87), kind=kOutput, calls=%fused_computation.47 | convolution fusion | flops 806092800 | bytes 5242880 | tf_op jit(solution)/shard_map/kmpi,skmd->psikd/dot_general | solution.py:39
  9.7 2.5 %copy.37 = bf16[128,1,4,4,384]{4,2,3,1,0:T(4,128)(2,1)} copy(bf16[128,1,4,4,384]{0,4,2,3,1:T(8,128)(2,1)S(1)} %fusion.44) | data formatting | bytes 3145728 | tf_op jit(solution)/shard_map/convert_element_type | solution.py:41
  12.2 16.5 %all-to-all-start = ((bf16[128,1,4,4,384]{4,2,3,1,0:T(4,128)(2,1)}), bf16[128,1,4,4,384]{4,2,3,1,0:T(4,128)(2,1)S(1)}, u32[]{:S(2)}, u32[]{:S(2)}) async-start(bf16[128,1,4,4,384]{4,2,3,1,0:T(4,128)(2,1)} %copy.37), calls=%async_computation | async-start | bytes 3145728 | tf_op jit(solution)/shard_map/all_to_all | solution.py:42
  29.4 3.5 %collective-permute-start = (bf16[1,3,384]{2,1,0:T(4,128)(2,1)S(1)}, bf16[1,3,384]{2,1,0:T(4,128)(2,1)S(1)}, u32[]{:S(2)}, u32[]{:S(2)}) collective-permute-start(bf16[1,3,384]{2,1,0:T(4,128)(2,1)S(1)} %slice.47), channel_id=1, source_target_pairs={{0,1},{1,2},{2,3},{3,4},{4,5},{5,6},{6,7},{7,8},{8,9},{9,10},{10,1... | collective-permute-start | bytes 6920 | tf_op jit(solution)/shard_map/ppermute | solution.py:10
  33.0 4.0 %reshape.138 = bf16[4,128,4,512]{3,2,1,0:T(4,128)(2,1)} reshape(bf16[4,512,512]{2,1,0:T(8,128)(2,1)} %param.7) | data formatting | bytes 4194304 | tf_op jit(solution)/shard_map/reshape | solution.py:33
  38.8 3.1 %multiply_convert_fusion = (bf16[1,2048,384]{2,1,0:T(8,128)(2,1)S(1)}, f32[1,2048,384]{2,1,0:T(8,128)}) fusion(f32[1,2051,384]{2,1,0:T(8,128)S(1)} %maximum_convert_fusion, f32[384]{0:T(512)S(1)} %get-tuple-element.11, f32[384]{0:T(512)S(1)} %get-tuple-element.12, f32[384]{0:T(512)S(1)} %get-tuple-element.10, f32[384]{0:T(512)S(1)} %get-tuple-element.9), kind=kLoop, calls=%fused_computation.18 | loop fusion | flops 9437184 | bytes 17307648 | tf_op jit(solution)/shard_map/convert_element_type | solution.py:31
  43.0 2.6 %fusion.41 = bf16[128,1,4,4,384]{0,4,3,2,1:T(8,128)(2,1)} fusion(bf16[4,512,384,1]{2,1,3,0:T(8,128)(2,1)S(1)} %bitcast.84, bf16[4,128,4,512]{3,2,1,0:T(4,128)(2,1)S(1)} %copy-done.3), kind=kOutput, calls=%fused_computation.46 | convolution fusion | flops 806092800 | bytes 5242880 | tf_op jit(solution)/shard_map/ipqj,sijd->psiqd/dot_general | solution.py:34
  45.6 4.0 %copy.47 = bf16[128,1,4,4,384]{4,3,2,1,0:T(4,128)(2,1)} copy(bf16[128,1,4,4,384]{0,4,3,2,1:T(8,128)(2,1)} %fusion.41) | data formatting | bytes 3145728 | tf_op jit(solution)/shard_map/convert_element_type | solution.py:36
  49.5 20.2 %all-to-all-done = bf16[128,1,4,4,384]{4,2,3,1,0:T(4,128)(2,1)S(1)} async-done(((bf16[128,1,4,4,384]{4,2,3,1,0:T(4,128)(2,1)}), bf16[128,1,4,4,384]{4,2,3,1,0:T(4,128)(2,1)S(1)}, u32[]{:S(2)}, u32[]{:S(2)}) %all-to-all-start) | async-done | bytes 1572896 | tf_op jit(solution)/shard_map/all_to_all | solution.py:42
  69.7 17.4 %all-to-all-start.1 = ((bf16[128,1,4,4,384]{4,3,2,1,0:T(4,128)(2,1)}), bf16[128,1,4,4,384]{4,3,2,1,0:T(4,128)(2,1)}, u32[]{:S(2)}, u32[]{:S(2)}) async-start(bf16[128,1,4,4,384]{4,3,2,1,0:T(4,128)(2,1)} %copy.47), calls=%async_computation.1 | async-start | bytes 3145728 | tf_op jit(solution)/shard_map/all_to_all | solution.py:43
  89.4 2.7 %copy.42 = f32[4,64,4,512]{3,0,2,1:T(4,128)} copy(f32[4,64,4,512]{3,1,2,0:T(8,128)S(1)} %fusion.37) | data formatting | bytes 4194304 | tf_op jit(solution)/shard_map/convert_element_type | solution.py:72
  94.6 2.7 %collective-permute-start.2 = (bf16[4,256,512]{2,0,1:T(4,128)(2,1)}, bf16[4,256,512]{2,0,1:T(4,128)(2,1)}, u32[]{:S(2)}, u32[]{:S(2)}) collective-permute-start(bf16[4,256,512]{2,0,1:T(4,128)(2,1)} %bitcast.18), channel_id=1, source_target_pairs={{0,128},{128,0},{1,129},{129,1},{2,130},{130,2},{3,131},{131,3},{4... | collective-permute-start | bytes 3145736 | tf_op jit(solution)/shard_map/ppermute | solution.py:64
  97.3 2.8 %copy.38 = bf16[128,1,4,4,384]{0,4,2,3,1:T(8,128)(2,1)} copy(bf16[128,1,4,4,384]{4,2,3,1,0:T(4,128)(2,1)S(1)} %all-to-all-done) | data formatting | bytes 3145728 | tf_op jit(solution)/shard_map/all_to_all | solution.py:42
  100.0 4.8 %fusion.17 = f32[1,4,512,384]{2,3,1,0:T(8,128)} fusion(bf16[4,128,4,512]{3,2,1,0:T(4,128)(2,1)} %reshape.138, bf16[128,1,4,4,384]{0,4,2,3,1:T(8,128)(2,1)} %copy.38), kind=kOutput, calls=%fused_computation.30 | convolution fusion | flops 805306368 | bytes 6815744 | tf_op jit(solution)/shard_map/ipqj,psiqd->sijd/dot_general | solution.py:65
  104.9 3.6 %copy.40 = f32[1,4,512,384]{3,2,1,0:T(8,128)} copy(f32[1,4,512,384]{2,3,1,0:T(8,128)} %fusion.17) | data formatting | bytes 6291456 | tf_op jit(solution)/shard_map/ipqj,psiqd->sijd/transpose | solution.py:65
  108.4 4.0 %fusion.8 = bf16[1,2048,384]{2,1,0:T(8,128)(2,1)S(1)} fusion(f32[1,4,512,384]{3,2,1,0:T(8,128)} %copy.40, f32[1,2048,384]{2,1,0:T(8,128)} %get-tuple-element.14), kind=kLoop, calls=%fused_computation.17 | loop fusion | flops 7077888 | bytes 7864320 | tf_op jit(solution)/shard_map/convert_element_type | solution.py:74
  112.4 3.3 %collective-permute-start.1 = (bf16[1,3,384]{2,1,0:T(4,128)(2,1)S(1)}, bf16[1,3,384]{2,1,0:T(4,128)(2,1)S(1)}, u32[]{:S(2)}, u32[]{:S(2)}) collective-permute-start(bf16[1,3,384]{2,1,0:T(4,128)(2,1)S(1)} %slice.64), channel_id=1, source_target_pairs={{1,0},{2,1},{3,2},{4,3},{5,4},{6,5},{7,6},{8,7},{9,8},{10,9},{11,1... | collective-permute-start | bytes 6920 | tf_op jit(solution)/shard_map/ppermute | solution.py:10
  115.7 8.1 %all-to-all-done.1 = bf16[128,1,4,4,384]{4,3,2,1,0:T(4,128)(2,1)} async-done(((bf16[128,1,4,4,384]{4,3,2,1,0:T(4,128)(2,1)}), bf16[128,1,4,4,384]{4,3,2,1,0:T(4,128)(2,1)}, u32[]{:S(2)}, u32[]{:S(2)}) %all-to-all-start.1) | async-done | bytes 1572896 | tf_op jit(solution)/shard_map/all_to_all | solution.py:43
  126.8 8.3 %collective-permute-start.3 = (bf16[4,256,512]{1,0,2:T(4,128)(2,1)S(1)}, bf16[4,256,512]{1,0,2:T(4,128)(2,1)S(1)}, u32[]{:S(2)}, u32[]{:S(2)}) collective-permute-start(bf16[4,256,512]{1,0,2:T(4,128)(2,1)S(1)} %bitcast.88), channel_id=1, source_target_pairs={{0,128},{128,0},{1,129},{129,1},{2,130},{130,2},{3,131},{131,3},{4... | collective-permute-start | bytes 3145736 | tf_op jit(solution)/shard_map/ppermute | solution.py:63
  135.3 2.2 %fusion.38 = f32[4,256,128,4]{1,2,3,0:T(8,128)S(1)} fusion(bf16[128,1,4,4,384]{4,3,2,1,0:T(4,128)(2,1)} %all-to-all-done.1, bf16[1,4,512,384]{3,2,1,0:T(8,128)(2,1)S(1)} %bitcast.82, s32[]{:T(128)S(6)} %select_n.14), kind=kOutput, calls=%fused_computation.45 | convolution fusion | flops 403701760 | bytes 4456452 | tf_op jit(solution)/shard_map/skmd,psikd->kmpi/dot_general | solution.py:52
  138.9 2.5 %fusion.1 = bf16[1,2048,384]{2,1,0:T(8,128)(2,1)} fusion(f32[1,2051,384]{2,1,0:T(8,128)S(1)} %maximum_convert_fusion.1, f32[384]{0:T(512)S(1)} %get-tuple-element.11, f32[384]{0:T(512)S(1)} %get-tuple-element.12, f32[384]{0:T(512)S(1)} %get-tuple-element.10, f32[384]{0:T(512)S(1)} %get-tuple-element.9), kind=kLoop, calls=%fused_computation.2 | loop fusion | flops 6291456 | bytes 14161920 | tf_op jit(solution)/shard_map/convert_element_type | solution.py:79
  141.4 4.5 %collective-permute-done.2 = bf16[4,256,512]{2,0,1:T(4,128)(2,1)} collective-permute-done((bf16[4,256,512]{2,0,1:T(4,128)(2,1)}, bf16[4,256,512]{2,0,1:T(4,128)(2,1)}, u32[]{:S(2)}, u32[]{:S(2)}) %collective-permute-start.2) | collective-permute-done | bytes 1048608 | tf_op jit(solution)/shard_map/ppermute | solution.py:64
  149.0 19.3 %collective-permute-done.3 = bf16[4,256,512]{1,0,2:T(4,128)(2,1)S(1)} collective-permute-done((bf16[4,256,512]{1,0,2:T(4,128)(2,1)S(1)}, bf16[4,256,512]{1,0,2:T(4,128)(2,1)S(1)}, u32[]{:S(2)}, u32[]{:S(2)}) %collective-permute-start.3) | collective-permute-done | bytes 1048608 | tf_op jit(solution)/shard_map/ppermute | solution.py:63
  (30 shorter events, 18.4 us)
Async XLA Ops:
  0.6 4.6 %copy-start = (bf16[1,2048,384]{2,1,0:T(8,128)(2,1)S(1)}, bf16[1,2048,384]{2,1,0:T(8,128)(2,1)}, u32[]{:S(2)}) copy-start(bf16[1,2048,384]{2,1,0:T(8,128)(2,1)} %param.9) | copy-start | bytes 4718596
  12.2 20.8 %copy-start.5 = (f32[4,384]{1,0:T(4,128)S(1)}, f32[4,384]{1,0:T(4,128)}, u32[]{:S(2)}) copy-start(f32[4,384]{1,0:T(4,128)} %param.6) | copy-start | bytes 18436
  12.2 57.6 %all-to-all-start = ((bf16[128,1,4,4,384]{4,2,3,1,0:T(4,128)(2,1)}), bf16[128,1,4,4,384]{4,2,3,1,0:T(4,128)(2,1)S(1)}, u32[]{:S(2)}, u32[]{:S(2)}) async-start(bf16[128,1,4,4,384]{4,2,3,1,0:T(4,128)(2,1)} %copy.37), calls=%async_computation | async-start | bytes 3145728 | tf_op jit(solution)/shard_map/all_to_all | solution.py:42
  29.4 7.6 %collective-permute-start = (bf16[1,3,384]{2,1,0:T(4,128)(2,1)S(1)}, bf16[1,3,384]{2,1,0:T(4,128)(2,1)S(1)}, u32[]{:S(2)}, u32[]{:S(2)}) collective-permute-start(bf16[1,3,384]{2,1,0:T(4,128)(2,1)S(1)} %slice.47), channel_id=1, source_target_pairs={{0,1},{1,2},{2,3},{3,4},{4,5},{5,6},{6,7},{7,8},{8,9},{9,10},{10,1... | collective-permute-start | bytes 6920 | tf_op jit(solution)/shard_map/ppermute | solution.py:10
  38.8 4.3 %copy-start.3 = (bf16[4,128,4,512]{3,2,1,0:T(4,128)(2,1)S(1)}, bf16[4,128,4,512]{3,2,1,0:T(4,128)(2,1)}, u32[]{:S(2)}) copy-start(bf16[4,128,4,512]{3,2,1,0:T(4,128)(2,1)} %reshape.138) | copy-start | bytes 6291460
  41.9 1.2 copy-start.1
  69.7 54.1 %all-to-all-start.1 = ((bf16[128,1,4,4,384]{4,3,2,1,0:T(4,128)(2,1)}), bf16[128,1,4,4,384]{4,3,2,1,0:T(4,128)(2,1)}, u32[]{:S(2)}, u32[]{:S(2)}) async-start(bf16[128,1,4,4,384]{4,3,2,1,0:T(4,128)(2,1)} %copy.47), calls=%async_computation.1 | async-start | bytes 3145728 | tf_op jit(solution)/shard_map/all_to_all | solution.py:43
  87.2 1.4 copy-start.2
  94.6 51.4 %collective-permute-start.2 = (bf16[4,256,512]{2,0,1:T(4,128)(2,1)}, bf16[4,256,512]{2,0,1:T(4,128)(2,1)}, u32[]{:S(2)}, u32[]{:S(2)}) collective-permute-start(bf16[4,256,512]{2,0,1:T(4,128)(2,1)} %bitcast.18), channel_id=1, source_target_pairs={{0,128},{128,0},{1,129},{129,1},{2,130},{130,2},{3,131},{131,3},{4... | collective-permute-start | bytes 3145736 | tf_op jit(solution)/shard_map/ppermute | solution.py:64
  112.4 22.7 %collective-permute-start.1 = (bf16[1,3,384]{2,1,0:T(4,128)(2,1)S(1)}, bf16[1,3,384]{2,1,0:T(4,128)(2,1)S(1)}, u32[]{:S(2)}, u32[]{:S(2)}) collective-permute-start(bf16[1,3,384]{2,1,0:T(4,128)(2,1)S(1)} %slice.64), channel_id=1, source_target_pairs={{1,0},{2,1},{3,2},{4,3},{5,4},{6,5},{7,6},{8,7},{9,8},{10,9},{11,1... | collective-permute-start | bytes 6920 | tf_op jit(solution)/shard_map/ppermute | solution.py:10
  126.8 41.5 %collective-permute-start.3 = (bf16[4,256,512]{1,0,2:T(4,128)(2,1)S(1)}, bf16[4,256,512]{1,0,2:T(4,128)(2,1)S(1)}, u32[]{:S(2)}, u32[]{:S(2)}) collective-permute-start(bf16[4,256,512]{1,0,2:T(4,128)(2,1)S(1)} %bitcast.88), channel_id=1, source_target_pairs={{0,128},{128,0},{1,129},{129,1},{2,130},{130,2},{3,131},{131,3},{4... | collective-permute-start | bytes 3145736 | tf_op jit(solution)/shard_map/ppermute | solution.py:63
  138.9 7.1 %copy-start.4 = (f32[4,64,4,512]{3,0,2,1:T(4,128)S(1)}, f32[4,64,4,512]{3,0,2,1:T(4,128)}, u32[]{:S(2)}) copy-start(f32[4,64,4,512]{3,0,2,1:T(4,128)} %copy.42) | copy-start | bytes 6291460

commit v3 on v2

--- a/solution.py
+++ b/solution.py
@@ -2,6 +2,77 @@
 import jax.numpy as jnp
 from jax import lax
 from jax.sharding import PartitionSpec as P
+from jax.experimental import pallas as pl
+from jax.experimental.pallas import tpu as pltpu
+import functools
+
+MESH = pl.DeviceIdType.MESH
+
+
+def _a2a_kernel(n, x_ref, o_ref, send_sem, recv_sem, local_sem):
+    me = lax.axis_index("seq")
+    barrier = pltpu.get_barrier_semaphore()
+
+    def greet(j, carry):
+        peer = lax.rem(me + j, n)
+        pl.semaphore_signal(barrier, inc=1, device_id={"seq": peer}, device_id_type=MESH)
+        return carry
+
+    lax.fori_loop(1, n, greet, 0)
+    pl.semaphore_wait(barrier, n - 1)
+    local = pltpu.make_async_copy(x_ref.at[me], o_ref.at[me], local_sem)
+    local.start()
+
+    def outgoing(j):
+        peer = lax.rem(me + j, n)
+        return pltpu.make_async_remote_copy(
+            src_ref=x_ref.at[peer],
+            dst_ref=o_ref.at[me],
+            send_sem=send_sem.at[peer],
+            recv_sem=recv_sem.at[me],
+            device_id={"seq": peer},
+            device_id_type=MESH,
+        )
+
+    def incoming(j):
+        source = lax.rem(me + n - j, n)
+        return pltpu.make_async_remote_copy(
+            src_ref=x_ref.at[me],
+            dst_ref=o_ref.at[source],
+            send_sem=send_sem.at[source],
+            recv_sem=recv_sem.at[source],
+            device_id={"seq": source},
+            device_id_type=MESH,
+        )
+
+    def send(j, carry):
+        outgoing(j).start()
+        return carry
+
+    lax.fori_loop(1, n, send, 0)
+
+    def drain(j, carry):
+        outgoing(j).wait_send()
+        incoming(j).wait_recv()
+        return carry
+
+    lax.fori_loop(1, n, drain, 0)
+    local.wait()
+
+
+def all_to_all(x, n, cid):
+    return pl.pallas_call(
+        functools.partial(_a2a_kernel, n),
+        out_shape=jax.ShapeDtypeStruct(x.shape, x.dtype),
+        in_specs=[pl.BlockSpec(memory_space=pl.ANY)],
+        out_specs=pl.BlockSpec(memory_space=pl.ANY),
+        scratch_shapes=[
+            pltpu.SemaphoreType.DMA((n,)),
+            pltpu.SemaphoreType.DMA((n,)),
+            pltpu.SemaphoreType.DMA(()),
+        ],
+        compiler_params=pltpu.CompilerParams(collective_id=cid, has_side_effects=True),
+    )(x)
 
 
 def passed_along(value, axis, steps):
@@ -39,8 +110,8 @@
     grad_chunks = jnp.einsum(
         "kmpi,skmd->psikd", second_split, upstream, preferred_element_type=jnp.float32
     ).astype(jnp.bfloat16)
-    grad_rows = lax.all_to_all(grad_chunks, "seq", split_axis=0, concat_axis=0, tiled=True)
-    columns = lax.all_to_all(mixed_chunks, "seq", split_axis=0, concat_axis=0, tiled=True)
+    grad_rows = all_to_all(grad_chunks, peers, 0)
+    columns = all_to_all(mixed_chunks, peers, 1)
     halves = lax.axis_size("batch")
     me = lax.axis_index("batch")
     other = halves - 1 - me

time: 172 us -> 195 us (1.13)
  the two profiles are of different devices: /device:TPU:1 before, /device:TPU:63 now
where the time goes in v3:
time: 195 us
  Pallas kernels  114 us (58%)
  local copies, waits for them, and re-layouts  29.4 us (15%)
  waiting for transfers between devices  15.5 us (8%)
  matrix products  13.1 us (7%)
  other arithmetic  12.3 us (6%)
  starting transfers between devices  9.35 us (5%)
    pallas_call x2, Pallas kernels, all_to_all(): pl.pallas_call(functools.partial(_a2a_kernel, n), out_shape=jax.ShapeDtyp...  114 us
    ppermute x2, waiting for transfers between devices, passed_along(): lax.ppermute(value, axis, [(source, source + steps) for source in range(i...  15.4 us
    unnamed x27, local copies, waits for them, and re-layouts  12.4 us
    ppermute x2, starting transfers between devices, passed_along(): lax.ppermute(value, axis, [(source, source + steps) for source in range(i...  7.6 us
    dot_general x1, matrix products, body(): jnp.einsum('kmpi,skmd->psikd', second_split, upstream, preferred_element_...  4.47 us
    reshape x1, local copies, waits for them, and re-layouts, body(): first_split = first_factor.reshape(blocks, peers, col_blocks, block_order)  4.15 us
  transfers between devices with their start and end apart: 4, of which 1 were waited for; matrix products, arithmetic and copies ran while one was open for 21% of the time, Pallas kernels for 59%

profile of v3, /device:TPU:63, one launch (start us, length us, event | category | flops | bytes accessed | tf_op | source)
XLA Modules:
  0.0 194.7 jit_solution(3005758448350812093)
XLA Ops:
  1.5 5.0 %collective-permute-start = (bf16[1,3,384]{2,1,0:T(4,128)(2,1)S(1)}, bf16[1,3,384]{2,1,0:T(4,128)(2,1)S(1)}, u32[]{:S(2)}, u32[]{:S(2)}) collective-permute-start(bf16[1,3,384]{2,1,0:T(4,128)(2,1)S(1)} %slice.47), channel_id=1, source_target_pairs={{0,1},{1,2},{2,3},{3,4},{4,5},{5,6},{6,7},{7,8},{8,9},{9,10},{10,1... | collective-permute-start | bytes 6920 | tf_op jit(solution)/shard_map/ppermute | solution.py:81
  6.5 4.5 %copy.18 = bf16[4,512,512]{1,0,2:T(4,128)(2,1)} copy(bf16[4,512,512]{2,1,0:T(8,128)(2,1)} %param.8) | data formatting | bytes 4194304 | tf_op args[3]
  11.0 4.5 %fusion.19 = bf16[4,384,128,4]{2,1,3,0:T(8,128)(2,1)S(1)} fusion(bf16[4,512,384,1]{2,1,3,0:T(8,128)(2,1)S(1)} %bitcast.68, bf16[4,512,128,4]{1,0,3,2:T(4,128)(2,1)} %bitcast.79), kind=kOutput, calls=%fused_computation.31 | convolution fusion | flops 806092800 | bytes 5242880 | tf_op jit(solution)/shard_map/kmpi,skmd->psikd/dot_general | solution.py:110
  15.5 2.5 %copy.48 = bf16[4,384,128,4]{1,0,3,2:T(4,128)(2,1)} copy(bf16[4,384,128,4]{2,1,3,0:T(8,128)(2,1)S(1)} %fusion.19) | data formatting | bytes 3145728
  17.9 50.3 %shard_map.76 = bf16[128,1,4,4,384]{4,3,2,1,0:T(4,128)(2,1)} custom-call(bf16[128,1,4,4,384]{4,3,2,1,0:T(4,128)(2,1)} %bitcast.77), custom_call_target="tpu_custom_call" | custom-call | tf_op jit(solution)/shard_map/pallas_call | solution.py:64
  68.2 4.2 %reshape.138 = bf16[4,128,4,512]{3,2,1,0:T(4,128)(2,1)} reshape(bf16[4,512,512]{2,1,0:T(8,128)(2,1)} %param.7) | data formatting | bytes 4194304 | tf_op jit(solution)/shard_map/reshape | solution.py:104
  72.4 1.7 constant_dynamic-slice_fusion
  74.1 2.7 %convolution_bitcast_fusion = f32[1,4,512,384]{2,3,1,0:T(8,128)} fusion(bf16[4,128,4,512]{3,2,1,0:T(4,128)(2,1)S(1)} %copy-done.2, bf16[128,4,4,384]{3,2,1,0:T(4,128)(2,1)S(1)} %bitcast.71), kind=kOutput, calls=%fused_computation.26 | convolution fusion | flops 805306368 | bytes 6815744 | tf_op jit(solution)/shard_map/ipqj,psiqd->sijd/dot_general | solution.py:136
  76.9 3.7 %copy.24 = f32[1,4,512,384]{3,2,1,0:T(8,128)} copy(f32[1,4,512,384]{2,3,1,0:T(8,128)} %convolution_bitcast_fusion) | data formatting | bytes 6291456 | tf_op jit(solution)/shard_map/ipqj,psiqd->sijd/transpose | solution.py:136
  80.9 3.1 %multiply_convert_fusion = (bf16[1,2048,384]{2,1,0:T(8,128)(2,1)S(1)}, f32[1,2048,384]{2,1,0:T(8,128)}) fusion(f32[1,2051,384]{2,1,0:T(8,128)S(1)} %maximum_convert_fusion, f32[384]{0:T(512)S(1)} %get-tuple-element.8, f32[384]{0:T(512)S(1)} %get-tuple-element.9, f32[384]{0:T(512)S(1)} %get-tuple-element.7, f32[384]{0:T(512)S(1)} %get-tuple-element.6), kind=kLoop, calls=%fused_computation.18 | loop fusion | flops 9437184 | bytes 17307648 | tf_op jit(solution)/shard_map/convert_element_type | solution.py:102
  84.0 1.3 fusion.16
  86.1 2.7 %copy.26 = f32[4,64,4,512]{3,0,2,1:T(4,128)} copy(f32[4,64,4,512]{3,1,2,0:T(8,128)S(1)} %fusion.23) | data formatting | bytes 4194304 | tf_op jit(solution)/shard_map/convert_element_type | solution.py:143
  89.6 1.8 copy.28
  91.4 1.7 collective-permute-start.2
  93.0 2.4 %copy.49 = bf16[4,384,128,4]{1,3,0,2:T(4,128)(2,1)} copy(bf16[4,384,128,4]{2,1,3,0:T(8,128)(2,1)S(1)} %fusion.16) | data formatting | bytes 3145728
  95.5 64.0 %shard_map.77 = bf16[128,1,4,4,384]{4,3,2,1,0:T(4,128)(2,1)} custom-call(bf16[128,1,4,4,384]{4,3,2,1,0:T(4,128)(2,1)} %bitcast.78), custom_call_target="tpu_custom_call" | custom-call | tf_op jit(solution)/shard_map/pallas_call | solution.py:64
  159.5 2.3 %convolution_convert_fusion = bf16[4,256,128,4]{1,2,3,0:T(8,128)(2,1)S(1)} fusion(bf16[128,4,4,384]{3,2,1,0:T(4,128)(2,1)} %bitcast.75, bf16[1,4,512,384]{3,2,1,0:T(8,128)(2,1)S(1)} %bitcast.70, s32[]{:T(128)S(6)} %select_n.15), kind=kOutput, calls=%fused_computation.35 | convolution fusion | flops 403177472 | bytes 3407876 | tf_op jit(solution)/shard_map/skmd,psikd->kmpi/dot_general | solution.py:123
  162.7 3.5 %fusion.8 = bf16[1,2048,384]{2,1,0:T(8,128)(2,1)S(1)} fusion(f32[1,4,512,384]{3,2,1,0:T(8,128)S(1)} %copy-done.4, f32[1,2048,384]{2,1,0:T(8,128)} %get-tuple-element.11), kind=kLoop, calls=%fused_computation.17 | loop fusion | flops 7077888 | bytes 7864320 | tf_op jit(solution)/shard_map/convert_element_type | solution.py:145
  166.2 2.6 %collective-permute-start.1 = (bf16[1,3,384]{2,1,0:T(4,128)(2,1)S(1)}, bf16[1,3,384]{2,1,0:T(4,128)(2,1)S(1)}, u32[]{:S(2)}, u32[]{:S(2)}) collective-permute-start(bf16[1,3,384]{2,1,0:T(4,128)(2,1)S(1)} %slice.64), channel_id=1, source_target_pairs={{1,0},{2,1},{3,2},{4,3},{5,4},{6,5},{7,6},{8,7},{9,8},{10,9},{11,1... | collective-permute-start | bytes 6920 | tf_op jit(solution)/shard_map/ppermute | solution.py:81
  169.6 1.4 copy.33
  171.0 15.4 %collective-permute-done.1 = bf16[1,3,384]{2,1,0:T(4,128)(2,1)S(1)} collective-permute-done((bf16[1,3,384]{2,1,0:T(4,128)(2,1)S(1)}, bf16[1,3,384]{2,1,0:T(4,128)(2,1)S(1)}, u32[]{:S(2)}, u32[]{:S(2)}) %collective-permute-start.1) | collective-permute-done | bytes 2336 | tf_op jit(solution)/shard_map/ppermute | solution.py:81
  186.6 2.5 %fusion.1 = bf16[1,2048,384]{2,1,0:T(8,128)(2,1)} fusion(f32[1,2051,384]{2,1,0:T(8,128)S(1)} %maximum_convert_fusion.1, f32[384]{0:T(512)S(1)} %get-tuple-element.8, f32[384]{0:T(512)S(1)} %get-tuple-element.9, f32[384]{0:T(512)S(1)} %get-tuple-element.7, f32[384]{0:T(512)S(1)} %get-tuple-element.6), kind=kLoop, calls=%fused_computation.2 | loop fusion | flops 6291456 | bytes 14161920 | tf_op jit(solution)/shard_map/convert_element_type | solution.py:150
  189.2 1.9 fusion.10
  193.0 1.7 copy.37
  (37 shorter events, 6.5 us)
Async XLA Ops:
  0.6 10.4 %copy-start = (bf16[1,2048,384]{2,1,0:T(8,128)(2,1)S(1)}, bf16[1,2048,384]{2,1,0:T(8,128)(2,1)}, u32[]{:S(2)}) copy-start(bf16[1,2048,384]{2,1,0:T(8,128)(2,1)} %param.9) | copy-start | bytes 4718596
  1.5 79.1 %collective-permute-start = (bf16[1,3,384]{2,1,0:T(4,128)(2,1)S(1)}, bf16[1,3,384]{2,1,0:T(4,128)(2,1)S(1)}, u32[]{:S(2)}, u32[]{:S(2)}) collective-permute-start(bf16[1,3,384]{2,1,0:T(4,128)(2,1)S(1)} %slice.47), channel_id=1, source_target_pairs={{0,1},{1,2},{2,3},{3,4},{4,5},{5,6},{6,7},{7,8},{8,9},{9,10},{10,1... | collective-permute-start | bytes 6920 | tf_op jit(solution)/shard_map/ppermute | solution.py:81
  68.2 4.2 %copy-start.1 = (bf16[128,1,4,4,384]{4,3,2,1,0:T(4,128)(2,1)S(1)}, bf16[128,1,4,4,384]{4,3,2,1,0:T(4,128)(2,1)}, u32[]{:S(2)}) copy-start(bf16[128,1,4,4,384]{4,3,2,1,0:T(4,128)(2,1)} %shard_map.76) | copy-start | bytes 4718596
  72.4 1.8 copy-start.2
  74.1 2.7 %copy-start.10 = (f32[4,384]{1,0:T(4,128)S(1)}, f32[4,384]{1,0:T(4,128)}, u32[]{:S(2)}) copy-start(f32[4,384]{1,0:T(4,128)} %param.6) | copy-start | bytes 18436
  76.9 3.7 %copy-start.9 = (bf16[1,2048,384]{2,1,0:T(8,128)(2,1)S(1)}, bf16[1,2048,384]{2,1,0:T(8,128)(2,1)}, u32[]{:S(2)}) copy-start(bf16[1,2048,384]{2,1,0:T(8,128)(2,1)} %param.5) | copy-start | bytes 4718596
  80.9 3.1 %copy-start.3 = (bf16[4,128,4,512]{3,2,1,0:T(4,128)(2,1)S(1)}, bf16[4,128,4,512]{3,2,1,0:T(4,128)(2,1)}, u32[]{:S(2)}) copy-start(bf16[4,128,4,512]{3,2,1,0:T(4,128)(2,1)} %reshape.138) | copy-start | bytes 6291460
  84.0 1.4 copy-start.8
  86.1 2.7 %copy-start.7 = (bf16[64,1,4,4,384]{4,3,2,1,0:T(4,128)(2,1)S(1)}, bf16[64,1,4,4,384]{4,3,2,1,0:T(4,128)(2,1)}, u32[]{:S(2)}) copy-start(bf16[64,1,4,4,384]{4,3,2,1,0:T(4,128)(2,1)} %get-tuple-element.12) | copy-start | bytes 2359300
  91.4 97.8 %collective-permute-start.2 = (bf16[4,256,512]{2,0,1:T(4,128)(2,1)}, bf16[4,256,512]{2,0,1:T(4,128)(2,1)}, u32[]{:S(2)}, u32[]{:S(2)}) collective-permute-start(bf16[4,256,512]{2,0,1:T(4,128)(2,1)} %bitcast.19), channel_id=1, source_target_pairs={{0,128},{128,0},{1,129},{129,1},{2,130},{130,2},{3,131},{131,3},{4... | collective-permute-start | bytes 3145736 | tf_op jit(solution)/shard_map/ppermute | solution.py:135
  159.5 3.3 %copy-start.4 = (f32[1,4,512,384]{3,2,1,0:T(8,128)S(1)}, f32[1,4,512,384]{3,2,1,0:T(8,128)}, u32[]{:S(2)}) copy-start(f32[1,4,512,384]{3,2,1,0:T(8,128)} %copy.24) | copy-start | bytes 9437188
  162.6 29.6 %collective-permute-start.3 = (bf16[4,256,512]{1,0,2:T(4,128)(2,1)S(1)}, bf16[4,256,512]{1,0,2:T(4,128)(2,1)S(1)}, u32[]{:S(2)}, u32[]{:S(2)}) collective-permute-start(bf16[4,256,512]{1,0,2:T(4,128)(2,1)S(1)} %bitcast.80), channel_id=1, source_target_pairs={{0,128},{128,0},{1,129},{129,1},{2,130},{130,2},{3,131},{131,3},{4... | collective-permute-start | bytes 3145736 | tf_op jit(solution)/shard_map/ppermute | solution.py:134
  162.7 6.1 %copy-start.6 = (bf16[128,1,4,4,384]{4,3,2,1,0:T(4,128)(2,1)S(1)}, bf16[128,1,4,4,384]{4,3,2,1,0:T(4,128)(2,1)}, u32[]{:S(2)}) copy-start(bf16[128,1,4,4,384]{4,3,2,1,0:T(4,128)(2,1)} %shard_map.77) | copy-start | bytes 4718596
  166.2 20.2 %collective-permute-start.1 = (bf16[1,3,384]{2,1,0:T(4,128)(2,1)S(1)}, bf16[1,3,384]{2,1,0:T(4,128)(2,1)S(1)}, u32[]{:S(2)}, u32[]{:S(2)}) collective-permute-start(bf16[1,3,384]{2,1,0:T(4,128)(2,1)S(1)} %slice.64), channel_id=1, source_target_pairs={{1,0},{2,1},{3,2},{4,3},{5,4},{6,5},{7,6},{8,7},{9,8},{10,9},{11,1... | collective-permute-start | bytes 6920 | tf_op jit(solution)/shard_map/ppermute | solution.py:81
  186.6 2.6 %copy-start.5 = (f32[4,64,4,512]{3,0,2,1:T(4,128)S(1)}, f32[4,64,4,512]{3,0,2,1:T(4,128)}, u32[]{:S(2)}) copy-start(f32[4,64,4,512]{3,0,2,1:T(4,128)} %copy.26) | copy-start | bytes 6291460

commit v4 on v3

--- a/solution.py
+++ b/solution.py
@@ -9,7 +9,7 @@
 MESH = pl.DeviceIdType.MESH
 
 
-def _a2a_kernel(n, x_ref, o_ref, send_sem, recv_sem, local_sem):
+def _a2a_kernel(n, x_refs, o_refs, send_sem, recv_sem, local_sem):
     me = lax.axis_index("seq")
     barrier = pltpu.get_barrier_semaphore()
 
@@ -20,59 +20,72 @@
 
     lax.fori_loop(1, n, greet, 0)
     pl.semaphore_wait(barrier, n - 1)
-    local = pltpu.make_async_copy(x_ref.at[me], o_ref.at[me], local_sem)
-    local.start()
+    count = len(x_refs)
+    locals_ = [
+        pltpu.make_async_copy(x_refs[c].at[me], o_refs[c].at[me], local_sem.at[c])
+        for c in range(count)
+    ]
+    for copy in locals_:
+        copy.start()
 
-    def outgoing(j):
+    def outgoing(c, j):
         peer = lax.rem(me + j, n)
         return pltpu.make_async_remote_copy(
-            src_ref=x_ref.at[peer],
-            dst_ref=o_ref.at[me],
-            send_sem=send_sem.at[peer],
-            recv_sem=recv_sem.at[me],
+            src_ref=x_refs[c].at[peer],
+            dst_ref=o_refs[c].at[me],
+            send_sem=send_sem.at[c, peer],
+            recv_sem=recv_sem.at[c, me],
             device_id={"seq": peer},
             device_id_type=MESH,
         )
 
-    def incoming(j):
+    def incoming(c, j):
         source = lax.rem(me + n - j, n)
         return pltpu.make_async_remote_copy(
-            src_ref=x_ref.at[me],
-            dst_ref=o_ref.at[source],
-            send_sem=send_sem.at[source],
-            recv_sem=recv_sem.at[source],
+            src_ref=x_refs[c].at[me],
+            dst_ref=o_refs[c].at[source],
+            send_sem=send_sem.at[c, source],
+            recv_sem=recv_sem.at[c, source],
             device_id={"seq": source},
             device_id_type=MESH,
         )
 
     def send(j, carry):
-        outgoing(j).start()
+        for c in range(count):
+            outgoing(c, j).start()
         return carry
 
     lax.fori_loop(1, n, send, 0)
 
     def drain(j, carry):
-        outgoing(j).wait_send()
-        incoming(j).wait_recv()
+        for c in range(count):
+            outgoing(c, j).wait_send()
+            incoming(c, j).wait_recv()
         return carry
 
     lax.fori_loop(1, n, drain, 0)
-    local.wait()
+    for copy in locals_:
+        copy.wait()
 
 
-def all_to_all(x, n, cid):
+def all_to_all(xs, n, cid):
+    count = len(xs)
+
+    def kernel(*refs):
+        _a2a_kernel(n, refs[:count], refs[count : 2 * count], *refs[2 * count :])
+
     return pl.pallas_call(
-        functools.partial(_a2a_kernel, n),
-        out_shape=jax.ShapeDtypeStruct(x.shape, x.dtype),
-        in_specs=[pl.BlockSpec(memory_space=pl.ANY)],
-        out_specs=pl.BlockSpec(memory_space=pl.ANY),
+        kernel,
+        out_shape=[jax.ShapeDtypeStruct(x.shape, x.dtype) for x in xs],
+        in_specs=[pl.BlockSpec(memory_space=pl.ANY)] * count,
+        out_specs=[pl.BlockSpec(memory_space=pl.ANY)] * count,
         scratch_shapes=[
-            pltpu.SemaphoreType.DMA((n,)),
-            pltpu.SemaphoreType.DMA((n,)),
-            pltpu.SemaphoreType.DMA(()),
+            pltpu.SemaphoreType.DMA((count, n)),
+            pltpu.SemaphoreType.DMA((count, n)),
+            pltpu.SemaphoreType.DMA((count,)),
         ],
         compiler_params=pltpu.CompilerParams(collective_id=cid, has_side_effects=True),
-    )(x)
+    )(*xs)
 
 
 def passed_along(value, axis, steps):
@@ -110,8 +123,7 @@
     grad_chunks = jnp.einsum(
         "kmpi,skmd->psikd", second_split, upstream, preferred_element_type=jnp.float32
     ).astype(jnp.bfloat16)
-    grad_rows = all_to_all(grad_chunks, peers, 0)
-    columns = all_to_all(mixed_chunks, peers, 1)
+    grad_rows, columns = all_to_all([grad_chunks, mixed_chunks], peers, 0)
     halves = lax.axis_size("batch")
     me = lax.axis_index("batch")
     other = halves - 1 - me

time: 195 us -> 204 us (1.046)
  the two profiles are of different devices: /device:TPU:63 before, /device:TPU:1 now
where the time goes in v4:
time: 204 us
  Pallas kernels  102 us (50%)
  waiting for transfers between devices  35.8 us (18%)
  local copies, waits for them, and re-layouts  28.8 us (14%)
  matrix products  15.9 us (8%)
  other arithmetic  11.7 us (6%)
  starting transfers between devices  8.9 us (4%)
    pallas_call x1, Pallas kernels, all_to_all(): pl.pallas_call(kernel, out_shape=[jax.ShapeDtypeStruct(x.shape, x.dtype)...  102 us
    ppermute x1, waiting for transfers between devices, body(): sent_second = lax.ppermute(second_part(other), 'batch', swap)  20.3 us
    ppermute x1, waiting for transfers between devices, body(): sent_first = lax.ppermute(first_part(other), 'batch', swap)  15.6 us
    unnamed x17, local copies, waits for them, and re-layouts  15.4 us
    ppermute x2, starting transfers between devices, passed_along(): lax.ppermute(value, axis, [(source, source + steps) for source in range(i...  7.06 us
    dot_general x1, matrix products, body(): jnp.einsum('kmpi,skmd->psikd', second_split, upstream, preferred_element_...  5.63 us
    dot_general x1, matrix products, body(): jnp.einsum('ipqj,psiqd->sijd', first_split, grad_rows, preferred_element_...  4.8 us
  transfers between devices with their start and end apart: 4, of which 2 were waited for; matrix products, arithmetic and copies ran while one was open for 15% of the time, Pallas kernels for 0%

profile of v4, /device:TPU:1, one launch (start us, length us, event | category | flops | bytes accessed | tf_op | source)
XLA Modules:
  0.0 203.5 jit_solution(8292743828690368242)
XLA Ops:
  0.6 0.8 slice.47
  1.5 4.5 %collective-permute-start = (bf16[1,3,384]{2,1,0:T(4,128)(2,1)S(1)}, bf16[1,3,384]{2,1,0:T(4,128)(2,1)S(1)}, u32[]{:S(2)}, u32[]{:S(2)}) collective-permute-start(bf16[1,3,384]{2,1,0:T(4,128)(2,1)S(1)} %slice.47), channel_id=1, source_target_pairs={{0,1},{1,2},{2,3},{3,4},{4,5},{5,6},{6,7},{7,8},{8,9},{9,10},{10,1... | collective-permute-start | bytes 6920 | tf_op jit(solution)/shard_map/ppermute | solution.py:94
  6.0 4.5 %copy.18 = bf16[4,512,512]{1,0,2:T(4,128)(2,1)} copy(bf16[4,512,512]{2,1,0:T(8,128)(2,1)} %param.8) | data formatting | bytes 4194304 | tf_op args[3]
  10.5 5.6 %fusion.19 = bf16[4,384,128,4]{2,1,3,0:T(8,128)(2,1)} fusion(bf16[4,512,384,1]{2,1,3,0:T(8,128)(2,1)S(1)} %bitcast.68, bf16[4,512,128,4]{1,0,3,2:T(4,128)(2,1)} %bitcast.77), kind=kOutput, calls=%fused_computation.31 | convolution fusion | flops 806092800 | bytes 5242880 | tf_op jit(solution)/shard_map/kmpi,skmd->psikd/dot_general | solution.py:123
  16.1 4.0 %reshape.138 = bf16[4,128,4,512]{3,2,1,0:T(4,128)(2,1)} reshape(bf16[4,512,512]{2,1,0:T(8,128)(2,1)} %param.7) | data formatting | bytes 4194304 | tf_op jit(solution)/shard_map/reshape | solution.py:117
  20.2 4.0 %copy.48 = bf16[4,384,128,4]{1,0,3,2:T(4,128)(2,1)} copy(bf16[4,384,128,4]{2,1,3,0:T(8,128)(2,1)} %fusion.19) | data formatting | bytes 3145728
  24.5 3.1 %multiply_convert_fusion = (bf16[1,2048,384]{2,1,0:T(8,128)(2,1)S(1)}, f32[1,2048,384]{2,1,0:T(8,128)}) fusion(f32[1,2051,384]{2,1,0:T(8,128)S(1)} %maximum_convert_fusion, f32[384]{0:T(512)S(1)} %get-tuple-element.12, f32[384]{0:T(512)S(1)} %get-tuple-element.13, f32[384]{0:T(512)S(1)} %get-tuple-element.11, f32[384]{0:T(512)S(1)} %get-tuple-element.10), kind=kLoop, calls=%fused_computation.18 | loop fusion | flops 9437184 | bytes 17307648 | tf_op jit(solution)/shard_map/convert_element_type | solution.py:115
  27.6 2.5 %fusion.16 = bf16[4,384,128,4]{2,1,3,0:T(8,128)(2,1)} fusion(bf16[4,512,384,1]{2,1,3,0:T(8,128)(2,1)S(1)} %bitcast.71, bf16[4,128,4,512]{3,2,1,0:T(4,128)(2,1)S(1)} %copy-done.1), kind=kOutput, calls=%fused_computation.30 | convolution fusion | flops 806092800 | bytes 5242880 | tf_op jit(solution)/shard_map/ipqj,sijd->psiqd/dot_general | solution.py:118
  30.1 4.0 %copy.49 = bf16[4,384,128,4]{1,3,0,2:T(4,128)(2,1)} copy(bf16[4,384,128,4]{2,1,3,0:T(8,128)(2,1)} %fusion.16) | data formatting | bytes 3145728
  34.1 101.6 %shard_map.76 = (bf16[128,1,4,4,384]{4,3,2,1,0:T(4,128)(2,1)}, bf16[128,1,4,4,384]{4,3,2,1,0:T(4,128)(2,1)}) custom-call(bf16[128,1,4,4,384]{4,3,2,1,0:T(4,128)(2,1)} %bitcast.75, bf16[128,1,4,4,384]{4,3,2,1,0:T(4,128)(2,1)} %bitcast.76), custom_call_target="tpu_custom_call" | custom-call | tf_op jit(solution)/shard_map/pallas_call | solution.py:77
  135.7 4.8 %convolution_bitcast_fusion = f32[1,4,512,384]{2,3,1,0:T(8,128)} fusion(bf16[4,128,4,512]{3,2,1,0:T(4,128)(2,1)} %reshape.138, bf16[128,4,4,384]{3,2,1,0:T(4,128)(2,1)} %bitcast.74), kind=kOutput, calls=%fused_computation.26 | convolution fusion | flops 805306368 | bytes 6815744 | tf_op jit(solution)/shard_map/ipqj,psiqd->sijd/dot_general | solution.py:148
  140.5 3.6 %copy.27 = f32[1,4,512,384]{3,2,1,0:T(8,128)} copy(f32[1,4,512,384]{2,3,1,0:T(8,128)} %convolution_bitcast_fusion) | data formatting | bytes 6291456 | tf_op jit(solution)/shard_map/ipqj,psiqd->sijd/transpose | solution.py:148
  144.1 4.1 %fusion.8 = bf16[1,2048,384]{2,1,0:T(8,128)(2,1)S(1)} fusion(f32[1,4,512,384]{3,2,1,0:T(8,128)} %copy.27, f32[1,2048,384]{2,1,0:T(8,128)} %get-tuple-element.15), kind=kLoop, calls=%fused_computation.17 | loop fusion | flops 7077888 | bytes 7864320 | tf_op jit(solution)/shard_map/convert_element_type | solution.py:157
  148.2 2.6 %collective-permute-start.1 = (bf16[1,3,384]{2,1,0:T(4,128)(2,1)S(1)}, bf16[1,3,384]{2,1,0:T(4,128)(2,1)S(1)}, u32[]{:S(2)}, u32[]{:S(2)}) collective-permute-start(bf16[1,3,384]{2,1,0:T(4,128)(2,1)S(1)} %slice.64), channel_id=1, source_target_pairs={{1,0},{2,1},{3,2},{4,3},{5,4},{6,5},{7,6},{8,7},{9,8},{10,9},{11,1... | collective-permute-start | bytes 6920 | tf_op jit(solution)/shard_map/ppermute | solution.py:94
  152.8 0.8 copy.31
  155.3 1.4 copy.29
  156.6 1.4 copy.33
  158.0 0.8 copy.35
  158.8 1.7 collective-permute-start.3
  160.8 2.5 %fusion.1 = bf16[1,2048,384]{2,1,0:T(8,128)(2,1)} fusion(f32[1,2051,384]{2,1,0:T(8,128)S(1)} %maximum_convert_fusion.1, f32[384]{0:T(512)S(1)} %get-tuple-element.12, f32[384]{0:T(512)S(1)} %get-tuple-element.13, f32[384]{0:T(512)S(1)} %get-tuple-element.11, f32[384]{0:T(512)S(1)} %get-tuple-element.10), kind=kLoop, calls=%fused_computation.2 | loop fusion | flops 6291456 | bytes 14161920 | tf_op jit(solution)/shard_map/convert_element_type | solution.py:162
  163.3 15.6 %collective-permute-done.2 = bf16[4,256,512]{2,0,1:T(4,128)(2,1)S(1)} collective-permute-done((bf16[4,256,512]{2,0,1:T(4,128)(2,1)S(1)}, bf16[4,256,512]{2,0,1:T(4,128)(2,1)S(1)}, u32[]{:S(2)}, u32[]{:S(2)}) %collective-permute-start.2) | collective-permute-done | bytes 1048608 | tf_op jit(solution)/shard_map/ppermute | solution.py:147
  179.6 1.2 copy.36
  180.8 20.3 %collective-permute-done.3 = bf16[4,256,512]{1,0,2:T(4,128)(2,1)S(1)} collective-permute-done((bf16[4,256,512]{1,0,2:T(4,128)(2,1)S(1)}, bf16[4,256,512]{1,0,2:T(4,128)(2,1)S(1)}, u32[]{:S(2)}, u32[]{:S(2)}) %collective-permute-start.3) | collective-permute-done | bytes 1048608 | tf_op jit(solution)/shard_map/ppermute | solution.py:146
  201.8 1.7 copy.37
  (26 shorter events, 5.7 us)
Async XLA Ops:
  0.6 9.8 %copy-start = (bf16[1,2048,384]{2,1,0:T(8,128)(2,1)S(1)}, bf16[1,2048,384]{2,1,0:T(8,128)(2,1)}, u32[]{:S(2)}) copy-start(bf16[1,2048,384]{2,1,0:T(8,128)(2,1)} %param.9) | copy-start | bytes 4718596
  1.5 22.7 %collective-permute-start = (bf16[1,3,384]{2,1,0:T(4,128)(2,1)S(1)}, bf16[1,3,384]{2,1,0:T(4,128)(2,1)S(1)}, u32[]{:S(2)}, u32[]{:S(2)}) collective-permute-start(bf16[1,3,384]{2,1,0:T(4,128)(2,1)S(1)} %slice.47), channel_id=1, source_target_pairs={{0,1},{1,2},{2,3},{3,4},{4,5},{5,6},{6,7},{7,8},{8,9},{9,10},{10,1... | collective-permute-start | bytes 6920 | tf_op jit(solution)/shard_map/ppermute | solution.py:94
  10.5 5.6 %copy-start.5 = (f32[4,384]{1,0:T(4,128)S(1)}, f32[4,384]{1,0:T(4,128)}, u32[]{:S(2)}) copy-start(f32[4,384]{1,0:T(4,128)} %param.6) | copy-start | bytes 18436
  20.2 4.0 %copy-start.3 = (bf16[1,2048,384]{2,1,0:T(8,128)(2,1)S(1)}, bf16[1,2048,384]{2,1,0:T(8,128)(2,1)}, u32[]{:S(2)}) copy-start(bf16[1,2048,384]{2,1,0:T(8,128)(2,1)} %param.5) | copy-start | bytes 4718596
  24.5 3.1 %copy-start.1 = (bf16[4,128,4,512]{3,2,1,0:T(4,128)(2,1)S(1)}, bf16[4,128,4,512]{3,2,1,0:T(4,128)(2,1)}, u32[]{:S(2)}) copy-start(bf16[4,128,4,512]{3,2,1,0:T(4,128)(2,1)} %reshape.138) | copy-start | bytes 6291460
  144.1 6.7 %copy-start.2 = (bf16[128,1,4,4,384]{4,3,2,1,0:T(4,128)(2,1)S(1)}, bf16[128,1,4,4,384]{4,3,2,1,0:T(4,128)(2,1)}, u32[]{:S(2)}) copy-start(bf16[128,1,4,4,384]{4,3,2,1,0:T(4,128)(2,1)} %get-tuple-element.5) | copy-start | bytes 4718596
  148.2 12.4 %collective-permute-start.1 = (bf16[1,3,384]{2,1,0:T(4,128)(2,1)S(1)}, bf16[1,3,384]{2,1,0:T(4,128)(2,1)S(1)}, u32[]{:S(2)}, u32[]{:S(2)}) collective-permute-start(bf16[1,3,384]{2,1,0:T(4,128)(2,1)S(1)} %slice.64), channel_id=1, source_target_pairs={{1,0},{2,1},{3,2},{4,3},{5,4},{6,5},{7,6},{8,7},{9,8},{10,9},{11,1... | collective-permute-start | bytes 6920 | tf_op jit(solution)/shard_map/ppermute | solution.py:94
  152.1 1.7 copy-start.4
  153.6 25.3 %collective-permute-start.2 = (bf16[4,256,512]{2,0,1:T(4,128)(2,1)S(1)}, bf16[4,256,512]{2,0,1:T(4,128)(2,1)S(1)}, u32[]{:S(2)}, u32[]{:S(2)}) collective-permute-start(bf16[4,256,512]{2,0,1:T(4,128)(2,1)S(1)} %bitcast.80), channel_id=1, source_target_pairs={{0,128},{128,0},{1,129},{129,1},{2,130},{130,2},{3,131},{131,3},{4... | collective-permute-start | bytes 3145736 | tf_op jit(solution)/shard_map/ppermute | solution.py:147
  158.8 42.2 %collective-permute-start.3 = (bf16[4,256,512]{1,0,2:T(4,128)(2,1)S(1)}, bf16[4,256,512]{1,0,2:T(4,128)(2,1)S(1)}, u32[]{:S(2)}, u32[]{:S(2)}) collective-permute-start(bf16[4,256,512]{1,0,2:T(4,128)(2,1)S(1)} %bitcast.81), channel_id=1, source_target_pairs={{0,128},{128,0},{1,129},{129,1},{2,130},{130,2},{3,131},{131,3},{4... | collective-permute-start | bytes 3145736 | tf_op jit(solution)/shard_map/ppermute | solution.py:146

commit v5 on v2

--- a/solution.py
+++ b/solution.py
@@ -2,6 +2,32 @@
 import jax.numpy as jnp
 from jax import lax
 from jax.sharding import PartitionSpec as P
+from jax.experimental import pallas as pl
+from jax.experimental.pallas import tpu as pltpu
+
+
+def _grad_payload_kernel(s_ref, g_ref, o_ref):
+    width = g_ref.shape[-1]
+    for k in range(s_ref.shape[0]):
+        product = lax.dot_general(
+            s_ref[k], g_ref[k], (((0,), (0,)), ((), ())), preferred_element_type=jnp.float32
+        )
+        o_ref[:, k * width : (k + 1) * width] = product.astype(o_ref.dtype)
+
+
+def grad_payload(second_factor, upstream):
+    col_blocks, rows, order = second_factor.shape
+    width = upstream.shape[-1]
+    flops = 2 * col_blocks * rows * order * width
+    return pl.pallas_call(
+        _grad_payload_kernel,
+        out_shape=jax.ShapeDtypeStruct((order, col_blocks * width), jnp.bfloat16),
+        in_specs=[pl.BlockSpec(memory_space=pltpu.VMEM)] * 2,
+        out_specs=pl.BlockSpec(memory_space=pltpu.VMEM),
+        cost_estimate=pl.CostEstimate(
+            flops=flops, transcendentals=0, bytes_accessed=2 * (second_factor.size + 2 * upstream.size)
+        ),
+    )(second_factor, upstream.reshape(col_blocks, rows, width))
 
 
 def passed_along(value, axis, steps):
@@ -35,10 +61,9 @@
         "ipqj,sijd->psiqd", first_split, hidden_blocks, preferred_element_type=jnp.float32
     ).astype(jnp.bfloat16)
     upstream = grad_output.reshape(seq_count, col_blocks, block_count, channels)
-    second_split = second_factor.reshape(col_blocks, block_count, peers, blocks)
-    grad_chunks = jnp.einsum(
-        "kmpi,skmd->psikd", second_split, upstream, preferred_element_type=jnp.float32
-    ).astype(jnp.bfloat16)
+    grad_chunks = grad_payload(second_factor, upstream).reshape(
+        peers, seq_count, blocks, col_blocks, channels
+    )
     grad_rows = lax.all_to_all(grad_chunks, "seq", split_axis=0, concat_axis=0, tiled=True)
     columns = lax.all_to_all(mixed_chunks, "seq", split_axis=0, concat_axis=0, tiled=True)
     halves = lax.axis_size("batch")

time: 172 us -> 166 us (0.965)
  local copies, waits for them, and re-layouts: 34.2 us -> 27.5 us
  waiting for transfers between devices: 52.1 us -> 57.9 us
  matrix products: 17.7 us -> 13 us
  Pallas kernels: 0 us -> 4.47 us
  starting transfers between devices: 51.8 us -> 49.2 us
  other arithmetic: 14.1 us -> 12.2 us
    unnamed x15 -> x16, local copies, waits for them, and re-layouts: 9.54 us -> 4.07 us
    pallas_call x0 -> x1, Pallas kernels: none -> 4.47 us  [grad_payload(): pl.pallas_call(_grad_payload_kernel, out_shape=jax.ShapeDtypeStruct((orde...]
    dot_general x1 -> x0, matrix products: 4.47 us -> none  [body(): jnp.einsum('kmpi,skmd->psikd', second_split, upstream, preferred_element_...]
    reshape x0 -> x1, local copies, waits for them, and re-layouts: none -> 3.94 us  [body(): grad_payload(second_factor, upstream)]
    all_to_all x1, waiting for transfers between devices: 20.2 us -> 23.5 us  [body(): lax.all_to_all(grad_chunks, 'seq', split_axis=0, concat_axis=0, tiled=True)]
    all_to_all x1, waiting for transfers between devices: 8.1 us -> 10.9 us  [body(): lax.all_to_all(mixed_chunks, 'seq', split_axis=0, concat_axis=0, tiled=True)]
    all_to_all x1, starting transfers between devices: 17.4 us -> 14.8 us  [body(): lax.all_to_all(mixed_chunks, 'seq', split_axis=0, concat_axis=0, tiled=True)]
    convert_element_type x1 -> x0, local copies, waits for them, and re-layouts: 2.46 us -> none  [body(): grad_chunks = jnp.einsum('kmpi,skmd->psikd', second_split, upstream, pref...]
  transfers between devices with their start and end apart: 6 -> 6, of which waited for: 4 -> 4; matrix products, arithmetic and copies ran while one was open for 29% -> 27% of each run, Pallas kernels for 0% -> 0%
where the time goes in v5:
time: 166 us; the launch traced here: 165 us
  waiting for transfers between devices  57.9 us (35%)
  starting transfers between devices  49.2 us (30%)
  local copies, waits for them, and re-layouts  27.5 us (17%)
  matrix products  13 us (8%)
  other arithmetic  12.2 us (7%)
  Pallas kernels  4.47 us (3%)
    all_to_all x1, waiting for transfers between devices, body(): lax.all_to_all(grad_chunks, 'seq', split_axis=0, concat_axis=0, tiled=True)  23.5 us
    ppermute x1, waiting for transfers between devices, body(): sent_second = lax.ppermute(second_part(other), 'batch', swap)  19.3 us
    all_to_all x1, starting transfers between devices, body(): lax.all_to_all(grad_chunks, 'seq', split_axis=0, concat_axis=0, tiled=True)  16.5 us
    all_to_all x1, starting transfers between devices, body(): lax.all_to_all(mixed_chunks, 'seq', split_axis=0, concat_axis=0, tiled=True)  14.8 us
    all_to_all x1, waiting for transfers between devices, body(): lax.all_to_all(mixed_chunks, 'seq', split_axis=0, concat_axis=0, tiled=True)  10.9 us
    ppermute x1, starting transfers between devices, body(): sent_second = lax.ppermute(second_part(other), 'batch', swap)  8.32 us
    ppermute x2, starting transfers between devices, passed_along(): lax.ppermute(value, axis, [(source, source + steps) for source in range(i...  6.85 us
    dot_general x2, matrix products, second_part(): jnp.einsum('skmd,psikd->kmpi', up, columns, preferred_element_type=jnp.fl...  4.68 us
  transfers between devices with their start and end apart: 6, of which 4 were waited for; matrix products, arithmetic and copies ran while one was open for 27% of the time, Pallas kernels for 0%

profile of v5, /device:TPU:1, one launch (start us, length us, event | category | flops | bytes accessed | tf_op | source)
XLA Modules:
  0.0 165.0 jit_solution(6375823206053584420)
XLA Ops:
  0.6 4.5 %shard_map.76 = bf16[512,1536]{1,0:T(8,128)(2,1)} custom-call(bf16[4,512,512]{2,1,0:T(8,128)(2,1)} %s_ref.1, bf16[4,512,384]{2,1,0:T(8,128)(2,1)} %bitcast.76), custom_call_target="tpu_custom_call" | custom-call | flops 805306368 | bytes 5242880 | tf_op jit(solution)/shard_map/pallas_call | solution.py:22
  5.1 3.9 %reshape.129 = bf16[128,1,4,4,384]{4,3,2,0,1:T(4,128)(2,1)} reshape(bf16[512,1536]{1,0:T(8,128)(2,1)} %shard_map.76) | data formatting | bytes 3145728 | tf_op jit(solution)/shard_map/reshape | solution.py:64
  9.0 16.5 %all-to-all-start = ((bf16[128,1,4,4,384]{4,3,2,1,0:T(4,128)(2,1)}), bf16[128,1,4,4,384]{4,3,2,1,0:T(4,128)(2,1)S(1)}, u32[]{:S(2)}, u32[]{:S(2)}) async-start(bf16[128,1,4,4,384]{4,3,2,1,0:T(4,128)(2,1)} %bitcast.1), calls=%async_computation | async-start | bytes 3145728 | tf_op jit(solution)/shard_map/all_to_all | solution.py:67
  25.6 3.5 %collective-permute-start = (bf16[1,3,384]{2,1,0:T(4,128)(2,1)S(1)}, bf16[1,3,384]{2,1,0:T(4,128)(2,1)S(1)}, u32[]{:S(2)}, u32[]{:S(2)}) collective-permute-start(bf16[1,3,384]{2,1,0:T(4,128)(2,1)S(1)} %slice.47), channel_id=1, source_target_pairs={{0,1},{1,2},{2,3},{3,4},{4,5},{5,6},{6,7},{7,8},{8,9},{9,10},{10,1... | collective-permute-start | bytes 6920 | tf_op jit(solution)/shard_map/ppermute | solution.py:36
  29.2 4.0 %reshape.131 = bf16[4,128,4,512]{3,2,1,0:T(4,128)(2,1)} reshape(bf16[4,512,512]{2,1,0:T(8,128)(2,1)} %param.7) | data formatting | bytes 4194304 | tf_op jit(solution)/shard_map/reshape | solution.py:59
  33.6 3.1 %multiply_convert_fusion = (bf16[1,2048,384]{2,1,0:T(8,128)(2,1)S(1)}, f32[1,2048,384]{2,1,0:T(8,128)}) fusion(f32[1,2051,384]{2,1,0:T(8,128)S(1)} %maximum_convert_fusion, f32[384]{0:T(512)S(1)} %get-tuple-element.11, f32[384]{0:T(512)S(1)} %get-tuple-element.12, f32[384]{0:T(512)S(1)} %get-tuple-element.10, f32[384]{0:T(512)S(1)} %get-tuple-element.9), kind=kLoop, calls=%fused_computation.18 | loop fusion | flops 9437184 | bytes 17307648 | tf_op jit(solution)/shard_map/convert_element_type | solution.py:57
  36.7 2.5 %fusion.32 = bf16[128,1,4,4,384]{0,4,3,2,1:T(8,128)(2,1)} fusion(bf16[4,512,384,1]{2,1,3,0:T(8,128)(2,1)S(1)} %bitcast.73, bf16[4,128,4,512]{3,2,1,0:T(4,128)(2,1)S(1)} %copy-done), kind=kOutput, calls=%fused_computation.42 | convolution fusion | flops 806092800 | bytes 5242880 | tf_op jit(solution)/shard_map/ipqj,sijd->psiqd/dot_general | solution.py:60
  39.2 3.9 %copy.39 = bf16[128,1,4,4,384]{4,3,2,1,0:T(4,128)(2,1)} copy(bf16[128,1,4,4,384]{0,4,3,2,1:T(8,128)(2,1)} %fusion.32) | data formatting | bytes 3145728 | tf_op jit(solution)/shard_map/convert_element_type | solution.py:62
  43.1 23.5 %all-to-all-done = bf16[128,1,4,4,384]{4,3,2,1,0:T(4,128)(2,1)S(1)} async-done(((bf16[128,1,4,4,384]{4,3,2,1,0:T(4,128)(2,1)}), bf16[128,1,4,4,384]{4,3,2,1,0:T(4,128)(2,1)S(1)}, u32[]{:S(2)}, u32[]{:S(2)}) %all-to-all-start) | async-done | bytes 1572896 | tf_op jit(solution)/shard_map/all_to_all | solution.py:67
  66.6 14.8 %all-to-all-start.1 = ((bf16[128,1,4,4,384]{4,3,2,1,0:T(4,128)(2,1)}), bf16[128,1,4,4,384]{4,3,2,1,0:T(4,128)(2,1)}, u32[]{:S(2)}, u32[]{:S(2)}) async-start(bf16[128,1,4,4,384]{4,3,2,1,0:T(4,128)(2,1)} %copy.39), calls=%async_computation.1 | async-start | bytes 3145728 | tf_op jit(solution)/shard_map/all_to_all | solution.py:68
  82.7 2.7 %copy.34 = f32[4,64,4,512]{3,0,2,1:T(4,128)} copy(f32[4,64,4,512]{3,1,2,0:T(8,128)S(1)} %fusion.28) | data formatting | bytes 4194304 | tf_op jit(solution)/shard_map/convert_element_type | solution.py:97
  87.9 2.7 %collective-permute-start.2 = (bf16[4,256,512]{2,0,1:T(4,128)(2,1)}, bf16[4,256,512]{2,0,1:T(4,128)(2,1)}, u32[]{:S(2)}, u32[]{:S(2)}) collective-permute-start(bf16[4,256,512]{2,0,1:T(4,128)(2,1)} %bitcast.16), channel_id=1, source_target_pairs={{0,128},{128,0},{1,129},{129,1},{2,130},{130,2},{3,131},{131,3},{4... | collective-permute-start | bytes 3145736 | tf_op jit(solution)/shard_map/ppermute | solution.py:89
  92.5 4.3 %convolution_bitcast_fusion = f32[1,4,512,384]{2,3,1,0:T(8,128)} fusion(bf16[4,128,4,512]{3,2,1,0:T(4,128)(2,1)} %reshape.131, bf16[128,1,4,4,384]{0,4,3,2,1:T(8,128)(2,1)S(1)} %copy.30), kind=kOutput, calls=%fused_computation.24 | convolution fusion | flops 805306368 | bytes 6815744 | tf_op jit(solution)/shard_map/ipqj,psiqd->sijd/dot_general | solution.py:90
  96.9 2.4 %copy.32 = f32[1,4,512,384]{3,2,1,0:T(8,128)S(1)} copy(f32[1,4,512,384]{2,3,1,0:T(8,128)} %convolution_bitcast_fusion) | data formatting | bytes 6291456 | tf_op jit(solution)/shard_map/ipqj,psiqd->sijd/transpose | solution.py:90
  99.3 3.4 %fusion.8 = bf16[1,2048,384]{2,1,0:T(8,128)(2,1)S(1)} fusion(f32[1,4,512,384]{3,2,1,0:T(8,128)S(1)} %copy.32, f32[1,2048,384]{2,1,0:T(8,128)} %get-tuple-element.14), kind=kLoop, calls=%fused_computation.17 | loop fusion | flops 7077888 | bytes 7864320 | tf_op jit(solution)/shard_map/convert_element_type | solution.py:99
  103.8 3.3 %collective-permute-start.1 = (bf16[1,3,384]{2,1,0:T(4,128)(2,1)S(1)}, bf16[1,3,384]{2,1,0:T(4,128)(2,1)S(1)}, u32[]{:S(2)}, u32[]{:S(2)}) collective-permute-start(bf16[1,3,384]{2,1,0:T(4,128)(2,1)S(1)} %slice.64), channel_id=1, source_target_pairs={{1,0},{2,1},{3,2},{4,3},{5,4},{6,5},{7,6},{8,7},{9,8},{10,9},{11,1... | collective-permute-start | bytes 6920 | tf_op jit(solution)/shard_map/ppermute | solution.py:36
  107.1 10.9 %all-to-all-done.1 = bf16[128,1,4,4,384]{4,3,2,1,0:T(4,128)(2,1)} async-done(((bf16[128,1,4,4,384]{4,3,2,1,0:T(4,128)(2,1)}), bf16[128,1,4,4,384]{4,3,2,1,0:T(4,128)(2,1)}, u32[]{:S(2)}, u32[]{:S(2)}) %all-to-all-start.1) | async-done | bytes 1572896 | tf_op jit(solution)/shard_map/all_to_all | solution.py:68
  118.0 2.5 %fusion.25 = bf16[4,256,128,4]{1,2,3,0:T(8,128)(2,1)S(1)} fusion(bf16[128,1,4,4,384]{4,3,2,1,0:T(4,128)(2,1)} %all-to-all-done.1, bf16[1,4,512,384]{3,2,1,0:T(8,128)(2,1)} %bitcast.77, s32[]{:T(128)S(6)} %select_n.15), kind=kOutput, calls=%fused_computation.37 | convolution fusion | flops 403177472 | bytes 3407876 | tf_op jit(solution)/shard_map/skmd,psikd->kmpi/dot_general | solution.py:77
  121.4 8.3 %collective-permute-start.3 = (bf16[4,256,512]{1,0,2:T(4,128)(2,1)S(1)}, bf16[4,256,512]{1,0,2:T(4,128)(2,1)S(1)}, u32[]{:S(2)}, u32[]{:S(2)}) collective-permute-start(bf16[4,256,512]{1,0,2:T(4,128)(2,1)S(1)} %bitcast.79), channel_id=1, source_target_pairs={{0,128},{128,0},{1,129},{129,1},{2,130},{130,2},{3,131},{131,3},{4... | collective-permute-start | bytes 3145736 | tf_op jit(solution)/shard_map/ppermute | solution.py:88
  129.9 2.2 %fusion.29 = f32[4,256,128,4]{1,2,3,0:T(8,128)S(1)} fusion(bf16[128,1,4,4,384]{4,3,2,1,0:T(4,128)(2,1)} %all-to-all-done.1, bf16[1,4,512,384]{3,2,1,0:T(8,128)(2,1)S(1)} %bitcast.78, s32[]{:T(128)S(6)} %select_n.14), kind=kOutput, calls=%fused_computation.41 | convolution fusion | flops 403701760 | bytes 4456452 | tf_op jit(solution)/shard_map/skmd,psikd->kmpi/dot_general | solution.py:77
  133.5 2.5 %fusion.1 = bf16[1,2048,384]{2,1,0:T(8,128)(2,1)} fusion(f32[1,2051,384]{2,1,0:T(8,128)S(1)} %maximum_convert_fusion.1, f32[384]{0:T(512)S(1)} %get-tuple-element.11, f32[384]{0:T(512)S(1)} %get-tuple-element.12, f32[384]{0:T(512)S(1)} %get-tuple-element.10, f32[384]{0:T(512)S(1)} %get-tuple-element.9), kind=kLoop, calls=%fused_computation.2 | loop fusion | flops 6291456 | bytes 14161920 | tf_op jit(solution)/shard_map/convert_element_type | solution.py:104
  136.0 4.1 %collective-permute-done.2 = bf16[4,256,512]{2,0,1:T(4,128)(2,1)} collective-permute-done((bf16[4,256,512]{2,0,1:T(4,128)(2,1)}, bf16[4,256,512]{2,0,1:T(4,128)(2,1)}, u32[]{:S(2)}, u32[]{:S(2)}) %collective-permute-start.2) | collective-permute-done | bytes 1048608 | tf_op jit(solution)/shard_map/ppermute | solution.py:89
  140.2 1.9 %fusion.10 = bf16[4,256,512]{2,0,1:T(4,128)(2,1)S(1)} fusion(f32[4,64,4,512]{3,0,2,1:T(4,128)S(1)} %copy-done.1, bf16[4,256,512]{2,0,1:T(4,128)(2,1)} %collective-permute-done.2), kind=kLoop, calls=%fused_computation.23 | loop fusion | flops 1572864 | bytes 4194304 | tf_op jit(solution)/shard_map/convert_element_type | solution.py:98
  143.2 19.3 %collective-permute-done.3 = bf16[4,256,512]{1,0,2:T(4,128)(2,1)S(1)} collective-permute-done((bf16[4,256,512]{1,0,2:T(4,128)(2,1)S(1)}, bf16[4,256,512]{1,0,2:T(4,128)(2,1)S(1)}, u32[]{:S(2)}, u32[]{:S(2)}) %collective-permute-start.3) | collective-permute-done | bytes 1048608 | tf_op jit(solution)/shard_map/ppermute | solution.py:88
  (31 shorter events, 13.2 us)
Async XLA Ops:
  9.0 16.5 %copy-start.5 = (bf16[1,2048,384]{2,1,0:T(8,128)(2,1)S(1)}, bf16[1,2048,384]{2,1,0:T(8,128)(2,1)}, u32[]{:S(2)}) copy-start(bf16[1,2048,384]{2,1,0:T(8,128)(2,1)} %param.5) | copy-start | bytes 4718596
  9.0 20.1 %copy-start.6 = (f32[4,384]{1,0:T(4,128)S(1)}, f32[4,384]{1,0:T(4,128)}, u32[]{:S(2)}) copy-start(f32[4,384]{1,0:T(4,128)} %param.6) | copy-start | bytes 18436
  9.0 57.6 %all-to-all-start = ((bf16[128,1,4,4,384]{4,3,2,1,0:T(4,128)(2,1)}), bf16[128,1,4,4,384]{4,3,2,1,0:T(4,128)(2,1)S(1)}, u32[]{:S(2)}, u32[]{:S(2)}) async-start(bf16[128,1,4,4,384]{4,3,2,1,0:T(4,128)(2,1)} %bitcast.1), calls=%async_computation | async-start | bytes 3145728 | tf_op jit(solution)/shard_map/all_to_all | solution.py:67
  25.6 7.6 %collective-permute-start = (bf16[1,3,384]{2,1,0:T(4,128)(2,1)S(1)}, bf16[1,3,384]{2,1,0:T(4,128)(2,1)S(1)}, u32[]{:S(2)}, u32[]{:S(2)}) collective-permute-start(bf16[1,3,384]{2,1,0:T(4,128)(2,1)S(1)} %slice.47), channel_id=1, source_target_pairs={{0,1},{1,2},{2,3},{3,4},{4,5},{5,6},{6,7},{7,8},{8,9},{9,10},{10,1... | collective-permute-start | bytes 6920 | tf_op jit(solution)/shard_map/ppermute | solution.py:36
  33.6 3.1 %copy-start = (bf16[4,128,4,512]{3,2,1,0:T(4,128)(2,1)S(1)}, bf16[4,128,4,512]{3,2,1,0:T(4,128)(2,1)}, u32[]{:S(2)}) copy-start(bf16[4,128,4,512]{3,2,1,0:T(4,128)(2,1)} %reshape.131) | copy-start | bytes 6291460
  66.6 51.4 %all-to-all-start.1 = ((bf16[128,1,4,4,384]{4,3,2,1,0:T(4,128)(2,1)}), bf16[128,1,4,4,384]{4,3,2,1,0:T(4,128)(2,1)}, u32[]{:S(2)}, u32[]{:S(2)}) async-start(bf16[128,1,4,4,384]{4,3,2,1,0:T(4,128)(2,1)} %copy.39), calls=%async_computation.1 | async-start | bytes 3145728 | tf_op jit(solution)/shard_map/all_to_all | solution.py:68
  87.9 52.2 %collective-permute-start.2 = (bf16[4,256,512]{2,0,1:T(4,128)(2,1)}, bf16[4,256,512]{2,0,1:T(4,128)(2,1)}, u32[]{:S(2)}, u32[]{:S(2)}) collective-permute-start(bf16[4,256,512]{2,0,1:T(4,128)(2,1)} %bitcast.16), channel_id=1, source_target_pairs={{0,128},{128,0},{1,129},{129,1},{2,130},{130,2},{3,131},{131,3},{4... | collective-permute-start | bytes 3145736 | tf_op jit(solution)/shard_map/ppermute | solution.py:89
  102.6 1.1 copy-start.2
  103.8 25.9 %collective-permute-start.1 = (bf16[1,3,384]{2,1,0:T(4,128)(2,1)S(1)}, bf16[1,3,384]{2,1,0:T(4,128)(2,1)S(1)}, u32[]{:S(2)}, u32[]{:S(2)}) collective-permute-start(bf16[1,3,384]{2,1,0:T(4,128)(2,1)S(1)} %slice.64), channel_id=1, source_target_pairs={{1,0},{2,1},{3,2},{4,3},{5,4},{6,5},{7,6},{8,7},{9,8},{10,9},{11,1... | collective-permute-start | bytes 6920 | tf_op jit(solution)/shard_map/ppermute | solution.py:36
  118.0 11.7 %copy-start.3 = (bf16[1,2048,384]{2,1,0:T(8,128)(2,1)S(1)}, bf16[1,2048,384]{2,1,0:T(8,128)(2,1)}, u32[]{:S(2)}) copy-start(bf16[1,2048,384]{2,1,0:T(8,128)(2,1)} %copy-done.2) | copy-start | bytes 4718596
  121.4 8.5 %copy-start.4 = (bf16[1,2048,384]{2,1,0:T(8,128)(2,1)S(1)}, bf16[1,2048,384]{2,1,0:T(8,128)(2,1)}, u32[]{:S(2)}) copy-start(bf16[1,2048,384]{2,1,0:T(8,128)(2,1)} %param.9) | copy-start | bytes 4718596
  121.4 41.1 %collective-permute-start.3 = (bf16[4,256,512]{1,0,2:T(4,128)(2,1)S(1)}, bf16[4,256,512]{1,0,2:T(4,128)(2,1)S(1)}, u32[]{:S(2)}, u32[]{:S(2)}) collective-permute-start(bf16[4,256,512]{1,0,2:T(4,128)(2,1)S(1)} %bitcast.79), channel_id=1, source_target_pairs={{0,128},{128,0},{1,129},{129,1},{2,130},{130,2},{3,131},{131,3},{4... | collective-permute-start | bytes 3145736 | tf_op jit(solution)/shard_map/ppermute | solution.py:88
  133.5 6.7 %copy-start.1 = (f32[4,64,4,512]{3,0,2,1:T(4,128)S(1)}, f32[4,64,4,512]{3,0,2,1:T(4,128)}, u32[]{:S(2)}) copy-start(f32[4,64,4,512]{3,0,2,1:T(4,128)} %copy.34) | copy-start | bytes 6291460

commit v6 on v5

--- a/solution.py
+++ b/solution.py
@@ -6,24 +6,33 @@
 from jax.experimental.pallas import tpu as pltpu
 
 
-def _grad_payload_kernel(s_ref, g_ref, o_ref):
+def _grad_payload_kernel(s_ref, g_ref, o_ref, product):
+    peers, group, _ = o_ref.shape
     width = g_ref.shape[-1]
+    lanes = product.shape[-1]
     for k in range(s_ref.shape[0]):
-        product = lax.dot_general(
+        full = lax.dot_general(
             s_ref[k], g_ref[k], (((0,), (0,)), ((), ())), preferred_element_type=jnp.float32
         )
-        o_ref[:, k * width : (k + 1) * width] = product.astype(o_ref.dtype)
+        for c in range(width // lanes):
+            product[c] = full[:, c * lanes : (c + 1) * lanes]
+        for i in range(group):
+            for c in range(width // lanes):
+                rows = product[c, pl.ds(i, peers, stride=group), :]
+                start = k * width + c * lanes
+                o_ref[:, i, start : start + lanes] = rows.astype(o_ref.dtype)
 
 
-def grad_payload(second_factor, upstream):
+def grad_payload(second_factor, upstream, peers):
     col_blocks, rows, order = second_factor.shape
     width = upstream.shape[-1]
     flops = 2 * col_blocks * rows * order * width
     return pl.pallas_call(
         _grad_payload_kernel,
-        out_shape=jax.ShapeDtypeStruct((order, col_blocks * width), jnp.bfloat16),
+        out_shape=jax.ShapeDtypeStruct((peers, order // peers, col_blocks * width), jnp.bfloat16),
         in_specs=[pl.BlockSpec(memory_space=pltpu.VMEM)] * 2,
         out_specs=pl.BlockSpec(memory_space=pltpu.VMEM),
+        scratch_shapes=[pltpu.VMEM((width // 128, order, 128), jnp.float32)],
         cost_estimate=pl.CostEstimate(
             flops=flops, transcendentals=0, bytes_accessed=2 * (second_factor.size + 2 * upstream.size)
         ),
@@ -61,10 +70,10 @@
         "ipqj,sijd->psiqd", first_split, hidden_blocks, preferred_element_type=jnp.float32
     ).astype(jnp.bfloat16)
     upstream = grad_output.reshape(seq_count, col_blocks, block_count, channels)
-    grad_chunks = grad_payload(second_factor, upstream).reshape(
+    grad_chunks = grad_payload(second_factor, upstream, peers)
+    grad_rows = lax.all_to_all(grad_chunks, "seq", split_axis=0, concat_axis=0, tiled=True).reshape(
         peers, seq_count, blocks, col_blocks, channels
     )
-    grad_rows = lax.all_to_all(grad_chunks, "seq", split_axis=0, concat_axis=0, tiled=True)
     columns = lax.all_to_all(mixed_chunks, "seq", split_axis=0, concat_axis=0, tiled=True)
     halves = lax.axis_size("batch")
     me = lax.axis_index("batch")

time: 166 us -> 166 us (level)
  Pallas kernels: 4.47 us -> 8.46 us
  waiting for transfers between devices: 57.9 us -> 55.3 us
    pallas_call x1, Pallas kernels: 4.47 us -> 8.46 us  [grad_payload(): pl.pallas_call(_grad_payload_kernel, out_shape=jax.ShapeDtypeStruct((peer...]
    all_to_all x1, waiting for transfers between devices: 10.9 us -> 8.45 us  [body(): lax.all_to_all(mixed_chunks, 'seq', split_axis=0, concat_axis=0, tiled=True)]
    reshape x1, local copies, waits for them, and re-layouts: 3.94 us -> 1.5 us  [body(): lax.all_to_all(grad_chunks, 'seq', split_axis=0, concat_axis=0, tiled=True)]
    all_to_all x1 -> x0, local copies, waits for them, and re-layouts: 1.88 us -> none  [body(): lax.all_to_all(grad_chunks, 'seq', split_axis=0, concat_axis=0, tiled=True)]
  transfers between devices with their start and end apart: 6 -> 6, of which waited for: 4 -> 4; matrix products, arithmetic and copies ran while one was open for 27% -> 29% of each run, Pallas kernels for 0% -> 0%
where the time goes in v6:
time: 166 us; the launch traced here: 165 us
  waiting for transfers between devices  55.3 us (33%)
  starting transfers between devices  49.3 us (30%)
  local copies, waits for them, and re-layouts  26 us (16%)
  matrix products  13.1 us (8%)
  other arithmetic  12.2 us (7%)
  Pallas kernels  8.46 us (5%)
    all_to_all x1, waiting for transfers between devices, body(): lax.all_to_all(grad_chunks, 'seq', split_axis=0, concat_axis=0, tiled=True)  23.4 us
    ppermute x1, waiting for transfers between devices, body(): sent_second = lax.ppermute(second_part(other), 'batch', swap)  19.3 us
    all_to_all x1, starting transfers between devices, body(): lax.all_to_all(grad_chunks, 'seq', split_axis=0, concat_axis=0, tiled=True)  16.5 us
    all_to_all x1, starting transfers between devices, body(): lax.all_to_all(mixed_chunks, 'seq', split_axis=0, concat_axis=0, tiled=True)  14.8 us
    pallas_call x1, Pallas kernels, grad_payload(): pl.pallas_call(_grad_payload_kernel, out_shape=jax.ShapeDtypeStruct((peer...  8.46 us
    all_to_all x1, waiting for transfers between devices, body(): lax.all_to_all(mixed_chunks, 'seq', split_axis=0, concat_axis=0, tiled=True)  8.45 us
    ppermute x1, starting transfers between devices, body(): sent_second = lax.ppermute(second_part(other), 'batch', swap)  8.32 us
    ppermute x2, starting transfers between devices, passed_along(): lax.ppermute(value, axis, [(source, source + steps) for source in range(i...  6.85 us
  transfers between devices with their start and end apart: 6, of which 4 were waited for; matrix products, arithmetic and copies ran while one was open for 29% of the time, Pallas kernels for 0%

profile of v6, /device:TPU:1, one launch (start us, length us, event | category | flops | bytes accessed | tf_op | source)
XLA Modules:
  0.0 165.0 jit_solution(10572670601490870297)
XLA Ops:
  0.6 8.5 %shard_map.76 = bf16[128,4,1536]{2,1,0:T(4,128)(2,1)} custom-call(bf16[4,512,512]{2,1,0:T(8,128)(2,1)} %s_ref.1, bf16[4,512,384]{2,1,0:T(8,128)(2,1)} %bitcast.75), custom_call_target="tpu_custom_call" | custom-call | flops 805306368 | bytes 5242880 | tf_op jit(solution)/shard_map/pallas_call | solution.py:30
  9.1 16.5 %all-to-all-start = ((bf16[128,4,1536]{2,1,0:T(4,128)(2,1)}), bf16[128,4,1536]{2,1,0:T(4,128)(2,1)S(1)}, u32[]{:S(2)}, u32[]{:S(2)}) async-start(bf16[128,4,1536]{2,1,0:T(4,128)(2,1)} %shard_map.76), calls=%async_computation | async-start | bytes 3145728 | tf_op jit(solution)/shard_map/all_to_all | solution.py:74
  25.7 3.5 %collective-permute-start = (bf16[1,3,384]{2,1,0:T(4,128)(2,1)S(1)}, bf16[1,3,384]{2,1,0:T(4,128)(2,1)S(1)}, u32[]{:S(2)}, u32[]{:S(2)}) collective-permute-start(bf16[1,3,384]{2,1,0:T(4,128)(2,1)S(1)} %slice.47), channel_id=1, source_target_pairs={{0,1},{1,2},{2,3},{3,4},{4,5},{5,6},{6,7},{7,8},{8,9},{9,10},{10,1... | collective-permute-start | bytes 6920 | tf_op jit(solution)/shard_map/ppermute | solution.py:45
  29.2 4.0 %reshape.131 = bf16[4,128,4,512]{3,2,1,0:T(4,128)(2,1)} reshape(bf16[4,512,512]{2,1,0:T(8,128)(2,1)} %param.7) | data formatting | bytes 4194304 | tf_op jit(solution)/shard_map/reshape | solution.py:68
  33.6 3.1 %multiply_convert_fusion = (bf16[1,2048,384]{2,1,0:T(8,128)(2,1)S(1)}, f32[1,2048,384]{2,1,0:T(8,128)}) fusion(f32[1,2051,384]{2,1,0:T(8,128)S(1)} %maximum_convert_fusion, f32[384]{0:T(512)S(1)} %get-tuple-element.11, f32[384]{0:T(512)S(1)} %get-tuple-element.12, f32[384]{0:T(512)S(1)} %get-tuple-element.10, f32[384]{0:T(512)S(1)} %get-tuple-element.9), kind=kLoop, calls=%fused_computation.18 | loop fusion | flops 9437184 | bytes 17307648 | tf_op jit(solution)/shard_map/convert_element_type | solution.py:66
  36.7 2.6 %fusion.31 = bf16[128,1,4,4,384]{0,4,3,2,1:T(8,128)(2,1)} fusion(bf16[4,512,384,1]{2,1,3,0:T(8,128)(2,1)S(1)} %bitcast.71, bf16[4,128,4,512]{3,2,1,0:T(4,128)(2,1)S(1)} %copy-done), kind=kOutput, calls=%fused_computation.41 | convolution fusion | flops 806092800 | bytes 5242880 | tf_op jit(solution)/shard_map/ipqj,sijd->psiqd/dot_general | solution.py:69
  39.3 3.9 %copy.40 = bf16[128,1,4,4,384]{4,3,2,1,0:T(4,128)(2,1)} copy(bf16[128,1,4,4,384]{0,4,3,2,1:T(8,128)(2,1)} %fusion.31) | data formatting | bytes 3145728 | tf_op jit(solution)/shard_map/convert_element_type | solution.py:71
  43.2 23.4 %all-to-all-done = bf16[128,4,1536]{2,1,0:T(4,128)(2,1)S(1)} async-done(((bf16[128,4,1536]{2,1,0:T(4,128)(2,1)}), bf16[128,4,1536]{2,1,0:T(4,128)(2,1)S(1)}, u32[]{:S(2)}, u32[]{:S(2)}) %all-to-all-start) | async-done | bytes 1572896 | tf_op jit(solution)/shard_map/all_to_all | solution.py:74
  66.6 14.8 %all-to-all-start.1 = ((bf16[128,1,4,4,384]{4,3,2,1,0:T(4,128)(2,1)}), bf16[128,1,4,4,384]{4,3,2,1,0:T(4,128)(2,1)}, u32[]{:S(2)}, u32[]{:S(2)}) async-start(bf16[128,1,4,4,384]{4,3,2,1,0:T(4,128)(2,1)} %copy.40), calls=%async_computation.1 | async-start | bytes 3145728 | tf_op jit(solution)/shard_map/all_to_all | solution.py:77
  82.9 1.9 %constant_dynamic-slice_fusion = (bf16[64,1,4,4,384]{4,3,2,0,1:T(4,128)(2,1)S(1)}, bf16[64,1,4,4,384]{4,3,2,0,1:T(4,128)(2,1)S(1)}) fusion(bf16[128,1,4,4,384]{4,3,2,0,1:T(4,128)(2,1)} %reshape.133, s32[]{:T(128)S(6)} %select_n.13, s32[]{:T(128)S(6)} %select_n.12), kind=kLoop, calls=%fused_computation.58 | loop fusion | bytes 3145736 | tf_op jit(solution)/shard_map/dynamic_slice | solution.py:91
  85.6 2.7 %copy.35 = f32[4,64,4,512]{3,0,2,1:T(4,128)} copy(f32[4,64,4,512]{3,1,2,0:T(8,128)S(1)} %fusion.27) | data formatting | bytes 4194304 | tf_op jit(solution)/shard_map/convert_element_type | solution.py:106
  90.8 2.8 %collective-permute-start.2 = (bf16[4,256,512]{2,0,1:T(4,128)(2,1)}, bf16[4,256,512]{2,0,1:T(4,128)(2,1)}, u32[]{:S(2)}, u32[]{:S(2)}) collective-permute-start(bf16[4,256,512]{2,0,1:T(4,128)(2,1)} %bitcast.15), channel_id=1, source_target_pairs={{0,128},{128,0},{1,129},{129,1},{2,130},{130,2},{3,131},{131,3},{4... | collective-permute-start | bytes 3145736 | tf_op jit(solution)/shard_map/ppermute | solution.py:98
  95.0 4.3 %convolution_bitcast_fusion = f32[1,4,512,384]{2,3,1,0:T(8,128)} fusion(bf16[128,4,4,384]{0,3,2,1:T(8,128)(2,1)S(1)} %bitcast.74, bf16[4,128,4,512]{3,2,1,0:T(4,128)(2,1)} %reshape.131), kind=kOutput, calls=%fused_computation.24 | convolution fusion | flops 805306368 | bytes 6815744 | tf_op jit(solution)/shard_map/ipqj,psiqd->sijd/dot_general | solution.py:99
  99.4 2.4 %copy.33 = f32[1,4,512,384]{3,2,1,0:T(8,128)S(1)} copy(f32[1,4,512,384]{2,3,1,0:T(8,128)} %convolution_bitcast_fusion) | data formatting | bytes 6291456 | tf_op jit(solution)/shard_map/ipqj,psiqd->sijd/transpose | solution.py:99
  101.8 3.4 %fusion.8 = bf16[1,2048,384]{2,1,0:T(8,128)(2,1)S(1)} fusion(f32[1,4,512,384]{3,2,1,0:T(8,128)S(1)} %copy.33, f32[1,2048,384]{2,1,0:T(8,128)} %get-tuple-element.14), kind=kLoop, calls=%fused_computation.17 | loop fusion | flops 7077888 | bytes 7864320 | tf_op jit(solution)/shard_map/convert_element_type | solution.py:108
  106.3 3.3 %collective-permute-start.1 = (bf16[1,3,384]{2,1,0:T(4,128)(2,1)S(1)}, bf16[1,3,384]{2,1,0:T(4,128)(2,1)S(1)}, u32[]{:S(2)}, u32[]{:S(2)}) collective-permute-start(bf16[1,3,384]{2,1,0:T(4,128)(2,1)S(1)} %slice.64), channel_id=1, source_target_pairs={{1,0},{2,1},{3,2},{4,3},{5,4},{6,5},{7,6},{8,7},{9,8},{10,9},{11,1... | collective-permute-start | bytes 6920 | tf_op jit(solution)/shard_map/ppermute | solution.py:45
  109.6 8.5 %all-to-all-done.1 = bf16[128,1,4,4,384]{4,3,2,1,0:T(4,128)(2,1)} async-done(((bf16[128,1,4,4,384]{4,3,2,1,0:T(4,128)(2,1)}), bf16[128,1,4,4,384]{4,3,2,1,0:T(4,128)(2,1)}, u32[]{:S(2)}, u32[]{:S(2)}) %all-to-all-start.1) | async-done | bytes 1572896 | tf_op jit(solution)/shard_map/all_to_all | solution.py:77
  118.1 2.5 %fusion.24 = bf16[4,256,128,4]{1,2,3,0:T(8,128)(2,1)S(1)} fusion(bf16[128,1,4,4,384]{4,3,2,1,0:T(4,128)(2,1)} %all-to-all-done.1, bf16[1,4,512,384]{3,2,1,0:T(8,128)(2,1)} %bitcast.76, s32[]{:T(128)S(6)} %select_n.15), kind=kOutput, calls=%fused_computation.36 | convolution fusion | flops 403177472 | bytes 3407876 | tf_op jit(solution)/shard_map/skmd,psikd->kmpi/dot_general | solution.py:86
  121.4 8.3 %collective-permute-start.3 = (bf16[4,256,512]{1,0,2:T(4,128)(2,1)S(1)}, bf16[4,256,512]{1,0,2:T(4,128)(2,1)S(1)}, u32[]{:S(2)}, u32[]{:S(2)}) collective-permute-start(bf16[4,256,512]{1,0,2:T(4,128)(2,1)S(1)} %bitcast.78), channel_id=1, source_target_pairs={{0,128},{128,0},{1,129},{129,1},{2,130},{130,2},{3,131},{131,3},{4... | collective-permute-start | bytes 3145736 | tf_op jit(solution)/shard_map/ppermute | solution.py:97
  130.0 2.2 %fusion.28 = f32[4,256,128,4]{1,2,3,0:T(8,128)S(1)} fusion(bf16[128,1,4,4,384]{4,3,2,1,0:T(4,128)(2,1)} %all-to-all-done.1, bf16[1,4,512,384]{3,2,1,0:T(8,128)(2,1)S(1)} %bitcast.77, s32[]{:T(128)S(6)} %select_n.14), kind=kOutput, calls=%fused_computation.40 | convolution fusion | flops 403701760 | bytes 4456452 | tf_op jit(solution)/shard_map/skmd,psikd->kmpi/dot_general | solution.py:86
  133.5 2.5 %fusion.1 = bf16[1,2048,384]{2,1,0:T(8,128)(2,1)} fusion(f32[1,2051,384]{2,1,0:T(8,128)S(1)} %maximum_convert_fusion.1, f32[384]{0:T(512)S(1)} %get-tuple-element.11, f32[384]{0:T(512)S(1)} %get-tuple-element.12, f32[384]{0:T(512)S(1)} %get-tuple-element.10, f32[384]{0:T(512)S(1)} %get-tuple-element.9), kind=kLoop, calls=%fused_computation.2 | loop fusion | flops 6291456 | bytes 14161920 | tf_op jit(solution)/shard_map/convert_element_type | solution.py:113
  136.0 4.1 %collective-permute-done.2 = bf16[4,256,512]{2,0,1:T(4,128)(2,1)} collective-permute-done((bf16[4,256,512]{2,0,1:T(4,128)(2,1)}, bf16[4,256,512]{2,0,1:T(4,128)(2,1)}, u32[]{:S(2)}, u32[]{:S(2)}) %collective-permute-start.2) | collective-permute-done | bytes 1048608 | tf_op jit(solution)/shard_map/ppermute | solution.py:98
  140.2 1.9 %fusion.10 = bf16[4,256,512]{2,0,1:T(4,128)(2,1)S(1)} fusion(f32[4,64,4,512]{3,0,2,1:T(4,128)S(1)} %copy-done.1, bf16[4,256,512]{2,0,1:T(4,128)(2,1)} %collective-permute-done.2), kind=kLoop, calls=%fused_computation.23 | loop fusion | flops 1572864 | bytes 4194304 | tf_op jit(solution)/shard_map/convert_element_type | solution.py:107
  143.3 19.3 %collective-permute-done.3 = bf16[4,256,512]{1,0,2:T(4,128)(2,1)S(1)} collective-permute-done((bf16[4,256,512]{1,0,2:T(4,128)(2,1)S(1)}, bf16[4,256,512]{1,0,2:T(4,128)(2,1)S(1)}, u32[]{:S(2)}, u32[]{:S(2)}) %collective-permute-start.3) | collective-permute-done | bytes 1048608 | tf_op jit(solution)/shard_map/ppermute | solution.py:97
  (31 shorter events, 13.7 us)
Async XLA Ops:
  9.1 16.5 %copy-start.5 = (bf16[1,2048,384]{2,1,0:T(8,128)(2,1)S(1)}, bf16[1,2048,384]{2,1,0:T(8,128)(2,1)}, u32[]{:S(2)}) copy-start(bf16[1,2048,384]{2,1,0:T(8,128)(2,1)} %param.5) | copy-start | bytes 4718596
  9.1 20.1 %copy-start.6 = (f32[4,384]{1,0:T(4,128)S(1)}, f32[4,384]{1,0:T(4,128)}, u32[]{:S(2)}) copy-start(f32[4,384]{1,0:T(4,128)} %param.6) | copy-start | bytes 18436
  9.1 57.5 %all-to-all-start = ((bf16[128,4,1536]{2,1,0:T(4,128)(2,1)}), bf16[128,4,1536]{2,1,0:T(4,128)(2,1)S(1)}, u32[]{:S(2)}, u32[]{:S(2)}) async-start(bf16[128,4,1536]{2,1,0:T(4,128)(2,1)} %shard_map.76), calls=%async_computation | async-start | bytes 3145728 | tf_op jit(solution)/shard_map/all_to_all | solution.py:74
  25.7 7.6 %collective-permute-start = (bf16[1,3,384]{2,1,0:T(4,128)(2,1)S(1)}, bf16[1,3,384]{2,1,0:T(4,128)(2,1)S(1)}, u32[]{:S(2)}, u32[]{:S(2)}) collective-permute-start(bf16[1,3,384]{2,1,0:T(4,128)(2,1)S(1)} %slice.47), channel_id=1, source_target_pairs={{0,1},{1,2},{2,3},{3,4},{4,5},{5,6},{6,7},{7,8},{8,9},{9,10},{10,1... | collective-permute-start | bytes 6920 | tf_op jit(solution)/shard_map/ppermute | solution.py:45
  33.6 3.1 %copy-start = (bf16[4,128,4,512]{3,2,1,0:T(4,128)(2,1)S(1)}, bf16[4,128,4,512]{3,2,1,0:T(4,128)(2,1)}, u32[]{:S(2)}) copy-start(bf16[4,128,4,512]{3,2,1,0:T(4,128)(2,1)} %reshape.131) | copy-start | bytes 6291460
  66.6 51.5 %all-to-all-start.1 = ((bf16[128,1,4,4,384]{4,3,2,1,0:T(4,128)(2,1)}), bf16[128,1,4,4,384]{4,3,2,1,0:T(4,128)(2,1)}, u32[]{:S(2)}, u32[]{:S(2)}) async-start(bf16[128,1,4,4,384]{4,3,2,1,0:T(4,128)(2,1)} %copy.40), calls=%async_computation.1 | async-start | bytes 3145728 | tf_op jit(solution)/shard_map/all_to_all | solution.py:77
  90.8 49.4 %collective-permute-start.2 = (bf16[4,256,512]{2,0,1:T(4,128)(2,1)}, bf16[4,256,512]{2,0,1:T(4,128)(2,1)}, u32[]{:S(2)}, u32[]{:S(2)}) collective-permute-start(bf16[4,256,512]{2,0,1:T(4,128)(2,1)} %bitcast.15), channel_id=1, source_target_pairs={{0,128},{128,0},{1,129},{129,1},{2,130},{130,2},{3,131},{131,3},{4... | collective-permute-start | bytes 3145736 | tf_op jit(solution)/shard_map/ppermute | solution.py:98
  105.1 1.1 copy-start.2
  106.3 23.4 %collective-permute-start.1 = (bf16[1,3,384]{2,1,0:T(4,128)(2,1)S(1)}, bf16[1,3,384]{2,1,0:T(4,128)(2,1)S(1)}, u32[]{:S(2)}, u32[]{:S(2)}) collective-permute-start(bf16[1,3,384]{2,1,0:T(4,128)(2,1)S(1)} %slice.64), channel_id=1, source_target_pairs={{1,0},{2,1},{3,2},{4,3},{5,4},{6,5},{7,6},{8,7},{9,8},{10,9},{11,1... | collective-permute-start | bytes 6920 | tf_op jit(solution)/shard_map/ppermute | solution.py:45
  118.1 11.7 %copy-start.3 = (bf16[1,2048,384]{2,1,0:T(8,128)(2,1)S(1)}, bf16[1,2048,384]{2,1,0:T(8,128)(2,1)}, u32[]{:S(2)}) copy-start(bf16[1,2048,384]{2,1,0:T(8,128)(2,1)} %copy-done.2) | copy-start | bytes 4718596
  121.4 8.6 %copy-start.4 = (bf16[1,2048,384]{2,1,0:T(8,128)(2,1)S(1)}, bf16[1,2048,384]{2,1,0:T(8,128)(2,1)}, u32[]{:S(2)}) copy-start(bf16[1,2048,384]{2,1,0:T(8,128)(2,1)} %param.9) | copy-start | bytes 4718596
  121.4 41.1 %collective-permute-start.3 = (bf16[4,256,512]{1,0,2:T(4,128)(2,1)S(1)}, bf16[4,256,512]{1,0,2:T(4,128)(2,1)S(1)}, u32[]{:S(2)}, u32[]{:S(2)}) collective-permute-start(bf16[4,256,512]{1,0,2:T(4,128)(2,1)S(1)} %bitcast.78), channel_id=1, source_target_pairs={{0,128},{128,0},{1,129},{129,1},{2,130},{130,2},{3,131},{131,3},{4... | collective-permute-start | bytes 3145736 | tf_op jit(solution)/shard_map/ppermute | solution.py:97
  133.5 6.7 %copy-start.1 = (f32[4,64,4,512]{3,0,2,1:T(4,128)S(1)}, f32[4,64,4,512]{3,0,2,1:T(4,128)}, u32[]{:S(2)}) copy-start(f32[4,64,4,512]{3,0,2,1:T(4,128)} %copy.35) | copy-start | bytes 6291460

commit v7 on v5

--- a/solution.py
+++ b/solution.py
@@ -7,12 +7,10 @@
 
 
 def _grad_payload_kernel(s_ref, g_ref, o_ref):
-    width = g_ref.shape[-1]
-    for k in range(s_ref.shape[0]):
-        product = lax.dot_general(
-            s_ref[k], g_ref[k], (((0,), (0,)), ((), ())), preferred_element_type=jnp.float32
-        )
-        o_ref[:, k * width : (k + 1) * width] = product.astype(o_ref.dtype)
+    product = lax.dot_general(
+        s_ref[0], g_ref[0], (((0,), (0,)), ((), ())), preferred_element_type=jnp.float32
+    )
+    o_ref[...] = product.astype(o_ref.dtype)
 
 
 def grad_payload(second_factor, upstream):
@@ -21,9 +19,13 @@
     flops = 2 * col_blocks * rows * order * width
     return pl.pallas_call(
         _grad_payload_kernel,
+        grid=(col_blocks,),
         out_shape=jax.ShapeDtypeStruct((order, col_blocks * width), jnp.bfloat16),
-        in_specs=[pl.BlockSpec(memory_space=pltpu.VMEM)] * 2,
-        out_specs=pl.BlockSpec(memory_space=pltpu.VMEM),
+        in_specs=[
+            pl.BlockSpec((1, rows, order), lambda k: (k, 0, 0)),
+            pl.BlockSpec((1, rows, width), lambda k: (k, 0, 0)),
+        ],
+        out_specs=pl.BlockSpec((order, width), lambda k: (0, k)),
         cost_estimate=pl.CostEstimate(
             flops=flops, transcendentals=0, bytes_accessed=2 * (second_factor.size + 2 * upstream.size)
         ),

time: 166 us -> 166 us (level)
  no operation moved by 1% of the time
where the time goes in v7:
time: 166 us; the launch traced here: 165 us
  waiting for transfers between devices  57.8 us (35%)
  starting transfers between devices  49.2 us (30%)
  local copies, waits for them, and re-layouts  27.5 us (17%)
  matrix products  13 us (8%)
  other arithmetic  12.2 us (7%)
  Pallas kernels  4.82 us (3%)
    all_to_all x1, waiting for transfers between devices, body(): lax.all_to_all(grad_chunks, 'seq', split_axis=0, concat_axis=0, tiled=True)  23.5 us
    ppermute x1, waiting for transfers between devices, body(): sent_second = lax.ppermute(second_part(other), 'batch', swap)  19.3 us
    all_to_all x1, starting transfers between devices, body(): lax.all_to_all(grad_chunks, 'seq', split_axis=0, concat_axis=0, tiled=True)  16.5 us
    all_to_all x1, starting transfers between devices, body(): lax.all_to_all(mixed_chunks, 'seq', split_axis=0, concat_axis=0, tiled=True)  14.8 us
    all_to_all x1, waiting for transfers between devices, body(): lax.all_to_all(mixed_chunks, 'seq', split_axis=0, concat_axis=0, tiled=True)  10.9 us
    ppermute x1, starting transfers between devices, body(): sent_second = lax.ppermute(second_part(other), 'batch', swap)  8.31 us
    ppermute x2, starting transfers between devices, passed_along(): lax.ppermute(value, axis, [(source, source + steps) for source in range(i...  6.84 us
    pallas_call x1, Pallas kernels, grad_payload(): pl.pallas_call(_grad_payload_kernel, grid=(col_blocks,), out_shape=jax.Sh...  4.82 us
  transfers between devices with their start and end apart: 6, of which 4 were waited for; matrix products, arithmetic and copies ran while one was open for 27% of the time, Pallas kernels for 0%

profile of v7, /device:TPU:1, one launch (start us, length us, event | category | flops | bytes accessed | tf_op | source)
XLA Modules:
  0.0 165.2 jit_solution(17670344065071723411)
XLA Ops:
  0.6 4.8 %shard_map.76 = bf16[512,1536]{1,0:T(8,128)(2,1)} custom-call(bf16[4,512,512]{2,1,0:T(8,128)(2,1)} %s_ref.1, bf16[4,512,384]{2,1,0:T(8,128)(2,1)} %bitcast.76), custom_call_target="tpu_custom_call" | custom-call | flops 805306368 | bytes 5242880 | tf_op jit(solution)/shard_map/pallas_call | solution.py:20
  5.4 3.9 %reshape.129 = bf16[128,1,4,4,384]{4,3,2,0,1:T(4,128)(2,1)} reshape(bf16[512,1536]{1,0:T(8,128)(2,1)} %shard_map.76) | data formatting | bytes 3145728 | tf_op jit(solution)/shard_map/reshape | solution.py:66
  9.4 16.5 %all-to-all-start = ((bf16[128,1,4,4,384]{4,3,2,1,0:T(4,128)(2,1)}), bf16[128,1,4,4,384]{4,3,2,1,0:T(4,128)(2,1)S(1)}, u32[]{:S(2)}, u32[]{:S(2)}) async-start(bf16[128,1,4,4,384]{4,3,2,1,0:T(4,128)(2,1)} %bitcast.1), calls=%async_computation | async-start | bytes 3145728 | tf_op jit(solution)/shard_map/all_to_all | solution.py:69
  26.0 3.5 %collective-permute-start = (bf16[1,3,384]{2,1,0:T(4,128)(2,1)S(1)}, bf16[1,3,384]{2,1,0:T(4,128)(2,1)S(1)}, u32[]{:S(2)}, u32[]{:S(2)}) collective-permute-start(bf16[1,3,384]{2,1,0:T(4,128)(2,1)S(1)} %slice.47), channel_id=1, source_target_pairs={{0,1},{1,2},{2,3},{3,4},{4,5},{5,6},{6,7},{7,8},{8,9},{9,10},{10,1... | collective-permute-start | bytes 6920 | tf_op jit(solution)/shard_map/ppermute | solution.py:38
  29.5 4.0 %reshape.131 = bf16[4,128,4,512]{3,2,1,0:T(4,128)(2,1)} reshape(bf16[4,512,512]{2,1,0:T(8,128)(2,1)} %param.7) | data formatting | bytes 4194304 | tf_op jit(solution)/shard_map/reshape | solution.py:61
  33.9 3.1 %multiply_convert_fusion = (bf16[1,2048,384]{2,1,0:T(8,128)(2,1)S(1)}, f32[1,2048,384]{2,1,0:T(8,128)}) fusion(f32[1,2051,384]{2,1,0:T(8,128)S(1)} %maximum_convert_fusion, f32[384]{0:T(512)S(1)} %get-tuple-element.11, f32[384]{0:T(512)S(1)} %get-tuple-element.12, f32[384]{0:T(512)S(1)} %get-tuple-element.10, f32[384]{0:T(512)S(1)} %get-tuple-element.9), kind=kLoop, calls=%fused_computation.18 | loop fusion | flops 9437184 | bytes 17307648 | tf_op jit(solution)/shard_map/convert_element_type | solution.py:59
  37.0 2.5 %fusion.32 = bf16[128,1,4,4,384]{0,4,3,2,1:T(8,128)(2,1)} fusion(bf16[4,512,384,1]{2,1,3,0:T(8,128)(2,1)S(1)} %bitcast.73, bf16[4,128,4,512]{3,2,1,0:T(4,128)(2,1)S(1)} %copy-done), kind=kOutput, calls=%fused_computation.42 | convolution fusion | flops 806092800 | bytes 5242880 | tf_op jit(solution)/shard_map/ipqj,sijd->psiqd/dot_general | solution.py:62
  39.5 3.9 %copy.39 = bf16[128,1,4,4,384]{4,3,2,1,0:T(4,128)(2,1)} copy(bf16[128,1,4,4,384]{0,4,3,2,1:T(8,128)(2,1)} %fusion.32) | data formatting | bytes 3145728 | tf_op jit(solution)/shard_map/convert_element_type | solution.py:64
  43.4 23.5 %all-to-all-done = bf16[128,1,4,4,384]{4,3,2,1,0:T(4,128)(2,1)S(1)} async-done(((bf16[128,1,4,4,384]{4,3,2,1,0:T(4,128)(2,1)}), bf16[128,1,4,4,384]{4,3,2,1,0:T(4,128)(2,1)S(1)}, u32[]{:S(2)}, u32[]{:S(2)}) %all-to-all-start) | async-done | bytes 1572896 | tf_op jit(solution)/shard_map/all_to_all | solution.py:69
  66.9 14.8 %all-to-all-start.1 = ((bf16[128,1,4,4,384]{4,3,2,1,0:T(4,128)(2,1)}), bf16[128,1,4,4,384]{4,3,2,1,0:T(4,128)(2,1)}, u32[]{:S(2)}, u32[]{:S(2)}) async-start(bf16[128,1,4,4,384]{4,3,2,1,0:T(4,128)(2,1)} %copy.39), calls=%async_computation.1 | async-start | bytes 3145728 | tf_op jit(solution)/shard_map/all_to_all | solution.py:70
  83.0 2.7 %copy.34 = f32[4,64,4,512]{3,0,2,1:T(4,128)} copy(f32[4,64,4,512]{3,1,2,0:T(8,128)S(1)} %fusion.28) | data formatting | bytes 4194304 | tf_op jit(solution)/shard_map/convert_element_type | solution.py:99
  88.2 2.7 %collective-permute-start.2 = (bf16[4,256,512]{2,0,1:T(4,128)(2,1)}, bf16[4,256,512]{2,0,1:T(4,128)(2,1)}, u32[]{:S(2)}, u32[]{:S(2)}) collective-permute-start(bf16[4,256,512]{2,0,1:T(4,128)(2,1)} %bitcast.16), channel_id=1, source_target_pairs={{0,128},{128,0},{1,129},{129,1},{2,130},{130,2},{3,131},{131,3},{4... | collective-permute-start | bytes 3145736 | tf_op jit(solution)/shard_map/ppermute | solution.py:91
  92.8 4.3 %convolution_bitcast_fusion = f32[1,4,512,384]{2,3,1,0:T(8,128)} fusion(bf16[4,128,4,512]{3,2,1,0:T(4,128)(2,1)} %reshape.131, bf16[128,1,4,4,384]{0,4,3,2,1:T(8,128)(2,1)S(1)} %copy.30), kind=kOutput, calls=%fused_computation.24 | convolution fusion | flops 805306368 | bytes 6815744 | tf_op jit(solution)/shard_map/ipqj,psiqd->sijd/dot_general | solution.py:92
  97.2 2.4 %copy.32 = f32[1,4,512,384]{3,2,1,0:T(8,128)S(1)} copy(f32[1,4,512,384]{2,3,1,0:T(8,128)} %convolution_bitcast_fusion) | data formatting | bytes 6291456 | tf_op jit(solution)/shard_map/ipqj,psiqd->sijd/transpose | solution.py:92
  99.6 3.4 %fusion.8 = bf16[1,2048,384]{2,1,0:T(8,128)(2,1)S(1)} fusion(f32[1,4,512,384]{3,2,1,0:T(8,128)S(1)} %copy.32, f32[1,2048,384]{2,1,0:T(8,128)} %get-tuple-element.14), kind=kLoop, calls=%fused_computation.17 | loop fusion | flops 7077888 | bytes 7864320 | tf_op jit(solution)/shard_map/convert_element_type | solution.py:101
  104.1 3.3 %collective-permute-start.1 = (bf16[1,3,384]{2,1,0:T(4,128)(2,1)S(1)}, bf16[1,3,384]{2,1,0:T(4,128)(2,1)S(1)}, u32[]{:S(2)}, u32[]{:S(2)}) collective-permute-start(bf16[1,3,384]{2,1,0:T(4,128)(2,1)S(1)} %slice.64), channel_id=1, source_target_pairs={{1,0},{2,1},{3,2},{4,3},{5,4},{6,5},{7,6},{8,7},{9,8},{10,9},{11,1... | collective-permute-start | bytes 6920 | tf_op jit(solution)/shard_map/ppermute | solution.py:38
  107.4 10.9 %all-to-all-done.1 = bf16[128,1,4,4,384]{4,3,2,1,0:T(4,128)(2,1)} async-done(((bf16[128,1,4,4,384]{4,3,2,1,0:T(4,128)(2,1)}), bf16[128,1,4,4,384]{4,3,2,1,0:T(4,128)(2,1)}, u32[]{:S(2)}, u32[]{:S(2)}) %all-to-all-start.1) | async-done | bytes 1572896 | tf_op jit(solution)/shard_map/all_to_all | solution.py:70
  118.3 2.5 %fusion.25 = bf16[4,256,128,4]{1,2,3,0:T(8,128)(2,1)S(1)} fusion(bf16[128,1,4,4,384]{4,3,2,1,0:T(4,128)(2,1)} %all-to-all-done.1, bf16[1,4,512,384]{3,2,1,0:T(8,128)(2,1)} %bitcast.77, s32[]{:T(128)S(6)} %select_n.15), kind=kOutput, calls=%fused_computation.37 | convolution fusion | flops 403177472 | bytes 3407876 | tf_op jit(solution)/shard_map/skmd,psikd->kmpi/dot_general | solution.py:79
  121.6 8.3 %collective-permute-start.3 = (bf16[4,256,512]{1,0,2:T(4,128)(2,1)S(1)}, bf16[4,256,512]{1,0,2:T(4,128)(2,1)S(1)}, u32[]{:S(2)}, u32[]{:S(2)}) collective-permute-start(bf16[4,256,512]{1,0,2:T(4,128)(2,1)S(1)} %bitcast.79), channel_id=1, source_target_pairs={{0,128},{128,0},{1,129},{129,1},{2,130},{130,2},{3,131},{131,3},{4... | collective-permute-start | bytes 3145736 | tf_op jit(solution)/shard_map/ppermute | solution.py:90
  130.2 2.2 %fusion.29 = f32[4,256,128,4]{1,2,3,0:T(8,128)S(1)} fusion(bf16[128,1,4,4,384]{4,3,2,1,0:T(4,128)(2,1)} %all-to-all-done.1, bf16[1,4,512,384]{3,2,1,0:T(8,128)(2,1)S(1)} %bitcast.78, s32[]{:T(128)S(6)} %select_n.14), kind=kOutput, calls=%fused_computation.41 | convolution fusion | flops 403701760 | bytes 4456452 | tf_op jit(solution)/shard_map/skmd,psikd->kmpi/dot_general | solution.py:79
  133.7 2.5 %fusion.1 = bf16[1,2048,384]{2,1,0:T(8,128)(2,1)} fusion(f32[1,2051,384]{2,1,0:T(8,128)S(1)} %maximum_convert_fusion.1, f32[384]{0:T(512)S(1)} %get-tuple-element.11, f32[384]{0:T(512)S(1)} %get-tuple-element.12, f32[384]{0:T(512)S(1)} %get-tuple-element.10, f32[384]{0:T(512)S(1)} %get-tuple-element.9), kind=kLoop, calls=%fused_computation.2 | loop fusion | flops 6291456 | bytes 14161920 | tf_op jit(solution)/shard_map/convert_element_type | solution.py:106
  136.3 4.1 %collective-permute-done.2 = bf16[4,256,512]{2,0,1:T(4,128)(2,1)} collective-permute-done((bf16[4,256,512]{2,0,1:T(4,128)(2,1)}, bf16[4,256,512]{2,0,1:T(4,128)(2,1)}, u32[]{:S(2)}, u32[]{:S(2)}) %collective-permute-start.2) | collective-permute-done | bytes 1048608 | tf_op jit(solution)/shard_map/ppermute | solution.py:91
  140.4 1.9 %fusion.10 = bf16[4,256,512]{2,0,1:T(4,128)(2,1)S(1)} fusion(f32[4,64,4,512]{3,0,2,1:T(4,128)S(1)} %copy-done.1, bf16[4,256,512]{2,0,1:T(4,128)(2,1)} %collective-permute-done.2), kind=kLoop, calls=%fused_computation.23 | loop fusion | flops 1572864 | bytes 4194304 | tf_op jit(solution)/shard_map/convert_element_type | solution.py:100
  143.5 19.3 %collective-permute-done.3 = bf16[4,256,512]{1,0,2:T(4,128)(2,1)S(1)} collective-permute-done((bf16[4,256,512]{1,0,2:T(4,128)(2,1)S(1)}, bf16[4,256,512]{1,0,2:T(4,128)(2,1)S(1)}, u32[]{:S(2)}, u32[]{:S(2)}) %collective-permute-start.3) | collective-permute-done | bytes 1048608 | tf_op jit(solution)/shard_map/ppermute | solution.py:90
  (31 shorter events, 13.2 us)
Async XLA Ops:
  9.4 16.5 %copy-start.5 = (bf16[1,2048,384]{2,1,0:T(8,128)(2,1)S(1)}, bf16[1,2048,384]{2,1,0:T(8,128)(2,1)}, u32[]{:S(2)}) copy-start(bf16[1,2048,384]{2,1,0:T(8,128)(2,1)} %param.5) | copy-start | bytes 4718596
  9.4 20.1 %copy-start.6 = (f32[4,384]{1,0:T(4,128)S(1)}, f32[4,384]{1,0:T(4,128)}, u32[]{:S(2)}) copy-start(f32[4,384]{1,0:T(4,128)} %param.6) | copy-start | bytes 18436
  9.4 57.5 %all-to-all-start = ((bf16[128,1,4,4,384]{4,3,2,1,0:T(4,128)(2,1)}), bf16[128,1,4,4,384]{4,3,2,1,0:T(4,128)(2,1)S(1)}, u32[]{:S(2)}, u32[]{:S(2)}) async-start(bf16[128,1,4,4,384]{4,3,2,1,0:T(4,128)(2,1)} %bitcast.1), calls=%async_computation | async-start | bytes 3145728 | tf_op jit(solution)/shard_map/all_to_all | solution.py:69
  26.0 7.6 %collective-permute-start = (bf16[1,3,384]{2,1,0:T(4,128)(2,1)S(1)}, bf16[1,3,384]{2,1,0:T(4,128)(2,1)S(1)}, u32[]{:S(2)}, u32[]{:S(2)}) collective-permute-start(bf16[1,3,384]{2,1,0:T(4,128)(2,1)S(1)} %slice.47), channel_id=1, source_target_pairs={{0,1},{1,2},{2,3},{3,4},{4,5},{5,6},{6,7},{7,8},{8,9},{9,10},{10,1... | collective-permute-start | bytes 6920 | tf_op jit(solution)/shard_map/ppermute | solution.py:38
  33.9 3.1 %copy-start = (bf16[4,128,4,512]{3,2,1,0:T(4,128)(2,1)S(1)}, bf16[4,128,4,512]{3,2,1,0:T(4,128)(2,1)}, u32[]{:S(2)}) copy-start(bf16[4,128,4,512]{3,2,1,0:T(4,128)(2,1)} %reshape.131) | copy-start | bytes 6291460
  66.9 51.4 %all-to-all-start.1 = ((bf16[128,1,4,4,384]{4,3,2,1,0:T(4,128)(2,1)}), bf16[128,1,4,4,384]{4,3,2,1,0:T(4,128)(2,1)}, u32[]{:S(2)}, u32[]{:S(2)}) async-start(bf16[128,1,4,4,384]{4,3,2,1,0:T(4,128)(2,1)} %copy.39), calls=%async_computation.1 | async-start | bytes 3145728 | tf_op jit(solution)/shard_map/all_to_all | solution.py:70
  88.2 52.2 %collective-permute-start.2 = (bf16[4,256,512]{2,0,1:T(4,128)(2,1)}, bf16[4,256,512]{2,0,1:T(4,128)(2,1)}, u32[]{:S(2)}, u32[]{:S(2)}) collective-permute-start(bf16[4,256,512]{2,0,1:T(4,128)(2,1)} %bitcast.16), channel_id=1, source_target_pairs={{0,128},{128,0},{1,129},{129,1},{2,130},{130,2},{3,131},{131,3},{4... | collective-permute-start | bytes 3145736 | tf_op jit(solution)/shard_map/ppermute | solution.py:91
  102.9 1.1 copy-start.2
  104.1 25.9 %collective-permute-start.1 = (bf16[1,3,384]{2,1,0:T(4,128)(2,1)S(1)}, bf16[1,3,384]{2,1,0:T(4,128)(2,1)S(1)}, u32[]{:S(2)}, u32[]{:S(2)}) collective-permute-start(bf16[1,3,384]{2,1,0:T(4,128)(2,1)S(1)} %slice.64), channel_id=1, source_target_pairs={{1,0},{2,1},{3,2},{4,3},{5,4},{6,5},{7,6},{8,7},{9,8},{10,9},{11,1... | collective-permute-start | bytes 6920 | tf_op jit(solution)/shard_map/ppermute | solution.py:38
  118.3 11.7 %copy-start.3 = (bf16[1,2048,384]{2,1,0:T(8,128)(2,1)S(1)}, bf16[1,2048,384]{2,1,0:T(8,128)(2,1)}, u32[]{:S(2)}) copy-start(bf16[1,2048,384]{2,1,0:T(8,128)(2,1)} %copy-done.2) | copy-start | bytes 4718596
  121.6 8.5 %copy-start.4 = (bf16[1,2048,384]{2,1,0:T(8,128)(2,1)S(1)}, bf16[1,2048,384]{2,1,0:T(8,128)(2,1)}, u32[]{:S(2)}) copy-start(bf16[1,2048,384]{2,1,0:T(8,128)(2,1)} %param.9) | copy-start | bytes 4718596
  121.6 41.1 %collective-permute-start.3 = (bf16[4,256,512]{1,0,2:T(4,128)(2,1)S(1)}, bf16[4,256,512]{1,0,2:T(4,128)(2,1)S(1)}, u32[]{:S(2)}, u32[]{:S(2)}) collective-permute-start(bf16[4,256,512]{1,0,2:T(4,128)(2,1)S(1)} %bitcast.79), channel_id=1, source_target_pairs={{0,128},{128,0},{1,129},{129,1},{2,130},{130,2},{3,131},{131,3},{4... | collective-permute-start | bytes 3145736 | tf_op jit(solution)/shard_map/ppermute | solution.py:90
  133.7 6.7 %copy-start.1 = (f32[4,64,4,512]{3,0,2,1:T(4,128)S(1)}, f32[4,64,4,512]{3,0,2,1:T(4,128)}, u32[]{:S(2)}) copy-start(f32[4,64,4,512]{3,0,2,1:T(4,128)} %copy.34) | copy-start | bytes 6291460

commit v8 on v5

--- a/solution.py
+++ b/solution.py
@@ -58,14 +58,14 @@
     hidden_blocks = hidden.reshape(seq_count, blocks, block_order, channels)
     first_split = first_factor.reshape(blocks, peers, col_blocks, block_order)
     mixed_chunks = jnp.einsum(
-        "ipqj,sijd->psiqd", first_split, hidden_blocks, preferred_element_type=jnp.float32
+        "ipqj,sijd->psqid", first_split, hidden_blocks, preferred_element_type=jnp.float32
     ).astype(jnp.bfloat16)
     upstream = grad_output.reshape(seq_count, col_blocks, block_count, channels)
     grad_chunks = grad_payload(second_factor, upstream).reshape(
         peers, seq_count, blocks, col_blocks, channels
     )
     grad_rows = lax.all_to_all(grad_chunks, "seq", split_axis=0, concat_axis=0, tiled=True)
-    columns = lax.all_to_all(mixed_chunks, "seq", split_axis=0, concat_axis=0, tiled=True)
+    columns = lax.all_to_all(mixed_chunks, "seq", split_axis=0, concat_axis=3, tiled=True)[0]
     halves = lax.axis_size("batch")
     me = lax.axis_index("batch")
     other = halves - 1 - me
@@ -75,8 +75,8 @@
     def second_part(half):
         up = lax.dynamic_slice_in_dim(upstream, half * rows_half, rows_half, 2)
         return jnp.einsum(
-            "skmd,psikd->kmpi", up, columns, preferred_element_type=jnp.float32
-        ).reshape(col_blocks, rows_half, peers * blocks).astype(jnp.bfloat16)
+            "skmd,skid->kmi", up, columns, preferred_element_type=jnp.float32
+        ).astype(jnp.bfloat16)
 
     def first_part(half):
         gr = lax.dynamic_slice_in_dim(grad_rows, half * peers_half, peers_half, 0)

time: 166 us -> 166 us (level)
  waiting for transfers between devices: 57.9 us -> 62.2 us
  local copies, waits for them, and re-layouts: 27.5 us -> 23.6 us
    ppermute x1, waiting for transfers between devices: 4.14 us -> 8.63 us  [body(): sent_first = lax.ppermute(first_part(other), 'batch', swap)]
    convert_element_type x3 -> x1, local copies, waits for them, and re-layouts: 6.08 us -> 3.94 us  [body(): mixed_chunks = jnp.einsum('ipqj,sijd->psqid', first_split, hidden_blocks,...]
    unnamed x16 -> x15, local copies, waits for them, and re-layouts: 4.07 us -> 2.33 us
  transfers between devices with their start and end apart: 6 -> 6, of which waited for: 4 -> 4; matrix products, arithmetic and copies ran while one was open for 27% -> 25% of each run, Pallas kernels for 0% -> 0%
where the time goes in v8:
time: 166 us
  waiting for transfers between devices  62.2 us (37%)
  starting transfers between devices  49.3 us (30%)
  local copies, waits for them, and re-layouts  23.6 us (14%)
  matrix products  13.8 us (8%)
  other arithmetic  11.5 us (7%)
  Pallas kernels  4.47 us (3%)
    all_to_all x1, waiting for transfers between devices, body(): lax.all_to_all(grad_chunks, 'seq', split_axis=0, concat_axis=0, tiled=True)  23.5 us
    ppermute x1, waiting for transfers between devices, body(): sent_second = lax.ppermute(second_part(other), 'batch', swap)  19.3 us
    all_to_all x1, starting transfers between devices, body(): lax.all_to_all(grad_chunks, 'seq', split_axis=0, concat_axis=0, tiled=True)  16.5 us
    all_to_all x1, starting transfers between devices, body(): lax.all_to_all(mixed_chunks, 'seq', split_axis=0, concat_axis=3, tiled=True)  14.8 us
    all_to_all x1, waiting for transfers between devices, body(): lax.all_to_all(mixed_chunks, 'seq', split_axis=0, concat_axis=3, tiled=True)  10.8 us
    ppermute x1, waiting for transfers between devices, body(): sent_first = lax.ppermute(first_part(other), 'batch', swap)  8.63 us
    ppermute x1, starting transfers between devices, body(): sent_second = lax.ppermute(second_part(other), 'batch', swap)  8.32 us
    ppermute x2, starting transfers between devices, passed_along(): lax.ppermute(value, axis, [(source, source + steps) for source in range(i...  6.98 us
  transfers between devices with their start and end apart: 6, of which 4 were waited for; matrix products, arithmetic and copies ran while one was open for 25% of the time, Pallas kernels for 0%

profile of v8, /device:TPU:1, one launch (start us, length us, event | category | flops | bytes accessed | tf_op | source)
XLA Modules:
  0.0 165.7 jit_solution(7517473220189677024)
XLA Ops:
  0.6 4.5 %shard_map.76 = bf16[512,1536]{1,0:T(8,128)(2,1)} custom-call(bf16[4,512,512]{2,1,0:T(8,128)(2,1)} %s_ref.1, bf16[4,512,384]{2,1,0:T(8,128)(2,1)} %bitcast.59), custom_call_target="tpu_custom_call" | custom-call | flops 805306368 | bytes 5242880 | tf_op jit(solution)/shard_map/pallas_call | solution.py:22
  5.1 3.9 %reshape.126 = bf16[128,1,4,4,384]{4,3,2,0,1:T(4,128)(2,1)} reshape(bf16[512,1536]{1,0:T(8,128)(2,1)} %shard_map.76) | data formatting | bytes 3145728 | tf_op jit(solution)/shard_map/reshape | solution.py:64
  9.1 16.5 %all-to-all-start = ((bf16[128,1,4,4,384]{4,3,2,1,0:T(4,128)(2,1)}), bf16[128,1,4,4,384]{4,3,2,1,0:T(4,128)(2,1)S(1)}, u32[]{:S(2)}, u32[]{:S(2)}) async-start(bf16[128,1,4,4,384]{4,3,2,1,0:T(4,128)(2,1)} %bitcast.1), calls=%async_computation | async-start | bytes 3145728 | tf_op jit(solution)/shard_map/all_to_all | solution.py:67
  25.6 3.5 %collective-permute-start = (bf16[1,3,384]{2,1,0:T(4,128)(2,1)S(1)}, bf16[1,3,384]{2,1,0:T(4,128)(2,1)S(1)}, u32[]{:S(2)}, u32[]{:S(2)}) collective-permute-start(bf16[1,3,384]{2,1,0:T(4,128)(2,1)S(1)} %slice.47), channel_id=1, source_target_pairs={{0,1},{1,2},{2,3},{3,4},{4,5},{5,6},{6,7},{7,8},{8,9},{9,10},{10,1... | collective-permute-start | bytes 6920 | tf_op jit(solution)/shard_map/ppermute | solution.py:36
  29.2 4.0 %reshape.128 = bf16[4,128,4,512]{3,2,1,0:T(4,128)(2,1)} reshape(bf16[4,512,512]{2,1,0:T(8,128)(2,1)} %param.7) | data formatting | bytes 4194304 | tf_op jit(solution)/shard_map/reshape | solution.py:59
  33.6 3.1 %multiply_convert_fusion = (bf16[1,2048,384]{2,1,0:T(8,128)(2,1)S(1)}, f32[1,2048,384]{2,1,0:T(8,128)}) fusion(f32[1,2051,384]{2,1,0:T(8,128)S(1)} %maximum_convert_fusion, f32[384]{0:T(512)S(1)} %get-tuple-element.11, f32[384]{0:T(512)S(1)} %get-tuple-element.12, f32[384]{0:T(512)S(1)} %get-tuple-element.10, f32[384]{0:T(512)S(1)} %get-tuple-element.9), kind=kLoop, calls=%fused_computation.18 | loop fusion | flops 9437184 | bytes 17307648 | tf_op jit(solution)/shard_map/convert_element_type | solution.py:57
  36.7 2.5 %fusion.18 = bf16[128,1,4,4,384]{0,4,2,3,1:T(8,128)(2,1)} fusion(bf16[4,512,384,1]{2,1,3,0:T(8,128)(2,1)S(1)} %bitcast.56, bf16[4,128,4,512]{3,2,1,0:T(4,128)(2,1)S(1)} %copy-done), kind=kOutput, calls=%fused_computation.36 | convolution fusion | flops 806092800 | bytes 5242880 | tf_op jit(solution)/shard_map/ipqj,sijd->psqid/dot_general | solution.py:60
  39.2 3.9 %copy.35 = bf16[128,1,4,4,384]{4,2,3,1,0:T(4,128)(2,1)} copy(bf16[128,1,4,4,384]{0,4,2,3,1:T(8,128)(2,1)} %fusion.18) | data formatting | bytes 3145728 | tf_op jit(solution)/shard_map/convert_element_type | solution.py:62
  43.1 23.5 %all-to-all-done = bf16[128,1,4,4,384]{4,3,2,1,0:T(4,128)(2,1)S(1)} async-done(((bf16[128,1,4,4,384]{4,3,2,1,0:T(4,128)(2,1)}), bf16[128,1,4,4,384]{4,3,2,1,0:T(4,128)(2,1)S(1)}, u32[]{:S(2)}, u32[]{:S(2)}) %all-to-all-start) | async-done | bytes 1572896 | tf_op jit(solution)/shard_map/all_to_all | solution.py:67
  66.6 14.8 %all-to-all-start.1 = ((bf16[128,1,4,4,384]{4,2,3,1,0:T(4,128)(2,1)}), bf16[128,1,4,4,384]{4,2,3,1,0:T(4,128)(2,1)}, u32[]{:S(2)}, u32[]{:S(2)}) async-start(bf16[128,1,4,4,384]{4,2,3,1,0:T(4,128)(2,1)} %copy.35), calls=%async_computation.1 | async-start | bytes 3145728 | tf_op jit(solution)/shard_map/all_to_all | solution.py:68
  82.7 2.7 %copy.30 = f32[4,64,4,512]{3,0,2,1:T(4,128)} copy(f32[4,64,4,512]{3,1,2,0:T(8,128)S(1)} %fusion.17) | data formatting | bytes 4194304 | tf_op jit(solution)/shard_map/convert_element_type | solution.py:97
  88.0 2.7 %collective-permute-start.2 = (bf16[4,256,512]{2,0,1:T(4,128)(2,1)}, bf16[4,256,512]{2,0,1:T(4,128)(2,1)}, u32[]{:S(2)}, u32[]{:S(2)}) collective-permute-start(bf16[4,256,512]{2,0,1:T(4,128)(2,1)} %bitcast.16), channel_id=1, source_target_pairs={{0,128},{128,0},{1,129},{129,1},{2,130},{130,2},{3,131},{131,3},{4... | collective-permute-start | bytes 3145736 | tf_op jit(solution)/shard_map/ppermute | solution.py:89
  92.6 4.3 %convolution_bitcast_fusion = f32[1,4,512,384]{2,3,1,0:T(8,128)} fusion(bf16[4,128,4,512]{3,2,1,0:T(4,128)(2,1)} %reshape.128, bf16[128,1,4,4,384]{0,4,3,2,1:T(8,128)(2,1)S(1)} %copy.26), kind=kOutput, calls=%fused_computation.23 | convolution fusion | flops 805306368 | bytes 6815744 | tf_op jit(solution)/shard_map/ipqj,psiqd->sijd/dot_general | solution.py:90
  96.9 2.4 %copy.28 = f32[1,4,512,384]{3,2,1,0:T(8,128)S(1)} copy(f32[1,4,512,384]{2,3,1,0:T(8,128)} %convolution_bitcast_fusion) | data formatting | bytes 6291456 | tf_op jit(solution)/shard_map/ipqj,psiqd->sijd/transpose | solution.py:90
  99.3 3.4 %fusion.8 = bf16[1,2048,384]{2,1,0:T(8,128)(2,1)S(1)} fusion(f32[1,4,512,384]{3,2,1,0:T(8,128)S(1)} %copy.28, f32[1,2048,384]{2,1,0:T(8,128)} %get-tuple-element.14), kind=kLoop, calls=%fused_computation.17 | loop fusion | flops 7077888 | bytes 7864320 | tf_op jit(solution)/shard_map/convert_element_type | solution.py:99
  103.8 3.4 %collective-permute-start.1 = (bf16[1,3,384]{2,1,0:T(4,128)(2,1)S(1)}, bf16[1,3,384]{2,1,0:T(4,128)(2,1)S(1)}, u32[]{:S(2)}, u32[]{:S(2)}) collective-permute-start(bf16[1,3,384]{2,1,0:T(4,128)(2,1)S(1)} %slice.64), channel_id=1, source_target_pairs={{1,0},{2,1},{3,2},{4,3},{5,4},{6,5},{7,6},{8,7},{9,8},{10,9},{11,1... | collective-permute-start | bytes 6920 | tf_op jit(solution)/shard_map/ppermute | solution.py:36
  107.3 10.8 %all-to-all-done.1 = bf16[128,1,4,4,384]{4,2,3,1,0:T(4,128)(2,1)} async-done(((bf16[128,1,4,4,384]{4,2,3,1,0:T(4,128)(2,1)}), bf16[128,1,4,4,384]{4,2,3,1,0:T(4,128)(2,1)}, u32[]{:S(2)}, u32[]{:S(2)}) %all-to-all-start.1) | async-done | bytes 1572896 | tf_op jit(solution)/shard_map/all_to_all | solution.py:68
  118.1 2.4 %convolution_convert_fusion = bf16[4,256,512]{2,1,0:T(8,128)(2,1)S(1)} fusion(bf16[4,512,384]{2,0,1:T(4,128)(2,1)} %bitcast.24, bf16[1,4,512,384]{3,2,1,0:T(8,128)(2,1)} %bitcast.60, s32[]{:T(128)S(6)} %select_n.15), kind=kOutput, calls=%fused_computation.31 | convolution fusion | flops 403177472 | bytes 3407876 | tf_op jit(solution)/shard_map/skmd,skid->kmi/dot_general | solution.py:77
  120.5 8.3 %collective-permute-start.3 = (bf16[4,256,512]{2,1,0:T(8,128)(2,1)S(1)}, bf16[4,256,512]{2,1,0:T(8,128)(2,1)S(1)}, u32[]{:S(2)}, u32[]{:S(2)}) collective-permute-start(bf16[4,256,512]{2,1,0:T(8,128)(2,1)S(1)} %convolution_convert_fusion), channel_id=1, source_target_pairs={{0,128},{128,0},{1,129},{129,1},{2,130},{130,2},{3,131},{131,3},{4... | collective-permute-start | bytes 3145736 | tf_op jit(solution)/shard_map/ppermute | solution.py:88
  129.0 2.5 %fusion.1 = bf16[1,2048,384]{2,1,0:T(8,128)(2,1)} fusion(f32[1,2051,384]{2,1,0:T(8,128)S(1)} %maximum_convert_fusion.1, f32[384]{0:T(512)S(1)} %get-tuple-element.11, f32[384]{0:T(512)S(1)} %get-tuple-element.12, f32[384]{0:T(512)S(1)} %get-tuple-element.10, f32[384]{0:T(512)S(1)} %get-tuple-element.9), kind=kLoop, calls=%fused_computation.2 | loop fusion | flops 6291456 | bytes 14161920 | tf_op jit(solution)/shard_map/convert_element_type | solution.py:104
  131.6 8.6 %collective-permute-done.2 = bf16[4,256,512]{2,0,1:T(4,128)(2,1)} collective-permute-done((bf16[4,256,512]{2,0,1:T(4,128)(2,1)}, bf16[4,256,512]{2,0,1:T(4,128)(2,1)}, u32[]{:S(2)}, u32[]{:S(2)}) %collective-permute-start.2) | collective-permute-done | bytes 1048608 | tf_op jit(solution)/shard_map/ppermute | solution.py:89
  140.2 1.9 %fusion.9 = bf16[4,256,512]{2,0,1:T(4,128)(2,1)S(1)} fusion(f32[4,64,4,512]{3,0,2,1:T(4,128)S(1)} %copy-done.1, bf16[4,256,512]{2,0,1:T(4,128)(2,1)} %collective-permute-done.2), kind=kLoop, calls=%fused_computation.21 | loop fusion | flops 1572864 | bytes 4194304 | tf_op jit(solution)/shard_map/convert_element_type | solution.py:98
  143.3 19.3 %collective-permute-done.3 = bf16[4,256,512]{2,1,0:T(8,128)(2,1)S(1)} collective-permute-done((bf16[4,256,512]{2,1,0:T(8,128)(2,1)S(1)}, bf16[4,256,512]{2,1,0:T(8,128)(2,1)S(1)}, u32[]{:S(2)}, u32[]{:S(2)}) %collective-permute-start.3) | collective-permute-done | bytes 1048608 | tf_op jit(solution)/shard_map/ppermute | solution.py:88
  162.6 3.1 %add_convert_fusion = bf16[4,256,512]{2,1,0:T(8,128)(2,1)} fusion(bf16[4,256,512]{2,1,0:T(8,128)(2,1)S(1)} %collective-permute-done.3, bf16[4,512,384]{2,0,1:T(4,128)(2,1)} %bitcast.24, bf16[1,4,512,384]{3,2,1,0:T(8,128)(2,1)S(1)} %bitcast.61, s32[]{:T(128)S(6)} %select_n.14), kind=kOutput, calls=%fused_computation.22 | convolution fusion | flops 405274624 | bytes 4456452 | tf_op jit(solution)/shard_map/skmd,skid->kmi/dot_general | solution.py:77
  (27 shorter events, 8.6 us)
Async XLA Ops:
  9.0 16.5 %copy-start.4 = (bf16[1,2048,384]{2,1,0:T(8,128)(2,1)S(1)}, bf16[1,2048,384]{2,1,0:T(8,128)(2,1)}, u32[]{:S(2)}) copy-start(bf16[1,2048,384]{2,1,0:T(8,128)(2,1)} %param.5) | copy-start | bytes 4718596
  9.0 20.1 %copy-start.6 = (f32[4,384]{1,0:T(4,128)S(1)}, f32[4,384]{1,0:T(4,128)}, u32[]{:S(2)}) copy-start(f32[4,384]{1,0:T(4,128)} %param.6) | copy-start | bytes 18436
  9.1 57.6 %all-to-all-start = ((bf16[128,1,4,4,384]{4,3,2,1,0:T(4,128)(2,1)}), bf16[128,1,4,4,384]{4,3,2,1,0:T(4,128)(2,1)S(1)}, u32[]{:S(2)}, u32[]{:S(2)}) async-start(bf16[128,1,4,4,384]{4,3,2,1,0:T(4,128)(2,1)} %bitcast.1), calls=%async_computation | async-start | bytes 3145728 | tf_op jit(solution)/shard_map/all_to_all | solution.py:67
  25.6 7.6 %collective-permute-start = (bf16[1,3,384]{2,1,0:T(4,128)(2,1)S(1)}, bf16[1,3,384]{2,1,0:T(4,128)(2,1)S(1)}, u32[]{:S(2)}, u32[]{:S(2)}) collective-permute-start(bf16[1,3,384]{2,1,0:T(4,128)(2,1)S(1)} %slice.47), channel_id=1, source_target_pairs={{0,1},{1,2},{2,3},{3,4},{4,5},{5,6},{6,7},{7,8},{8,9},{9,10},{10,1... | collective-permute-start | bytes 6920 | tf_op jit(solution)/shard_map/ppermute | solution.py:36
  33.6 3.1 %copy-start = (bf16[4,128,4,512]{3,2,1,0:T(4,128)(2,1)S(1)}, bf16[4,128,4,512]{3,2,1,0:T(4,128)(2,1)}, u32[]{:S(2)}) copy-start(bf16[4,128,4,512]{3,2,1,0:T(4,128)(2,1)} %reshape.128) | copy-start | bytes 6291460
  66.6 51.4 %all-to-all-start.1 = ((bf16[128,1,4,4,384]{4,2,3,1,0:T(4,128)(2,1)}), bf16[128,1,4,4,384]{4,2,3,1,0:T(4,128)(2,1)}, u32[]{:S(2)}, u32[]{:S(2)}) async-start(bf16[128,1,4,4,384]{4,2,3,1,0:T(4,128)(2,1)} %copy.35), calls=%async_computation.1 | async-start | bytes 3145728 | tf_op jit(solution)/shard_map/all_to_all | solution.py:68
  88.0 52.2 %collective-permute-start.2 = (bf16[4,256,512]{2,0,1:T(4,128)(2,1)}, bf16[4,256,512]{2,0,1:T(4,128)(2,1)}, u32[]{:S(2)}, u32[]{:S(2)}) collective-permute-start(bf16[4,256,512]{2,0,1:T(4,128)(2,1)} %bitcast.16), channel_id=1, source_target_pairs={{0,128},{128,0},{1,129},{129,1},{2,130},{130,2},{3,131},{131,3},{4... | collective-permute-start | bytes 3145736 | tf_op jit(solution)/shard_map/ppermute | solution.py:89
  102.7 1.1 copy-start.2
  103.8 25.0 %copy-start.3 = (bf16[1,2048,384]{2,1,0:T(8,128)(2,1)S(1)}, bf16[1,2048,384]{2,1,0:T(8,128)(2,1)}, u32[]{:S(2)}) copy-start(bf16[1,2048,384]{2,1,0:T(8,128)(2,1)} %copy-done.2) | copy-start | bytes 4718596
  103.8 25.0 %collective-permute-start.1 = (bf16[1,3,384]{2,1,0:T(4,128)(2,1)S(1)}, bf16[1,3,384]{2,1,0:T(4,128)(2,1)S(1)}, u32[]{:S(2)}, u32[]{:S(2)}) collective-permute-start(bf16[1,3,384]{2,1,0:T(4,128)(2,1)S(1)} %slice.64), channel_id=1, source_target_pairs={{1,0},{2,1},{3,2},{4,3},{5,4},{6,5},{7,6},{8,7},{9,8},{10,9},{11,1... | collective-permute-start | bytes 6920 | tf_op jit(solution)/shard_map/ppermute | solution.py:36
  120.5 42.1 %collective-permute-start.3 = (bf16[4,256,512]{2,1,0:T(8,128)(2,1)S(1)}, bf16[4,256,512]{2,1,0:T(8,128)(2,1)S(1)}, u32[]{:S(2)}, u32[]{:S(2)}) collective-permute-start(bf16[4,256,512]{2,1,0:T(8,128)(2,1)S(1)} %convolution_convert_fusion), channel_id=1, source_target_pairs={{0,128},{128,0},{1,129},{129,1},{2,130},{130,2},{3,131},{131,3},{4... | collective-permute-start | bytes 3145736 | tf_op jit(solution)/shard_map/ppermute | solution.py:88
  129.0 11.2 %copy-start.1 = (f32[4,64,4,512]{3,0,2,1:T(4,128)S(1)}, f32[4,64,4,512]{3,0,2,1:T(4,128)}, u32[]{:S(2)}) copy-start(f32[4,64,4,512]{3,0,2,1:T(4,128)} %copy.30) | copy-start | bytes 6291460
  142.1 20.5 %copy-start.5 = (bf16[1,2048,384]{2,1,0:T(8,128)(2,1)S(1)}, bf16[1,2048,384]{2,1,0:T(8,128)(2,1)}, u32[]{:S(2)}) copy-start(bf16[1,2048,384]{2,1,0:T(8,128)(2,1)} %param.9) | copy-start | bytes 4718596

commit v9 on v5

--- a/solution.py
+++ b/solution.py
@@ -90,12 +90,9 @@
     grad_hidden = jnp.einsum(
         "ipqj,psiqd->sijd", first_split, grad_rows, preferred_element_type=jnp.float32
     ).reshape(seq_count, tok_rows, channels)
-    part_second = (
-        second_part(me).astype(jnp.float32) + sent_second.astype(jnp.float32)
-    ).astype(jnp.bfloat16)
-    part_first = (
-        first_part(me).astype(jnp.float32) + sent_first.astype(jnp.float32)
-    ).astype(jnp.bfloat16)
+    kept = lambda part: lax.reduce_precision(part.astype(jnp.float32), exponent_bits=8, mantissa_bits=7)
+    part_second = (kept(second_part(me)) + sent_second.astype(jnp.float32)).astype(jnp.bfloat16)
+    part_first = (kept(first_part(me)) + sent_first.astype(jnp.float32)).astype(jnp.bfloat16)
     grad_conv = (grad_hidden * gate_val * (1.0 + conv_out * (1.0 - gate_val))).astype(jnp.bfloat16)
     following = passed_along(grad_conv[:, : tap_count - 1, :], "seq", -1)
     extended = jnp.concatenate([grad_conv, following], axis=1).astype(jnp.float32)

time: 166 us -> 166 us (level)
    convert_element_type x2 -> x0, local copies, waits for them, and re-layouts: 4.06 us -> none  [the longest x1 2.71 us: body(): first_part(me).astype(jnp.float32) + sent_first.astype(jnp.float32)]
    reduce_precision x0 -> x2, local copies, waits for them, and re-layouts: none -> 4.06 us  [body(): lax.reduce_precision(part.astype(jnp.float32), exponent_bits=8, mantissa_...]
where the time goes in v9:
time: 166 us; the launch traced here: 165 us
  waiting for transfers between devices  57.9 us (35%)
  starting transfers between devices  49.2 us (30%)
  local copies, waits for them, and re-layouts  27.5 us (17%)
  matrix products  13 us (8%)
  other arithmetic  12.2 us (7%)
  Pallas kernels  4.47 us (3%)
    all_to_all x1, waiting for transfers between devices, body(): lax.all_to_all(grad_chunks, 'seq', split_axis=0, concat_axis=0, tiled=True)  23.5 us
    ppermute x1, waiting for transfers between devices, body(): sent_second = lax.ppermute(second_part(other), 'batch', swap)  19.3 us
    all_to_all x1, starting transfers between devices, body(): lax.all_to_all(grad_chunks, 'seq', split_axis=0, concat_axis=0, tiled=True)  16.5 us
    all_to_all x1, starting transfers between devices, body(): lax.all_to_all(mixed_chunks, 'seq', split_axis=0, concat_axis=0, tiled=True)  14.8 us
    all_to_all x1, waiting for transfers between devices, body(): lax.all_to_all(mixed_chunks, 'seq', split_axis=0, concat_axis=0, tiled=True)  10.9 us
    ppermute x1, starting transfers between devices, body(): sent_second = lax.ppermute(second_part(other), 'batch', swap)  8.32 us
    ppermute x2, starting transfers between devices, passed_along(): lax.ppermute(value, axis, [(source, source + steps) for source in range(i...  6.84 us
    dot_general x2, matrix products, second_part(): jnp.einsum('skmd,psikd->kmpi', up, columns, preferred_element_type=jnp.fl...  4.68 us
  transfers between devices with their start and end apart: 6, of which 4 were waited for; matrix products, arithmetic and copies ran while one was open for 27% of the time, Pallas kernels for 0%

profile of v9, /device:TPU:1, one launch (start us, length us, event | category | flops | bytes accessed | tf_op | source)
XLA Modules:
  0.0 165.0 jit_solution(11004309431134693832)
XLA Ops:
  0.6 4.5 %shard_map.76 = bf16[512,1536]{1,0:T(8,128)(2,1)} custom-call(bf16[4,512,512]{2,1,0:T(8,128)(2,1)} %s_ref.1, bf16[4,512,384]{2,1,0:T(8,128)(2,1)} %bitcast.76), custom_call_target="tpu_custom_call" | custom-call | flops 805306368 | bytes 5242880 | tf_op jit(solution)/shard_map/pallas_call | solution.py:22
  5.1 3.9 %reshape.129 = bf16[128,1,4,4,384]{4,3,2,0,1:T(4,128)(2,1)} reshape(bf16[512,1536]{1,0:T(8,128)(2,1)} %shard_map.76) | data formatting | bytes 3145728 | tf_op jit(solution)/shard_map/reshape | solution.py:64
  9.0 16.5 %all-to-all-start = ((bf16[128,1,4,4,384]{4,3,2,1,0:T(4,128)(2,1)}), bf16[128,1,4,4,384]{4,3,2,1,0:T(4,128)(2,1)S(1)}, u32[]{:S(2)}, u32[]{:S(2)}) async-start(bf16[128,1,4,4,384]{4,3,2,1,0:T(4,128)(2,1)} %bitcast.1), calls=%async_computation | async-start | bytes 3145728 | tf_op jit(solution)/shard_map/all_to_all | solution.py:67
  25.6 3.5 %collective-permute-start = (bf16[1,3,384]{2,1,0:T(4,128)(2,1)S(1)}, bf16[1,3,384]{2,1,0:T(4,128)(2,1)S(1)}, u32[]{:S(2)}, u32[]{:S(2)}) collective-permute-start(bf16[1,3,384]{2,1,0:T(4,128)(2,1)S(1)} %slice.47), channel_id=1, source_target_pairs={{0,1},{1,2},{2,3},{3,4},{4,5},{5,6},{6,7},{7,8},{8,9},{9,10},{10,1... | collective-permute-start | bytes 6920 | tf_op jit(solution)/shard_map/ppermute | solution.py:36
  29.2 4.0 %reshape.131 = bf16[4,128,4,512]{3,2,1,0:T(4,128)(2,1)} reshape(bf16[4,512,512]{2,1,0:T(8,128)(2,1)} %param.7) | data formatting | bytes 4194304 | tf_op jit(solution)/shard_map/reshape | solution.py:59
  33.6 3.1 %multiply_convert_fusion = (bf16[1,2048,384]{2,1,0:T(8,128)(2,1)S(1)}, f32[1,2048,384]{2,1,0:T(8,128)}) fusion(f32[1,2051,384]{2,1,0:T(8,128)S(1)} %maximum_convert_fusion, f32[384]{0:T(512)S(1)} %get-tuple-element.11, f32[384]{0:T(512)S(1)} %get-tuple-element.12, f32[384]{0:T(512)S(1)} %get-tuple-element.10, f32[384]{0:T(512)S(1)} %get-tuple-element.9), kind=kLoop, calls=%fused_computation.18 | loop fusion | flops 9437184 | bytes 17307648 | tf_op jit(solution)/shard_map/convert_element_type | solution.py:57
  36.7 2.5 %fusion.30 = bf16[128,1,4,4,384]{0,4,3,2,1:T(8,128)(2,1)} fusion(bf16[4,512,384,1]{2,1,3,0:T(8,128)(2,1)S(1)} %bitcast.73, bf16[4,128,4,512]{3,2,1,0:T(4,128)(2,1)S(1)} %copy-done), kind=kOutput, calls=%fused_computation.42 | convolution fusion | flops 806092800 | bytes 5242880 | tf_op jit(solution)/shard_map/ipqj,sijd->psiqd/dot_general | solution.py:60
  39.2 3.9 %copy.39 = bf16[128,1,4,4,384]{4,3,2,1,0:T(4,128)(2,1)} copy(bf16[128,1,4,4,384]{0,4,3,2,1:T(8,128)(2,1)} %fusion.30) | data formatting | bytes 3145728 | tf_op jit(solution)/shard_map/convert_element_type | solution.py:62
  43.1 23.5 %all-to-all-done = bf16[128,1,4,4,384]{4,3,2,1,0:T(4,128)(2,1)S(1)} async-done(((bf16[128,1,4,4,384]{4,3,2,1,0:T(4,128)(2,1)}), bf16[128,1,4,4,384]{4,3,2,1,0:T(4,128)(2,1)S(1)}, u32[]{:S(2)}, u32[]{:S(2)}) %all-to-all-start) | async-done | bytes 1572896 | tf_op jit(solution)/shard_map/all_to_all | solution.py:67
  66.6 14.8 %all-to-all-start.1 = ((bf16[128,1,4,4,384]{4,3,2,1,0:T(4,128)(2,1)}), bf16[128,1,4,4,384]{4,3,2,1,0:T(4,128)(2,1)}, u32[]{:S(2)}, u32[]{:S(2)}) async-start(bf16[128,1,4,4,384]{4,3,2,1,0:T(4,128)(2,1)} %copy.39), calls=%async_computation.1 | async-start | bytes 3145728 | tf_op jit(solution)/shard_map/all_to_all | solution.py:68
  82.7 2.7 %copy.34 = f32[4,64,4,512]{3,0,2,1:T(4,128)} copy(f32[4,64,4,512]{3,1,2,0:T(8,128)S(1)} %convert_reduce-precision_fusion.1) | data formatting | bytes 4194304 | tf_op jit(solution)/shard_map/reduce_precision | solution.py:93
  87.9 2.7 %collective-permute-start.2 = (bf16[4,256,512]{2,0,1:T(4,128)(2,1)}, bf16[4,256,512]{2,0,1:T(4,128)(2,1)}, u32[]{:S(2)}, u32[]{:S(2)}) collective-permute-start(bf16[4,256,512]{2,0,1:T(4,128)(2,1)} %bitcast.16), channel_id=1, source_target_pairs={{0,128},{128,0},{1,129},{129,1},{2,130},{130,2},{3,131},{131,3},{4... | collective-permute-start | bytes 3145736 | tf_op jit(solution)/shard_map/ppermute | solution.py:89
  92.5 4.3 %convolution_bitcast_fusion = f32[1,4,512,384]{2,3,1,0:T(8,128)} fusion(bf16[4,128,4,512]{3,2,1,0:T(4,128)(2,1)} %reshape.131, bf16[128,1,4,4,384]{0,4,3,2,1:T(8,128)(2,1)S(1)} %copy.30), kind=kOutput, calls=%fused_computation.26 | convolution fusion | flops 805306368 | bytes 6815744 | tf_op jit(solution)/shard_map/ipqj,psiqd->sijd/dot_general | solution.py:90
  96.9 2.4 %copy.32 = f32[1,4,512,384]{3,2,1,0:T(8,128)S(1)} copy(f32[1,4,512,384]{2,3,1,0:T(8,128)} %convolution_bitcast_fusion) | data formatting | bytes 6291456 | tf_op jit(solution)/shard_map/ipqj,psiqd->sijd/transpose | solution.py:90
  99.3 3.4 %fusion.8 = bf16[1,2048,384]{2,1,0:T(8,128)(2,1)S(1)} fusion(f32[1,4,512,384]{3,2,1,0:T(8,128)S(1)} %copy.32, f32[1,2048,384]{2,1,0:T(8,128)} %get-tuple-element.14), kind=kLoop, calls=%fused_computation.17 | loop fusion | flops 7077888 | bytes 7864320 | tf_op jit(solution)/shard_map/convert_element_type | solution.py:96
  103.8 3.3 %collective-permute-start.1 = (bf16[1,3,384]{2,1,0:T(4,128)(2,1)S(1)}, bf16[1,3,384]{2,1,0:T(4,128)(2,1)S(1)}, u32[]{:S(2)}, u32[]{:S(2)}) collective-permute-start(bf16[1,3,384]{2,1,0:T(4,128)(2,1)S(1)} %slice.64), channel_id=1, source_target_pairs={{1,0},{2,1},{3,2},{4,3},{5,4},{6,5},{7,6},{8,7},{9,8},{10,9},{11,1... | collective-permute-start | bytes 6920 | tf_op jit(solution)/shard_map/ppermute | solution.py:36
  107.1 10.9 %all-to-all-done.1 = bf16[128,1,4,4,384]{4,3,2,1,0:T(4,128)(2,1)} async-done(((bf16[128,1,4,4,384]{4,3,2,1,0:T(4,128)(2,1)}), bf16[128,1,4,4,384]{4,3,2,1,0:T(4,128)(2,1)}, u32[]{:S(2)}, u32[]{:S(2)}) %all-to-all-start.1) | async-done | bytes 1572896 | tf_op jit(solution)/shard_map/all_to_all | solution.py:68
  118.0 2.5 %fusion.25 = bf16[4,256,128,4]{1,2,3,0:T(8,128)(2,1)S(1)} fusion(bf16[128,1,4,4,384]{4,3,2,1,0:T(4,128)(2,1)} %all-to-all-done.1, bf16[1,4,512,384]{3,2,1,0:T(8,128)(2,1)} %bitcast.77, s32[]{:T(128)S(6)} %select_n.15), kind=kOutput, calls=%fused_computation.39 | convolution fusion | flops 403177472 | bytes 3407876 | tf_op jit(solution)/shard_map/skmd,psikd->kmpi/dot_general | solution.py:77
  121.4 8.3 %collective-permute-start.3 = (bf16[4,256,512]{1,0,2:T(4,128)(2,1)S(1)}, bf16[4,256,512]{1,0,2:T(4,128)(2,1)S(1)}, u32[]{:S(2)}, u32[]{:S(2)}) collective-permute-start(bf16[4,256,512]{1,0,2:T(4,128)(2,1)S(1)} %bitcast.79), channel_id=1, source_target_pairs={{0,128},{128,0},{1,129},{129,1},{2,130},{130,2},{3,131},{131,3},{4... | collective-permute-start | bytes 3145736 | tf_op jit(solution)/shard_map/ppermute | solution.py:88
  129.9 2.2 %convert_reduce-precision_fusion = f32[4,256,128,4]{1,2,3,0:T(8,128)S(1)} fusion(bf16[128,1,4,4,384]{4,3,2,1,0:T(4,128)(2,1)} %all-to-all-done.1, bf16[1,4,512,384]{3,2,1,0:T(8,128)(2,1)S(1)} %bitcast.78, s32[]{:T(128)S(6)} %select_n.14), kind=kOutput, calls=%fused_computation.24 | convolution fusion | flops 404226048 | bytes 4456452 | tf_op jit(solution)/shard_map/skmd,psikd->kmpi/dot_general | solution.py:77
  133.5 2.5 %fusion.1 = bf16[1,2048,384]{2,1,0:T(8,128)(2,1)} fusion(f32[1,2051,384]{2,1,0:T(8,128)S(1)} %maximum_convert_fusion.1, f32[384]{0:T(512)S(1)} %get-tuple-element.11, f32[384]{0:T(512)S(1)} %get-tuple-element.12, f32[384]{0:T(512)S(1)} %get-tuple-element.10, f32[384]{0:T(512)S(1)} %get-tuple-element.9), kind=kLoop, calls=%fused_computation.2 | loop fusion | flops 6291456 | bytes 14161920 | tf_op jit(solution)/shard_map/convert_element_type | solution.py:101
  136.0 4.1 %collective-permute-done.2 = bf16[4,256,512]{2,0,1:T(4,128)(2,1)} collective-permute-done((bf16[4,256,512]{2,0,1:T(4,128)(2,1)}, bf16[4,256,512]{2,0,1:T(4,128)(2,1)}, u32[]{:S(2)}, u32[]{:S(2)}) %collective-permute-start.2) | collective-permute-done | bytes 1048608 | tf_op jit(solution)/shard_map/ppermute | solution.py:89
  140.2 1.9 %fusion.10 = bf16[4,256,512]{2,0,1:T(4,128)(2,1)S(1)} fusion(f32[4,64,4,512]{3,0,2,1:T(4,128)S(1)} %copy-done.1, bf16[4,256,512]{2,0,1:T(4,128)(2,1)} %collective-permute-done.2), kind=kLoop, calls=%fused_computation.23 | loop fusion | flops 1572864 | bytes 4194304 | tf_op jit(solution)/shard_map/convert_element_type | solution.py:95
  143.2 19.3 %collective-permute-done.3 = bf16[4,256,512]{1,0,2:T(4,128)(2,1)S(1)} collective-permute-done((bf16[4,256,512]{1,0,2:T(4,128)(2,1)S(1)}, bf16[4,256,512]{1,0,2:T(4,128)(2,1)S(1)}, u32[]{:S(2)}, u32[]{:S(2)}) %collective-permute-start.3) | collective-permute-done | bytes 1048608 | tf_op jit(solution)/shard_map/ppermute | solution.py:88
  (31 shorter events, 13.2 us)
Async XLA Ops:
  9.0 16.5 %copy-start.5 = (bf16[1,2048,384]{2,1,0:T(8,128)(2,1)S(1)}, bf16[1,2048,384]{2,1,0:T(8,128)(2,1)}, u32[]{:S(2)}) copy-start(bf16[1,2048,384]{2,1,0:T(8,128)(2,1)} %param.5) | copy-start | bytes 4718596
  9.0 20.1 %copy-start.6 = (f32[4,384]{1,0:T(4,128)S(1)}, f32[4,384]{1,0:T(4,128)}, u32[]{:S(2)}) copy-start(f32[4,384]{1,0:T(4,128)} %param.6) | copy-start | bytes 18436
  9.0 57.6 %all-to-all-start = ((bf16[128,1,4,4,384]{4,3,2,1,0:T(4,128)(2,1)}), bf16[128,1,4,4,384]{4,3,2,1,0:T(4,128)(2,1)S(1)}, u32[]{:S(2)}, u32[]{:S(2)}) async-start(bf16[128,1,4,4,384]{4,3,2,1,0:T(4,128)(2,1)} %bitcast.1), calls=%async_computation | async-start | bytes 3145728 | tf_op jit(solution)/shard_map/all_to_all | solution.py:67
  25.6 7.6 %collective-permute-start = (bf16[1,3,384]{2,1,0:T(4,128)(2,1)S(1)}, bf16[1,3,384]{2,1,0:T(4,128)(2,1)S(1)}, u32[]{:S(2)}, u32[]{:S(2)}) collective-permute-start(bf16[1,3,384]{2,1,0:T(4,128)(2,1)S(1)} %slice.47), channel_id=1, source_target_pairs={{0,1},{1,2},{2,3},{3,4},{4,5},{5,6},{6,7},{7,8},{8,9},{9,10},{10,1... | collective-permute-start | bytes 6920 | tf_op jit(solution)/shard_map/ppermute | solution.py:36
  33.6 3.1 %copy-start = (bf16[4,128,4,512]{3,2,1,0:T(4,128)(2,1)S(1)}, bf16[4,128,4,512]{3,2,1,0:T(4,128)(2,1)}, u32[]{:S(2)}) copy-start(bf16[4,128,4,512]{3,2,1,0:T(4,128)(2,1)} %reshape.131) | copy-start | bytes 6291460
  66.6 51.4 %all-to-all-start.1 = ((bf16[128,1,4,4,384]{4,3,2,1,0:T(4,128)(2,1)}), bf16[128,1,4,4,384]{4,3,2,1,0:T(4,128)(2,1)}, u32[]{:S(2)}, u32[]{:S(2)}) async-start(bf16[128,1,4,4,384]{4,3,2,1,0:T(4,128)(2,1)} %copy.39), calls=%async_computation.1 | async-start | bytes 3145728 | tf_op jit(solution)/shard_map/all_to_all | solution.py:68
  87.9 52.2 %collective-permute-start.2 = (bf16[4,256,512]{2,0,1:T(4,128)(2,1)}, bf16[4,256,512]{2,0,1:T(4,128)(2,1)}, u32[]{:S(2)}, u32[]{:S(2)}) collective-permute-start(bf16[4,256,512]{2,0,1:T(4,128)(2,1)} %bitcast.16), channel_id=1, source_target_pairs={{0,128},{128,0},{1,129},{129,1},{2,130},{130,2},{3,131},{131,3},{4... | collective-permute-start | bytes 3145736 | tf_op jit(solution)/shard_map/ppermute | solution.py:89
  102.7 1.1 copy-start.2
  103.8 25.9 %collective-permute-start.1 = (bf16[1,3,384]{2,1,0:T(4,128)(2,1)S(1)}, bf16[1,3,384]{2,1,0:T(4,128)(2,1)S(1)}, u32[]{:S(2)}, u32[]{:S(2)}) collective-permute-start(bf16[1,3,384]{2,1,0:T(4,128)(2,1)S(1)} %slice.64), channel_id=1, source_target_pairs={{1,0},{2,1},{3,2},{4,3},{5,4},{6,5},{7,6},{8,7},{9,8},{10,9},{11,1... | collective-permute-start | bytes 6920 | tf_op jit(solution)/shard_map/ppermute | solution.py:36
  118.0 11.7 %copy-start.3 = (bf16[1,2048,384]{2,1,0:T(8,128)(2,1)S(1)}, bf16[1,2048,384]{2,1,0:T(8,128)(2,1)}, u32[]{:S(2)}) copy-start(bf16[1,2048,384]{2,1,0:T(8,128)(2,1)} %copy-done.2) | copy-start | bytes 4718596
  121.4 8.5 %copy-start.4 = (bf16[1,2048,384]{2,1,0:T(8,128)(2,1)S(1)}, bf16[1,2048,384]{2,1,0:T(8,128)(2,1)}, u32[]{:S(2)}) copy-start(bf16[1,2048,384]{2,1,0:T(8,128)(2,1)} %param.9) | copy-start | bytes 4718596
  121.4 41.1 %collective-permute-start.3 = (bf16[4,256,512]{1,0,2:T(4,128)(2,1)S(1)}, bf16[4,256,512]{1,0,2:T(4,128)(2,1)S(1)}, u32[]{:S(2)}, u32[]{:S(2)}) collective-permute-start(bf16[4,256,512]{1,0,2:T(4,128)(2,1)S(1)} %bitcast.79), channel_id=1, source_target_pairs={{0,128},{128,0},{1,129},{129,1},{2,130},{130,2},{3,131},{131,3},{4... | collective-permute-start | bytes 3145736 | tf_op jit(solution)/shard_map/ppermute | solution.py:88
  133.5 6.7 %copy-start.1 = (f32[4,64,4,512]{3,0,2,1:T(4,128)S(1)}, f32[4,64,4,512]{3,0,2,1:T(4,128)}, u32[]{:S(2)}) copy-start(f32[4,64,4,512]{3,0,2,1:T(4,128)} %copy.34) | copy-start | bytes 6291460

commit v10 on v8

--- a/solution.py
+++ b/solution.py
@@ -90,12 +90,10 @@
     grad_hidden = jnp.einsum(
         "ipqj,psiqd->sijd", first_split, grad_rows, preferred_element_type=jnp.float32
     ).reshape(seq_count, tok_rows, channels)
-    part_second = (
-        second_part(me).astype(jnp.float32) + sent_second.astype(jnp.float32)
-    ).astype(jnp.bfloat16)
-    part_first = (
-        first_part(me).astype(jnp.float32) + sent_first.astype(jnp.float32)
-    ).astype(jnp.bfloat16)
+    kept = lambda part: lax.reduce_precision(part.astype(jnp.float32), exponent_bits=8, mantissa_bits=7)
+    own_second = lax.optimization_barrier(kept(second_part(me)))
+    part_second = (own_second + sent_second.astype(jnp.float32)).astype(jnp.bfloat16)
+    part_first = (kept(first_part(me)) + sent_first.astype(jnp.float32)).astype(jnp.bfloat16)
     grad_conv = (grad_hidden * gate_val * (1.0 + conv_out * (1.0 - gate_val))).astype(jnp.bfloat16)
     following = passed_along(grad_conv[:, : tap_count - 1, :], "seq", -1)
     extended = jnp.concatenate([grad_conv, following], axis=1).astype(jnp.float32)

time: 166 us -> 165 us (level)
  waiting for transfers between devices: 62.2 us -> 60 us
    convert_element_type x1 -> x0, local copies, waits for them, and re-layouts: 2.71 us -> none  [body(): first_part(me).astype(jnp.float32) + sent_first.astype(jnp.float32)]
    reduce_precision x0 -> x1, local copies, waits for them, and re-layouts: none -> 2.71 us  [body(): lax.reduce_precision(part.astype(jnp.float32), exponent_bits=8, mantissa_...]
    ppermute x1, waiting for transfers between devices: 8.63 us -> 6.44 us  [body(): sent_first = lax.ppermute(first_part(other), 'batch', swap)]
  transfers between devices with their start and end apart: 6 -> 6, of which waited for: 4 -> 4; matrix products, arithmetic and copies ran while one was open for 25% -> 26% of each run, Pallas kernels for 0% -> 0%
where the time goes in v10:
time: 165 us; the launch traced here: 164 us
  waiting for transfers between devices  60 us (36%)
  starting transfers between devices  49.3 us (30%)
  local copies, waits for them, and re-layouts  23.6 us (14%)
  matrix products  12.9 us (8%)
  other arithmetic  12.8 us (8%)
  Pallas kernels  4.47 us (3%)
    all_to_all x1, waiting for transfers between devices, body(): lax.all_to_all(grad_chunks, 'seq', split_axis=0, concat_axis=0, tiled=True)  23.5 us
    ppermute x1, waiting for transfers between devices, body(): sent_second = lax.ppermute(second_part(other), 'batch', swap)  19.3 us
    all_to_all x1, starting transfers between devices, body(): lax.all_to_all(grad_chunks, 'seq', split_axis=0, concat_axis=0, tiled=True)  16.5 us
    all_to_all x1, starting transfers between devices, body(): lax.all_to_all(mixed_chunks, 'seq', split_axis=0, concat_axis=3, tiled=True)  14.8 us
    all_to_all x1, waiting for transfers between devices, body(): lax.all_to_all(mixed_chunks, 'seq', split_axis=0, concat_axis=3, tiled=True)  10.8 us
    ppermute x1, starting transfers between devices, body(): sent_second = lax.ppermute(second_part(other), 'batch', swap)  8.32 us
    ppermute x2, starting transfers between devices, passed_along(): lax.ppermute(value, axis, [(source, source + steps) for source in range(i...  6.98 us
    ppermute x1, waiting for transfers between devices, body(): sent_first = lax.ppermute(first_part(other), 'batch', swap)  6.44 us
  transfers between devices with their start and end apart: 6, of which 4 were waited for; matrix products, arithmetic and copies ran while one was open for 26% of the time, Pallas kernels for 0%

profile of v10, /device:TPU:1, one launch (start us, length us, event | category | flops | bytes accessed | tf_op | source)
XLA Modules:
  0.0 163.9 jit_solution(8993473385603291399)
XLA Ops:
  0.6 4.5 %shard_map.76 = bf16[512,1536]{1,0:T(8,128)(2,1)} custom-call(bf16[4,512,512]{2,1,0:T(8,128)(2,1)} %s_ref.1, bf16[4,512,384]{2,1,0:T(8,128)(2,1)} %bitcast.59), custom_call_target="tpu_custom_call" | custom-call | flops 805306368 | bytes 5242880 | tf_op jit(solution)/shard_map/pallas_call | solution.py:22
  5.1 3.9 %reshape.126 = bf16[128,1,4,4,384]{4,3,2,0,1:T(4,128)(2,1)} reshape(bf16[512,1536]{1,0:T(8,128)(2,1)} %shard_map.76) | data formatting | bytes 3145728 | tf_op jit(solution)/shard_map/reshape | solution.py:64
  9.0 16.5 %all-to-all-start = ((bf16[128,1,4,4,384]{4,3,2,1,0:T(4,128)(2,1)}), bf16[128,1,4,4,384]{4,3,2,1,0:T(4,128)(2,1)S(1)}, u32[]{:S(2)}, u32[]{:S(2)}) async-start(bf16[128,1,4,4,384]{4,3,2,1,0:T(4,128)(2,1)} %bitcast.1), calls=%async_computation | async-start | bytes 3145728 | tf_op jit(solution)/shard_map/all_to_all | solution.py:67
  25.6 3.5 %collective-permute-start = (bf16[1,3,384]{2,1,0:T(4,128)(2,1)S(1)}, bf16[1,3,384]{2,1,0:T(4,128)(2,1)S(1)}, u32[]{:S(2)}, u32[]{:S(2)}) collective-permute-start(bf16[1,3,384]{2,1,0:T(4,128)(2,1)S(1)} %slice.47), channel_id=1, source_target_pairs={{0,1},{1,2},{2,3},{3,4},{4,5},{5,6},{6,7},{7,8},{8,9},{9,10},{10,1... | collective-permute-start | bytes 6920 | tf_op jit(solution)/shard_map/ppermute | solution.py:36
  29.2 4.0 %reshape.128 = bf16[4,128,4,512]{3,2,1,0:T(4,128)(2,1)} reshape(bf16[4,512,512]{2,1,0:T(8,128)(2,1)} %param.7) | data formatting | bytes 4194304 | tf_op jit(solution)/shard_map/reshape | solution.py:59
  33.6 3.1 %multiply_convert_fusion = (bf16[1,2048,384]{2,1,0:T(8,128)(2,1)S(1)}, f32[1,2048,384]{2,1,0:T(8,128)}) fusion(f32[1,2051,384]{2,1,0:T(8,128)S(1)} %maximum_convert_fusion, f32[384]{0:T(512)S(1)} %get-tuple-element.11, f32[384]{0:T(512)S(1)} %get-tuple-element.12, f32[384]{0:T(512)S(1)} %get-tuple-element.10, f32[384]{0:T(512)S(1)} %get-tuple-element.9), kind=kLoop, calls=%fused_computation.18 | loop fusion | flops 9437184 | bytes 17307648 | tf_op jit(solution)/shard_map/convert_element_type | solution.py:57
  36.7 2.5 %fusion.17 = bf16[128,1,4,4,384]{0,4,2,3,1:T(8,128)(2,1)} fusion(bf16[4,512,384,1]{2,1,3,0:T(8,128)(2,1)S(1)} %bitcast.56, bf16[4,128,4,512]{3,2,1,0:T(4,128)(2,1)S(1)} %copy-done), kind=kOutput, calls=%fused_computation.37 | convolution fusion | flops 806092800 | bytes 5242880 | tf_op jit(solution)/shard_map/ipqj,sijd->psqid/dot_general | solution.py:60
  39.2 3.9 %copy.35 = bf16[128,1,4,4,384]{4,2,3,1,0:T(4,128)(2,1)} copy(bf16[128,1,4,4,384]{0,4,2,3,1:T(8,128)(2,1)} %fusion.17) | data formatting | bytes 3145728 | tf_op jit(solution)/shard_map/convert_element_type | solution.py:62
  43.1 23.5 %all-to-all-done = bf16[128,1,4,4,384]{4,3,2,1,0:T(4,128)(2,1)S(1)} async-done(((bf16[128,1,4,4,384]{4,3,2,1,0:T(4,128)(2,1)}), bf16[128,1,4,4,384]{4,3,2,1,0:T(4,128)(2,1)S(1)}, u32[]{:S(2)}, u32[]{:S(2)}) %all-to-all-start) | async-done | bytes 1572896 | tf_op jit(solution)/shard_map/all_to_all | solution.py:67
  66.6 14.8 %all-to-all-start.1 = ((bf16[128,1,4,4,384]{4,2,3,1,0:T(4,128)(2,1)}), bf16[128,1,4,4,384]{4,2,3,1,0:T(4,128)(2,1)}, u32[]{:S(2)}, u32[]{:S(2)}) async-start(bf16[128,1,4,4,384]{4,2,3,1,0:T(4,128)(2,1)} %copy.35), calls=%async_computation.1 | async-start | bytes 3145728 | tf_op jit(solution)/shard_map/all_to_all | solution.py:68
  82.7 2.7 %copy.30 = f32[4,64,4,512]{3,0,2,1:T(4,128)} copy(f32[4,64,4,512]{3,1,2,0:T(8,128)S(1)} %convert_reduce-precision_fusion.1) | data formatting | bytes 4194304 | tf_op jit(solution)/shard_map/reduce_precision | solution.py:93
  87.9 2.7 %collective-permute-start.2 = (bf16[4,256,512]{2,0,1:T(4,128)(2,1)}, bf16[4,256,512]{2,0,1:T(4,128)(2,1)}, u32[]{:S(2)}, u32[]{:S(2)}) collective-permute-start(bf16[4,256,512]{2,0,1:T(4,128)(2,1)} %bitcast.16), channel_id=1, source_target_pairs={{0,128},{128,0},{1,129},{129,1},{2,130},{130,2},{3,131},{131,3},{4... | collective-permute-start | bytes 3145736 | tf_op jit(solution)/shard_map/ppermute | solution.py:89
  92.5 4.3 %convolution_bitcast_fusion = f32[1,4,512,384]{2,3,1,0:T(8,128)} fusion(bf16[4,128,4,512]{3,2,1,0:T(4,128)(2,1)} %reshape.128, bf16[128,1,4,4,384]{0,4,3,2,1:T(8,128)(2,1)S(1)} %copy.26), kind=kOutput, calls=%fused_computation.25 | convolution fusion | flops 805306368 | bytes 6815744 | tf_op jit(solution)/shard_map/ipqj,psiqd->sijd/dot_general | solution.py:90
  96.9 2.4 %copy.28 = f32[1,4,512,384]{3,2,1,0:T(8,128)S(1)} copy(f32[1,4,512,384]{2,3,1,0:T(8,128)} %convolution_bitcast_fusion) | data formatting | bytes 6291456 | tf_op jit(solution)/shard_map/ipqj,psiqd->sijd/transpose | solution.py:90
  99.3 3.4 %fusion.8 = bf16[1,2048,384]{2,1,0:T(8,128)(2,1)S(1)} fusion(f32[1,4,512,384]{3,2,1,0:T(8,128)S(1)} %copy.28, f32[1,2048,384]{2,1,0:T(8,128)} %get-tuple-element.14), kind=kLoop, calls=%fused_computation.17 | loop fusion | flops 7077888 | bytes 7864320 | tf_op jit(solution)/shard_map/convert_element_type | solution.py:97
  103.8 3.4 %collective-permute-start.1 = (bf16[1,3,384]{2,1,0:T(4,128)(2,1)S(1)}, bf16[1,3,384]{2,1,0:T(4,128)(2,1)S(1)}, u32[]{:S(2)}, u32[]{:S(2)}) collective-permute-start(bf16[1,3,384]{2,1,0:T(4,128)(2,1)S(1)} %slice.64), channel_id=1, source_target_pairs={{1,0},{2,1},{3,2},{4,3},{5,4},{6,5},{7,6},{8,7},{9,8},{10,9},{11,1... | collective-permute-start | bytes 6920 | tf_op jit(solution)/shard_map/ppermute | solution.py:36
  107.2 10.8 %all-to-all-done.1 = bf16[128,1,4,4,384]{4,2,3,1,0:T(4,128)(2,1)} async-done(((bf16[128,1,4,4,384]{4,2,3,1,0:T(4,128)(2,1)}), bf16[128,1,4,4,384]{4,2,3,1,0:T(4,128)(2,1)}, u32[]{:S(2)}, u32[]{:S(2)}) %all-to-all-start.1) | async-done | bytes 1572896 | tf_op jit(solution)/shard_map/all_to_all | solution.py:68
  118.0 2.4 %convolution_convert_fusion = bf16[4,256,512]{2,1,0:T(8,128)(2,1)S(1)} fusion(bf16[4,512,384]{2,0,1:T(4,128)(2,1)} %bitcast.24, bf16[1,4,512,384]{3,2,1,0:T(8,128)(2,1)} %bitcast.60, s32[]{:T(128)S(6)} %select_n.15), kind=kOutput, calls=%fused_computation.33 | convolution fusion | flops 403177472 | bytes 3407876 | tf_op jit(solution)/shard_map/skmd,skid->kmi/dot_general | solution.py:77
  120.4 8.3 %collective-permute-start.3 = (bf16[4,256,512]{2,1,0:T(8,128)(2,1)S(1)}, bf16[4,256,512]{2,1,0:T(8,128)(2,1)S(1)}, u32[]{:S(2)}, u32[]{:S(2)}) collective-permute-start(bf16[4,256,512]{2,1,0:T(8,128)(2,1)S(1)} %convolution_convert_fusion), channel_id=1, source_target_pairs={{0,128},{128,0},{1,129},{129,1},{2,130},{130,2},{3,131},{131,3},{4... | collective-permute-start | bytes 3145736 | tf_op jit(solution)/shard_map/ppermute | solution.py:88
  129.0 2.2 %convert_reduce-precision_fusion = f32[4,256,512]{2,1,0:T(8,128)S(1)} fusion(bf16[4,512,384]{2,0,1:T(4,128)(2,1)} %bitcast.24, bf16[1,4,512,384]{3,2,1,0:T(8,128)(2,1)S(1)} %bitcast.61, s32[]{:T(128)S(6)} %select_n.14), kind=kOutput, calls=%fused_computation.23 | convolution fusion | flops 404226048 | bytes 4456452 | tf_op jit(solution)/shard_map/skmd,skid->kmi/dot_general | solution.py:77
  131.2 2.5 %fusion.1 = bf16[1,2048,384]{2,1,0:T(8,128)(2,1)} fusion(f32[1,2051,384]{2,1,0:T(8,128)S(1)} %maximum_convert_fusion.1, f32[384]{0:T(512)S(1)} %get-tuple-element.11, f32[384]{0:T(512)S(1)} %get-tuple-element.12, f32[384]{0:T(512)S(1)} %get-tuple-element.10, f32[384]{0:T(512)S(1)} %get-tuple-element.9), kind=kLoop, calls=%fused_computation.2 | loop fusion | flops 6291456 | bytes 14161920 | tf_op jit(solution)/shard_map/convert_element_type | solution.py:102
  133.7 6.4 %collective-permute-done.2 = bf16[4,256,512]{2,0,1:T(4,128)(2,1)} collective-permute-done((bf16[4,256,512]{2,0,1:T(4,128)(2,1)}, bf16[4,256,512]{2,0,1:T(4,128)(2,1)}, u32[]{:S(2)}, u32[]{:S(2)}) %collective-permute-start.2) | collective-permute-done | bytes 1048608 | tf_op jit(solution)/shard_map/ppermute | solution.py:89
  140.2 1.9 %fusion.9 = bf16[4,256,512]{2,0,1:T(4,128)(2,1)S(1)} fusion(f32[4,64,4,512]{3,0,2,1:T(4,128)S(1)} %copy-done.1, bf16[4,256,512]{2,0,1:T(4,128)(2,1)} %collective-permute-done.2), kind=kLoop, calls=%fused_computation.21 | loop fusion | flops 1572864 | bytes 4194304 | tf_op jit(solution)/shard_map/convert_element_type | solution.py:96
  143.2 19.3 %collective-permute-done.3 = bf16[4,256,512]{2,1,0:T(8,128)(2,1)S(1)} collective-permute-done((bf16[4,256,512]{2,1,0:T(8,128)(2,1)S(1)}, bf16[4,256,512]{2,1,0:T(8,128)(2,1)S(1)}, u32[]{:S(2)}, u32[]{:S(2)}) %collective-permute-start.3) | collective-permute-done | bytes 1048608 | tf_op jit(solution)/shard_map/ppermute | solution.py:88
  (28 shorter events, 9.9 us)
Async XLA Ops:
  9.0 16.5 %copy-start.5 = (bf16[1,2048,384]{2,1,0:T(8,128)(2,1)S(1)}, bf16[1,2048,384]{2,1,0:T(8,128)(2,1)}, u32[]{:S(2)}) copy-start(bf16[1,2048,384]{2,1,0:T(8,128)(2,1)} %param.5) | copy-start | bytes 4718596
  9.0 20.1 %copy-start.6 = (f32[4,384]{1,0:T(4,128)S(1)}, f32[4,384]{1,0:T(4,128)}, u32[]{:S(2)}) copy-start(f32[4,384]{1,0:T(4,128)} %param.6) | copy-start | bytes 18436
  9.0 57.6 %all-to-all-start = ((bf16[128,1,4,4,384]{4,3,2,1,0:T(4,128)(2,1)}), bf16[128,1,4,4,384]{4,3,2,1,0:T(4,128)(2,1)S(1)}, u32[]{:S(2)}, u32[]{:S(2)}) async-start(bf16[128,1,4,4,384]{4,3,2,1,0:T(4,128)(2,1)} %bitcast.1), calls=%async_computation | async-start | bytes 3145728 | tf_op jit(solution)/shard_map/all_to_all | solution.py:67
  25.6 7.6 %collective-permute-start = (bf16[1,3,384]{2,1,0:T(4,128)(2,1)S(1)}, bf16[1,3,384]{2,1,0:T(4,128)(2,1)S(1)}, u32[]{:S(2)}, u32[]{:S(2)}) collective-permute-start(bf16[1,3,384]{2,1,0:T(4,128)(2,1)S(1)} %slice.47), channel_id=1, source_target_pairs={{0,1},{1,2},{2,3},{3,4},{4,5},{5,6},{6,7},{7,8},{8,9},{9,10},{10,1... | collective-permute-start | bytes 6920 | tf_op jit(solution)/shard_map/ppermute | solution.py:36
  33.6 3.1 %copy-start = (bf16[4,128,4,512]{3,2,1,0:T(4,128)(2,1)S(1)}, bf16[4,128,4,512]{3,2,1,0:T(4,128)(2,1)}, u32[]{:S(2)}) copy-start(bf16[4,128,4,512]{3,2,1,0:T(4,128)(2,1)} %reshape.128) | copy-start | bytes 6291460
  66.6 51.4 %all-to-all-start.1 = ((bf16[128,1,4,4,384]{4,2,3,1,0:T(4,128)(2,1)}), bf16[128,1,4,4,384]{4,2,3,1,0:T(4,128)(2,1)}, u32[]{:S(2)}, u32[]{:S(2)}) async-start(bf16[128,1,4,4,384]{4,2,3,1,0:T(4,128)(2,1)} %copy.35), calls=%async_computation.1 | async-start | bytes 3145728 | tf_op jit(solution)/shard_map/all_to_all | solution.py:68
  87.9 52.2 %collective-permute-start.2 = (bf16[4,256,512]{2,0,1:T(4,128)(2,1)}, bf16[4,256,512]{2,0,1:T(4,128)(2,1)}, u32[]{:S(2)}, u32[]{:S(2)}) collective-permute-start(bf16[4,256,512]{2,0,1:T(4,128)(2,1)} %bitcast.16), channel_id=1, source_target_pairs={{0,128},{128,0},{1,129},{129,1},{2,130},{130,2},{3,131},{131,3},{4... | collective-permute-start | bytes 3145736 | tf_op jit(solution)/shard_map/ppermute | solution.py:89
  102.7 1.1 copy-start.2
  103.8 25.0 %copy-start.3 = (bf16[1,2048,384]{2,1,0:T(8,128)(2,1)S(1)}, bf16[1,2048,384]{2,1,0:T(8,128)(2,1)}, u32[]{:S(2)}) copy-start(bf16[1,2048,384]{2,1,0:T(8,128)(2,1)} %copy-done.2) | copy-start | bytes 4718596
  103.8 25.0 %collective-permute-start.1 = (bf16[1,3,384]{2,1,0:T(4,128)(2,1)S(1)}, bf16[1,3,384]{2,1,0:T(4,128)(2,1)S(1)}, u32[]{:S(2)}, u32[]{:S(2)}) collective-permute-start(bf16[1,3,384]{2,1,0:T(4,128)(2,1)S(1)} %slice.64), channel_id=1, source_target_pairs={{1,0},{2,1},{3,2},{4,3},{5,4},{6,5},{7,6},{8,7},{9,8},{10,9},{11,1... | collective-permute-start | bytes 6920 | tf_op jit(solution)/shard_map/ppermute | solution.py:36
  120.4 8.6 %copy-start.4 = (bf16[1,2048,384]{2,1,0:T(8,128)(2,1)S(1)}, bf16[1,2048,384]{2,1,0:T(8,128)(2,1)}, u32[]{:S(2)}) copy-start(bf16[1,2048,384]{2,1,0:T(8,128)(2,1)} %param.9) | copy-start | bytes 4718596
  120.4 42.1 %collective-permute-start.3 = (bf16[4,256,512]{2,1,0:T(8,128)(2,1)S(1)}, bf16[4,256,512]{2,1,0:T(8,128)(2,1)S(1)}, u32[]{:S(2)}, u32[]{:S(2)}) collective-permute-start(bf16[4,256,512]{2,1,0:T(8,128)(2,1)S(1)} %convolution_convert_fusion), channel_id=1, source_target_pairs={{0,128},{128,0},{1,129},{129,1},{2,130},{130,2},{3,131},{131,3},{4... | collective-permute-start | bytes 3145736 | tf_op jit(solution)/shard_map/ppermute | solution.py:88
  131.2 9.0 %copy-start.1 = (f32[4,64,4,512]{3,0,2,1:T(4,128)S(1)}, f32[4,64,4,512]{3,0,2,1:T(4,128)}, u32[]{:S(2)}) copy-start(f32[4,64,4,512]{3,0,2,1:T(4,128)} %copy.30) | copy-start | bytes 6291460

commit v11 on v10

--- a/solution.py
+++ b/solution.py
@@ -7,21 +7,22 @@
 
 
 def _grad_payload_kernel(s_ref, g_ref, o_ref):
+    peers, group, _ = o_ref.shape
     width = g_ref.shape[-1]
     for k in range(s_ref.shape[0]):
         product = lax.dot_general(
             s_ref[k], g_ref[k], (((0,), (0,)), ((), ())), preferred_element_type=jnp.float32
         )
-        o_ref[:, k * width : (k + 1) * width] = product.astype(o_ref.dtype)
+        o_ref[:, :, k * width : (k + 1) * width] = product.reshape(peers, group, width).astype(o_ref.dtype)
 
 
-def grad_payload(second_factor, upstream):
+def grad_payload(second_factor, upstream, peers):
     col_blocks, rows, order = second_factor.shape
     width = upstream.shape[-1]
     flops = 2 * col_blocks * rows * order * width
     return pl.pallas_call(
         _grad_payload_kernel,
-        out_shape=jax.ShapeDtypeStruct((order, col_blocks * width), jnp.bfloat16),
+        out_shape=jax.ShapeDtypeStruct((peers, order // peers, col_blocks * width), jnp.bfloat16),
         in_specs=[pl.BlockSpec(memory_space=pltpu.VMEM)] * 2,
         out_specs=pl.BlockSpec(memory_space=pltpu.VMEM),
         cost_estimate=pl.CostEstimate(
@@ -61,10 +62,10 @@
         "ipqj,sijd->psqid", first_split, hidden_blocks, preferred_element_type=jnp.float32
     ).astype(jnp.bfloat16)
     upstream = grad_output.reshape(seq_count, col_blocks, block_count, channels)
-    grad_chunks = grad_payload(second_factor, upstream).reshape(
+    grad_chunks = grad_payload(second_factor, upstream, peers)
+    grad_rows = lax.all_to_all(grad_chunks, "seq", split_axis=0, concat_axis=0, tiled=True).reshape(
         peers, seq_count, blocks, col_blocks, channels
     )
-    grad_rows = lax.all_to_all(grad_chunks, "seq", split_axis=0, concat_axis=0, tiled=True)
     columns = lax.all_to_all(mixed_chunks, "seq", split_axis=0, concat_axis=3, tiled=True)[0]
     halves = lax.axis_size("batch")
     me = lax.axis_index("batch")

time: 165 us -> 161 us (0.976)
  waiting for transfers between devices: 60 us -> 57.6 us
    reshape x1, local copies, waits for them, and re-layouts: 3.94 us -> 1.5 us  [body(): lax.all_to_all(grad_chunks, 'seq', split_axis=0, concat_axis=0, tiled=True)]
    all_to_all x1, waiting for transfers between devices: 10.8 us -> 8.36 us  [body(): lax.all_to_all(mixed_chunks, 'seq', split_axis=0, concat_axis=3, tiled=True)]
    all_to_all x1 -> x0, local copies, waits for them, and re-layouts: 1.88 us -> none  [body(): lax.all_to_all(grad_chunks, 'seq', split_axis=0, concat_axis=0, tiled=True)]
  transfers between devices with their start and end apart: 6 -> 6, of which waited for: 4 -> 4; matrix products, arithmetic and copies ran while one was open for 26% -> 28% of each run, Pallas kernels for 0% -> 0%
where the time goes in v11:
time: 161 us; the launch traced here: 160 us
  waiting for transfers between devices  57.6 us (36%)
  starting transfers between devices  49.4 us (31%)
  local copies, waits for them, and re-layouts  22 us (14%)
  matrix products  12.9 us (8%)
  other arithmetic  12.8 us (8%)
  Pallas kernels  4.49 us (3%)
    all_to_all x1, waiting for transfers between devices, body(): lax.all_to_all(grad_chunks, 'seq', split_axis=0, concat_axis=0, tiled=True)  23.5 us
    ppermute x1, waiting for transfers between devices, body(): sent_second = lax.ppermute(second_part(other), 'batch', swap)  19.3 us
    all_to_all x1, starting transfers between devices, body(): lax.all_to_all(grad_chunks, 'seq', split_axis=0, concat_axis=0, tiled=True)  16.5 us
    all_to_all x1, starting transfers between devices, body(): lax.all_to_all(mixed_chunks, 'seq', split_axis=0, concat_axis=3, tiled=True)  14.9 us
    all_to_all x1, waiting for transfers between devices, body(): lax.all_to_all(mixed_chunks, 'seq', split_axis=0, concat_axis=3, tiled=True)  8.36 us
    ppermute x1, starting transfers between devices, body(): sent_second = lax.ppermute(second_part(other), 'batch', swap)  8.32 us
    ppermute x2, starting transfers between devices, passed_along(): lax.ppermute(value, axis, [(source, source + steps) for source in range(i...  6.98 us
    ppermute x1, waiting for transfers between devices, body(): sent_first = lax.ppermute(first_part(other), 'batch', swap)  6.44 us
  transfers between devices with their start and end apart: 6, of which 4 were waited for; matrix products, arithmetic and copies ran while one was open for 28% of the time, Pallas kernels for 0%

profile of v11, /device:TPU:1, one launch (start us, length us, event | category | flops | bytes accessed | tf_op | source)
XLA Modules:
  0.0 160.0 jit_solution(14608808246949650541)
XLA Ops:
  0.6 4.5 %shard_map.76 = bf16[128,4,1536]{2,1,0:T(4,128)(2,1)} custom-call(bf16[4,512,512]{2,1,0:T(8,128)(2,1)} %s_ref.1, bf16[4,512,384]{2,1,0:T(8,128)(2,1)} %bitcast.58), custom_call_target="tpu_custom_call" | custom-call | flops 805306368 | bytes 5242880 | tf_op jit(solution)/shard_map/pallas_call | solution.py:23
  5.1 16.5 %all-to-all-start = ((bf16[128,4,1536]{2,1,0:T(4,128)(2,1)}), bf16[128,4,1536]{2,1,0:T(4,128)(2,1)S(1)}, u32[]{:S(2)}, u32[]{:S(2)}) async-start(bf16[128,4,1536]{2,1,0:T(4,128)(2,1)} %shard_map.76), calls=%async_computation | async-start | bytes 3145728 | tf_op jit(solution)/shard_map/all_to_all | solution.py:66
  21.7 3.5 %collective-permute-start = (bf16[1,3,384]{2,1,0:T(4,128)(2,1)S(1)}, bf16[1,3,384]{2,1,0:T(4,128)(2,1)S(1)}, u32[]{:S(2)}, u32[]{:S(2)}) collective-permute-start(bf16[1,3,384]{2,1,0:T(4,128)(2,1)S(1)} %slice.47), channel_id=1, source_target_pairs={{0,1},{1,2},{2,3},{3,4},{4,5},{5,6},{6,7},{7,8},{8,9},{9,10},{10,1... | collective-permute-start | bytes 6920 | tf_op jit(solution)/shard_map/ppermute | solution.py:37
  25.3 4.0 %reshape.128 = bf16[4,128,4,512]{3,2,1,0:T(4,128)(2,1)} reshape(bf16[4,512,512]{2,1,0:T(8,128)(2,1)} %param.7) | data formatting | bytes 4194304 | tf_op jit(solution)/shard_map/reshape | solution.py:60
  29.6 3.1 %multiply_convert_fusion = (bf16[1,2048,384]{2,1,0:T(8,128)(2,1)S(1)}, f32[1,2048,384]{2,1,0:T(8,128)}) fusion(f32[1,2051,384]{2,1,0:T(8,128)S(1)} %maximum_convert_fusion, f32[384]{0:T(512)S(1)} %get-tuple-element.11, f32[384]{0:T(512)S(1)} %get-tuple-element.12, f32[384]{0:T(512)S(1)} %get-tuple-element.10, f32[384]{0:T(512)S(1)} %get-tuple-element.9), kind=kLoop, calls=%fused_computation.18 | loop fusion | flops 9437184 | bytes 17307648 | tf_op jit(solution)/shard_map/convert_element_type | solution.py:58
  32.8 2.6 %fusion.16 = bf16[128,1,4,4,384]{0,4,2,3,1:T(8,128)(2,1)} fusion(bf16[4,512,384,1]{2,1,3,0:T(8,128)(2,1)S(1)} %bitcast.54, bf16[4,128,4,512]{3,2,1,0:T(4,128)(2,1)S(1)} %copy-done), kind=kOutput, calls=%fused_computation.36 | convolution fusion | flops 806092800 | bytes 5242880 | tf_op jit(solution)/shard_map/ipqj,sijd->psqid/dot_general | solution.py:61
  35.3 3.9 %copy.36 = bf16[128,1,4,4,384]{4,2,3,1,0:T(4,128)(2,1)} copy(bf16[128,1,4,4,384]{0,4,2,3,1:T(8,128)(2,1)} %fusion.16) | data formatting | bytes 3145728 | tf_op jit(solution)/shard_map/convert_element_type | solution.py:63
  39.2 23.5 %all-to-all-done = bf16[128,4,1536]{2,1,0:T(4,128)(2,1)S(1)} async-done(((bf16[128,4,1536]{2,1,0:T(4,128)(2,1)}), bf16[128,4,1536]{2,1,0:T(4,128)(2,1)S(1)}, u32[]{:S(2)}, u32[]{:S(2)}) %all-to-all-start) | async-done | bytes 1572896 | tf_op jit(solution)/shard_map/all_to_all | solution.py:66
  62.7 14.9 %all-to-all-start.1 = ((bf16[128,1,4,4,384]{4,2,3,1,0:T(4,128)(2,1)}), bf16[128,1,4,4,384]{4,2,3,1,0:T(4,128)(2,1)}, u32[]{:S(2)}, u32[]{:S(2)}) async-start(bf16[128,1,4,4,384]{4,2,3,1,0:T(4,128)(2,1)} %copy.36), calls=%async_computation.1 | async-start | bytes 3145728 | tf_op jit(solution)/shard_map/all_to_all | solution.py:69
  79.0 1.9 %constant_dynamic-slice_fusion = (bf16[64,1,4,4,384]{4,3,2,0,1:T(4,128)(2,1)S(1)}, bf16[64,1,4,4,384]{4,3,2,0,1:T(4,128)(2,1)S(1)}) fusion(bf16[128,1,4,4,384]{4,3,2,0,1:T(4,128)(2,1)} %reshape.130, s32[]{:T(128)S(6)} %select_n.13, s32[]{:T(128)S(6)} %select_n.12), kind=kLoop, calls=%fused_computation.53 | loop fusion | bytes 3145736 | tf_op jit(solution)/shard_map/dynamic_slice | solution.py:83
  81.7 2.7 %copy.31 = f32[4,64,4,512]{3,0,2,1:T(4,128)} copy(f32[4,64,4,512]{3,1,2,0:T(8,128)S(1)} %convert_reduce-precision_fusion.1) | data formatting | bytes 4194304 | tf_op jit(solution)/shard_map/reduce_precision | solution.py:94
  87.0 2.7 %collective-permute-start.2 = (bf16[4,256,512]{2,0,1:T(4,128)(2,1)}, bf16[4,256,512]{2,0,1:T(4,128)(2,1)}, u32[]{:S(2)}, u32[]{:S(2)}) collective-permute-start(bf16[4,256,512]{2,0,1:T(4,128)(2,1)} %bitcast.15), channel_id=1, source_target_pairs={{0,128},{128,0},{1,129},{129,1},{2,130},{130,2},{3,131},{131,3},{4... | collective-permute-start | bytes 3145736 | tf_op jit(solution)/shard_map/ppermute | solution.py:90
  91.1 4.3 %convolution_bitcast_fusion = f32[1,4,512,384]{2,3,1,0:T(8,128)} fusion(bf16[128,4,4,384]{0,3,2,1:T(8,128)(2,1)S(1)} %bitcast.57, bf16[4,128,4,512]{3,2,1,0:T(4,128)(2,1)} %reshape.128), kind=kOutput, calls=%fused_computation.25 | convolution fusion | flops 805306368 | bytes 6815744 | tf_op jit(solution)/shard_map/ipqj,psiqd->sijd/dot_general | solution.py:91
  95.5 2.4 %copy.29 = f32[1,4,512,384]{3,2,1,0:T(8,128)S(1)} copy(f32[1,4,512,384]{2,3,1,0:T(8,128)} %convolution_bitcast_fusion) | data formatting | bytes 6291456 | tf_op jit(solution)/shard_map/ipqj,psiqd->sijd/transpose | solution.py:91
  97.8 3.4 %fusion.8 = bf16[1,2048,384]{2,1,0:T(8,128)(2,1)S(1)} fusion(f32[1,4,512,384]{3,2,1,0:T(8,128)S(1)} %copy.29, f32[1,2048,384]{2,1,0:T(8,128)} %get-tuple-element.14), kind=kLoop, calls=%fused_computation.17 | loop fusion | flops 7077888 | bytes 7864320 | tf_op jit(solution)/shard_map/convert_element_type | solution.py:98
  102.4 3.4 %collective-permute-start.1 = (bf16[1,3,384]{2,1,0:T(4,128)(2,1)S(1)}, bf16[1,3,384]{2,1,0:T(4,128)(2,1)S(1)}, u32[]{:S(2)}, u32[]{:S(2)}) collective-permute-start(bf16[1,3,384]{2,1,0:T(4,128)(2,1)S(1)} %slice.64), channel_id=1, source_target_pairs={{1,0},{2,1},{3,2},{4,3},{5,4},{6,5},{7,6},{8,7},{9,8},{10,9},{11,1... | collective-permute-start | bytes 6920 | tf_op jit(solution)/shard_map/ppermute | solution.py:37
  105.8 8.4 %all-to-all-done.1 = bf16[128,1,4,4,384]{4,2,3,1,0:T(4,128)(2,1)} async-done(((bf16[128,1,4,4,384]{4,2,3,1,0:T(4,128)(2,1)}), bf16[128,1,4,4,384]{4,2,3,1,0:T(4,128)(2,1)}, u32[]{:S(2)}, u32[]{:S(2)}) %all-to-all-start.1) | async-done | bytes 1572896 | tf_op jit(solution)/shard_map/all_to_all | solution.py:69
  114.2 2.4 %convolution_convert_fusion = bf16[4,256,512]{2,1,0:T(8,128)(2,1)S(1)} fusion(bf16[4,512,384]{2,0,1:T(4,128)(2,1)} %bitcast.23, bf16[1,4,512,384]{3,2,1,0:T(8,128)(2,1)} %bitcast.59, s32[]{:T(128)S(6)} %select_n.15), kind=kOutput, calls=%fused_computation.32 | convolution fusion | flops 403177472 | bytes 3407876 | tf_op jit(solution)/shard_map/skmd,skid->kmi/dot_general | solution.py:78
  116.6 8.3 %collective-permute-start.3 = (bf16[4,256,512]{2,1,0:T(8,128)(2,1)S(1)}, bf16[4,256,512]{2,1,0:T(8,128)(2,1)S(1)}, u32[]{:S(2)}, u32[]{:S(2)}) collective-permute-start(bf16[4,256,512]{2,1,0:T(8,128)(2,1)S(1)} %convolution_convert_fusion), channel_id=1, source_target_pairs={{0,128},{128,0},{1,129},{129,1},{2,130},{130,2},{3,131},{131,3},{4... | collective-permute-start | bytes 3145736 | tf_op jit(solution)/shard_map/ppermute | solution.py:89
  125.1 2.2 %convert_reduce-precision_fusion = f32[4,256,512]{2,1,0:T(8,128)S(1)} fusion(bf16[4,512,384]{2,0,1:T(4,128)(2,1)} %bitcast.23, bf16[1,4,512,384]{3,2,1,0:T(8,128)(2,1)S(1)} %bitcast.60, s32[]{:T(128)S(6)} %select_n.14), kind=kOutput, calls=%fused_computation.23 | convolution fusion | flops 404226048 | bytes 4456452 | tf_op jit(solution)/shard_map/skmd,skid->kmi/dot_general | solution.py:78
  127.3 2.5 %fusion.1 = bf16[1,2048,384]{2,1,0:T(8,128)(2,1)} fusion(f32[1,2051,384]{2,1,0:T(8,128)S(1)} %maximum_convert_fusion.1, f32[384]{0:T(512)S(1)} %get-tuple-element.11, f32[384]{0:T(512)S(1)} %get-tuple-element.12, f32[384]{0:T(512)S(1)} %get-tuple-element.10, f32[384]{0:T(512)S(1)} %get-tuple-element.9), kind=kLoop, calls=%fused_computation.2 | loop fusion | flops 6291456 | bytes 14161920 | tf_op jit(solution)/shard_map/convert_element_type | solution.py:103
  129.9 6.4 %collective-permute-done.2 = bf16[4,256,512]{2,0,1:T(4,128)(2,1)} collective-permute-done((bf16[4,256,512]{2,0,1:T(4,128)(2,1)}, bf16[4,256,512]{2,0,1:T(4,128)(2,1)}, u32[]{:S(2)}, u32[]{:S(2)}) %collective-permute-start.2) | collective-permute-done | bytes 1048608 | tf_op jit(solution)/shard_map/ppermute | solution.py:90
  136.3 1.9 %fusion.9 = bf16[4,256,512]{2,0,1:T(4,128)(2,1)S(1)} fusion(f32[4,64,4,512]{3,0,2,1:T(4,128)S(1)} %copy-done.1, bf16[4,256,512]{2,0,1:T(4,128)(2,1)} %collective-permute-done.2), kind=kLoop, calls=%fused_computation.21 | loop fusion | flops 1572864 | bytes 4194304 | tf_op jit(solution)/shard_map/convert_element_type | solution.py:97
  139.4 19.3 %collective-permute-done.3 = bf16[4,256,512]{2,1,0:T(8,128)(2,1)S(1)} collective-permute-done((bf16[4,256,512]{2,1,0:T(8,128)(2,1)S(1)}, bf16[4,256,512]{2,1,0:T(8,128)(2,1)S(1)}, u32[]{:S(2)}, u32[]{:S(2)}) %collective-permute-start.3) | collective-permute-done | bytes 1048608 | tf_op jit(solution)/shard_map/ppermute | solution.py:89
  (28 shorter events, 10.4 us)
Async XLA Ops:
  5.1 16.5 %copy-start.5 = (bf16[1,2048,384]{2,1,0:T(8,128)(2,1)S(1)}, bf16[1,2048,384]{2,1,0:T(8,128)(2,1)}, u32[]{:S(2)}) copy-start(bf16[1,2048,384]{2,1,0:T(8,128)(2,1)} %param.5) | copy-start | bytes 4718596
  5.1 20.1 %copy-start.6 = (f32[4,384]{1,0:T(4,128)S(1)}, f32[4,384]{1,0:T(4,128)}, u32[]{:S(2)}) copy-start(f32[4,384]{1,0:T(4,128)} %param.6) | copy-start | bytes 18436
  5.1 57.6 %all-to-all-start = ((bf16[128,4,1536]{2,1,0:T(4,128)(2,1)}), bf16[128,4,1536]{2,1,0:T(4,128)(2,1)S(1)}, u32[]{:S(2)}, u32[]{:S(2)}) async-start(bf16[128,4,1536]{2,1,0:T(4,128)(2,1)} %shard_map.76), calls=%async_computation | async-start | bytes 3145728 | tf_op jit(solution)/shard_map/all_to_all | solution.py:66
  21.7 7.6 %collective-permute-start = (bf16[1,3,384]{2,1,0:T(4,128)(2,1)S(1)}, bf16[1,3,384]{2,1,0:T(4,128)(2,1)S(1)}, u32[]{:S(2)}, u32[]{:S(2)}) collective-permute-start(bf16[1,3,384]{2,1,0:T(4,128)(2,1)S(1)} %slice.47), channel_id=1, source_target_pairs={{0,1},{1,2},{2,3},{3,4},{4,5},{5,6},{6,7},{7,8},{8,9},{9,10},{10,1... | collective-permute-start | bytes 6920 | tf_op jit(solution)/shard_map/ppermute | solution.py:37
  29.6 3.1 %copy-start = (bf16[4,128,4,512]{3,2,1,0:T(4,128)(2,1)S(1)}, bf16[4,128,4,512]{3,2,1,0:T(4,128)(2,1)}, u32[]{:S(2)}) copy-start(bf16[4,128,4,512]{3,2,1,0:T(4,128)(2,1)} %reshape.128) | copy-start | bytes 6291460
  62.7 51.5 %all-to-all-start.1 = ((bf16[128,1,4,4,384]{4,2,3,1,0:T(4,128)(2,1)}), bf16[128,1,4,4,384]{4,2,3,1,0:T(4,128)(2,1)}, u32[]{:S(2)}, u32[]{:S(2)}) async-start(bf16[128,1,4,4,384]{4,2,3,1,0:T(4,128)(2,1)} %copy.36), calls=%async_computation.1 | async-start | bytes 3145728 | tf_op jit(solution)/shard_map/all_to_all | solution.py:69
  87.0 49.4 %collective-permute-start.2 = (bf16[4,256,512]{2,0,1:T(4,128)(2,1)}, bf16[4,256,512]{2,0,1:T(4,128)(2,1)}, u32[]{:S(2)}, u32[]{:S(2)}) collective-permute-start(bf16[4,256,512]{2,0,1:T(4,128)(2,1)} %bitcast.15), channel_id=1, source_target_pairs={{0,128},{128,0},{1,129},{129,1},{2,130},{130,2},{3,131},{131,3},{4... | collective-permute-start | bytes 3145736 | tf_op jit(solution)/shard_map/ppermute | solution.py:90
  101.2 1.1 copy-start.2
  102.4 22.6 %copy-start.3 = (bf16[1,2048,384]{2,1,0:T(8,128)(2,1)S(1)}, bf16[1,2048,384]{2,1,0:T(8,128)(2,1)}, u32[]{:S(2)}) copy-start(bf16[1,2048,384]{2,1,0:T(8,128)(2,1)} %copy-done.2) | copy-start | bytes 4718596
  102.4 22.5 %collective-permute-start.1 = (bf16[1,3,384]{2,1,0:T(4,128)(2,1)S(1)}, bf16[1,3,384]{2,1,0:T(4,128)(2,1)S(1)}, u32[]{:S(2)}, u32[]{:S(2)}) collective-permute-start(bf16[1,3,384]{2,1,0:T(4,128)(2,1)S(1)} %slice.64), channel_id=1, source_target_pairs={{1,0},{2,1},{3,2},{4,3},{5,4},{6,5},{7,6},{8,7},{9,8},{10,9},{11,1... | collective-permute-start | bytes 6920 | tf_op jit(solution)/shard_map/ppermute | solution.py:37
  116.6 8.5 %copy-start.4 = (bf16[1,2048,384]{2,1,0:T(8,128)(2,1)S(1)}, bf16[1,2048,384]{2,1,0:T(8,128)(2,1)}, u32[]{:S(2)}) copy-start(bf16[1,2048,384]{2,1,0:T(8,128)(2,1)} %param.9) | copy-start | bytes 4718596
  116.6 42.1 %collective-permute-start.3 = (bf16[4,256,512]{2,1,0:T(8,128)(2,1)S(1)}, bf16[4,256,512]{2,1,0:T(8,128)(2,1)S(1)}, u32[]{:S(2)}, u32[]{:S(2)}) collective-permute-start(bf16[4,256,512]{2,1,0:T(8,128)(2,1)S(1)} %convolution_convert_fusion), channel_id=1, source_target_pairs={{0,128},{128,0},{1,129},{129,1},{2,130},{130,2},{3,131},{131,3},{4... | collective-permute-start | bytes 3145736 | tf_op jit(solution)/shard_map/ppermute | solution.py:89
  127.3 9.0 %copy-start.1 = (f32[4,64,4,512]{3,0,2,1:T(4,128)S(1)}, f32[4,64,4,512]{3,0,2,1:T(4,128)}, u32[]{:S(2)}) copy-start(f32[4,64,4,512]{3,0,2,1:T(4,128)} %copy.31) | copy-start | bytes 6291460

commit v12 on v11

--- a/solution.py
+++ b/solution.py
@@ -29,6 +29,36 @@
             flops=flops, transcendentals=0, bytes_accessed=2 * (second_factor.size + 2 * upstream.size)
         ),
     )(second_factor, upstream.reshape(col_blocks, rows, width))
+
+
+def _second_half_kernel(half_ref, up_ref, col_ref, o_ref):
+    o_ref[0] = lax.dot_general(
+        up_ref[0], col_ref[0], (((1,), (1,)), ((), ())), preferred_element_type=jnp.float32
+    ).astype(o_ref.dtype)
+
+
+def second_half(half, upstream, columns):
+    col_blocks, rows, width = upstream.shape
+    order = columns.shape[1]
+    rows_half = rows // 2
+    return pl.pallas_call(
+        _second_half_kernel,
+        grid_spec=pltpu.PrefetchScalarGridSpec(
+            num_scalar_prefetch=1,
+            grid=(col_blocks,),
+            in_specs=[
+                pl.BlockSpec((1, rows_half, width), lambda q, h: (q, h[0], 0)),
+                pl.BlockSpec((1, order, width), lambda q, h: (q, 0, 0)),
+            ],
+            out_specs=pl.BlockSpec((1, rows_half, order), lambda q, h: (q, 0, 0)),
+        ),
+        out_shape=jax.ShapeDtypeStruct((col_blocks, rows_half, order), jnp.bfloat16),
+        cost_estimate=pl.CostEstimate(
+            flops=2 * col_blocks * rows_half * order * width,
+            transcendentals=0,
+            bytes_accessed=2 * (col_blocks * rows_half * width + columns.size + col_blocks * rows_half * order),
+        ),
+    )(jnp.reshape(half, (1,)).astype(jnp.int32), upstream, columns)
 
 
 def passed_along(value, axis, steps):
@@ -74,10 +104,11 @@
     peers_half = peers // halves
 
     def second_part(half):
-        up = lax.dynamic_slice_in_dim(upstream, half * rows_half, rows_half, 2)
-        return jnp.einsum(
-            "skmd,skid->kmi", up, columns, preferred_element_type=jnp.float32
-        ).astype(jnp.bfloat16)
+        return second_half(
+            half,
+            upstream.reshape(col_blocks, block_count, channels),
+            columns.reshape(col_blocks, peers * blocks, channels),
+        )
 
     def first_part(half):
         gr = lax.dynamic_slice_in_dim(grad_rows, half * peers_half, peers_half, 0)

time: 161 us -> 162 us (level)
  waiting for transfers between devices: 57.6 us -> 47.7 us
  Pallas kernels: 4.49 us -> 13.2 us
  other arithmetic: 12.8 us -> 18 us
  matrix products: 12.9 us -> 8.3 us
  local copies, waits for them, and re-layouts: 22 us -> 24.4 us
    pallas_call x0 -> x2, Pallas kernels: none -> 8.57 us  [second_half(): pl.pallas_call(_second_half_kernel, grid_spec=pltpu.PrefetchScalarGridSpe...]
    ppermute x1, waiting for transfers between devices: 6.44 us -> 0.01 us  [body(): sent_first = lax.ppermute(first_part(other), 'batch', swap)]
    dot_general x2 -> x0, matrix products: 4.55 us -> none  [second_part(): jnp.einsum('skmd,skid->kmi', up, columns, preferred_element_type=jnp.floa...]
    ppermute x1, waiting for transfers between devices: 19.3 us -> 16.4 us  [body(): sent_second = lax.ppermute(second_part(other), 'batch', swap)]
    another operation x1 -> x2, local copies, waits for them, and re-layouts: 1.44 us -> 4.28 us  [the longest x1 2.84 us: second_part(): columns.reshape(col_blocks, peers * blocks, channels)]
  transfers between devices with their start and end apart: 6 -> 6, of which waited for: 4 -> 3; matrix products, arithmetic and copies ran while one was open for 28% -> 30% of each run, Pallas kernels for 0% -> 5%
where the time goes in v12:
time: 162 us; the launch traced here: 161 us
  starting transfers between devices  48.8 us (30%)
  waiting for transfers between devices  47.7 us (29%)
  local copies, waits for them, and re-layouts  24.4 us (15%)
  other arithmetic  18 us (11%)
  Pallas kernels  13.2 us (8%)
  matrix products  8.3 us (5%)
    all_to_all x1, waiting for transfers between devices, body(): lax.all_to_all(grad_chunks, 'seq', split_axis=0, concat_axis=0, tiled=True)  23.5 us
    ppermute x1, waiting for transfers between devices, body(): sent_second = lax.ppermute(second_part(other), 'batch', swap)  16.4 us
    all_to_all x1, starting transfers between devices, body(): lax.all_to_all(grad_chunks, 'seq', split_axis=0, concat_axis=0, tiled=True)  16.4 us
    all_to_all x1, starting transfers between devices, body(): lax.all_to_all(mixed_chunks, 'seq', split_axis=0, concat_axis=3, tiled=True)  14.8 us
    pallas_call x2, Pallas kernels, second_half(): pl.pallas_call(_second_half_kernel, grid_spec=pltpu.PrefetchScalarGridSpe...  8.57 us
    ppermute x1, starting transfers between devices, body(): sent_second = lax.ppermute(second_part(other), 'batch', swap)  8.01 us
    all_to_all x1, waiting for transfers between devices, body(): lax.all_to_all(mixed_chunks, 'seq', split_axis=0, concat_axis=3, tiled=True)  7.8 us
    ppermute x2, starting transfers between devices, passed_along(): lax.ppermute(value, axis, [(source, source + steps) for source in range(i...  6.84 us
  transfers between devices with their start and end apart: 6, of which 3 were waited for; matrix products, arithmetic and copies ran while one was open for 30% of the time, Pallas kernels for 5%

profile of v12, /device:TPU:1, one launch (start us, length us, event | category | flops | bytes accessed | tf_op | source)
XLA Modules:
  0.0 161.2 jit_solution(14670802684925694013)
XLA Ops:
  0.7 4.6 %shard_map.76 = bf16[128,4,1536]{2,1,0:T(4,128)(2,1)} custom-call(bf16[4,512,512]{2,1,0:T(8,128)(2,1)} %s_ref.1, bf16[4,512,384]{2,1,0:T(8,128)(2,1)} %bitcast.49), custom_call_target="tpu_custom_call" | custom-call | flops 805306368 | bytes 5242880 | tf_op jit(solution)/shard_map/pallas_call | solution.py:23
  5.3 16.4 %all-to-all-start = ((bf16[128,4,1536]{2,1,0:T(4,128)(2,1)}), bf16[128,4,1536]{2,1,0:T(4,128)(2,1)S(1)}, u32[]{:S(2)}, u32[]{:S(2)}) async-start(bf16[128,4,1536]{2,1,0:T(4,128)(2,1)} %shard_map.76), calls=%async_computation | async-start | bytes 3145728 | tf_op jit(solution)/shard_map/all_to_all | solution.py:96
  21.7 3.5 %collective-permute-start = (bf16[1,3,384]{2,1,0:T(4,128)(2,1)S(1)}, bf16[1,3,384]{2,1,0:T(4,128)(2,1)S(1)}, u32[]{:S(2)}, u32[]{:S(2)}) collective-permute-start(bf16[1,3,384]{2,1,0:T(4,128)(2,1)S(1)} %slice.47), channel_id=1, source_target_pairs={{0,1},{1,2},{2,3},{3,4},{4,5},{5,6},{6,7},{7,8},{8,9},{9,10},{10,1... | collective-permute-start | bytes 6920 | tf_op jit(solution)/shard_map/ppermute | solution.py:67
  25.3 4.0 %reshape.119 = bf16[4,128,4,512]{3,2,1,0:T(4,128)(2,1)} reshape(bf16[4,512,512]{2,1,0:T(8,128)(2,1)} %param.7) | data formatting | bytes 4194304 | tf_op jit(solution)/shard_map/reshape | solution.py:90
  29.6 3.1 %multiply_convert_fusion = (bf16[1,2048,384]{2,1,0:T(8,128)(2,1)S(1)}, f32[1,2048,384]{2,1,0:T(8,128)}) fusion(f32[1,2051,384]{2,1,0:T(8,128)S(1)} %maximum_convert_fusion, f32[384]{0:T(512)S(1)} %get-tuple-element.11, f32[384]{0:T(512)S(1)} %get-tuple-element.12, f32[384]{0:T(512)S(1)} %get-tuple-element.10, f32[384]{0:T(512)S(1)} %get-tuple-element.9), kind=kLoop, calls=%fused_computation.18 | loop fusion | flops 9437184 | bytes 17307648 | tf_op jit(solution)/shard_map/convert_element_type | solution.py:88
  32.7 2.5 %fusion.16 = bf16[128,1,4,4,384]{0,4,2,3,1:T(8,128)(2,1)} fusion(bf16[4,512,384,1]{2,1,3,0:T(8,128)(2,1)S(1)} %bitcast.52, bf16[4,128,4,512]{3,2,1,0:T(4,128)(2,1)S(1)} %copy-done), kind=kOutput, calls=%fused_computation.34 | convolution fusion | flops 806092800 | bytes 5242880 | tf_op jit(solution)/shard_map/ipqj,sijd->psqid/dot_general | solution.py:91
  35.2 3.9 %copy.35 = bf16[128,1,4,4,384]{4,2,3,1,0:T(4,128)(2,1)} copy(bf16[128,1,4,4,384]{0,4,2,3,1:T(8,128)(2,1)} %fusion.16) | data formatting | bytes 3145728 | tf_op jit(solution)/shard_map/convert_element_type | solution.py:93
  39.1 23.5 %all-to-all-done = bf16[128,4,1536]{2,1,0:T(4,128)(2,1)S(1)} async-done(((bf16[128,4,1536]{2,1,0:T(4,128)(2,1)}), bf16[128,4,1536]{2,1,0:T(4,128)(2,1)S(1)}, u32[]{:S(2)}, u32[]{:S(2)}) %all-to-all-start) | async-done | bytes 1572896 | tf_op jit(solution)/shard_map/all_to_all | solution.py:96
  62.6 14.8 %all-to-all-start.1 = ((bf16[128,1,4,4,384]{4,2,3,1,0:T(4,128)(2,1)}), bf16[128,1,4,4,384]{4,2,3,1,0:T(4,128)(2,1)}, u32[]{:S(2)}, u32[]{:S(2)}) async-start(bf16[128,1,4,4,384]{4,2,3,1,0:T(4,128)(2,1)} %copy.35), calls=%async_computation.1 | async-start | bytes 3145728 | tf_op jit(solution)/shard_map/all_to_all | solution.py:99
  78.9 1.9 %constant_dynamic-slice_fusion = (bf16[64,1,4,4,384]{4,3,2,0,1:T(4,128)(2,1)S(1)}, bf16[64,1,4,4,384]{4,3,2,0,1:T(4,128)(2,1)S(1)}) fusion(bf16[128,1,4,4,384]{4,3,2,0,1:T(4,128)(2,1)} %reshape.121, s32[]{:T(128)S(6)} %select_n.7, s32[]{:T(128)S(6)} %select_n.6), kind=kLoop, calls=%fused_computation.43 | loop fusion | bytes 3145736 | tf_op jit(solution)/shard_map/dynamic_slice | solution.py:114
  81.6 2.7 %copy.30 = f32[4,64,4,512]{3,0,2,1:T(4,128)} copy(f32[4,64,4,512]{3,1,2,0:T(8,128)S(1)} %convert_reduce-precision_fusion.1) | data formatting | bytes 4194304 | tf_op jit(solution)/shard_map/reduce_precision | solution.py:125
  86.8 2.8 %collective-permute-start.2 = (bf16[4,256,512]{2,0,1:T(4,128)(2,1)}, bf16[4,256,512]{2,0,1:T(4,128)(2,1)}, u32[]{:S(2)}, u32[]{:S(2)}) collective-permute-start(bf16[4,256,512]{2,0,1:T(4,128)(2,1)} %bitcast.15), channel_id=1, source_target_pairs={{0,128},{128,0},{1,129},{129,1},{2,130},{130,2},{3,131},{131,3},{4... | collective-permute-start | bytes 3145736 | tf_op jit(solution)/shard_map/ppermute | solution.py:121
  91.0 4.3 %convolution_bitcast_fusion = f32[1,4,512,384]{2,3,1,0:T(8,128)} fusion(bf16[128,4,4,384]{0,3,2,1:T(8,128)(2,1)S(1)} %bitcast.55, bf16[4,128,4,512]{3,2,1,0:T(4,128)(2,1)} %reshape.119), kind=kOutput, calls=%fused_computation.25 | convolution fusion | flops 805306368 | bytes 6815744 | tf_op jit(solution)/shard_map/ipqj,psiqd->sijd/dot_general | solution.py:122
  95.3 2.4 %copy.28 = f32[1,4,512,384]{3,2,1,0:T(8,128)S(1)} copy(f32[1,4,512,384]{2,3,1,0:T(8,128)} %convolution_bitcast_fusion) | data formatting | bytes 6291456 | tf_op jit(solution)/shard_map/ipqj,psiqd->sijd/transpose | solution.py:122
  97.7 4.5 %fusion.8 = bf16[1,2048,384]{2,1,0:T(8,128)(2,1)} fusion(f32[1,4,512,384]{3,2,1,0:T(8,128)S(1)} %copy.28, f32[1,2048,384]{2,1,0:T(8,128)} %get-tuple-element.14), kind=kLoop, calls=%fused_computation.17 | loop fusion | flops 7077888 | bytes 7864320 | tf_op jit(solution)/shard_map/convert_element_type | solution.py:129
  102.9 3.3 %collective-permute-start.1 = (bf16[1,3,384]{2,1,0:T(4,128)(2,1)S(1)}, bf16[1,3,384]{2,1,0:T(4,128)(2,1)S(1)}, u32[]{:S(2)}, u32[]{:S(2)}) collective-permute-start(bf16[1,3,384]{2,1,0:T(4,128)(2,1)S(1)} %slice.64), channel_id=1, source_target_pairs={{1,0},{2,1},{3,2},{4,3},{5,4},{6,5},{7,6},{8,7},{9,8},{10,9},{11,1... | collective-permute-start | bytes 6920 | tf_op jit(solution)/shard_map/ppermute | solution.py:67
  106.2 7.8 %all-to-all-done.1 = bf16[128,1,4,4,384]{4,2,3,1,0:T(4,128)(2,1)} async-done(((bf16[128,1,4,4,384]{4,2,3,1,0:T(4,128)(2,1)}), bf16[128,1,4,4,384]{4,2,3,1,0:T(4,128)(2,1)}, u32[]{:S(2)}, u32[]{:S(2)}) %all-to-all-start.1) | async-done | bytes 1572896 | tf_op jit(solution)/shard_map/all_to_all | solution.py:99
  114.0 2.8 %copy.44.col_ref = bf16[4,512,384]{2,1,0:T(8,128)(2,1)} copy(bf16[4,512,384]{2,0,1:T(4,128)(2,1)} %bitcast.22) | data formatting | bytes 3145728 | tf_op jit(solution)/shard_map/reshape;squeeze | solution.py:110
  116.9 4.3 %shard_map.78 = bf16[4,256,512]{2,1,0:T(8,128)(2,1)} custom-call(s32[1]{0:T(128)} %bitcast.23.half_ref, bf16[4,512,384]{2,1,0:T(8,128)(2,1)} %bitcast.50, bf16[4,512,384]{2,1,0:T(8,128)(2,1)} %copy.44.col_ref), custom_call_target="tpu_custom_call" | custom-call | flops 402653184 | bytes 3407872 | tf_op jit(solution)/shard_map/pallas_call | solution.py:44
  121.1 8.0 %collective-permute-start.3 = (bf16[4,256,512]{2,1,0:T(8,128)(2,1)}, bf16[4,256,512]{2,1,0:T(8,128)(2,1)}, u32[]{:S(2)}, u32[]{:S(2)}) collective-permute-start(bf16[4,256,512]{2,1,0:T(8,128)(2,1)} %shard_map.78), channel_id=1, source_target_pairs={{0,128},{128,0},{1,129},{129,1},{2,130},{130,2},{3,131},{131,3},{4... | collective-permute-start | bytes 3145736 | tf_op jit(solution)/shard_map/ppermute | solution.py:120
  130.8 4.3 %shard_map.77 = bf16[4,256,512]{2,1,0:T(8,128)(2,1)} custom-call(s32[1]{0:T(128)} %bitcast.16.half_ref, bf16[4,512,384]{2,1,0:T(8,128)(2,1)} %bitcast.51, bf16[4,512,384]{2,1,0:T(8,128)(2,1)} %copy.44.col_ref), custom_call_target="tpu_custom_call" | custom-call | flops 402653184 | bytes 3407872 | tf_op jit(solution)/shard_map/pallas_call | solution.py:44
  136.6 2.5 %fusion.1 = bf16[1,2048,384]{2,1,0:T(8,128)(2,1)} fusion(f32[1,2051,384]{2,1,0:T(8,128)S(1)} %maximum_convert_fusion.1, f32[384]{0:T(512)S(1)} %get-tuple-element.11, f32[384]{0:T(512)S(1)} %get-tuple-element.12, f32[384]{0:T(512)S(1)} %get-tuple-element.10, f32[384]{0:T(512)S(1)} %get-tuple-element.9), kind=kLoop, calls=%fused_computation.2 | loop fusion | flops 6291456 | bytes 14161920 | tf_op jit(solution)/shard_map/convert_element_type | solution.py:134
  142.2 16.4 %collective-permute-done.3 = bf16[4,256,512]{2,1,0:T(8,128)(2,1)} collective-permute-done((bf16[4,256,512]{2,1,0:T(8,128)(2,1)}, bf16[4,256,512]{2,1,0:T(8,128)(2,1)}, u32[]{:S(2)}, u32[]{:S(2)}) %collective-permute-start.3) | collective-permute-done | bytes 1048608 | tf_op jit(solution)/shard_map/ppermute | solution.py:120
  158.6 2.5 %add_convert_fusion = bf16[4,256,512]{2,1,0:T(8,128)(2,1)} fusion(f32[4,256,512]{2,1,0:T(8,128)S(1)} %convert_reduce-precision_fusion, bf16[4,256,512]{2,1,0:T(8,128)(2,1)} %collective-permute-done.3), kind=kLoop, calls=%fused_computation.22 | loop fusion | flops 1572864 | bytes 4194304 | tf_op jit(solution)/shard_map/convert_element_type | solution.py:127
  (24 shorter events, 13.5 us)
Async XLA Ops:
  0.6 21.0 %copy-start.2 = (bf16[1,2048,384]{2,1,0:T(8,128)(2,1)S(1)}, bf16[1,2048,384]{2,1,0:T(8,128)(2,1)}, u32[]{:S(2)}) copy-start(bf16[1,2048,384]{2,1,0:T(8,128)(2,1)} %param.5) | copy-start | bytes 4718596
  0.6 24.6 %copy-start.3 = (f32[4,384]{1,0:T(4,128)S(1)}, f32[4,384]{1,0:T(4,128)}, u32[]{:S(2)}) copy-start(f32[4,384]{1,0:T(4,128)} %param.6) | copy-start | bytes 18436
  5.3 57.4 %all-to-all-start = ((bf16[128,4,1536]{2,1,0:T(4,128)(2,1)}), bf16[128,4,1536]{2,1,0:T(4,128)(2,1)S(1)}, u32[]{:S(2)}, u32[]{:S(2)}) async-start(bf16[128,4,1536]{2,1,0:T(4,128)(2,1)} %shard_map.76), calls=%async_computation | async-start | bytes 3145728 | tf_op jit(solution)/shard_map/all_to_all | solution.py:96
  21.7 7.6 %collective-permute-start = (bf16[1,3,384]{2,1,0:T(4,128)(2,1)S(1)}, bf16[1,3,384]{2,1,0:T(4,128)(2,1)S(1)}, u32[]{:S(2)}, u32[]{:S(2)}) collective-permute-start(bf16[1,3,384]{2,1,0:T(4,128)(2,1)S(1)} %slice.47), channel_id=1, source_target_pairs={{0,1},{1,2},{2,3},{3,4},{4,5},{5,6},{6,7},{7,8},{8,9},{9,10},{10,1... | collective-permute-start | bytes 6920 | tf_op jit(solution)/shard_map/ppermute | solution.py:67
  29.6 3.1 %copy-start = (bf16[4,128,4,512]{3,2,1,0:T(4,128)(2,1)S(1)}, bf16[4,128,4,512]{3,2,1,0:T(4,128)(2,1)}, u32[]{:S(2)}) copy-start(bf16[4,128,4,512]{3,2,1,0:T(4,128)(2,1)} %reshape.119) | copy-start | bytes 6291460
  62.6 51.4 %all-to-all-start.1 = ((bf16[128,1,4,4,384]{4,2,3,1,0:T(4,128)(2,1)}), bf16[128,1,4,4,384]{4,2,3,1,0:T(4,128)(2,1)}, u32[]{:S(2)}, u32[]{:S(2)}) async-start(bf16[128,1,4,4,384]{4,2,3,1,0:T(4,128)(2,1)} %copy.35), calls=%async_computation.1 | async-start | bytes 3145728 | tf_op jit(solution)/shard_map/all_to_all | solution.py:99
  86.8 52.3 %collective-permute-start.2 = (bf16[4,256,512]{2,0,1:T(4,128)(2,1)}, bf16[4,256,512]{2,0,1:T(4,128)(2,1)}, u32[]{:S(2)}, u32[]{:S(2)}) collective-permute-start(bf16[4,256,512]{2,0,1:T(4,128)(2,1)} %bitcast.15), channel_id=1, source_target_pairs={{0,128},{128,0},{1,129},{129,1},{2,130},{130,2},{3,131},{131,3},{4... | collective-permute-start | bytes 3145736 | tf_op jit(solution)/shard_map/ppermute | solution.py:121
  102.9 26.2 %collective-permute-start.1 = (bf16[1,3,384]{2,1,0:T(4,128)(2,1)S(1)}, bf16[1,3,384]{2,1,0:T(4,128)(2,1)S(1)}, u32[]{:S(2)}, u32[]{:S(2)}) collective-permute-start(bf16[1,3,384]{2,1,0:T(4,128)(2,1)S(1)} %slice.64), channel_id=1, source_target_pairs={{1,0},{2,1},{3,2},{4,3},{5,4},{6,5},{7,6},{8,7},{9,8},{10,9},{11,1... | collective-permute-start | bytes 6920 | tf_op jit(solution)/shard_map/ppermute | solution.py:67
  121.1 37.5 %collective-permute-start.3 = (bf16[4,256,512]{2,1,0:T(8,128)(2,1)}, bf16[4,256,512]{2,1,0:T(8,128)(2,1)}, u32[]{:S(2)}, u32[]{:S(2)}) collective-permute-start(bf16[4,256,512]{2,1,0:T(8,128)(2,1)} %shard_map.78), channel_id=1, source_target_pairs={{0,128},{128,0},{1,129},{129,1},{2,130},{130,2},{3,131},{131,3},{4... | collective-permute-start | bytes 3145736 | tf_op jit(solution)/shard_map/ppermute | solution.py:120
  136.6 2.6 %copy-start.1 = (f32[4,64,4,512]{3,0,2,1:T(4,128)S(1)}, f32[4,64,4,512]{3,0,2,1:T(4,128)}, u32[]{:S(2)}) copy-start(f32[4,64,4,512]{3,0,2,1:T(4,128)} %copy.30) | copy-start | bytes 6291460

commit v13 on v11

--- a/solution.py
+++ b/solution.py
@@ -94,7 +94,12 @@
     kept = lambda part: lax.reduce_precision(part.astype(jnp.float32), exponent_bits=8, mantissa_bits=7)
     own_second = lax.optimization_barrier(kept(second_part(me)))
     part_second = (own_second + sent_second.astype(jnp.float32)).astype(jnp.bfloat16)
-    part_first = (kept(first_part(me)) + sent_first.astype(jnp.float32)).astype(jnp.bfloat16)
+    rows_late, sent_first = lax.optimization_barrier((grad_rows, sent_first))
+    gr_own = lax.dynamic_slice_in_dim(rows_late, me * peers_half, peers_half, 0)
+    own_first = jnp.einsum(
+        "psiqd,sijd->ipqj", gr_own, hidden_blocks, preferred_element_type=jnp.float32
+    ).reshape(blocks, peers_half * col_blocks, block_order)
+    part_first = (kept(own_first) + sent_first.astype(jnp.float32)).astype(jnp.bfloat16)
     grad_conv = (grad_hidden * gate_val * (1.0 + conv_out * (1.0 - gate_val))).astype(jnp.bfloat16)
     following = passed_along(grad_conv[:, : tap_count - 1, :], "seq", -1)
     extended = jnp.concatenate([grad_conv, following], axis=1).astype(jnp.float32)

time: 161 us -> 161 us (level)
    ppermute x1, waiting for transfers between devices: 19.3 us -> 16.9 us  [body(): sent_second = lax.ppermute(second_part(other), 'batch', swap)]
    all_to_all x1, waiting for transfers between devices: 8.36 us -> 10.5 us  [body(): lax.all_to_all(mixed_chunks, 'seq', split_axis=0, concat_axis=3, tiled=True)]
  transfers between devices with their start and end apart: 6 -> 6, of which waited for: 4 -> 4; matrix products, arithmetic and copies ran while one was open for 28% -> 29% of each run, Pallas kernels for 0% -> 0%
where the time goes in v13:
time: 161 us; the launch traced here: 160 us
  waiting for transfers between devices  57.5 us (36%)
  starting transfers between devices  48.8 us (30%)
  local copies, waits for them, and re-layouts  21.5 us (13%)
  matrix products  13.5 us (8%)
  other arithmetic  13.4 us (8%)
  Pallas kernels  4.49 us (3%)
    all_to_all x1, waiting for transfers between devices, body(): lax.all_to_all(grad_chunks, 'seq', split_axis=0, concat_axis=0, tiled=True)  23.5 us
    ppermute x1, waiting for transfers between devices, body(): sent_second = lax.ppermute(second_part(other), 'batch', swap)  16.9 us
    all_to_all x1, starting transfers between devices, body(): lax.all_to_all(grad_chunks, 'seq', split_axis=0, concat_axis=0, tiled=True)  16.5 us
    all_to_all x1, starting transfers between devices, body(): lax.all_to_all(mixed_chunks, 'seq', split_axis=0, concat_axis=3, tiled=True)  14.8 us
    all_to_all x1, waiting for transfers between devices, body(): lax.all_to_all(mixed_chunks, 'seq', split_axis=0, concat_axis=3, tiled=True)  10.5 us
    ppermute x1, starting transfers between devices, body(): sent_second = lax.ppermute(second_part(other), 'batch', swap)  8.1 us
    ppermute x2, starting transfers between devices, passed_along(): lax.ppermute(value, axis, [(source, source + steps) for source in range(i...  6.69 us
    ppermute x1, waiting for transfers between devices, body(): sent_first = lax.ppermute(first_part(other), 'batch', swap)  6.57 us
  transfers between devices with their start and end apart: 6, of which 4 were waited for; matrix products, arithmetic and copies ran while one was open for 29% of the time, Pallas kernels for 0%

profile of v13, /device:TPU:1, one launch (start us, length us, event | category | flops | bytes accessed | tf_op | source)
XLA Modules:
  0.0 160.0 jit_solution(8153730118758695810)
XLA Ops:
  0.6 4.5 %shard_map.76 = bf16[128,4,1536]{2,1,0:T(4,128)(2,1)} custom-call(bf16[4,512,512]{2,1,0:T(8,128)(2,1)} %s_ref.1, bf16[4,512,384]{2,1,0:T(8,128)(2,1)} %bitcast.57), custom_call_target="tpu_custom_call" | custom-call | flops 805306368 | bytes 5242880 | tf_op jit(solution)/shard_map/pallas_call | solution.py:23
  5.1 16.5 %all-to-all-start = ((bf16[128,4,1536]{2,1,0:T(4,128)(2,1)}), bf16[128,4,1536]{2,1,0:T(4,128)(2,1)S(1)}, u32[]{:S(2)}, u32[]{:S(2)}) async-start(bf16[128,4,1536]{2,1,0:T(4,128)(2,1)} %shard_map.76), calls=%async_computation | async-start | bytes 3145728 | tf_op jit(solution)/shard_map/all_to_all | solution.py:66
  21.7 3.5 %collective-permute-start = (bf16[1,3,384]{2,1,0:T(4,128)(2,1)S(1)}, bf16[1,3,384]{2,1,0:T(4,128)(2,1)S(1)}, u32[]{:S(2)}, u32[]{:S(2)}) collective-permute-start(bf16[1,3,384]{2,1,0:T(4,128)(2,1)S(1)} %slice.47), channel_id=1, source_target_pairs={{0,1},{1,2},{2,3},{3,4},{4,5},{5,6},{6,7},{7,8},{8,9},{9,10},{10,1... | collective-permute-start | bytes 6920 | tf_op jit(solution)/shard_map/ppermute | solution.py:37
  25.3 4.0 %reshape.126 = bf16[4,128,4,512]{3,2,1,0:T(4,128)(2,1)} reshape(bf16[4,512,512]{2,1,0:T(8,128)(2,1)} %param.7) | data formatting | bytes 4194304 | tf_op jit(solution)/shard_map/reshape | solution.py:60
  29.6 3.1 %multiply_convert_fusion = (bf16[1,2048,384]{2,1,0:T(8,128)(2,1)S(1)}, f32[1,2048,384]{2,1,0:T(8,128)}) fusion(f32[1,2051,384]{2,1,0:T(8,128)S(1)} %maximum_convert_fusion, f32[384]{0:T(512)S(1)} %get-tuple-element.15, f32[384]{0:T(512)S(1)} %get-tuple-element.16, f32[384]{0:T(512)S(1)} %get-tuple-element.14, f32[384]{0:T(512)S(1)} %get-tuple-element.13), kind=kLoop, calls=%fused_computation.18 | loop fusion | flops 9437184 | bytes 17307648 | tf_op jit(solution)/shard_map/convert_element_type | solution.py:58
  32.7 2.5 %fusion.16 = bf16[128,1,4,4,384]{0,4,2,3,1:T(8,128)(2,1)} fusion(bf16[4,512,384,1]{2,1,3,0:T(8,128)(2,1)S(1)} %bitcast.53, bf16[4,128,4,512]{3,2,1,0:T(4,128)(2,1)S(1)} %copy-done), kind=kOutput, calls=%fused_computation.35 | convolution fusion | flops 806092800 | bytes 5242880 | tf_op jit(solution)/shard_map/ipqj,sijd->psqid/dot_general | solution.py:61
  35.2 3.9 %copy.36 = bf16[128,1,4,4,384]{4,2,3,1,0:T(4,128)(2,1)} copy(bf16[128,1,4,4,384]{0,4,2,3,1:T(8,128)(2,1)} %fusion.16) | data formatting | bytes 3145728 | tf_op jit(solution)/shard_map/convert_element_type | solution.py:63
  39.1 23.5 %all-to-all-done = bf16[128,4,1536]{2,1,0:T(4,128)(2,1)S(1)} async-done(((bf16[128,4,1536]{2,1,0:T(4,128)(2,1)}), bf16[128,4,1536]{2,1,0:T(4,128)(2,1)S(1)}, u32[]{:S(2)}, u32[]{:S(2)}) %all-to-all-start) | async-done | bytes 1572896 | tf_op jit(solution)/shard_map/all_to_all | solution.py:66
  62.7 14.8 %all-to-all-start.1 = ((bf16[128,1,4,4,384]{4,2,3,1,0:T(4,128)(2,1)}), bf16[128,1,4,4,384]{4,2,3,1,0:T(4,128)(2,1)}, u32[]{:S(2)}, u32[]{:S(2)}) async-start(bf16[128,1,4,4,384]{4,2,3,1,0:T(4,128)(2,1)} %copy.36), calls=%async_computation.1 | async-start | bytes 3145728 | tf_op jit(solution)/shard_map/all_to_all | solution.py:69
  81.1 1.8 %copy.31 = bf16[4,64,4,512]{3,0,2,1:T(4,128)(2,1)} copy(bf16[4,64,4,512]{3,1,2,0:T(8,128)(2,1)S(1)} %convolution_convert_fusion.2) | data formatting | bytes 2097152 | tf_op jit(solution)/shard_map/convert_element_type | solution.py:86
  82.9 2.7 %collective-permute-start.2 = (bf16[4,256,512]{2,0,1:T(4,128)(2,1)}, bf16[4,256,512]{2,0,1:T(4,128)(2,1)}, u32[]{:S(2)}, u32[]{:S(2)}) collective-permute-start(bf16[4,256,512]{2,0,1:T(4,128)(2,1)} %bitcast.11), channel_id=1, source_target_pairs={{0,128},{128,0},{1,129},{129,1},{2,130},{130,2},{3,131},{131,3},{4... | collective-permute-start | bytes 3145736 | tf_op jit(solution)/shard_map/ppermute | solution.py:90
  85.6 2.5 %copy.43 = bf16[128,4,1536]{0,2,1:T(8,128)(2,1)} copy(bf16[128,4,1536]{2,1,0:T(4,128)(2,1)S(1)} %all-to-all-done) | data formatting | bytes 3145728 | tf_op jit(solution)/shard_map/reshape.1
  88.1 4.8 %convolution_bitcast_fusion = f32[1,4,512,384]{2,3,1,0:T(8,128)} fusion(bf16[128,4,4,384]{0,3,2,1:T(8,128)(2,1)} %bitcast.56, bf16[4,128,4,512]{3,2,1,0:T(4,128)(2,1)} %reshape.126), kind=kOutput, calls=%fused_computation.24 | convolution fusion | flops 805306368 | bytes 6815744 | tf_op jit(solution)/shard_map/ipqj,psiqd->sijd/dot_general | solution.py:91
  92.9 3.6 %copy.29 = f32[1,4,512,384]{3,2,1,0:T(8,128)} copy(f32[1,4,512,384]{2,3,1,0:T(8,128)} %convolution_bitcast_fusion) | data formatting | bytes 6291456 | tf_op jit(solution)/shard_map/ipqj,psiqd->sijd/transpose | solution.py:91
  96.5 4.0 %fusion.8 = bf16[1,2048,384]{2,1,0:T(8,128)(2,1)S(1)} fusion(f32[1,4,512,384]{3,2,1,0:T(8,128)} %copy.29, f32[1,2048,384]{2,1,0:T(8,128)} %get-tuple-element.18), kind=kLoop, calls=%fused_computation.17 | loop fusion | flops 7077888 | bytes 7864320 | tf_op jit(solution)/shard_map/convert_element_type | solution.py:103
  100.5 3.1 %collective-permute-start.1 = (bf16[1,3,384]{2,1,0:T(4,128)(2,1)S(1)}, bf16[1,3,384]{2,1,0:T(4,128)(2,1)S(1)}, u32[]{:S(2)}, u32[]{:S(2)}) collective-permute-start(bf16[1,3,384]{2,1,0:T(4,128)(2,1)S(1)} %slice.64), channel_id=1, source_target_pairs={{1,0},{2,1},{3,2},{4,3},{5,4},{6,5},{7,6},{8,7},{9,8},{10,9},{11,1... | collective-permute-start | bytes 6920 | tf_op jit(solution)/shard_map/ppermute | solution.py:37
  103.6 10.5 %all-to-all-done.1 = bf16[128,1,4,4,384]{4,2,3,1,0:T(4,128)(2,1)} async-done(((bf16[128,1,4,4,384]{4,2,3,1,0:T(4,128)(2,1)}), bf16[128,1,4,4,384]{4,2,3,1,0:T(4,128)(2,1)}, u32[]{:S(2)}, u32[]{:S(2)}) %all-to-all-start.1) | async-done | bytes 1572896 | tf_op jit(solution)/shard_map/all_to_all | solution.py:69
  114.1 2.4 %convolution_convert_fusion = bf16[4,256,512]{2,1,0:T(8,128)(2,1)S(1)} fusion(bf16[4,512,384]{2,0,1:T(4,128)(2,1)} %bitcast.21, bf16[1,4,512,384]{3,2,1,0:T(8,128)(2,1)} %bitcast.58, s32[]{:T(128)S(6)} %select_n.15), kind=kOutput, calls=%fused_computation.32 | convolution fusion | flops 403177472 | bytes 3407876 | tf_op jit(solution)/shard_map/skmd,skid->kmi/dot_general | solution.py:78
  116.5 8.1 %collective-permute-start.3 = (bf16[4,256,512]{2,1,0:T(8,128)(2,1)S(1)}, bf16[4,256,512]{2,1,0:T(8,128)(2,1)S(1)}, u32[]{:S(2)}, u32[]{:S(2)}) collective-permute-start(bf16[4,256,512]{2,1,0:T(8,128)(2,1)S(1)} %convolution_convert_fusion), channel_id=1, source_target_pairs={{0,128},{128,0},{1,129},{129,1},{2,130},{130,2},{3,131},{131,3},{4... | collective-permute-start | bytes 3145736 | tf_op jit(solution)/shard_map/ppermute | solution.py:89
  124.8 2.5 %fusion.1 = bf16[1,2048,384]{2,1,0:T(8,128)(2,1)} fusion(f32[1,2051,384]{2,1,0:T(8,128)S(1)} %maximum_convert_fusion.1, f32[384]{0:T(512)S(1)} %get-tuple-element.15, f32[384]{0:T(512)S(1)} %get-tuple-element.16, f32[384]{0:T(512)S(1)} %get-tuple-element.14, f32[384]{0:T(512)S(1)} %get-tuple-element.13), kind=kLoop, calls=%fused_computation.2 | loop fusion | flops 6291456 | bytes 14161920 | tf_op jit(solution)/shard_map/convert_element_type | solution.py:108
  127.4 2.3 %convert_reduce-precision_fusion = f32[4,256,512]{2,1,0:T(8,128)S(1)} fusion(bf16[4,512,384]{2,0,1:T(4,128)(2,1)} %bitcast.21, bf16[1,4,512,384]{3,2,1,0:T(8,128)(2,1)S(1)} %bitcast.59, s32[]{:T(128)S(6)} %select_n.14), kind=kOutput, calls=%fused_computation.23 | convolution fusion | flops 404226048 | bytes 4456452 | tf_op jit(solution)/shard_map/skmd,skid->kmi/dot_general | solution.py:78
  129.7 6.6 %collective-permute-done.2 = bf16[4,256,512]{2,0,1:T(4,128)(2,1)} collective-permute-done((bf16[4,256,512]{2,0,1:T(4,128)(2,1)}, bf16[4,256,512]{2,0,1:T(4,128)(2,1)}, u32[]{:S(2)}, u32[]{:S(2)}) %collective-permute-start.2) | collective-permute-done | bytes 1048608 | tf_op jit(solution)/shard_map/ppermute | solution.py:90
  138.6 1.9 %fusion.9 = bf16[4,256,512]{2,0,1:T(4,128)(2,1)S(1)} fusion(f32[4,64,4,512]{3,0,2,1:T(4,128)S(1)} %copy.33, bf16[4,256,512]{2,0,1:T(4,128)(2,1)} %collective-permute-done.2), kind=kLoop, calls=%fused_computation.21 | loop fusion | flops 1572864 | bytes 4194304 | tf_op jit(solution)/shard_map/convert_element_type | solution.py:102
  141.7 16.9 %collective-permute-done.3 = bf16[4,256,512]{2,1,0:T(8,128)(2,1)S(1)} collective-permute-done((bf16[4,256,512]{2,1,0:T(8,128)(2,1)S(1)}, bf16[4,256,512]{2,1,0:T(8,128)(2,1)S(1)}, u32[]{:S(2)}, u32[]{:S(2)}) %collective-permute-start.3) | collective-permute-done | bytes 1048608 | tf_op jit(solution)/shard_map/ppermute | solution.py:89
  (25 shorter events, 9.2 us)
Async XLA Ops:
  5.1 16.5 %copy-start.3 = (bf16[1,2048,384]{2,1,0:T(8,128)(2,1)S(1)}, bf16[1,2048,384]{2,1,0:T(8,128)(2,1)}, u32[]{:S(2)}) copy-start(bf16[1,2048,384]{2,1,0:T(8,128)(2,1)} %param.5) | copy-start | bytes 4718596
  5.1 20.1 %copy-start.4 = (f32[4,384]{1,0:T(4,128)S(1)}, f32[4,384]{1,0:T(4,128)}, u32[]{:S(2)}) copy-start(f32[4,384]{1,0:T(4,128)} %param.6) | copy-start | bytes 18436
  5.1 57.6 %all-to-all-start = ((bf16[128,4,1536]{2,1,0:T(4,128)(2,1)}), bf16[128,4,1536]{2,1,0:T(4,128)(2,1)S(1)}, u32[]{:S(2)}, u32[]{:S(2)}) async-start(bf16[128,4,1536]{2,1,0:T(4,128)(2,1)} %shard_map.76), calls=%async_computation | async-start | bytes 3145728 | tf_op jit(solution)/shard_map/all_to_all | solution.py:66
  21.7 7.6 %collective-permute-start = (bf16[1,3,384]{2,1,0:T(4,128)(2,1)S(1)}, bf16[1,3,384]{2,1,0:T(4,128)(2,1)S(1)}, u32[]{:S(2)}, u32[]{:S(2)}) collective-permute-start(bf16[1,3,384]{2,1,0:T(4,128)(2,1)S(1)} %slice.47), channel_id=1, source_target_pairs={{0,1},{1,2},{2,3},{3,4},{4,5},{5,6},{6,7},{7,8},{8,9},{9,10},{10,1... | collective-permute-start | bytes 6920 | tf_op jit(solution)/shard_map/ppermute | solution.py:37
  29.6 3.1 %copy-start = (bf16[4,128,4,512]{3,2,1,0:T(4,128)(2,1)S(1)}, bf16[4,128,4,512]{3,2,1,0:T(4,128)(2,1)}, u32[]{:S(2)}) copy-start(bf16[4,128,4,512]{3,2,1,0:T(4,128)(2,1)} %reshape.126) | copy-start | bytes 6291460
  62.7 51.4 %all-to-all-start.1 = ((bf16[128,1,4,4,384]{4,2,3,1,0:T(4,128)(2,1)}), bf16[128,1,4,4,384]{4,2,3,1,0:T(4,128)(2,1)}, u32[]{:S(2)}, u32[]{:S(2)}) async-start(bf16[128,1,4,4,384]{4,2,3,1,0:T(4,128)(2,1)} %copy.36), calls=%async_computation.1 | async-start | bytes 3145728 | tf_op jit(solution)/shard_map/all_to_all | solution.py:69
  82.9 53.3 %collective-permute-start.2 = (bf16[4,256,512]{2,0,1:T(4,128)(2,1)}, bf16[4,256,512]{2,0,1:T(4,128)(2,1)}, u32[]{:S(2)}, u32[]{:S(2)}) collective-permute-start(bf16[4,256,512]{2,0,1:T(4,128)(2,1)} %bitcast.11), channel_id=1, source_target_pairs={{0,128},{128,0},{1,129},{129,1},{2,130},{130,2},{3,131},{131,3},{4... | collective-permute-start | bytes 3145736 | tf_op jit(solution)/shard_map/ppermute | solution.py:90
  100.5 24.1 %collective-permute-start.1 = (bf16[1,3,384]{2,1,0:T(4,128)(2,1)S(1)}, bf16[1,3,384]{2,1,0:T(4,128)(2,1)S(1)}, u32[]{:S(2)}, u32[]{:S(2)}) collective-permute-start(bf16[1,3,384]{2,1,0:T(4,128)(2,1)S(1)} %slice.64), channel_id=1, source_target_pairs={{1,0},{2,1},{3,2},{4,3},{5,4},{6,5},{7,6},{8,7},{9,8},{10,9},{11,1... | collective-permute-start | bytes 6920 | tf_op jit(solution)/shard_map/ppermute | solution.py:37
  116.5 42.1 %collective-permute-start.3 = (bf16[4,256,512]{2,1,0:T(8,128)(2,1)S(1)}, bf16[4,256,512]{2,1,0:T(8,128)(2,1)S(1)}, u32[]{:S(2)}, u32[]{:S(2)}) collective-permute-start(bf16[4,256,512]{2,1,0:T(8,128)(2,1)S(1)} %convolution_convert_fusion), channel_id=1, source_target_pairs={{0,128},{128,0},{1,129},{129,1},{2,130},{130,2},{3,131},{131,3},{4... | collective-permute-start | bytes 3145736 | tf_op jit(solution)/shard_map/ppermute | solution.py:89
  124.8 2.6 %copy-start.2 = (bf16[1,2048,384]{2,1,0:T(8,128)(2,1)S(1)}, bf16[1,2048,384]{2,1,0:T(8,128)(2,1)}, u32[]{:S(2)}) copy-start(bf16[1,2048,384]{2,1,0:T(8,128)(2,1)} %param.9) | copy-start | bytes 4718596
  127.4 8.9 %copy-start.1 = (bf16[128,1,4,4,384]{4,3,2,0,1:T(4,128)(2,1)S(1)}, bf16[128,1,4,4,384]{4,3,2,0,1:T(4,128)(2,1)}, u32[]{:S(2)}) copy-start(bf16[128,1,4,4,384]{4,3,2,0,1:T(4,128)(2,1)} %reshape.128) | copy-start | bytes 4718596

commit v14 on v11

--- a/solution.py
+++ b/solution.py
@@ -11,8 +11,8 @@
     width = g_ref.shape[-1]
     for k in range(s_ref.shape[0]):
         product = lax.dot_general(
-            s_ref[k], g_ref[k], (((0,), (0,)), ((), ())), preferred_element_type=jnp.float32
-        )
+            g_ref[k], s_ref[k], (((0,), (0,)), ((), ())), preferred_element_type=jnp.float32
+        ).T
         o_ref[:, :, k * width : (k + 1) * width] = product.reshape(peers, group, width).astype(o_ref.dtype)
 
 

time: 161 us -> 161 us (level)
  no operation moved by 1% of the time
where the time goes in v14:
time: 161 us
  waiting for transfers between devices  57.3 us (36%)
  starting transfers between devices  49.5 us (31%)
  local copies, waits for them, and re-layouts  22 us (14%)
  matrix products  12.9 us (8%)
  other arithmetic  12.8 us (8%)
  Pallas kernels  5.25 us (3%)
    all_to_all x1, waiting for transfers between devices, body(): lax.all_to_all(grad_chunks, 'seq', split_axis=0, concat_axis=0, tiled=True)  23.3 us
    ppermute x1, waiting for transfers between devices, body(): sent_second = lax.ppermute(second_part(other), 'batch', swap)  19.3 us
    all_to_all x1, starting transfers between devices, body(): lax.all_to_all(grad_chunks, 'seq', split_axis=0, concat_axis=0, tiled=True)  16.5 us
    all_to_all x1, starting transfers between devices, body(): lax.all_to_all(mixed_chunks, 'seq', split_axis=0, concat_axis=3, tiled=True)  14.8 us
    ppermute x1, starting transfers between devices, body(): sent_second = lax.ppermute(second_part(other), 'batch', swap)  8.32 us
    all_to_all x1, waiting for transfers between devices, body(): lax.all_to_all(mixed_chunks, 'seq', split_axis=0, concat_axis=3, tiled=True)  8.2 us
    ppermute x2, starting transfers between devices, passed_along(): lax.ppermute(value, axis, [(source, source + steps) for source in range(i...  6.98 us
    ppermute x1, waiting for transfers between devices, body(): sent_first = lax.ppermute(first_part(other), 'batch', swap)  6.44 us
  transfers between devices with their start and end apart: 6, of which 4 were waited for; matrix products, arithmetic and copies ran while one was open for 28% of the time, Pallas kernels for 0%

profile of v14, /device:TPU:1, one launch (start us, length us, event | category | flops | bytes accessed | tf_op | source)
XLA Modules:
  0.0 160.6 jit_solution(6290796980310519612)
XLA Ops:
  0.6 5.2 %shard_map.76 = bf16[128,4,1536]{2,1,0:T(4,128)(2,1)} custom-call(bf16[4,512,512]{2,1,0:T(8,128)(2,1)} %s_ref.1, bf16[4,512,384]{2,1,0:T(8,128)(2,1)} %bitcast.58), custom_call_target="tpu_custom_call" | custom-call | flops 805306368 | bytes 5242880 | tf_op jit(solution)/shard_map/pallas_call | solution.py:23
  5.9 16.5 %all-to-all-start = ((bf16[128,4,1536]{2,1,0:T(4,128)(2,1)}), bf16[128,4,1536]{2,1,0:T(4,128)(2,1)S(1)}, u32[]{:S(2)}, u32[]{:S(2)}) async-start(bf16[128,4,1536]{2,1,0:T(4,128)(2,1)} %shard_map.76), calls=%async_computation | async-start | bytes 3145728 | tf_op jit(solution)/shard_map/all_to_all | solution.py:66
  22.4 3.5 %collective-permute-start = (bf16[1,3,384]{2,1,0:T(4,128)(2,1)S(1)}, bf16[1,3,384]{2,1,0:T(4,128)(2,1)S(1)}, u32[]{:S(2)}, u32[]{:S(2)}) collective-permute-start(bf16[1,3,384]{2,1,0:T(4,128)(2,1)S(1)} %slice.47), channel_id=1, source_target_pairs={{0,1},{1,2},{2,3},{3,4},{4,5},{5,6},{6,7},{7,8},{8,9},{9,10},{10,1... | collective-permute-start | bytes 6920 | tf_op jit(solution)/shard_map/ppermute | solution.py:37
  26.0 4.0 %reshape.128 = bf16[4,128,4,512]{3,2,1,0:T(4,128)(2,1)} reshape(bf16[4,512,512]{2,1,0:T(8,128)(2,1)} %param.7) | data formatting | bytes 4194304 | tf_op jit(solution)/shard_map/reshape | solution.py:60
  30.4 3.1 %multiply_convert_fusion = (bf16[1,2048,384]{2,1,0:T(8,128)(2,1)S(1)}, f32[1,2048,384]{2,1,0:T(8,128)}) fusion(f32[1,2051,384]{2,1,0:T(8,128)S(1)} %maximum_convert_fusion, f32[384]{0:T(512)S(1)} %get-tuple-element.11, f32[384]{0:T(512)S(1)} %get-tuple-element.12, f32[384]{0:T(512)S(1)} %get-tuple-element.10, f32[384]{0:T(512)S(1)} %get-tuple-element.9), kind=kLoop, calls=%fused_computation.18 | loop fusion | flops 9437184 | bytes 17307648 | tf_op jit(solution)/shard_map/convert_element_type | solution.py:58
  33.5 2.6 %fusion.16 = bf16[128,1,4,4,384]{0,4,2,3,1:T(8,128)(2,1)} fusion(bf16[4,512,384,1]{2,1,3,0:T(8,128)(2,1)S(1)} %bitcast.54, bf16[4,128,4,512]{3,2,1,0:T(4,128)(2,1)S(1)} %copy-done), kind=kOutput, calls=%fused_computation.36 | convolution fusion | flops 806092800 | bytes 5242880 | tf_op jit(solution)/shard_map/ipqj,sijd->psqid/dot_general | solution.py:61
  36.1 3.9 %copy.36 = bf16[128,1,4,4,384]{4,2,3,1,0:T(4,128)(2,1)} copy(bf16[128,1,4,4,384]{0,4,2,3,1:T(8,128)(2,1)} %fusion.16) | data formatting | bytes 3145728 | tf_op jit(solution)/shard_map/convert_element_type | solution.py:63
  40.0 23.3 %all-to-all-done = bf16[128,4,1536]{2,1,0:T(4,128)(2,1)S(1)} async-done(((bf16[128,4,1536]{2,1,0:T(4,128)(2,1)}), bf16[128,4,1536]{2,1,0:T(4,128)(2,1)S(1)}, u32[]{:S(2)}, u32[]{:S(2)}) %all-to-all-start) | async-done | bytes 1572896 | tf_op jit(solution)/shard_map/all_to_all | solution.py:66
  63.3 14.8 %all-to-all-start.1 = ((bf16[128,1,4,4,384]{4,2,3,1,0:T(4,128)(2,1)}), bf16[128,1,4,4,384]{4,2,3,1,0:T(4,128)(2,1)}, u32[]{:S(2)}, u32[]{:S(2)}) async-start(bf16[128,1,4,4,384]{4,2,3,1,0:T(4,128)(2,1)} %copy.36), calls=%async_computation.1 | async-start | bytes 3145728 | tf_op jit(solution)/shard_map/all_to_all | solution.py:69
  79.6 1.9 %constant_dynamic-slice_fusion = (bf16[64,1,4,4,384]{4,3,2,0,1:T(4,128)(2,1)S(1)}, bf16[64,1,4,4,384]{4,3,2,0,1:T(4,128)(2,1)S(1)}) fusion(bf16[128,1,4,4,384]{4,3,2,0,1:T(4,128)(2,1)} %reshape.130, s32[]{:T(128)S(6)} %select_n.13, s32[]{:T(128)S(6)} %select_n.12), kind=kLoop, calls=%fused_computation.53 | loop fusion | bytes 3145736 | tf_op jit(solution)/shard_map/dynamic_slice | solution.py:83
  82.3 2.7 %copy.31 = f32[4,64,4,512]{3,0,2,1:T(4,128)} copy(f32[4,64,4,512]{3,1,2,0:T(8,128)S(1)} %convert_reduce-precision_fusion.1) | data formatting | bytes 4194304 | tf_op jit(solution)/shard_map/reduce_precision | solution.py:94
  87.5 2.9 %collective-permute-start.2 = (bf16[4,256,512]{2,0,1:T(4,128)(2,1)}, bf16[4,256,512]{2,0,1:T(4,128)(2,1)}, u32[]{:S(2)}, u32[]{:S(2)}) collective-permute-start(bf16[4,256,512]{2,0,1:T(4,128)(2,1)} %bitcast.15), channel_id=1, source_target_pairs={{0,128},{128,0},{1,129},{129,1},{2,130},{130,2},{3,131},{131,3},{4... | collective-permute-start | bytes 3145736 | tf_op jit(solution)/shard_map/ppermute | solution.py:90
  91.8 4.3 %convolution_bitcast_fusion = f32[1,4,512,384]{2,3,1,0:T(8,128)} fusion(bf16[128,4,4,384]{0,3,2,1:T(8,128)(2,1)S(1)} %bitcast.57, bf16[4,128,4,512]{3,2,1,0:T(4,128)(2,1)} %reshape.128), kind=kOutput, calls=%fused_computation.25 | convolution fusion | flops 805306368 | bytes 6815744 | tf_op jit(solution)/shard_map/ipqj,psiqd->sijd/dot_general | solution.py:91
  96.2 2.4 %copy.29 = f32[1,4,512,384]{3,2,1,0:T(8,128)S(1)} copy(f32[1,4,512,384]{2,3,1,0:T(8,128)} %convolution_bitcast_fusion) | data formatting | bytes 6291456 | tf_op jit(solution)/shard_map/ipqj,psiqd->sijd/transpose | solution.py:91
  98.6 3.4 %fusion.8 = bf16[1,2048,384]{2,1,0:T(8,128)(2,1)S(1)} fusion(f32[1,4,512,384]{3,2,1,0:T(8,128)S(1)} %copy.29, f32[1,2048,384]{2,1,0:T(8,128)} %get-tuple-element.14), kind=kLoop, calls=%fused_computation.17 | loop fusion | flops 7077888 | bytes 7864320 | tf_op jit(solution)/shard_map/convert_element_type | solution.py:98
  103.1 3.4 %collective-permute-start.1 = (bf16[1,3,384]{2,1,0:T(4,128)(2,1)S(1)}, bf16[1,3,384]{2,1,0:T(4,128)(2,1)S(1)}, u32[]{:S(2)}, u32[]{:S(2)}) collective-permute-start(bf16[1,3,384]{2,1,0:T(4,128)(2,1)S(1)} %slice.64), channel_id=1, source_target_pairs={{1,0},{2,1},{3,2},{4,3},{5,4},{6,5},{7,6},{8,7},{9,8},{10,9},{11,1... | collective-permute-start | bytes 6920 | tf_op jit(solution)/shard_map/ppermute | solution.py:37
  106.6 8.2 %all-to-all-done.1 = bf16[128,1,4,4,384]{4,2,3,1,0:T(4,128)(2,1)} async-done(((bf16[128,1,4,4,384]{4,2,3,1,0:T(4,128)(2,1)}), bf16[128,1,4,4,384]{4,2,3,1,0:T(4,128)(2,1)}, u32[]{:S(2)}, u32[]{:S(2)}) %all-to-all-start.1) | async-done | bytes 1572896 | tf_op jit(solution)/shard_map/all_to_all | solution.py:69
  114.8 2.4 %convolution_convert_fusion = bf16[4,256,512]{2,1,0:T(8,128)(2,1)S(1)} fusion(bf16[4,512,384]{2,0,1:T(4,128)(2,1)} %bitcast.23, bf16[1,4,512,384]{3,2,1,0:T(8,128)(2,1)} %bitcast.59, s32[]{:T(128)S(6)} %select_n.15), kind=kOutput, calls=%fused_computation.32 | convolution fusion | flops 403177472 | bytes 3407876 | tf_op jit(solution)/shard_map/skmd,skid->kmi/dot_general | solution.py:78
  117.2 8.3 %collective-permute-start.3 = (bf16[4,256,512]{2,1,0:T(8,128)(2,1)S(1)}, bf16[4,256,512]{2,1,0:T(8,128)(2,1)S(1)}, u32[]{:S(2)}, u32[]{:S(2)}) collective-permute-start(bf16[4,256,512]{2,1,0:T(8,128)(2,1)S(1)} %convolution_convert_fusion), channel_id=1, source_target_pairs={{0,128},{128,0},{1,129},{129,1},{2,130},{130,2},{3,131},{131,3},{4... | collective-permute-start | bytes 3145736 | tf_op jit(solution)/shard_map/ppermute | solution.py:89
  125.7 2.2 %convert_reduce-precision_fusion = f32[4,256,512]{2,1,0:T(8,128)S(1)} fusion(bf16[4,512,384]{2,0,1:T(4,128)(2,1)} %bitcast.23, bf16[1,4,512,384]{3,2,1,0:T(8,128)(2,1)S(1)} %bitcast.60, s32[]{:T(128)S(6)} %select_n.14), kind=kOutput, calls=%fused_computation.23 | convolution fusion | flops 404226048 | bytes 4456452 | tf_op jit(solution)/shard_map/skmd,skid->kmi/dot_general | solution.py:78
  127.9 2.5 %fusion.1 = bf16[1,2048,384]{2,1,0:T(8,128)(2,1)} fusion(f32[1,2051,384]{2,1,0:T(8,128)S(1)} %maximum_convert_fusion.1, f32[384]{0:T(512)S(1)} %get-tuple-element.11, f32[384]{0:T(512)S(1)} %get-tuple-element.12, f32[384]{0:T(512)S(1)} %get-tuple-element.10, f32[384]{0:T(512)S(1)} %get-tuple-element.9), kind=kLoop, calls=%fused_computation.2 | loop fusion | flops 6291456 | bytes 14161920 | tf_op jit(solution)/shard_map/convert_element_type | solution.py:103
  130.4 6.4 %collective-permute-done.2 = bf16[4,256,512]{2,0,1:T(4,128)(2,1)} collective-permute-done((bf16[4,256,512]{2,0,1:T(4,128)(2,1)}, bf16[4,256,512]{2,0,1:T(4,128)(2,1)}, u32[]{:S(2)}, u32[]{:S(2)}) %collective-permute-start.2) | collective-permute-done | bytes 1048608 | tf_op jit(solution)/shard_map/ppermute | solution.py:90
  136.9 1.9 %fusion.9 = bf16[4,256,512]{2,0,1:T(4,128)(2,1)S(1)} fusion(f32[4,64,4,512]{3,0,2,1:T(4,128)S(1)} %copy-done.1, bf16[4,256,512]{2,0,1:T(4,128)(2,1)} %collective-permute-done.2), kind=kLoop, calls=%fused_computation.21 | loop fusion | flops 1572864 | bytes 4194304 | tf_op jit(solution)/shard_map/convert_element_type | solution.py:97
  140.0 19.3 %collective-permute-done.3 = bf16[4,256,512]{2,1,0:T(8,128)(2,1)S(1)} collective-permute-done((bf16[4,256,512]{2,1,0:T(8,128)(2,1)S(1)}, bf16[4,256,512]{2,1,0:T(8,128)(2,1)S(1)}, u32[]{:S(2)}, u32[]{:S(2)}) %collective-permute-start.3) | collective-permute-done | bytes 1048608 | tf_op jit(solution)/shard_map/ppermute | solution.py:89
  (28 shorter events, 10.5 us)
Async XLA Ops:
  5.9 16.5 %copy-start.5 = (bf16[1,2048,384]{2,1,0:T(8,128)(2,1)S(1)}, bf16[1,2048,384]{2,1,0:T(8,128)(2,1)}, u32[]{:S(2)}) copy-start(bf16[1,2048,384]{2,1,0:T(8,128)(2,1)} %param.5) | copy-start | bytes 4718596
  5.9 20.1 %copy-start.6 = (f32[4,384]{1,0:T(4,128)S(1)}, f32[4,384]{1,0:T(4,128)}, u32[]{:S(2)}) copy-start(f32[4,384]{1,0:T(4,128)} %param.6) | copy-start | bytes 18436
  5.9 57.4 %all-to-all-start = ((bf16[128,4,1536]{2,1,0:T(4,128)(2,1)}), bf16[128,4,1536]{2,1,0:T(4,128)(2,1)S(1)}, u32[]{:S(2)}, u32[]{:S(2)}) async-start(bf16[128,4,1536]{2,1,0:T(4,128)(2,1)} %shard_map.76), calls=%async_computation | async-start | bytes 3145728 | tf_op jit(solution)/shard_map/all_to_all | solution.py:66
  22.4 7.6 %collective-permute-start = (bf16[1,3,384]{2,1,0:T(4,128)(2,1)S(1)}, bf16[1,3,384]{2,1,0:T(4,128)(2,1)S(1)}, u32[]{:S(2)}, u32[]{:S(2)}) collective-permute-start(bf16[1,3,384]{2,1,0:T(4,128)(2,1)S(1)} %slice.47), channel_id=1, source_target_pairs={{0,1},{1,2},{2,3},{3,4},{4,5},{5,6},{6,7},{7,8},{8,9},{9,10},{10,1... | collective-permute-start | bytes 6920 | tf_op jit(solution)/shard_map/ppermute | solution.py:37
  30.4 3.1 %copy-start = (bf16[4,128,4,512]{3,2,1,0:T(4,128)(2,1)S(1)}, bf16[4,128,4,512]{3,2,1,0:T(4,128)(2,1)}, u32[]{:S(2)}) copy-start(bf16[4,128,4,512]{3,2,1,0:T(4,128)(2,1)} %reshape.128) | copy-start | bytes 6291460
  63.3 51.5 %all-to-all-start.1 = ((bf16[128,1,4,4,384]{4,2,3,1,0:T(4,128)(2,1)}), bf16[128,1,4,4,384]{4,2,3,1,0:T(4,128)(2,1)}, u32[]{:S(2)}, u32[]{:S(2)}) async-start(bf16[128,1,4,4,384]{4,2,3,1,0:T(4,128)(2,1)} %copy.36), calls=%async_computation.1 | async-start | bytes 3145728 | tf_op jit(solution)/shard_map/all_to_all | solution.py:69
  87.5 49.3 %collective-permute-start.2 = (bf16[4,256,512]{2,0,1:T(4,128)(2,1)}, bf16[4,256,512]{2,0,1:T(4,128)(2,1)}, u32[]{:S(2)}, u32[]{:S(2)}) collective-permute-start(bf16[4,256,512]{2,0,1:T(4,128)(2,1)} %bitcast.15), channel_id=1, source_target_pairs={{0,128},{128,0},{1,129},{129,1},{2,130},{130,2},{3,131},{131,3},{4... | collective-permute-start | bytes 3145736 | tf_op jit(solution)/shard_map/ppermute | solution.py:90
  102.0 1.1 copy-start.2
  103.1 22.4 %copy-start.3 = (bf16[1,2048,384]{2,1,0:T(8,128)(2,1)S(1)}, bf16[1,2048,384]{2,1,0:T(8,128)(2,1)}, u32[]{:S(2)}) copy-start(bf16[1,2048,384]{2,1,0:T(8,128)(2,1)} %copy-done.2) | copy-start | bytes 4718596
  103.1 22.4 %collective-permute-start.1 = (bf16[1,3,384]{2,1,0:T(4,128)(2,1)S(1)}, bf16[1,3,384]{2,1,0:T(4,128)(2,1)S(1)}, u32[]{:S(2)}, u32[]{:S(2)}) collective-permute-start(bf16[1,3,384]{2,1,0:T(4,128)(2,1)S(1)} %slice.64), channel_id=1, source_target_pairs={{1,0},{2,1},{3,2},{4,3},{5,4},{6,5},{7,6},{8,7},{9,8},{10,9},{11,1... | collective-permute-start | bytes 6920 | tf_op jit(solution)/shard_map/ppermute | solution.py:37
  117.2 8.5 %copy-start.4 = (bf16[1,2048,384]{2,1,0:T(8,128)(2,1)S(1)}, bf16[1,2048,384]{2,1,0:T(8,128)(2,1)}, u32[]{:S(2)}) copy-start(bf16[1,2048,384]{2,1,0:T(8,128)(2,1)} %param.9) | copy-start | bytes 4718596
  117.2 42.1 %collective-permute-start.3 = (bf16[4,256,512]{2,1,0:T(8,128)(2,1)S(1)}, bf16[4,256,512]{2,1,0:T(8,128)(2,1)S(1)}, u32[]{:S(2)}, u32[]{:S(2)}) collective-permute-start(bf16[4,256,512]{2,1,0:T(8,128)(2,1)S(1)} %convolution_convert_fusion), channel_id=1, source_target_pairs={{0,128},{128,0},{1,129},{129,1},{2,130},{130,2},{3,131},{131,3},{4... | collective-permute-start | bytes 3145736 | tf_op jit(solution)/shard_map/ppermute | solution.py:89
  127.9 9.0 %copy-start.1 = (f32[4,64,4,512]{3,0,2,1:T(4,128)S(1)}, f32[4,64,4,512]{3,0,2,1:T(4,128)}, u32[]{:S(2)}) copy-start(f32[4,64,4,512]{3,0,2,1:T(4,128)} %copy.31) | copy-start | bytes 6291460

commit v15 on v11

--- a/solution.py
+++ b/solution.py
@@ -6,12 +6,24 @@
 from jax.experimental.pallas import tpu as pltpu
 
 
-def _grad_payload_kernel(s_ref, g_ref, o_ref):
+def _grad_payload_kernel(s_hbm, g_hbm, o_ref, s_vmem, g_vmem, sems):
     peers, group, _ = o_ref.shape
-    width = g_ref.shape[-1]
-    for k in range(s_ref.shape[0]):
+    col_blocks = s_hbm.shape[0]
+    width = g_hbm.shape[-1]
+    loads = []
+    for k in range(col_blocks):
+        pair = (
+            pltpu.make_async_copy(s_hbm.at[k], s_vmem.at[k], sems.at[0, k]),
+            pltpu.make_async_copy(g_hbm.at[k], g_vmem.at[k], sems.at[1, k]),
+        )
+        for copy in pair:
+            copy.start()
+        loads.append(pair)
+    for k in range(col_blocks):
+        for copy in loads[k]:
+            copy.wait()
         product = lax.dot_general(
-            s_ref[k], g_ref[k], (((0,), (0,)), ((), ())), preferred_element_type=jnp.float32
+            s_vmem[k], g_vmem[k], (((0,), (0,)), ((), ())), preferred_element_type=jnp.float32
         )
         o_ref[:, :, k * width : (k + 1) * width] = product.reshape(peers, group, width).astype(o_ref.dtype)
 
@@ -23,8 +35,13 @@
     return pl.pallas_call(
         _grad_payload_kernel,
         out_shape=jax.ShapeDtypeStruct((peers, order // peers, col_blocks * width), jnp.bfloat16),
-        in_specs=[pl.BlockSpec(memory_space=pltpu.VMEM)] * 2,
+        in_specs=[pl.BlockSpec(memory_space=pl.ANY)] * 2,
         out_specs=pl.BlockSpec(memory_space=pltpu.VMEM),
+        scratch_shapes=[
+            pltpu.VMEM((col_blocks, rows, order), jnp.bfloat16),
+            pltpu.VMEM((col_blocks, rows, width), jnp.bfloat16),
+            pltpu.SemaphoreType.DMA((2, col_blocks)),
+        ],
         cost_estimate=pl.CostEstimate(
             flops=flops, transcendentals=0, bytes_accessed=2 * (second_factor.size + 2 * upstream.size)
         ),

time: 161 us -> 160 us (level)
  no operation moved by 1% of the time
where the time goes in v15:
time: 160 us
  waiting for transfers between devices  57.4 us (36%)
  starting transfers between devices  49.4 us (31%)
  local copies, waits for them, and re-layouts  22 us (14%)
  matrix products  12.9 us (8%)
  other arithmetic  12.8 us (8%)
  Pallas kernels  4.28 us (3%)
    all_to_all x1, waiting for transfers between devices, body(): lax.all_to_all(grad_chunks, 'seq', split_axis=0, concat_axis=0, tiled=True)  23.4 us
    ppermute x1, waiting for transfers between devices, body(): sent_second = lax.ppermute(second_part(other), 'batch', swap)  19.3 us
    all_to_all x1, starting transfers between devices, body(): lax.all_to_all(grad_chunks, 'seq', split_axis=0, concat_axis=0, tiled=True)  16.5 us
    all_to_all x1, starting transfers between devices, body(): lax.all_to_all(mixed_chunks, 'seq', split_axis=0, concat_axis=3, tiled=True)  14.8 us
    ppermute x1, starting transfers between devices, body(): sent_second = lax.ppermute(second_part(other), 'batch', swap)  8.32 us
    all_to_all x1, waiting for transfers between devices, body(): lax.all_to_all(mixed_chunks, 'seq', split_axis=0, concat_axis=3, tiled=True)  8.31 us
    ppermute x2, starting transfers between devices, passed_along(): lax.ppermute(value, axis, [(source, source + steps) for source in range(i...  6.98 us
    ppermute x1, waiting for transfers between devices, body(): sent_first = lax.ppermute(first_part(other), 'batch', swap)  6.44 us
  transfers between devices with their start and end apart: 6, of which 4 were waited for; matrix products, arithmetic and copies ran while one was open for 28% of the time, Pallas kernels for 0%

profile of v15, /device:TPU:1, one launch (start us, length us, event | category | flops | bytes accessed | tf_op | source)
XLA Modules:
  0.0 159.7 jit_solution(2659661434094305765)
XLA Ops:
  0.6 4.3 %shard_map.76 = bf16[128,4,1536]{2,1,0:T(4,128)(2,1)} custom-call(bf16[4,512,512]{2,1,0:T(8,128)(2,1)} %s_hbm.1, bf16[4,512,384]{2,1,0:T(8,128)(2,1)} %bitcast.58), custom_call_target="tpu_custom_call" | custom-call | flops 805306368 | bytes 5242880 | tf_op jit(solution)/shard_map/pallas_call | solution.py:35
  4.9 16.5 %all-to-all-start = ((bf16[128,4,1536]{2,1,0:T(4,128)(2,1)}), bf16[128,4,1536]{2,1,0:T(4,128)(2,1)S(1)}, u32[]{:S(2)}, u32[]{:S(2)}) async-start(bf16[128,4,1536]{2,1,0:T(4,128)(2,1)} %shard_map.76), calls=%async_computation | async-start | bytes 3145728 | tf_op jit(solution)/shard_map/all_to_all | solution.py:83
  21.5 3.5 %collective-permute-start = (bf16[1,3,384]{2,1,0:T(4,128)(2,1)S(1)}, bf16[1,3,384]{2,1,0:T(4,128)(2,1)S(1)}, u32[]{:S(2)}, u32[]{:S(2)}) collective-permute-start(bf16[1,3,384]{2,1,0:T(4,128)(2,1)S(1)} %slice.47), channel_id=1, source_target_pairs={{0,1},{1,2},{2,3},{3,4},{4,5},{5,6},{6,7},{7,8},{8,9},{9,10},{10,1... | collective-permute-start | bytes 6920 | tf_op jit(solution)/shard_map/ppermute | solution.py:54
  25.1 4.0 %reshape.128 = bf16[4,128,4,512]{3,2,1,0:T(4,128)(2,1)} reshape(bf16[4,512,512]{2,1,0:T(8,128)(2,1)} %param.7) | data formatting | bytes 4194304 | tf_op jit(solution)/shard_map/reshape | solution.py:77
  29.5 3.1 %multiply_convert_fusion = (bf16[1,2048,384]{2,1,0:T(8,128)(2,1)S(1)}, f32[1,2048,384]{2,1,0:T(8,128)}) fusion(f32[1,2051,384]{2,1,0:T(8,128)S(1)} %maximum_convert_fusion, f32[384]{0:T(512)S(1)} %get-tuple-element.11, f32[384]{0:T(512)S(1)} %get-tuple-element.12, f32[384]{0:T(512)S(1)} %get-tuple-element.10, f32[384]{0:T(512)S(1)} %get-tuple-element.9), kind=kLoop, calls=%fused_computation.18 | loop fusion | flops 9437184 | bytes 17307648 | tf_op jit(solution)/shard_map/convert_element_type | solution.py:75
  32.6 2.6 %fusion.16 = bf16[128,1,4,4,384]{0,4,2,3,1:T(8,128)(2,1)} fusion(bf16[4,512,384,1]{2,1,3,0:T(8,128)(2,1)S(1)} %bitcast.54, bf16[4,128,4,512]{3,2,1,0:T(4,128)(2,1)S(1)} %copy-done), kind=kOutput, calls=%fused_computation.36 | convolution fusion | flops 806092800 | bytes 5242880 | tf_op jit(solution)/shard_map/ipqj,sijd->psqid/dot_general | solution.py:78
  35.1 3.9 %copy.36 = bf16[128,1,4,4,384]{4,2,3,1,0:T(4,128)(2,1)} copy(bf16[128,1,4,4,384]{0,4,2,3,1:T(8,128)(2,1)} %fusion.16) | data formatting | bytes 3145728 | tf_op jit(solution)/shard_map/convert_element_type | solution.py:80
  39.0 23.4 %all-to-all-done = bf16[128,4,1536]{2,1,0:T(4,128)(2,1)S(1)} async-done(((bf16[128,4,1536]{2,1,0:T(4,128)(2,1)}), bf16[128,4,1536]{2,1,0:T(4,128)(2,1)S(1)}, u32[]{:S(2)}, u32[]{:S(2)}) %all-to-all-start) | async-done | bytes 1572896 | tf_op jit(solution)/shard_map/all_to_all | solution.py:83
  62.4 14.8 %all-to-all-start.1 = ((bf16[128,1,4,4,384]{4,2,3,1,0:T(4,128)(2,1)}), bf16[128,1,4,4,384]{4,2,3,1,0:T(4,128)(2,1)}, u32[]{:S(2)}, u32[]{:S(2)}) async-start(bf16[128,1,4,4,384]{4,2,3,1,0:T(4,128)(2,1)} %copy.36), calls=%async_computation.1 | async-start | bytes 3145728 | tf_op jit(solution)/shard_map/all_to_all | solution.py:86
  78.8 1.9 %constant_dynamic-slice_fusion = (bf16[64,1,4,4,384]{4,3,2,0,1:T(4,128)(2,1)S(1)}, bf16[64,1,4,4,384]{4,3,2,0,1:T(4,128)(2,1)S(1)}) fusion(bf16[128,1,4,4,384]{4,3,2,0,1:T(4,128)(2,1)} %reshape.130, s32[]{:T(128)S(6)} %select_n.13, s32[]{:T(128)S(6)} %select_n.12), kind=kLoop, calls=%fused_computation.53 | loop fusion | bytes 3145736 | tf_op jit(solution)/shard_map/dynamic_slice | solution.py:100
  81.4 2.7 %copy.31 = f32[4,64,4,512]{3,0,2,1:T(4,128)} copy(f32[4,64,4,512]{3,1,2,0:T(8,128)S(1)} %convert_reduce-precision_fusion.1) | data formatting | bytes 4194304 | tf_op jit(solution)/shard_map/reduce_precision | solution.py:111
  86.7 2.8 %collective-permute-start.2 = (bf16[4,256,512]{2,0,1:T(4,128)(2,1)}, bf16[4,256,512]{2,0,1:T(4,128)(2,1)}, u32[]{:S(2)}, u32[]{:S(2)}) collective-permute-start(bf16[4,256,512]{2,0,1:T(4,128)(2,1)} %bitcast.15), channel_id=1, source_target_pairs={{0,128},{128,0},{1,129},{129,1},{2,130},{130,2},{3,131},{131,3},{4... | collective-permute-start | bytes 3145736 | tf_op jit(solution)/shard_map/ppermute | solution.py:107
  90.9 4.3 %convolution_bitcast_fusion = f32[1,4,512,384]{2,3,1,0:T(8,128)} fusion(bf16[128,4,4,384]{0,3,2,1:T(8,128)(2,1)S(1)} %bitcast.57, bf16[4,128,4,512]{3,2,1,0:T(4,128)(2,1)} %reshape.128), kind=kOutput, calls=%fused_computation.25 | convolution fusion | flops 805306368 | bytes 6815744 | tf_op jit(solution)/shard_map/ipqj,psiqd->sijd/dot_general | solution.py:108
  95.2 2.4 %copy.29 = f32[1,4,512,384]{3,2,1,0:T(8,128)S(1)} copy(f32[1,4,512,384]{2,3,1,0:T(8,128)} %convolution_bitcast_fusion) | data formatting | bytes 6291456 | tf_op jit(solution)/shard_map/ipqj,psiqd->sijd/transpose | solution.py:108
  97.6 3.4 %fusion.8 = bf16[1,2048,384]{2,1,0:T(8,128)(2,1)S(1)} fusion(f32[1,4,512,384]{3,2,1,0:T(8,128)S(1)} %copy.29, f32[1,2048,384]{2,1,0:T(8,128)} %get-tuple-element.14), kind=kLoop, calls=%fused_computation.17 | loop fusion | flops 7077888 | bytes 7864320 | tf_op jit(solution)/shard_map/convert_element_type | solution.py:115
  102.2 3.4 %collective-permute-start.1 = (bf16[1,3,384]{2,1,0:T(4,128)(2,1)S(1)}, bf16[1,3,384]{2,1,0:T(4,128)(2,1)S(1)}, u32[]{:S(2)}, u32[]{:S(2)}) collective-permute-start(bf16[1,3,384]{2,1,0:T(4,128)(2,1)S(1)} %slice.64), channel_id=1, source_target_pairs={{1,0},{2,1},{3,2},{4,3},{5,4},{6,5},{7,6},{8,7},{9,8},{10,9},{11,1... | collective-permute-start | bytes 6920 | tf_op jit(solution)/shard_map/ppermute | solution.py:54
  105.6 8.3 %all-to-all-done.1 = bf16[128,1,4,4,384]{4,2,3,1,0:T(4,128)(2,1)} async-done(((bf16[128,1,4,4,384]{4,2,3,1,0:T(4,128)(2,1)}), bf16[128,1,4,4,384]{4,2,3,1,0:T(4,128)(2,1)}, u32[]{:S(2)}, u32[]{:S(2)}) %all-to-all-start.1) | async-done | bytes 1572896 | tf_op jit(solution)/shard_map/all_to_all | solution.py:86
  113.9 2.4 %convolution_convert_fusion = bf16[4,256,512]{2,1,0:T(8,128)(2,1)S(1)} fusion(bf16[4,512,384]{2,0,1:T(4,128)(2,1)} %bitcast.23, bf16[1,4,512,384]{3,2,1,0:T(8,128)(2,1)} %bitcast.59, s32[]{:T(128)S(6)} %select_n.15), kind=kOutput, calls=%fused_computation.32 | convolution fusion | flops 403177472 | bytes 3407876 | tf_op jit(solution)/shard_map/skmd,skid->kmi/dot_general | solution.py:95
  116.3 8.3 %collective-permute-start.3 = (bf16[4,256,512]{2,1,0:T(8,128)(2,1)S(1)}, bf16[4,256,512]{2,1,0:T(8,128)(2,1)S(1)}, u32[]{:S(2)}, u32[]{:S(2)}) collective-permute-start(bf16[4,256,512]{2,1,0:T(8,128)(2,1)S(1)} %convolution_convert_fusion), channel_id=1, source_target_pairs={{0,128},{128,0},{1,129},{129,1},{2,130},{130,2},{3,131},{131,3},{4... | collective-permute-start | bytes 3145736 | tf_op jit(solution)/shard_map/ppermute | solution.py:106
  124.9 2.2 %convert_reduce-precision_fusion = f32[4,256,512]{2,1,0:T(8,128)S(1)} fusion(bf16[4,512,384]{2,0,1:T(4,128)(2,1)} %bitcast.23, bf16[1,4,512,384]{3,2,1,0:T(8,128)(2,1)S(1)} %bitcast.60, s32[]{:T(128)S(6)} %select_n.14), kind=kOutput, calls=%fused_computation.23 | convolution fusion | flops 404226048 | bytes 4456452 | tf_op jit(solution)/shard_map/skmd,skid->kmi/dot_general | solution.py:95
  127.0 2.5 %fusion.1 = bf16[1,2048,384]{2,1,0:T(8,128)(2,1)} fusion(f32[1,2051,384]{2,1,0:T(8,128)S(1)} %maximum_convert_fusion.1, f32[384]{0:T(512)S(1)} %get-tuple-element.11, f32[384]{0:T(512)S(1)} %get-tuple-element.12, f32[384]{0:T(512)S(1)} %get-tuple-element.10, f32[384]{0:T(512)S(1)} %get-tuple-element.9), kind=kLoop, calls=%fused_computation.2 | loop fusion | flops 6291456 | bytes 14161920 | tf_op jit(solution)/shard_map/convert_element_type | solution.py:120
  129.6 6.4 %collective-permute-done.2 = bf16[4,256,512]{2,0,1:T(4,128)(2,1)} collective-permute-done((bf16[4,256,512]{2,0,1:T(4,128)(2,1)}, bf16[4,256,512]{2,0,1:T(4,128)(2,1)}, u32[]{:S(2)}, u32[]{:S(2)}) %collective-permute-start.2) | collective-permute-done | bytes 1048608 | tf_op jit(solution)/shard_map/ppermute | solution.py:107
  136.0 1.9 %fusion.9 = bf16[4,256,512]{2,0,1:T(4,128)(2,1)S(1)} fusion(f32[4,64,4,512]{3,0,2,1:T(4,128)S(1)} %copy-done.1, bf16[4,256,512]{2,0,1:T(4,128)(2,1)} %collective-permute-done.2), kind=kLoop, calls=%fused_computation.21 | loop fusion | flops 1572864 | bytes 4194304 | tf_op jit(solution)/shard_map/convert_element_type | solution.py:114
  139.1 19.3 %collective-permute-done.3 = bf16[4,256,512]{2,1,0:T(8,128)(2,1)S(1)} collective-permute-done((bf16[4,256,512]{2,1,0:T(8,128)(2,1)S(1)}, bf16[4,256,512]{2,1,0:T(8,128)(2,1)S(1)}, u32[]{:S(2)}, u32[]{:S(2)}) %collective-permute-start.3) | collective-permute-done | bytes 1048608 | tf_op jit(solution)/shard_map/ppermute | solution.py:106
  (28 shorter events, 10.4 us)
Async XLA Ops:
  4.9 16.6 %copy-start.5 = (bf16[1,2048,384]{2,1,0:T(8,128)(2,1)S(1)}, bf16[1,2048,384]{2,1,0:T(8,128)(2,1)}, u32[]{:S(2)}) copy-start(bf16[1,2048,384]{2,1,0:T(8,128)(2,1)} %param.5) | copy-start | bytes 4718596
  4.9 20.1 %copy-start.6 = (f32[4,384]{1,0:T(4,128)S(1)}, f32[4,384]{1,0:T(4,128)}, u32[]{:S(2)}) copy-start(f32[4,384]{1,0:T(4,128)} %param.6) | copy-start | bytes 18436
  4.9 57.5 %all-to-all-start = ((bf16[128,4,1536]{2,1,0:T(4,128)(2,1)}), bf16[128,4,1536]{2,1,0:T(4,128)(2,1)S(1)}, u32[]{:S(2)}, u32[]{:S(2)}) async-start(bf16[128,4,1536]{2,1,0:T(4,128)(2,1)} %shard_map.76), calls=%async_computation | async-start | bytes 3145728 | tf_op jit(solution)/shard_map/all_to_all | solution.py:83
  21.5 7.6 %collective-permute-start = (bf16[1,3,384]{2,1,0:T(4,128)(2,1)S(1)}, bf16[1,3,384]{2,1,0:T(4,128)(2,1)S(1)}, u32[]{:S(2)}, u32[]{:S(2)}) collective-permute-start(bf16[1,3,384]{2,1,0:T(4,128)(2,1)S(1)} %slice.47), channel_id=1, source_target_pairs={{0,1},{1,2},{2,3},{3,4},{4,5},{5,6},{6,7},{7,8},{8,9},{9,10},{10,1... | collective-permute-start | bytes 6920 | tf_op jit(solution)/shard_map/ppermute | solution.py:54
  29.5 3.1 %copy-start = (bf16[4,128,4,512]{3,2,1,0:T(4,128)(2,1)S(1)}, bf16[4,128,4,512]{3,2,1,0:T(4,128)(2,1)}, u32[]{:S(2)}) copy-start(bf16[4,128,4,512]{3,2,1,0:T(4,128)(2,1)} %reshape.128) | copy-start | bytes 6291460
  62.4 51.5 %all-to-all-start.1 = ((bf16[128,1,4,4,384]{4,2,3,1,0:T(4,128)(2,1)}), bf16[128,1,4,4,384]{4,2,3,1,0:T(4,128)(2,1)}, u32[]{:S(2)}, u32[]{:S(2)}) async-start(bf16[128,1,4,4,384]{4,2,3,1,0:T(4,128)(2,1)} %copy.36), calls=%async_computation.1 | async-start | bytes 3145728 | tf_op jit(solution)/shard_map/all_to_all | solution.py:86
  86.7 49.4 %collective-permute-start.2 = (bf16[4,256,512]{2,0,1:T(4,128)(2,1)}, bf16[4,256,512]{2,0,1:T(4,128)(2,1)}, u32[]{:S(2)}, u32[]{:S(2)}) collective-permute-start(bf16[4,256,512]{2,0,1:T(4,128)(2,1)} %bitcast.15), channel_id=1, source_target_pairs={{0,128},{128,0},{1,129},{129,1},{2,130},{130,2},{3,131},{131,3},{4... | collective-permute-start | bytes 3145736 | tf_op jit(solution)/shard_map/ppermute | solution.py:107
  101.0 1.1 copy-start.2
  102.2 22.5 %copy-start.3 = (bf16[1,2048,384]{2,1,0:T(8,128)(2,1)S(1)}, bf16[1,2048,384]{2,1,0:T(8,128)(2,1)}, u32[]{:S(2)}) copy-start(bf16[1,2048,384]{2,1,0:T(8,128)(2,1)} %copy-done.2) | copy-start | bytes 4718596
  102.2 22.5 %collective-permute-start.1 = (bf16[1,3,384]{2,1,0:T(4,128)(2,1)S(1)}, bf16[1,3,384]{2,1,0:T(4,128)(2,1)S(1)}, u32[]{:S(2)}, u32[]{:S(2)}) collective-permute-start(bf16[1,3,384]{2,1,0:T(4,128)(2,1)S(1)} %slice.64), channel_id=1, source_target_pairs={{1,0},{2,1},{3,2},{4,3},{5,4},{6,5},{7,6},{8,7},{9,8},{10,9},{11,1... | collective-permute-start | bytes 6920 | tf_op jit(solution)/shard_map/ppermute | solution.py:54
  116.3 8.5 %copy-start.4 = (bf16[1,2048,384]{2,1,0:T(8,128)(2,1)S(1)}, bf16[1,2048,384]{2,1,0:T(8,128)(2,1)}, u32[]{:S(2)}) copy-start(bf16[1,2048,384]{2,1,0:T(8,128)(2,1)} %param.9) | copy-start | bytes 4718596
  116.3 42.1 %collective-permute-start.3 = (bf16[4,256,512]{2,1,0:T(8,128)(2,1)S(1)}, bf16[4,256,512]{2,1,0:T(8,128)(2,1)S(1)}, u32[]{:S(2)}, u32[]{:S(2)}) collective-permute-start(bf16[4,256,512]{2,1,0:T(8,128)(2,1)S(1)} %convolution_convert_fusion), channel_id=1, source_target_pairs={{0,128},{128,0},{1,129},{129,1},{2,130},{130,2},{3,131},{131,3},{4... | collective-permute-start | bytes 3145736 | tf_op jit(solution)/shard_map/ppermute | solution.py:106
  127.0 9.0 %copy-start.1 = (f32[4,64,4,512]{3,0,2,1:T(4,128)S(1)}, f32[4,64,4,512]{3,0,2,1:T(4,128)}, u32[]{:S(2)}) copy-start(f32[4,64,4,512]{3,0,2,1:T(4,128)} %copy.31) | copy-start | bytes 6291460

commit v16 on v15

--- a/solution.py
+++ b/solution.py
@@ -6,9 +6,8 @@
 from jax.experimental.pallas import tpu as pltpu
 
 
-def _grad_payload_kernel(s_hbm, g_hbm, o_ref, s_vmem, g_vmem, sems):
-    peers, group, _ = o_ref.shape
-    col_blocks = s_hbm.shape[0]
+def _grad_payload_kernel(s_hbm, g_hbm, o_hbm, s_vmem, g_vmem, o_vmem, sems):
+    col_blocks, peers, group, _ = o_vmem.shape
     width = g_hbm.shape[-1]
     loads = []
     for k in range(col_blocks):
@@ -19,13 +18,21 @@
         for copy in pair:
             copy.start()
         loads.append(pair)
+    stores = []
     for k in range(col_blocks):
         for copy in loads[k]:
             copy.wait()
         product = lax.dot_general(
             s_vmem[k], g_vmem[k], (((0,), (0,)), ((), ())), preferred_element_type=jnp.float32
         )
-        o_ref[:, :, k * width : (k + 1) * width] = product.reshape(peers, group, width).astype(o_ref.dtype)
+        o_vmem[k] = product.reshape(peers, group, width).astype(o_vmem.dtype)
+        store = pltpu.make_async_copy(
+            o_vmem.at[k], o_hbm.at[:, :, pl.ds(k * width, width)], sems.at[2, k]
+        )
+        store.start()
+        stores.append(store)
+    for store in stores:
+        store.wait()
 
 
 def grad_payload(second_factor, upstream, peers):
@@ -36,11 +43,12 @@
         _grad_payload_kernel,
         out_shape=jax.ShapeDtypeStruct((peers, order // peers, col_blocks * width), jnp.bfloat16),
         in_specs=[pl.BlockSpec(memory_space=pl.ANY)] * 2,
-        out_specs=pl.BlockSpec(memory_space=pltpu.VMEM),
+        out_specs=pl.BlockSpec(memory_space=pl.ANY),
         scratch_shapes=[
             pltpu.VMEM((col_blocks, rows, order), jnp.bfloat16),
             pltpu.VMEM((col_blocks, rows, width), jnp.bfloat16),
-            pltpu.SemaphoreType.DMA((2, col_blocks)),
+            pltpu.VMEM((col_blocks, peers, order // peers, width), jnp.bfloat16),
+            pltpu.SemaphoreType.DMA((3, col_blocks)),
         ],
         cost_estimate=pl.CostEstimate(
             flops=flops, transcendentals=0, bytes_accessed=2 * (second_factor.size + 2 * upstream.size)

time: 160 us -> 160 us (level)
  no operation moved by 1% of the time
where the time goes in v16:
time: 160 us; the launch traced here: 159 us
  waiting for transfers between devices  57.5 us (36%)
  starting transfers between devices  49.4 us (31%)
  local copies, waits for them, and re-layouts  22 us (14%)
  matrix products  12.9 us (8%)
  other arithmetic  12.8 us (8%)
  Pallas kernels  3.92 us (2%)
    all_to_all x1, waiting for transfers between devices, body(): lax.all_to_all(grad_chunks, 'seq', split_axis=0, concat_axis=0, tiled=True)  23.4 us
    ppermute x1, waiting for transfers between devices, body(): sent_second = lax.ppermute(second_part(other), 'batch', swap)  19.3 us
    all_to_all x1, starting transfers between devices, body(): lax.all_to_all(grad_chunks, 'seq', split_axis=0, concat_axis=0, tiled=True)  16.5 us
    all_to_all x1, starting transfers between devices, body(): lax.all_to_all(mixed_chunks, 'seq', split_axis=0, concat_axis=3, tiled=True)  14.8 us
    all_to_all x1, waiting for transfers between devices, body(): lax.all_to_all(mixed_chunks, 'seq', split_axis=0, concat_axis=3, tiled=True)  8.33 us
    ppermute x1, starting transfers between devices, body(): sent_second = lax.ppermute(second_part(other), 'batch', swap)  8.32 us
    ppermute x2, starting transfers between devices, passed_along(): lax.ppermute(value, axis, [(source, source + steps) for source in range(i...  6.97 us
    ppermute x1, waiting for transfers between devices, body(): sent_first = lax.ppermute(first_part(other), 'batch', swap)  6.44 us
  transfers between devices with their start and end apart: 6, of which 4 were waited for; matrix products, arithmetic and copies ran while one was open for 28% of the time, Pallas kernels for 0%

profile of v16, /device:TPU:1, one launch (start us, length us, event | category | flops | bytes accessed | tf_op | source)
XLA Modules:
  0.0 159.4 jit_solution(9946251133071539152)
XLA Ops:
  0.6 3.9 %shard_map.76 = bf16[128,4,1536]{2,1,0:T(4,128)(2,1)} custom-call(bf16[4,512,512]{2,1,0:T(8,128)(2,1)} %s_hbm.1, bf16[4,512,384]{2,1,0:T(8,128)(2,1)} %bitcast.58), custom_call_target="tpu_custom_call" | custom-call | flops 805306368 | bytes 5242880 | tf_op jit(solution)/shard_map/pallas_call | solution.py:42
  4.6 16.5 %all-to-all-start = ((bf16[128,4,1536]{2,1,0:T(4,128)(2,1)}), bf16[128,4,1536]{2,1,0:T(4,128)(2,1)S(1)}, u32[]{:S(2)}, u32[]{:S(2)}) async-start(bf16[128,4,1536]{2,1,0:T(4,128)(2,1)} %shard_map.76), calls=%async_computation | async-start | bytes 3145728 | tf_op jit(solution)/shard_map/all_to_all | solution.py:91
  21.2 3.5 %collective-permute-start = (bf16[1,3,384]{2,1,0:T(4,128)(2,1)S(1)}, bf16[1,3,384]{2,1,0:T(4,128)(2,1)S(1)}, u32[]{:S(2)}, u32[]{:S(2)}) collective-permute-start(bf16[1,3,384]{2,1,0:T(4,128)(2,1)S(1)} %slice.47), channel_id=1, source_target_pairs={{0,1},{1,2},{2,3},{3,4},{4,5},{5,6},{6,7},{7,8},{8,9},{9,10},{10,1... | collective-permute-start | bytes 6920 | tf_op jit(solution)/shard_map/ppermute | solution.py:62
  24.7 4.0 %reshape.128 = bf16[4,128,4,512]{3,2,1,0:T(4,128)(2,1)} reshape(bf16[4,512,512]{2,1,0:T(8,128)(2,1)} %param.7) | data formatting | bytes 4194304 | tf_op jit(solution)/shard_map/reshape | solution.py:85
  29.1 3.1 %multiply_convert_fusion = (bf16[1,2048,384]{2,1,0:T(8,128)(2,1)S(1)}, f32[1,2048,384]{2,1,0:T(8,128)}) fusion(f32[1,2051,384]{2,1,0:T(8,128)S(1)} %maximum_convert_fusion, f32[384]{0:T(512)S(1)} %get-tuple-element.11, f32[384]{0:T(512)S(1)} %get-tuple-element.12, f32[384]{0:T(512)S(1)} %get-tuple-element.10, f32[384]{0:T(512)S(1)} %get-tuple-element.9), kind=kLoop, calls=%fused_computation.18 | loop fusion | flops 9437184 | bytes 17307648 | tf_op jit(solution)/shard_map/convert_element_type | solution.py:83
  32.2 2.6 %fusion.16 = bf16[128,1,4,4,384]{0,4,2,3,1:T(8,128)(2,1)} fusion(bf16[4,512,384,1]{2,1,3,0:T(8,128)(2,1)S(1)} %bitcast.54, bf16[4,128,4,512]{3,2,1,0:T(4,128)(2,1)S(1)} %copy-done), kind=kOutput, calls=%fused_computation.36 | convolution fusion | flops 806092800 | bytes 5242880 | tf_op jit(solution)/shard_map/ipqj,sijd->psqid/dot_general | solution.py:86
  34.8 3.9 %copy.36 = bf16[128,1,4,4,384]{4,2,3,1,0:T(4,128)(2,1)} copy(bf16[128,1,4,4,384]{0,4,2,3,1:T(8,128)(2,1)} %fusion.16) | data formatting | bytes 3145728 | tf_op jit(solution)/shard_map/convert_element_type | solution.py:88
  38.7 23.4 %all-to-all-done = bf16[128,4,1536]{2,1,0:T(4,128)(2,1)S(1)} async-done(((bf16[128,4,1536]{2,1,0:T(4,128)(2,1)}), bf16[128,4,1536]{2,1,0:T(4,128)(2,1)S(1)}, u32[]{:S(2)}, u32[]{:S(2)}) %all-to-all-start) | async-done | bytes 1572896 | tf_op jit(solution)/shard_map/all_to_all | solution.py:91
  62.1 14.8 %all-to-all-start.1 = ((bf16[128,1,4,4,384]{4,2,3,1,0:T(4,128)(2,1)}), bf16[128,1,4,4,384]{4,2,3,1,0:T(4,128)(2,1)}, u32[]{:S(2)}, u32[]{:S(2)}) async-start(bf16[128,1,4,4,384]{4,2,3,1,0:T(4,128)(2,1)} %copy.36), calls=%async_computation.1 | async-start | bytes 3145728 | tf_op jit(solution)/shard_map/all_to_all | solution.py:94
  78.4 1.9 %constant_dynamic-slice_fusion = (bf16[64,1,4,4,384]{4,3,2,0,1:T(4,128)(2,1)S(1)}, bf16[64,1,4,4,384]{4,3,2,0,1:T(4,128)(2,1)S(1)}) fusion(bf16[128,1,4,4,384]{4,3,2,0,1:T(4,128)(2,1)} %reshape.130, s32[]{:T(128)S(6)} %select_n.13, s32[]{:T(128)S(6)} %select_n.12), kind=kLoop, calls=%fused_computation.53 | loop fusion | bytes 3145736 | tf_op jit(solution)/shard_map/dynamic_slice | solution.py:108
  81.1 2.7 %copy.31 = f32[4,64,4,512]{3,0,2,1:T(4,128)} copy(f32[4,64,4,512]{3,1,2,0:T(8,128)S(1)} %convert_reduce-precision_fusion.1) | data formatting | bytes 4194304 | tf_op jit(solution)/shard_map/reduce_precision | solution.py:119
  86.3 2.8 %collective-permute-start.2 = (bf16[4,256,512]{2,0,1:T(4,128)(2,1)}, bf16[4,256,512]{2,0,1:T(4,128)(2,1)}, u32[]{:S(2)}, u32[]{:S(2)}) collective-permute-start(bf16[4,256,512]{2,0,1:T(4,128)(2,1)} %bitcast.15), channel_id=1, source_target_pairs={{0,128},{128,0},{1,129},{129,1},{2,130},{130,2},{3,131},{131,3},{4... | collective-permute-start | bytes 3145736 | tf_op jit(solution)/shard_map/ppermute | solution.py:115
  90.5 4.3 %convolution_bitcast_fusion = f32[1,4,512,384]{2,3,1,0:T(8,128)} fusion(bf16[128,4,4,384]{0,3,2,1:T(8,128)(2,1)S(1)} %bitcast.57, bf16[4,128,4,512]{3,2,1,0:T(4,128)(2,1)} %reshape.128), kind=kOutput, calls=%fused_computation.25 | convolution fusion | flops 805306368 | bytes 6815744 | tf_op jit(solution)/shard_map/ipqj,psiqd->sijd/dot_general | solution.py:116
  94.9 2.4 %copy.29 = f32[1,4,512,384]{3,2,1,0:T(8,128)S(1)} copy(f32[1,4,512,384]{2,3,1,0:T(8,128)} %convolution_bitcast_fusion) | data formatting | bytes 6291456 | tf_op jit(solution)/shard_map/ipqj,psiqd->sijd/transpose | solution.py:116
  97.3 3.4 %fusion.8 = bf16[1,2048,384]{2,1,0:T(8,128)(2,1)S(1)} fusion(f32[1,4,512,384]{3,2,1,0:T(8,128)S(1)} %copy.29, f32[1,2048,384]{2,1,0:T(8,128)} %get-tuple-element.14), kind=kLoop, calls=%fused_computation.17 | loop fusion | flops 7077888 | bytes 7864320 | tf_op jit(solution)/shard_map/convert_element_type | solution.py:123
  101.8 3.4 %collective-permute-start.1 = (bf16[1,3,384]{2,1,0:T(4,128)(2,1)S(1)}, bf16[1,3,384]{2,1,0:T(4,128)(2,1)S(1)}, u32[]{:S(2)}, u32[]{:S(2)}) collective-permute-start(bf16[1,3,384]{2,1,0:T(4,128)(2,1)S(1)} %slice.64), channel_id=1, source_target_pairs={{1,0},{2,1},{3,2},{4,3},{5,4},{6,5},{7,6},{8,7},{9,8},{10,9},{11,1... | collective-permute-start | bytes 6920 | tf_op jit(solution)/shard_map/ppermute | solution.py:62
  105.2 8.3 %all-to-all-done.1 = bf16[128,1,4,4,384]{4,2,3,1,0:T(4,128)(2,1)} async-done(((bf16[128,1,4,4,384]{4,2,3,1,0:T(4,128)(2,1)}), bf16[128,1,4,4,384]{4,2,3,1,0:T(4,128)(2,1)}, u32[]{:S(2)}, u32[]{:S(2)}) %all-to-all-start.1) | async-done | bytes 1572896 | tf_op jit(solution)/shard_map/all_to_all | solution.py:94
  113.6 2.4 %convolution_convert_fusion = bf16[4,256,512]{2,1,0:T(8,128)(2,1)S(1)} fusion(bf16[4,512,384]{2,0,1:T(4,128)(2,1)} %bitcast.23, bf16[1,4,512,384]{3,2,1,0:T(8,128)(2,1)} %bitcast.59, s32[]{:T(128)S(6)} %select_n.15), kind=kOutput, calls=%fused_computation.32 | convolution fusion | flops 403177472 | bytes 3407876 | tf_op jit(solution)/shard_map/skmd,skid->kmi/dot_general | solution.py:103
  116.0 8.3 %collective-permute-start.3 = (bf16[4,256,512]{2,1,0:T(8,128)(2,1)S(1)}, bf16[4,256,512]{2,1,0:T(8,128)(2,1)S(1)}, u32[]{:S(2)}, u32[]{:S(2)}) collective-permute-start(bf16[4,256,512]{2,1,0:T(8,128)(2,1)S(1)} %convolution_convert_fusion), channel_id=1, source_target_pairs={{0,128},{128,0},{1,129},{129,1},{2,130},{130,2},{3,131},{131,3},{4... | collective-permute-start | bytes 3145736 | tf_op jit(solution)/shard_map/ppermute | solution.py:114
  124.5 2.2 %convert_reduce-precision_fusion = f32[4,256,512]{2,1,0:T(8,128)S(1)} fusion(bf16[4,512,384]{2,0,1:T(4,128)(2,1)} %bitcast.23, bf16[1,4,512,384]{3,2,1,0:T(8,128)(2,1)S(1)} %bitcast.60, s32[]{:T(128)S(6)} %select_n.14), kind=kOutput, calls=%fused_computation.23 | convolution fusion | flops 404226048 | bytes 4456452 | tf_op jit(solution)/shard_map/skmd,skid->kmi/dot_general | solution.py:103
  126.7 2.5 %fusion.1 = bf16[1,2048,384]{2,1,0:T(8,128)(2,1)} fusion(f32[1,2051,384]{2,1,0:T(8,128)S(1)} %maximum_convert_fusion.1, f32[384]{0:T(512)S(1)} %get-tuple-element.11, f32[384]{0:T(512)S(1)} %get-tuple-element.12, f32[384]{0:T(512)S(1)} %get-tuple-element.10, f32[384]{0:T(512)S(1)} %get-tuple-element.9), kind=kLoop, calls=%fused_computation.2 | loop fusion | flops 6291456 | bytes 14161920 | tf_op jit(solution)/shard_map/convert_element_type | solution.py:128
  129.3 6.4 %collective-permute-done.2 = bf16[4,256,512]{2,0,1:T(4,128)(2,1)} collective-permute-done((bf16[4,256,512]{2,0,1:T(4,128)(2,1)}, bf16[4,256,512]{2,0,1:T(4,128)(2,1)}, u32[]{:S(2)}, u32[]{:S(2)}) %collective-permute-start.2) | collective-permute-done | bytes 1048608 | tf_op jit(solution)/shard_map/ppermute | solution.py:115
  135.7 1.9 %fusion.9 = bf16[4,256,512]{2,0,1:T(4,128)(2,1)S(1)} fusion(f32[4,64,4,512]{3,0,2,1:T(4,128)S(1)} %copy-done.1, bf16[4,256,512]{2,0,1:T(4,128)(2,1)} %collective-permute-done.2), kind=kLoop, calls=%fused_computation.21 | loop fusion | flops 1572864 | bytes 4194304 | tf_op jit(solution)/shard_map/convert_element_type | solution.py:122
  138.8 19.3 %collective-permute-done.3 = bf16[4,256,512]{2,1,0:T(8,128)(2,1)S(1)} collective-permute-done((bf16[4,256,512]{2,1,0:T(8,128)(2,1)S(1)}, bf16[4,256,512]{2,1,0:T(8,128)(2,1)S(1)}, u32[]{:S(2)}, u32[]{:S(2)}) %collective-permute-start.3) | collective-permute-done | bytes 1048608 | tf_op jit(solution)/shard_map/ppermute | solution.py:114
  (28 shorter events, 10.4 us)
Async XLA Ops:
  4.6 16.6 %copy-start.5 = (bf16[1,2048,384]{2,1,0:T(8,128)(2,1)S(1)}, bf16[1,2048,384]{2,1,0:T(8,128)(2,1)}, u32[]{:S(2)}) copy-start(bf16[1,2048,384]{2,1,0:T(8,128)(2,1)} %param.5) | copy-start | bytes 4718596
  4.6 20.1 %copy-start.6 = (f32[4,384]{1,0:T(4,128)S(1)}, f32[4,384]{1,0:T(4,128)}, u32[]{:S(2)}) copy-start(f32[4,384]{1,0:T(4,128)} %param.6) | copy-start | bytes 18436
  4.6 57.5 %all-to-all-start = ((bf16[128,4,1536]{2,1,0:T(4,128)(2,1)}), bf16[128,4,1536]{2,1,0:T(4,128)(2,1)S(1)}, u32[]{:S(2)}, u32[]{:S(2)}) async-start(bf16[128,4,1536]{2,1,0:T(4,128)(2,1)} %shard_map.76), calls=%async_computation | async-start | bytes 3145728 | tf_op jit(solution)/shard_map/all_to_all | solution.py:91
  21.2 7.6 %collective-permute-start = (bf16[1,3,384]{2,1,0:T(4,128)(2,1)S(1)}, bf16[1,3,384]{2,1,0:T(4,128)(2,1)S(1)}, u32[]{:S(2)}, u32[]{:S(2)}) collective-permute-start(bf16[1,3,384]{2,1,0:T(4,128)(2,1)S(1)} %slice.47), channel_id=1, source_target_pairs={{0,1},{1,2},{2,3},{3,4},{4,5},{5,6},{6,7},{7,8},{8,9},{9,10},{10,1... | collective-permute-start | bytes 6920 | tf_op jit(solution)/shard_map/ppermute | solution.py:62
  29.1 3.1 %copy-start = (bf16[4,128,4,512]{3,2,1,0:T(4,128)(2,1)S(1)}, bf16[4,128,4,512]{3,2,1,0:T(4,128)(2,1)}, u32[]{:S(2)}) copy-start(bf16[4,128,4,512]{3,2,1,0:T(4,128)(2,1)} %reshape.128) | copy-start | bytes 6291460
  62.1 51.5 %all-to-all-start.1 = ((bf16[128,1,4,4,384]{4,2,3,1,0:T(4,128)(2,1)}), bf16[128,1,4,4,384]{4,2,3,1,0:T(4,128)(2,1)}, u32[]{:S(2)}, u32[]{:S(2)}) async-start(bf16[128,1,4,4,384]{4,2,3,1,0:T(4,128)(2,1)} %copy.36), calls=%async_computation.1 | async-start | bytes 3145728 | tf_op jit(solution)/shard_map/all_to_all | solution.py:94
  86.3 49.4 %collective-permute-start.2 = (bf16[4,256,512]{2,0,1:T(4,128)(2,1)}, bf16[4,256,512]{2,0,1:T(4,128)(2,1)}, u32[]{:S(2)}, u32[]{:S(2)}) collective-permute-start(bf16[4,256,512]{2,0,1:T(4,128)(2,1)} %bitcast.15), channel_id=1, source_target_pairs={{0,128},{128,0},{1,129},{129,1},{2,130},{130,2},{3,131},{131,3},{4... | collective-permute-start | bytes 3145736 | tf_op jit(solution)/shard_map/ppermute | solution.py:115
  100.6 1.1 copy-start.2
  101.8 22.5 %copy-start.3 = (bf16[1,2048,384]{2,1,0:T(8,128)(2,1)S(1)}, bf16[1,2048,384]{2,1,0:T(8,128)(2,1)}, u32[]{:S(2)}) copy-start(bf16[1,2048,384]{2,1,0:T(8,128)(2,1)} %copy-done.2) | copy-start | bytes 4718596
  101.8 22.5 %collective-permute-start.1 = (bf16[1,3,384]{2,1,0:T(4,128)(2,1)S(1)}, bf16[1,3,384]{2,1,0:T(4,128)(2,1)S(1)}, u32[]{:S(2)}, u32[]{:S(2)}) collective-permute-start(bf16[1,3,384]{2,1,0:T(4,128)(2,1)S(1)} %slice.64), channel_id=1, source_target_pairs={{1,0},{2,1},{3,2},{4,3},{5,4},{6,5},{7,6},{8,7},{9,8},{10,9},{11,1... | collective-permute-start | bytes 6920 | tf_op jit(solution)/shard_map/ppermute | solution.py:62
  116.0 8.5 %copy-start.4 = (bf16[1,2048,384]{2,1,0:T(8,128)(2,1)S(1)}, bf16[1,2048,384]{2,1,0:T(8,128)(2,1)}, u32[]{:S(2)}) copy-start(bf16[1,2048,384]{2,1,0:T(8,128)(2,1)} %param.9) | copy-start | bytes 4718596
  116.0 42.1 %collective-permute-start.3 = (bf16[4,256,512]{2,1,0:T(8,128)(2,1)S(1)}, bf16[4,256,512]{2,1,0:T(8,128)(2,1)S(1)}, u32[]{:S(2)}, u32[]{:S(2)}) collective-permute-start(bf16[4,256,512]{2,1,0:T(8,128)(2,1)S(1)} %convolution_convert_fusion), channel_id=1, source_target_pairs={{0,128},{128,0},{1,129},{129,1},{2,130},{130,2},{3,131},{131,3},{4... | collective-permute-start | bytes 3145736 | tf_op jit(solution)/shard_map/ppermute | solution.py:114
  126.7 9.0 %copy-start.1 = (f32[4,64,4,512]{3,0,2,1:T(4,128)S(1)}, f32[4,64,4,512]{3,0,2,1:T(4,128)}, u32[]{:S(2)}) copy-start(f32[4,64,4,512]{3,0,2,1:T(4,128)} %copy.31) | copy-start | bytes 6291460

commit v17 on v15

--- a/solution.py
+++ b/solution.py
@@ -109,8 +109,8 @@
         "ipqj,psiqd->sijd", first_split, grad_rows, preferred_element_type=jnp.float32
     ).reshape(seq_count, tok_rows, channels)
     kept = lambda part: lax.reduce_precision(part.astype(jnp.float32), exponent_bits=8, mantissa_bits=7)
-    own_second = lax.optimization_barrier(kept(second_part(me)))
-    part_second = (own_second + sent_second.astype(jnp.float32)).astype(jnp.bfloat16)
+    own_second = lax.optimization_barrier(second_part(me))
+    part_second = (own_second.astype(jnp.float32) + sent_second.astype(jnp.float32)).astype(jnp.bfloat16)
     part_first = (kept(first_part(me)) + sent_first.astype(jnp.float32)).astype(jnp.bfloat16)
     grad_conv = (grad_hidden * gate_val * (1.0 + conv_out * (1.0 - gate_val))).astype(jnp.bfloat16)
     following = passed_along(grad_conv[:, : tap_count - 1, :], "seq", -1)

time: 160 us -> 160 us (level)
  no operation moved by 1% of the time
where the time goes in v17:
time: 160 us
  waiting for transfers between devices  57.4 us (36%)
  starting transfers between devices  49.4 us (31%)
  local copies, waits for them, and re-layouts  22 us (14%)
  matrix products  12.9 us (8%)
  other arithmetic  12.7 us (8%)
  Pallas kernels  4.28 us (3%)
    all_to_all x1, waiting for transfers between devices, body(): lax.all_to_all(grad_chunks, 'seq', split_axis=0, concat_axis=0, tiled=True)  23.4 us
    ppermute x1, waiting for transfers between devices, body(): sent_second = lax.ppermute(second_part(other), 'batch', swap)  19.3 us
    all_to_all x1, starting transfers between devices, body(): lax.all_to_all(grad_chunks, 'seq', split_axis=0, concat_axis=0, tiled=True)  16.5 us
    all_to_all x1, starting transfers between devices, body(): lax.all_to_all(mixed_chunks, 'seq', split_axis=0, concat_axis=3, tiled=True)  14.8 us
    ppermute x1, starting transfers between devices, body(): sent_second = lax.ppermute(second_part(other), 'batch', swap)  8.32 us
    all_to_all x1, waiting for transfers between devices, body(): lax.all_to_all(mixed_chunks, 'seq', split_axis=0, concat_axis=3, tiled=True)  8.31 us
    ppermute x2, starting transfers between devices, passed_along(): lax.ppermute(value, axis, [(source, source + steps) for source in range(i...  6.98 us
    ppermute x1, waiting for transfers between devices, body(): sent_first = lax.ppermute(first_part(other), 'batch', swap)  6.45 us
  transfers between devices with their start and end apart: 6, of which 4 were waited for; matrix products, arithmetic and copies ran while one was open for 28% of the time, Pallas kernels for 0%

profile of v17, /device:TPU:1, one launch (start us, length us, event | category | flops | bytes accessed | tf_op | source)
XLA Modules:
  0.0 159.7 jit_solution(18377276329009611271)
XLA Ops:
  0.6 4.3 %shard_map.76 = bf16[128,4,1536]{2,1,0:T(4,128)(2,1)} custom-call(bf16[4,512,512]{2,1,0:T(8,128)(2,1)} %s_hbm.1, bf16[4,512,384]{2,1,0:T(8,128)(2,1)} %bitcast.58), custom_call_target="tpu_custom_call" | custom-call | flops 805306368 | bytes 5242880 | tf_op jit(solution)/shard_map/pallas_call | solution.py:35
  4.9 16.5 %all-to-all-start = ((bf16[128,4,1536]{2,1,0:T(4,128)(2,1)}), bf16[128,4,1536]{2,1,0:T(4,128)(2,1)S(1)}, u32[]{:S(2)}, u32[]{:S(2)}) async-start(bf16[128,4,1536]{2,1,0:T(4,128)(2,1)} %shard_map.76), calls=%async_computation | async-start | bytes 3145728 | tf_op jit(solution)/shard_map/all_to_all | solution.py:83
  21.5 3.5 %collective-permute-start = (bf16[1,3,384]{2,1,0:T(4,128)(2,1)S(1)}, bf16[1,3,384]{2,1,0:T(4,128)(2,1)S(1)}, u32[]{:S(2)}, u32[]{:S(2)}) collective-permute-start(bf16[1,3,384]{2,1,0:T(4,128)(2,1)S(1)} %slice.47), channel_id=1, source_target_pairs={{0,1},{1,2},{2,3},{3,4},{4,5},{5,6},{6,7},{7,8},{8,9},{9,10},{10,1... | collective-permute-start | bytes 6920 | tf_op jit(solution)/shard_map/ppermute | solution.py:54
  25.1 4.0 %reshape.128 = bf16[4,128,4,512]{3,2,1,0:T(4,128)(2,1)} reshape(bf16[4,512,512]{2,1,0:T(8,128)(2,1)} %param.7) | data formatting | bytes 4194304 | tf_op jit(solution)/shard_map/reshape | solution.py:77
  29.5 3.1 %multiply_convert_fusion = (bf16[1,2048,384]{2,1,0:T(8,128)(2,1)S(1)}, f32[1,2048,384]{2,1,0:T(8,128)}) fusion(f32[1,2051,384]{2,1,0:T(8,128)S(1)} %maximum_convert_fusion, f32[384]{0:T(512)S(1)} %get-tuple-element.11, f32[384]{0:T(512)S(1)} %get-tuple-element.12, f32[384]{0:T(512)S(1)} %get-tuple-element.10, f32[384]{0:T(512)S(1)} %get-tuple-element.9), kind=kLoop, calls=%fused_computation.18 | loop fusion | flops 9437184 | bytes 17307648 | tf_op jit(solution)/shard_map/convert_element_type | solution.py:75
  32.6 2.6 %fusion.16 = bf16[128,1,4,4,384]{0,4,2,3,1:T(8,128)(2,1)} fusion(bf16[4,512,384,1]{2,1,3,0:T(8,128)(2,1)S(1)} %bitcast.54, bf16[4,128,4,512]{3,2,1,0:T(4,128)(2,1)S(1)} %copy-done), kind=kOutput, calls=%fused_computation.35 | convolution fusion | flops 806092800 | bytes 5242880 | tf_op jit(solution)/shard_map/ipqj,sijd->psqid/dot_general | solution.py:78
  35.1 3.9 %copy.36 = bf16[128,1,4,4,384]{4,2,3,1,0:T(4,128)(2,1)} copy(bf16[128,1,4,4,384]{0,4,2,3,1:T(8,128)(2,1)} %fusion.16) | data formatting | bytes 3145728 | tf_op jit(solution)/shard_map/convert_element_type | solution.py:80
  39.0 23.4 %all-to-all-done = bf16[128,4,1536]{2,1,0:T(4,128)(2,1)S(1)} async-done(((bf16[128,4,1536]{2,1,0:T(4,128)(2,1)}), bf16[128,4,1536]{2,1,0:T(4,128)(2,1)S(1)}, u32[]{:S(2)}, u32[]{:S(2)}) %all-to-all-start) | async-done | bytes 1572896 | tf_op jit(solution)/shard_map/all_to_all | solution.py:83
  62.4 14.8 %all-to-all-start.1 = ((bf16[128,1,4,4,384]{4,2,3,1,0:T(4,128)(2,1)}), bf16[128,1,4,4,384]{4,2,3,1,0:T(4,128)(2,1)}, u32[]{:S(2)}, u32[]{:S(2)}) async-start(bf16[128,1,4,4,384]{4,2,3,1,0:T(4,128)(2,1)} %copy.36), calls=%async_computation.1 | async-start | bytes 3145728 | tf_op jit(solution)/shard_map/all_to_all | solution.py:86
  78.8 1.9 %constant_dynamic-slice_fusion = (bf16[64,1,4,4,384]{4,3,2,0,1:T(4,128)(2,1)S(1)}, bf16[64,1,4,4,384]{4,3,2,0,1:T(4,128)(2,1)S(1)}) fusion(bf16[128,1,4,4,384]{4,3,2,0,1:T(4,128)(2,1)} %reshape.130, s32[]{:T(128)S(6)} %select_n.13, s32[]{:T(128)S(6)} %select_n.12), kind=kLoop, calls=%fused_computation.52 | loop fusion | bytes 3145736 | tf_op jit(solution)/shard_map/dynamic_slice | solution.py:100
  81.4 2.7 %copy.31 = f32[4,64,4,512]{3,0,2,1:T(4,128)} copy(f32[4,64,4,512]{3,1,2,0:T(8,128)S(1)} %convert_reduce-precision_fusion) | data formatting | bytes 4194304 | tf_op jit(solution)/shard_map/reduce_precision | solution.py:111
  86.7 2.8 %collective-permute-start.2 = (bf16[4,256,512]{2,0,1:T(4,128)(2,1)}, bf16[4,256,512]{2,0,1:T(4,128)(2,1)}, u32[]{:S(2)}, u32[]{:S(2)}) collective-permute-start(bf16[4,256,512]{2,0,1:T(4,128)(2,1)} %bitcast.15), channel_id=1, source_target_pairs={{0,128},{128,0},{1,129},{129,1},{2,130},{130,2},{3,131},{131,3},{4... | collective-permute-start | bytes 3145736 | tf_op jit(solution)/shard_map/ppermute | solution.py:107
  90.9 4.3 %convolution_bitcast_fusion = f32[1,4,512,384]{2,3,1,0:T(8,128)} fusion(bf16[128,4,4,384]{0,3,2,1:T(8,128)(2,1)S(1)} %bitcast.57, bf16[4,128,4,512]{3,2,1,0:T(4,128)(2,1)} %reshape.128), kind=kOutput, calls=%fused_computation.24 | convolution fusion | flops 805306368 | bytes 6815744 | tf_op jit(solution)/shard_map/ipqj,psiqd->sijd/dot_general | solution.py:108
  95.2 2.4 %copy.29 = f32[1,4,512,384]{3,2,1,0:T(8,128)S(1)} copy(f32[1,4,512,384]{2,3,1,0:T(8,128)} %convolution_bitcast_fusion) | data formatting | bytes 6291456 | tf_op jit(solution)/shard_map/ipqj,psiqd->sijd/transpose | solution.py:108
  97.6 3.4 %fusion.8 = bf16[1,2048,384]{2,1,0:T(8,128)(2,1)S(1)} fusion(f32[1,4,512,384]{3,2,1,0:T(8,128)S(1)} %copy.29, f32[1,2048,384]{2,1,0:T(8,128)} %get-tuple-element.14), kind=kLoop, calls=%fused_computation.17 | loop fusion | flops 7077888 | bytes 7864320 | tf_op jit(solution)/shard_map/convert_element_type | solution.py:115
  102.2 3.4 %collective-permute-start.1 = (bf16[1,3,384]{2,1,0:T(4,128)(2,1)S(1)}, bf16[1,3,384]{2,1,0:T(4,128)(2,1)S(1)}, u32[]{:S(2)}, u32[]{:S(2)}) collective-permute-start(bf16[1,3,384]{2,1,0:T(4,128)(2,1)S(1)} %slice.64), channel_id=1, source_target_pairs={{1,0},{2,1},{3,2},{4,3},{5,4},{6,5},{7,6},{8,7},{9,8},{10,9},{11,1... | collective-permute-start | bytes 6920 | tf_op jit(solution)/shard_map/ppermute | solution.py:54
  105.6 8.3 %all-to-all-done.1 = bf16[128,1,4,4,384]{4,2,3,1,0:T(4,128)(2,1)} async-done(((bf16[128,1,4,4,384]{4,2,3,1,0:T(4,128)(2,1)}), bf16[128,1,4,4,384]{4,2,3,1,0:T(4,128)(2,1)}, u32[]{:S(2)}, u32[]{:S(2)}) %all-to-all-start.1) | async-done | bytes 1572896 | tf_op jit(solution)/shard_map/all_to_all | solution.py:86
  113.9 2.4 %convolution_convert_fusion = bf16[4,256,512]{2,1,0:T(8,128)(2,1)S(1)} fusion(bf16[4,512,384]{2,0,1:T(4,128)(2,1)} %bitcast.23, bf16[1,4,512,384]{3,2,1,0:T(8,128)(2,1)} %bitcast.59, s32[]{:T(128)S(6)} %select_n.15), kind=kOutput, calls=%fused_computation.31 | convolution fusion | flops 403177472 | bytes 3407876 | tf_op jit(solution)/shard_map/skmd,skid->kmi/dot_general | solution.py:95
  116.3 8.3 %collective-permute-start.3 = (bf16[4,256,512]{2,1,0:T(8,128)(2,1)S(1)}, bf16[4,256,512]{2,1,0:T(8,128)(2,1)S(1)}, u32[]{:S(2)}, u32[]{:S(2)}) collective-permute-start(bf16[4,256,512]{2,1,0:T(8,128)(2,1)S(1)} %convolution_convert_fusion), channel_id=1, source_target_pairs={{0,128},{128,0},{1,129},{129,1},{2,130},{130,2},{3,131},{131,3},{4... | collective-permute-start | bytes 3145736 | tf_op jit(solution)/shard_map/ppermute | solution.py:106
  124.9 2.2 %convolution_convert_fusion.1 = bf16[4,256,512]{2,1,0:T(8,128)(2,1)S(1)} fusion(bf16[4,512,384]{2,0,1:T(4,128)(2,1)} %bitcast.23, bf16[1,4,512,384]{3,2,1,0:T(8,128)(2,1)S(1)} %bitcast.60, s32[]{:T(128)S(6)} %select_n.14), kind=kOutput, calls=%fused_computation.32 | convolution fusion | flops 403177472 | bytes 3407876 | tf_op jit(solution)/shard_map/skmd,skid->kmi/dot_general | solution.py:95
  127.0 2.5 %fusion.1 = bf16[1,2048,384]{2,1,0:T(8,128)(2,1)} fusion(f32[1,2051,384]{2,1,0:T(8,128)S(1)} %maximum_convert_fusion.1, f32[384]{0:T(512)S(1)} %get-tuple-element.11, f32[384]{0:T(512)S(1)} %get-tuple-element.12, f32[384]{0:T(512)S(1)} %get-tuple-element.10, f32[384]{0:T(512)S(1)} %get-tuple-element.9), kind=kLoop, calls=%fused_computation.2 | loop fusion | flops 6291456 | bytes 14161920 | tf_op jit(solution)/shard_map/convert_element_type | solution.py:120
  129.6 6.4 %collective-permute-done.2 = bf16[4,256,512]{2,0,1:T(4,128)(2,1)} collective-permute-done((bf16[4,256,512]{2,0,1:T(4,128)(2,1)}, bf16[4,256,512]{2,0,1:T(4,128)(2,1)}, u32[]{:S(2)}, u32[]{:S(2)}) %collective-permute-start.2) | collective-permute-done | bytes 1048608 | tf_op jit(solution)/shard_map/ppermute | solution.py:107
  136.0 1.9 %fusion.9 = bf16[4,256,512]{2,0,1:T(4,128)(2,1)S(1)} fusion(f32[4,64,4,512]{3,0,2,1:T(4,128)S(1)} %copy-done.1, bf16[4,256,512]{2,0,1:T(4,128)(2,1)} %collective-permute-done.2), kind=kLoop, calls=%fused_computation.21 | loop fusion | flops 1572864 | bytes 4194304 | tf_op jit(solution)/shard_map/convert_element_type | solution.py:114
  139.1 19.3 %collective-permute-done.3 = bf16[4,256,512]{2,1,0:T(8,128)(2,1)S(1)} collective-permute-done((bf16[4,256,512]{2,1,0:T(8,128)(2,1)S(1)}, bf16[4,256,512]{2,1,0:T(8,128)(2,1)S(1)}, u32[]{:S(2)}, u32[]{:S(2)}) %collective-permute-start.3) | collective-permute-done | bytes 1048608 | tf_op jit(solution)/shard_map/ppermute | solution.py:106
  (28 shorter events, 10.4 us)
Async XLA Ops:
  4.9 16.6 %copy-start.4 = (bf16[1,2048,384]{2,1,0:T(8,128)(2,1)S(1)}, bf16[1,2048,384]{2,1,0:T(8,128)(2,1)}, u32[]{:S(2)}) copy-start(bf16[1,2048,384]{2,1,0:T(8,128)(2,1)} %param.5) | copy-start | bytes 4718596
  4.9 20.1 %copy-start.6 = (f32[4,384]{1,0:T(4,128)S(1)}, f32[4,384]{1,0:T(4,128)}, u32[]{:S(2)}) copy-start(f32[4,384]{1,0:T(4,128)} %param.6) | copy-start | bytes 18436
  4.9 57.5 %all-to-all-start = ((bf16[128,4,1536]{2,1,0:T(4,128)(2,1)}), bf16[128,4,1536]{2,1,0:T(4,128)(2,1)S(1)}, u32[]{:S(2)}, u32[]{:S(2)}) async-start(bf16[128,4,1536]{2,1,0:T(4,128)(2,1)} %shard_map.76), calls=%async_computation | async-start | bytes 3145728 | tf_op jit(solution)/shard_map/all_to_all | solution.py:83
  21.5 7.6 %collective-permute-start = (bf16[1,3,384]{2,1,0:T(4,128)(2,1)S(1)}, bf16[1,3,384]{2,1,0:T(4,128)(2,1)S(1)}, u32[]{:S(2)}, u32[]{:S(2)}) collective-permute-start(bf16[1,3,384]{2,1,0:T(4,128)(2,1)S(1)} %slice.47), channel_id=1, source_target_pairs={{0,1},{1,2},{2,3},{3,4},{4,5},{5,6},{6,7},{7,8},{8,9},{9,10},{10,1... | collective-permute-start | bytes 6920 | tf_op jit(solution)/shard_map/ppermute | solution.py:54
  29.5 3.1 %copy-start = (bf16[4,128,4,512]{3,2,1,0:T(4,128)(2,1)S(1)}, bf16[4,128,4,512]{3,2,1,0:T(4,128)(2,1)}, u32[]{:S(2)}) copy-start(bf16[4,128,4,512]{3,2,1,0:T(4,128)(2,1)} %reshape.128) | copy-start | bytes 6291460
  62.4 51.5 %all-to-all-start.1 = ((bf16[128,1,4,4,384]{4,2,3,1,0:T(4,128)(2,1)}), bf16[128,1,4,4,384]{4,2,3,1,0:T(4,128)(2,1)}, u32[]{:S(2)}, u32[]{:S(2)}) async-start(bf16[128,1,4,4,384]{4,2,3,1,0:T(4,128)(2,1)} %copy.36), calls=%async_computation.1 | async-start | bytes 3145728 | tf_op jit(solution)/shard_map/all_to_all | solution.py:86
  86.7 49.4 %collective-permute-start.2 = (bf16[4,256,512]{2,0,1:T(4,128)(2,1)}, bf16[4,256,512]{2,0,1:T(4,128)(2,1)}, u32[]{:S(2)}, u32[]{:S(2)}) collective-permute-start(bf16[4,256,512]{2,0,1:T(4,128)(2,1)} %bitcast.15), channel_id=1, source_target_pairs={{0,128},{128,0},{1,129},{129,1},{2,130},{130,2},{3,131},{131,3},{4... | collective-permute-start | bytes 3145736 | tf_op jit(solution)/shard_map/ppermute | solution.py:107
  101.0 1.1 copy-start.2
  102.2 22.5 %copy-start.3 = (bf16[1,2048,384]{2,1,0:T(8,128)(2,1)S(1)}, bf16[1,2048,384]{2,1,0:T(8,128)(2,1)}, u32[]{:S(2)}) copy-start(bf16[1,2048,384]{2,1,0:T(8,128)(2,1)} %copy-done.2) | copy-start | bytes 4718596
  102.2 22.5 %collective-permute-start.1 = (bf16[1,3,384]{2,1,0:T(4,128)(2,1)S(1)}, bf16[1,3,384]{2,1,0:T(4,128)(2,1)S(1)}, u32[]{:S(2)}, u32[]{:S(2)}) collective-permute-start(bf16[1,3,384]{2,1,0:T(4,128)(2,1)S(1)} %slice.64), channel_id=1, source_target_pairs={{1,0},{2,1},{3,2},{4,3},{5,4},{6,5},{7,6},{8,7},{9,8},{10,9},{11,1... | collective-permute-start | bytes 6920 | tf_op jit(solution)/shard_map/ppermute | solution.py:54
  116.3 8.5 %copy-start.5 = (bf16[1,2048,384]{2,1,0:T(8,128)(2,1)S(1)}, bf16[1,2048,384]{2,1,0:T(8,128)(2,1)}, u32[]{:S(2)}) copy-start(bf16[1,2048,384]{2,1,0:T(8,128)(2,1)} %param.9) | copy-start | bytes 4718596
  116.3 42.1 %collective-permute-start.3 = (bf16[4,256,512]{2,1,0:T(8,128)(2,1)S(1)}, bf16[4,256,512]{2,1,0:T(8,128)(2,1)S(1)}, u32[]{:S(2)}, u32[]{:S(2)}) collective-permute-start(bf16[4,256,512]{2,1,0:T(8,128)(2,1)S(1)} %convolution_convert_fusion), channel_id=1, source_target_pairs={{0,128},{128,0},{1,129},{129,1},{2,130},{130,2},{3,131},{131,3},{4... | collective-permute-start | bytes 3145736 | tf_op jit(solution)/shard_map/ppermute | solution.py:106
  127.0 9.0 %copy-start.1 = (f32[4,64,4,512]{3,0,2,1:T(4,128)S(1)}, f32[4,64,4,512]{3,0,2,1:T(4,128)}, u32[]{:S(2)}) copy-start(f32[4,64,4,512]{3,0,2,1:T(4,128)} %copy.31) | copy-start | bytes 6291460

commit v18 on v16

--- a/solution.py
+++ b/solution.py
@@ -117,8 +117,8 @@
         "ipqj,psiqd->sijd", first_split, grad_rows, preferred_element_type=jnp.float32
     ).reshape(seq_count, tok_rows, channels)
     kept = lambda part: lax.reduce_precision(part.astype(jnp.float32), exponent_bits=8, mantissa_bits=7)
-    own_second = lax.optimization_barrier(kept(second_part(me)))
-    part_second = (own_second + sent_second.astype(jnp.float32)).astype(jnp.bfloat16)
+    own_second = lax.optimization_barrier(second_part(me))
+    part_second = (own_second.astype(jnp.float32) + sent_second.astype(jnp.float32)).astype(jnp.bfloat16)
     part_first = (kept(first_part(me)) + sent_first.astype(jnp.float32)).astype(jnp.bfloat16)
     grad_conv = (grad_hidden * gate_val * (1.0 + conv_out * (1.0 - gate_val))).astype(jnp.bfloat16)
     following = passed_along(grad_conv[:, : tap_count - 1, :], "seq", -1)

time: 160 us -> 160 us (level)
  no operation moved by 1% of the time
where the time goes in v18:
time: 160 us; the launch traced here: 159 us
  waiting for transfers between devices  57.5 us (36%)
  starting transfers between devices  49.4 us (31%)
  local copies, waits for them, and re-layouts  22 us (14%)
  matrix products  12.9 us (8%)
  other arithmetic  12.7 us (8%)
  Pallas kernels  3.92 us (2%)
    all_to_all x1, waiting for transfers between devices, body(): lax.all_to_all(grad_chunks, 'seq', split_axis=0, concat_axis=0, tiled=True)  23.4 us
    ppermute x1, waiting for transfers between devices, body(): sent_second = lax.ppermute(second_part(other), 'batch', swap)  19.3 us
    all_to_all x1, starting transfers between devices, body(): lax.all_to_all(grad_chunks, 'seq', split_axis=0, concat_axis=0, tiled=True)  16.5 us
    all_to_all x1, starting transfers between devices, body(): lax.all_to_all(mixed_chunks, 'seq', split_axis=0, concat_axis=3, tiled=True)  14.8 us
    all_to_all x1, waiting for transfers between devices, body(): lax.all_to_all(mixed_chunks, 'seq', split_axis=0, concat_axis=3, tiled=True)  8.33 us
    ppermute x1, starting transfers between devices, body(): sent_second = lax.ppermute(second_part(other), 'batch', swap)  8.32 us
    ppermute x2, starting transfers between devices, passed_along(): lax.ppermute(value, axis, [(source, source + steps) for source in range(i...  6.97 us
    ppermute x1, waiting for transfers between devices, body(): sent_first = lax.ppermute(first_part(other), 'batch', swap)  6.45 us
  transfers between devices with their start and end apart: 6, of which 4 were waited for; matrix products, arithmetic and copies ran while one was open for 28% of the time, Pallas kernels for 0%

profile of v18, /device:TPU:1, one launch (start us, length us, event | category | flops | bytes accessed | tf_op | source)
XLA Modules:
  0.0 159.4 jit_solution(7431407903947540659)
XLA Ops:
  0.6 3.9 %shard_map.76 = bf16[128,4,1536]{2,1,0:T(4,128)(2,1)} custom-call(bf16[4,512,512]{2,1,0:T(8,128)(2,1)} %s_hbm.1, bf16[4,512,384]{2,1,0:T(8,128)(2,1)} %bitcast.58), custom_call_target="tpu_custom_call" | custom-call | flops 805306368 | bytes 5242880 | tf_op jit(solution)/shard_map/pallas_call | solution.py:42
  4.6 16.5 %all-to-all-start = ((bf16[128,4,1536]{2,1,0:T(4,128)(2,1)}), bf16[128,4,1536]{2,1,0:T(4,128)(2,1)S(1)}, u32[]{:S(2)}, u32[]{:S(2)}) async-start(bf16[128,4,1536]{2,1,0:T(4,128)(2,1)} %shard_map.76), calls=%async_computation | async-start | bytes 3145728 | tf_op jit(solution)/shard_map/all_to_all | solution.py:91
  21.2 3.5 %collective-permute-start = (bf16[1,3,384]{2,1,0:T(4,128)(2,1)S(1)}, bf16[1,3,384]{2,1,0:T(4,128)(2,1)S(1)}, u32[]{:S(2)}, u32[]{:S(2)}) collective-permute-start(bf16[1,3,384]{2,1,0:T(4,128)(2,1)S(1)} %slice.47), channel_id=1, source_target_pairs={{0,1},{1,2},{2,3},{3,4},{4,5},{5,6},{6,7},{7,8},{8,9},{9,10},{10,1... | collective-permute-start | bytes 6920 | tf_op jit(solution)/shard_map/ppermute | solution.py:62
  24.7 4.0 %reshape.128 = bf16[4,128,4,512]{3,2,1,0:T(4,128)(2,1)} reshape(bf16[4,512,512]{2,1,0:T(8,128)(2,1)} %param.7) | data formatting | bytes 4194304 | tf_op jit(solution)/shard_map/reshape | solution.py:85
  29.1 3.1 %multiply_convert_fusion = (bf16[1,2048,384]{2,1,0:T(8,128)(2,1)S(1)}, f32[1,2048,384]{2,1,0:T(8,128)}) fusion(f32[1,2051,384]{2,1,0:T(8,128)S(1)} %maximum_convert_fusion, f32[384]{0:T(512)S(1)} %get-tuple-element.11, f32[384]{0:T(512)S(1)} %get-tuple-element.12, f32[384]{0:T(512)S(1)} %get-tuple-element.10, f32[384]{0:T(512)S(1)} %get-tuple-element.9), kind=kLoop, calls=%fused_computation.18 | loop fusion | flops 9437184 | bytes 17307648 | tf_op jit(solution)/shard_map/convert_element_type | solution.py:83
  32.2 2.6 %fusion.16 = bf16[128,1,4,4,384]{0,4,2,3,1:T(8,128)(2,1)} fusion(bf16[4,512,384,1]{2,1,3,0:T(8,128)(2,1)S(1)} %bitcast.54, bf16[4,128,4,512]{3,2,1,0:T(4,128)(2,1)S(1)} %copy-done), kind=kOutput, calls=%fused_computation.35 | convolution fusion | flops 806092800 | bytes 5242880 | tf_op jit(solution)/shard_map/ipqj,sijd->psqid/dot_general | solution.py:86
  34.8 3.9 %copy.36 = bf16[128,1,4,4,384]{4,2,3,1,0:T(4,128)(2,1)} copy(bf16[128,1,4,4,384]{0,4,2,3,1:T(8,128)(2,1)} %fusion.16) | data formatting | bytes 3145728 | tf_op jit(solution)/shard_map/convert_element_type | solution.py:88
  38.7 23.4 %all-to-all-done = bf16[128,4,1536]{2,1,0:T(4,128)(2,1)S(1)} async-done(((bf16[128,4,1536]{2,1,0:T(4,128)(2,1)}), bf16[128,4,1536]{2,1,0:T(4,128)(2,1)S(1)}, u32[]{:S(2)}, u32[]{:S(2)}) %all-to-all-start) | async-done | bytes 1572896 | tf_op jit(solution)/shard_map/all_to_all | solution.py:91
  62.1 14.8 %all-to-all-start.1 = ((bf16[128,1,4,4,384]{4,2,3,1,0:T(4,128)(2,1)}), bf16[128,1,4,4,384]{4,2,3,1,0:T(4,128)(2,1)}, u32[]{:S(2)}, u32[]{:S(2)}) async-start(bf16[128,1,4,4,384]{4,2,3,1,0:T(4,128)(2,1)} %copy.36), calls=%async_computation.1 | async-start | bytes 3145728 | tf_op jit(solution)/shard_map/all_to_all | solution.py:94
  78.4 1.9 %constant_dynamic-slice_fusion = (bf16[64,1,4,4,384]{4,3,2,0,1:T(4,128)(2,1)S(1)}, bf16[64,1,4,4,384]{4,3,2,0,1:T(4,128)(2,1)S(1)}) fusion(bf16[128,1,4,4,384]{4,3,2,0,1:T(4,128)(2,1)} %reshape.130, s32[]{:T(128)S(6)} %select_n.13, s32[]{:T(128)S(6)} %select_n.12), kind=kLoop, calls=%fused_computation.52 | loop fusion | bytes 3145736 | tf_op jit(solution)/shard_map/dynamic_slice | solution.py:108
  81.1 2.7 %copy.31 = f32[4,64,4,512]{3,0,2,1:T(4,128)} copy(f32[4,64,4,512]{3,1,2,0:T(8,128)S(1)} %convert_reduce-precision_fusion) | data formatting | bytes 4194304 | tf_op jit(solution)/shard_map/reduce_precision | solution.py:119
  86.3 2.8 %collective-permute-start.2 = (bf16[4,256,512]{2,0,1:T(4,128)(2,1)}, bf16[4,256,512]{2,0,1:T(4,128)(2,1)}, u32[]{:S(2)}, u32[]{:S(2)}) collective-permute-start(bf16[4,256,512]{2,0,1:T(4,128)(2,1)} %bitcast.15), channel_id=1, source_target_pairs={{0,128},{128,0},{1,129},{129,1},{2,130},{130,2},{3,131},{131,3},{4... | collective-permute-start | bytes 3145736 | tf_op jit(solution)/shard_map/ppermute | solution.py:115
  90.5 4.3 %convolution_bitcast_fusion = f32[1,4,512,384]{2,3,1,0:T(8,128)} fusion(bf16[128,4,4,384]{0,3,2,1:T(8,128)(2,1)S(1)} %bitcast.57, bf16[4,128,4,512]{3,2,1,0:T(4,128)(2,1)} %reshape.128), kind=kOutput, calls=%fused_computation.24 | convolution fusion | flops 805306368 | bytes 6815744 | tf_op jit(solution)/shard_map/ipqj,psiqd->sijd/dot_general | solution.py:116
  94.9 2.4 %copy.29 = f32[1,4,512,384]{3,2,1,0:T(8,128)S(1)} copy(f32[1,4,512,384]{2,3,1,0:T(8,128)} %convolution_bitcast_fusion) | data formatting | bytes 6291456 | tf_op jit(solution)/shard_map/ipqj,psiqd->sijd/transpose | solution.py:116
  97.3 3.4 %fusion.8 = bf16[1,2048,384]{2,1,0:T(8,128)(2,1)S(1)} fusion(f32[1,4,512,384]{3,2,1,0:T(8,128)S(1)} %copy.29, f32[1,2048,384]{2,1,0:T(8,128)} %get-tuple-element.14), kind=kLoop, calls=%fused_computation.17 | loop fusion | flops 7077888 | bytes 7864320 | tf_op jit(solution)/shard_map/convert_element_type | solution.py:123
  101.8 3.4 %collective-permute-start.1 = (bf16[1,3,384]{2,1,0:T(4,128)(2,1)S(1)}, bf16[1,3,384]{2,1,0:T(4,128)(2,1)S(1)}, u32[]{:S(2)}, u32[]{:S(2)}) collective-permute-start(bf16[1,3,384]{2,1,0:T(4,128)(2,1)S(1)} %slice.64), channel_id=1, source_target_pairs={{1,0},{2,1},{3,2},{4,3},{5,4},{6,5},{7,6},{8,7},{9,8},{10,9},{11,1... | collective-permute-start | bytes 6920 | tf_op jit(solution)/shard_map/ppermute | solution.py:62
  105.2 8.3 %all-to-all-done.1 = bf16[128,1,4,4,384]{4,2,3,1,0:T(4,128)(2,1)} async-done(((bf16[128,1,4,4,384]{4,2,3,1,0:T(4,128)(2,1)}), bf16[128,1,4,4,384]{4,2,3,1,0:T(4,128)(2,1)}, u32[]{:S(2)}, u32[]{:S(2)}) %all-to-all-start.1) | async-done | bytes 1572896 | tf_op jit(solution)/shard_map/all_to_all | solution.py:94
  113.6 2.4 %convolution_convert_fusion = bf16[4,256,512]{2,1,0:T(8,128)(2,1)S(1)} fusion(bf16[4,512,384]{2,0,1:T(4,128)(2,1)} %bitcast.23, bf16[1,4,512,384]{3,2,1,0:T(8,128)(2,1)} %bitcast.59, s32[]{:T(128)S(6)} %select_n.15), kind=kOutput, calls=%fused_computation.31 | convolution fusion | flops 403177472 | bytes 3407876 | tf_op jit(solution)/shard_map/skmd,skid->kmi/dot_general | solution.py:103
  116.0 8.3 %collective-permute-start.3 = (bf16[4,256,512]{2,1,0:T(8,128)(2,1)S(1)}, bf16[4,256,512]{2,1,0:T(8,128)(2,1)S(1)}, u32[]{:S(2)}, u32[]{:S(2)}) collective-permute-start(bf16[4,256,512]{2,1,0:T(8,128)(2,1)S(1)} %convolution_convert_fusion), channel_id=1, source_target_pairs={{0,128},{128,0},{1,129},{129,1},{2,130},{130,2},{3,131},{131,3},{4... | collective-permute-start | bytes 3145736 | tf_op jit(solution)/shard_map/ppermute | solution.py:114
  124.5 2.2 %convolution_convert_fusion.1 = bf16[4,256,512]{2,1,0:T(8,128)(2,1)S(1)} fusion(bf16[4,512,384]{2,0,1:T(4,128)(2,1)} %bitcast.23, bf16[1,4,512,384]{3,2,1,0:T(8,128)(2,1)S(1)} %bitcast.60, s32[]{:T(128)S(6)} %select_n.14), kind=kOutput, calls=%fused_computation.32 | convolution fusion | flops 403177472 | bytes 3407876 | tf_op jit(solution)/shard_map/skmd,skid->kmi/dot_general | solution.py:103
  126.7 2.5 %fusion.1 = bf16[1,2048,384]{2,1,0:T(8,128)(2,1)} fusion(f32[1,2051,384]{2,1,0:T(8,128)S(1)} %maximum_convert_fusion.1, f32[384]{0:T(512)S(1)} %get-tuple-element.11, f32[384]{0:T(512)S(1)} %get-tuple-element.12, f32[384]{0:T(512)S(1)} %get-tuple-element.10, f32[384]{0:T(512)S(1)} %get-tuple-element.9), kind=kLoop, calls=%fused_computation.2 | loop fusion | flops 6291456 | bytes 14161920 | tf_op jit(solution)/shard_map/convert_element_type | solution.py:128
  129.2 6.4 %collective-permute-done.2 = bf16[4,256,512]{2,0,1:T(4,128)(2,1)} collective-permute-done((bf16[4,256,512]{2,0,1:T(4,128)(2,1)}, bf16[4,256,512]{2,0,1:T(4,128)(2,1)}, u32[]{:S(2)}, u32[]{:S(2)}) %collective-permute-start.2) | collective-permute-done | bytes 1048608 | tf_op jit(solution)/shard_map/ppermute | solution.py:115
  135.7 1.9 %fusion.9 = bf16[4,256,512]{2,0,1:T(4,128)(2,1)S(1)} fusion(f32[4,64,4,512]{3,0,2,1:T(4,128)S(1)} %copy-done.1, bf16[4,256,512]{2,0,1:T(4,128)(2,1)} %collective-permute-done.2), kind=kLoop, calls=%fused_computation.21 | loop fusion | flops 1572864 | bytes 4194304 | tf_op jit(solution)/shard_map/convert_element_type | solution.py:122
  138.8 19.3 %collective-permute-done.3 = bf16[4,256,512]{2,1,0:T(8,128)(2,1)S(1)} collective-permute-done((bf16[4,256,512]{2,1,0:T(8,128)(2,1)S(1)}, bf16[4,256,512]{2,1,0:T(8,128)(2,1)S(1)}, u32[]{:S(2)}, u32[]{:S(2)}) %collective-permute-start.3) | collective-permute-done | bytes 1048608 | tf_op jit(solution)/shard_map/ppermute | solution.py:114
  (28 shorter events, 10.4 us)
Async XLA Ops:
  4.6 16.6 %copy-start.4 = (bf16[1,2048,384]{2,1,0:T(8,128)(2,1)S(1)}, bf16[1,2048,384]{2,1,0:T(8,128)(2,1)}, u32[]{:S(2)}) copy-start(bf16[1,2048,384]{2,1,0:T(8,128)(2,1)} %param.5) | copy-start | bytes 4718596
  4.6 20.1 %copy-start.6 = (f32[4,384]{1,0:T(4,128)S(1)}, f32[4,384]{1,0:T(4,128)}, u32[]{:S(2)}) copy-start(f32[4,384]{1,0:T(4,128)} %param.6) | copy-start | bytes 18436
  4.6 57.5 %all-to-all-start = ((bf16[128,4,1536]{2,1,0:T(4,128)(2,1)}), bf16[128,4,1536]{2,1,0:T(4,128)(2,1)S(1)}, u32[]{:S(2)}, u32[]{:S(2)}) async-start(bf16[128,4,1536]{2,1,0:T(4,128)(2,1)} %shard_map.76), calls=%async_computation | async-start | bytes 3145728 | tf_op jit(solution)/shard_map/all_to_all | solution.py:91
  21.2 7.6 %collective-permute-start = (bf16[1,3,384]{2,1,0:T(4,128)(2,1)S(1)}, bf16[1,3,384]{2,1,0:T(4,128)(2,1)S(1)}, u32[]{:S(2)}, u32[]{:S(2)}) collective-permute-start(bf16[1,3,384]{2,1,0:T(4,128)(2,1)S(1)} %slice.47), channel_id=1, source_target_pairs={{0,1},{1,2},{2,3},{3,4},{4,5},{5,6},{6,7},{7,8},{8,9},{9,10},{10,1... | collective-permute-start | bytes 6920 | tf_op jit(solution)/shard_map/ppermute | solution.py:62
  29.1 3.1 %copy-start = (bf16[4,128,4,512]{3,2,1,0:T(4,128)(2,1)S(1)}, bf16[4,128,4,512]{3,2,1,0:T(4,128)(2,1)}, u32[]{:S(2)}) copy-start(bf16[4,128,4,512]{3,2,1,0:T(4,128)(2,1)} %reshape.128) | copy-start | bytes 6291460
  62.1 51.5 %all-to-all-start.1 = ((bf16[128,1,4,4,384]{4,2,3,1,0:T(4,128)(2,1)}), bf16[128,1,4,4,384]{4,2,3,1,0:T(4,128)(2,1)}, u32[]{:S(2)}, u32[]{:S(2)}) async-start(bf16[128,1,4,4,384]{4,2,3,1,0:T(4,128)(2,1)} %copy.36), calls=%async_computation.1 | async-start | bytes 3145728 | tf_op jit(solution)/shard_map/all_to_all | solution.py:94
  86.3 49.4 %collective-permute-start.2 = (bf16[4,256,512]{2,0,1:T(4,128)(2,1)}, bf16[4,256,512]{2,0,1:T(4,128)(2,1)}, u32[]{:S(2)}, u32[]{:S(2)}) collective-permute-start(bf16[4,256,512]{2,0,1:T(4,128)(2,1)} %bitcast.15), channel_id=1, source_target_pairs={{0,128},{128,0},{1,129},{129,1},{2,130},{130,2},{3,131},{131,3},{4... | collective-permute-start | bytes 3145736 | tf_op jit(solution)/shard_map/ppermute | solution.py:115
  100.6 1.1 copy-start.2
  101.8 22.5 %copy-start.3 = (bf16[1,2048,384]{2,1,0:T(8,128)(2,1)S(1)}, bf16[1,2048,384]{2,1,0:T(8,128)(2,1)}, u32[]{:S(2)}) copy-start(bf16[1,2048,384]{2,1,0:T(8,128)(2,1)} %copy-done.2) | copy-start | bytes 4718596
  101.8 22.5 %collective-permute-start.1 = (bf16[1,3,384]{2,1,0:T(4,128)(2,1)S(1)}, bf16[1,3,384]{2,1,0:T(4,128)(2,1)S(1)}, u32[]{:S(2)}, u32[]{:S(2)}) collective-permute-start(bf16[1,3,384]{2,1,0:T(4,128)(2,1)S(1)} %slice.64), channel_id=1, source_target_pairs={{1,0},{2,1},{3,2},{4,3},{5,4},{6,5},{7,6},{8,7},{9,8},{10,9},{11,1... | collective-permute-start | bytes 6920 | tf_op jit(solution)/shard_map/ppermute | solution.py:62
  116.0 8.5 %copy-start.5 = (bf16[1,2048,384]{2,1,0:T(8,128)(2,1)S(1)}, bf16[1,2048,384]{2,1,0:T(8,128)(2,1)}, u32[]{:S(2)}) copy-start(bf16[1,2048,384]{2,1,0:T(8,128)(2,1)} %param.9) | copy-start | bytes 4718596
  116.0 42.1 %collective-permute-start.3 = (bf16[4,256,512]{2,1,0:T(8,128)(2,1)S(1)}, bf16[4,256,512]{2,1,0:T(8,128)(2,1)S(1)}, u32[]{:S(2)}, u32[]{:S(2)}) collective-permute-start(bf16[4,256,512]{2,1,0:T(8,128)(2,1)S(1)} %convolution_convert_fusion), channel_id=1, source_target_pairs={{0,128},{128,0},{1,129},{129,1},{2,130},{130,2},{3,131},{131,3},{4... | collective-permute-start | bytes 3145736 | tf_op jit(solution)/shard_map/ppermute | solution.py:114
  126.7 9.0 %copy-start.1 = (f32[4,64,4,512]{3,0,2,1:T(4,128)S(1)}, f32[4,64,4,512]{3,0,2,1:T(4,128)}, u32[]{:S(2)}) copy-start(f32[4,64,4,512]{3,0,2,1:T(4,128)} %copy.31) | copy-start | bytes 6291460
